TPU v7x, 32 devices: a whole 2x2x4 slice. The times are simulated.
32 devices in a mesh: lat: 4 (over y, x), lon: 8 (over z, core).
Axes of the slice: x: 2, y: 2, z: 4, core: 2. Of those that a mesh axis runs over, the one named last changes fastest.
Arguments:
- fine_map: bfloat16 [4, 48, 256, 400], P(None, 'lat', 'lon'), may hold values from -26 to 26
- ocean_mask: int32 [4, 48, 256], P(None, 'lat', 'lon'), may hold values from 0 to 1
- out_grad: bfloat16 [4, 48, 256, 400], P(None, 'lat', 'lon'), may hold values from -6 to 6
- encode_depth: bfloat16 [7, 7, 400], replicated, may hold values from -0.875 to 0.875
- encode_gain: bfloat16 [400], replicated, may hold values from 0.099609375 to 1.8984375
- encode_shift: bfloat16 [400], replicated, may hold values from -3 to 3
- encode_up: bfloat16 [400, 1600], P('lat'), may hold values from -0.3125 to 0.3125
- encode_up_bias: bfloat16 [1600], replicated, may hold values from -3 to 3
- encode_down: bfloat16 [1600, 400], P('lat'), may hold values from -0.15625 to 0.15625
- encode_down_bias: bfloat16 [400], replicated, may hold values from -3 to 3
- widen_weight: bfloat16 [400, 800], P('lat'), may hold values from -0.3125 to 0.3125
- widen_bias: bfloat16 [800], replicated, may hold values from -3 to 3
- bottle_depth: bfloat16 [7, 7, 800], replicated, may hold values from -0.875 to 0.875
- bottle_gain: bfloat16 [800], replicated, may hold values from 0.099609375 to 1.8984375
- bottle_shift: bfloat16 [800], replicated, may hold values from -3 to 3
- bottle_up: bfloat16 [800, 3200], P('lat'), may hold values from -0.21875 to 0.21875
- bottle_up_bias: bfloat16 [3200], replicated, may hold values from -3 to 3
- bottle_down: bfloat16 [3200, 800], P('lat'), may hold values from -0.109375 to 0.109375
- bottle_down_bias: bfloat16 [800], replicated, may hold values from -3 to 3
- merge_weight: bfloat16 [1200, 400], P('lat'), may hold values from -0.1875 to 0.1875
- merge_bias: bfloat16 [400], replicated, may hold values from -3 to 3
- decode_depth: bfloat16 [7, 7, 400], replicated, may hold values from -0.875 to 0.875
- decode_gain: bfloat16 [400], replicated, may hold values from 0.099609375 to 1.8984375
- decode_shift: bfloat16 [400], replicated, may hold values from -3 to 3
- decode_up: bfloat16 [400, 1600], P('lat'), may hold values from -0.3125 to 0.3125
- decode_up_bias: bfloat16 [1600], replicated, may hold values from -3 to 3
- decode_down: bfloat16 [1600, 400], P('lat'), may hold values from -0.15625 to 0.15625
- decode_down_bias: bfloat16 [400], replicated, may hold values from -3 to 3
Outputs:
- result: bfloat16 [4, 48, 256, 400], P(None, 'lat', 'lon')
- fine_grad: bfloat16 [4, 48, 256, 400], P(None, 'lat', 'lon')
- encode_depth_grad: float32 [7, 7, 400], replicated
- encode_gain_grad: float32 [400], replicated
- encode_shift_grad: float32 [400], replicated
- encode_up_grad: float32 [400, 1600], replicated
- encode_up_bias_grad: float32 [1600], replicated
- encode_down_grad: float32 [1600, 400], replicated
- encode_down_bias_grad: float32 [400], replicated
- widen_weight_grad: float32 [400, 800], replicated
- widen_bias_grad: float32 [800], replicated
- bottle_depth_grad: float32 [7, 7, 800], replicated
- bottle_gain_grad: float32 [800], replicated
- bottle_shift_grad: float32 [800], replicated
- bottle_up_grad: float32 [800, 3200], replicated
- bottle_up_bias_grad: float32 [3200], replicated
- bottle_down_grad: float32 [3200, 800], replicated
- bottle_down_bias_grad: float32 [800], replicated
- merge_weight_grad: float32 [1200, 400], replicated
- merge_bias_grad: float32 [400], replicated
- decode_depth_grad: float32 [7, 7, 400], replicated
- decode_gain_grad: float32 [400], replicated
- decode_shift_grad: float32 [400], replicated
- decode_up_grad: float32 [400, 1600], replicated
- decode_up_bias_grad: float32 [1600], replicated
- decode_down_grad: float32 [1600, 400], replicated
- decode_down_bias_grad: float32 [400], replicated
All inputs are finite; a program needn't handle non-finite values.
Results may differ from a plain program's by a relative error of at most 0.018.
Values may be sent and summed in bfloat16 or wider, within the bound.
No kernel may reach another device: no remote copies, remote signals or barrier semaphores. Data moves between devices by JAX's collectives and lax.ppermute only.
A program may use at most 320 MiB of HBM per device.

v0:
```python
import math

import jax
import jax.numpy as jnp
from jax import lax
from jax.sharding import PartitionSpec as P

epsilon = 1e-05


def padded(block, sides, width, periodic):
    for axis, dim in sides:
        count = lax.axis_size(axis)
        forward = [(i, i + 1) for i in range(count - 1)]
        if periodic:
            forward.append((count - 1, 0))
        backward = [(target, source) for source, target in forward]
        low = lax.ppermute(
            lax.slice_in_dim(block, block.shape[dim] - width, None, axis=dim), axis, forward
        )
        high = lax.ppermute(lax.slice_in_dim(block, 0, width, axis=dim), axis, backward)
        block = jnp.concatenate([low, block, high], axis=dim)
    return block


def widen_map(source):
    wrapped = padded(source, (("lon", 2),), 3, True)
    return padded(wrapped, (("lat", 1),), 3, False)


def stencil(extended, kernel, height, breadth):
    taps = kernel.astype(jnp.float32)
    summed = jnp.zeros((extended.shape[0], height, breadth, extended.shape[3]), jnp.float32)
    for across in range(7):
        for column in range(7):
            summed = summed + taps[across, column] * extended[
                :, across : across + height, column : column + breadth, :
            ].astype(jnp.float32)
    return summed


def kernel_terms(extended, grad_mixed, height, breadth):
    upstream = grad_mixed.astype(jnp.float32)
    all_rows = []
    for across in range(7):
        row_terms = []
        for column in range(7):
            window = extended[:, across : across + height, column : column + breadth, :].astype(
                jnp.float32
            )
            row_terms.append(jnp.sum(window * upstream, axis=(0, 1, 2)))
        all_rows.append(jnp.stack(row_terms))
    return jnp.stack(all_rows)


def cross_rows(former, latter):
    return lax.dot_general(
        former, latter, (((0,), (0,)), ((), ())), preferred_element_type=jnp.float32
    )


def by_transpose(former, latter):
    return lax.dot_general(
        former, latter, (((1,), (1,)), ((), ())), preferred_element_type=jnp.float32
    )


def exact_gelu(values):
    return jax.nn.gelu(values, approximate=False)


def block_forward(source, params, sea_mask):
    kernel, scale_gain, norm_shift, up_weight, up_bias, down_weight, down_bias = params
    date_count, height, breadth, channels = source.shape
    extended = widen_map(source)
    mixed = stencil(extended, kernel, height, breadth)
    local_sums = (
        jnp.sum(sea_mask * mixed, axis=(0, 1, 2)),
        jnp.sum(sea_mask * mixed * mixed, axis=(0, 1, 2)),
        jnp.sum(sea_mask),
    )
    first_sum, square_sum, ocean_count = lax.psum(
        (local_sums[0], local_sums[1], local_sums[2]), ("lat", "lon")
    )
    mean_value = first_sum / ocean_count
    norm_factor = lax.rsqrt(square_sum / ocean_count - mean_value * mean_value + epsilon)
    unit_norm = (mixed - mean_value) * norm_factor
    normed = (
        (unit_norm * scale_gain.astype(jnp.float32) + norm_shift.astype(jnp.float32))
        .astype(jnp.bfloat16)
        .reshape(-1, channels)
    )
    hidden = jnp.dot(normed, up_weight, preferred_element_type=jnp.float32) + up_bias.astype(
        jnp.float32
    )
    active = exact_gelu(hidden).astype(jnp.bfloat16)
    branch = jnp.dot(active, down_weight, preferred_element_type=jnp.float32) + down_bias.astype(
        jnp.float32
    )
    output = sea_mask * (source.astype(jnp.float32) + branch.reshape(source.shape))
    stored = (extended, unit_norm, norm_factor, ocean_count, normed, hidden, active)
    return (output, stored)


def block_backward(grad_output, params, sea_mask, stored):
    kernel, scale_gain, norm_shift, up_weight, up_bias, down_weight, down_bias = params
    extended, unit_norm, norm_factor, ocean_count, normed, hidden_store, active = stored
    date_count, height, breadth, channels = unit_norm.shape
    grad_branch = (sea_mask * grad_output).astype(jnp.bfloat16).reshape(-1, channels)
    grad_down = cross_rows(active, grad_branch)
    grad_down_bias = jnp.sum(grad_branch.astype(jnp.float32), axis=0)
    grad_active = by_transpose(grad_branch, down_weight)
    unused_value, gelu_back = jax.vjp(exact_gelu, hidden_store)
    grad_hidden = gelu_back(grad_active)[0].astype(jnp.bfloat16)
    grad_up = cross_rows(normed, grad_hidden)
    grad_up_bias = jnp.sum(grad_hidden.astype(jnp.float32), axis=0)
    grad_normed = by_transpose(grad_hidden, up_weight).reshape(unit_norm.shape)
    local_back = (
        jnp.sum(grad_normed, axis=(0, 1, 2)),
        jnp.sum(grad_normed * unit_norm, axis=(0, 1, 2)),
    )
    grad_shift, grad_gain = lax.psum((local_back[0], local_back[1]), ("lat", "lon"))
    gain_float = scale_gain.astype(jnp.float32)
    grad_mixed = norm_factor * (
        gain_float * grad_normed
        - sea_mask / ocean_count * (gain_float * grad_shift + unit_norm * (gain_float * grad_gain))
    )
    grad_mixed = grad_mixed.astype(jnp.bfloat16)
    grad_extended = widen_map(grad_mixed)
    grad_source = sea_mask * grad_output + stencil(
        grad_extended, kernel[::-1, ::-1], height, breadth
    )
    grad_kernel = kernel_terms(extended, grad_mixed, height, breadth)
    return (
        grad_source,
        (grad_kernel, grad_gain, grad_shift, grad_up, grad_up_bias, grad_down, grad_down_bias),
    )


def unpack(vector, extents):
    pieces = []
    offset = 0
    for extent in extents:
        length = math.prod(extent)
        pieces.append(vector[offset : offset + length].reshape(extent))
        offset = offset + length
    return pieces


def shards(
    fine_map,
    ocean_mask,
    out_grad,
    encode_depth,
    encode_gain,
    encode_shift,
    encode_up,
    encode_up_bias,
    encode_down,
    encode_down_bias,
    widen_weight,
    widen_bias,
    bottle_depth,
    bottle_gain,
    bottle_shift,
    bottle_up,
    bottle_up_bias,
    bottle_down,
    bottle_down_bias,
    merge_weight,
    merge_bias,
    decode_depth,
    decode_gain,
    decode_shift,
    decode_up,
    decode_up_bias,
    decode_down,
    decode_down_bias,
):
    (
        encode_up,
        encode_down,
        widen_weight,
        bottle_up,
        bottle_down,
        merge_weight,
        decode_up,
        decode_down,
    ) = (
        lax.all_gather(encode_up, "lat", axis=0, tiled=True),
        lax.all_gather(encode_down, "lat", axis=0, tiled=True),
        lax.all_gather(widen_weight, "lat", axis=0, tiled=True),
        lax.all_gather(bottle_up, "lat", axis=0, tiled=True),
        lax.all_gather(bottle_down, "lat", axis=0, tiled=True),
        lax.all_gather(merge_weight, "lat", axis=0, tiled=True),
        lax.all_gather(decode_up, "lat", axis=0, tiled=True),
        lax.all_gather(decode_down, "lat", axis=0, tiled=True),
    )
    date_count, height, breadth, channels = fine_map.shape
    half_height, half_breadth = (height // 2, breadth // 2)
    wide_channels = widen_weight.shape[1]
    sea_fine = ocean_mask.astype(jnp.float32)[..., None]
    sea_coarse = jnp.max(
        sea_fine.reshape(date_count, half_height, 2, half_breadth, 2, 1), axis=(2, 4)
    )
    encode = (
        encode_depth,
        encode_gain,
        encode_shift,
        encode_up,
        encode_up_bias,
        encode_down,
        encode_down_bias,
    )
    bottle = (
        bottle_depth,
        bottle_gain,
        bottle_shift,
        bottle_up,
        bottle_up_bias,
        bottle_down,
        bottle_down_bias,
    )
    decode = (
        decode_depth,
        decode_gain,
        decode_shift,
        decode_up,
        decode_up_bias,
        decode_down,
        decode_down_bias,
    )
    merge_upper = merge_weight[:wide_channels]
    merge_lower = merge_weight[wide_channels:]
    encode_out, encode_stored = block_forward(fine_map, encode, sea_fine)
    skip_map = encode_out.astype(jnp.bfloat16)
    skip_rows = skip_map.reshape(-1, channels)
    blocks_fine = skip_map.reshape(date_count, half_height, 2, half_breadth, 2, channels).astype(
        jnp.float32
    )
    pooled = (jnp.sum(blocks_fine, axis=(2, 4)) * 0.25).astype(jnp.bfloat16).reshape(-1, channels)
    coarse_in = jnp.dot(
        pooled, widen_weight, preferred_element_type=jnp.float32
    ) + widen_bias.astype(jnp.float32)
    coarse_in = coarse_in.astype(jnp.bfloat16).reshape(
        date_count, half_height, half_breadth, wide_channels
    )
    coarse_out, coarse_stored = block_forward(coarse_in, bottle, sea_coarse)
    coarse_low = coarse_out.astype(jnp.bfloat16).reshape(-1, wide_channels)
    upper_part = jnp.dot(coarse_low, merge_upper, preferred_element_type=jnp.float32)
    upper_part = upper_part.reshape(date_count, half_height, 1, half_breadth, 1, channels)
    lower_part = jnp.dot(skip_rows, merge_lower, preferred_element_type=jnp.float32)
    lower_part = lower_part.reshape(date_count, half_height, 2, half_breadth, 2, channels)
    merged = (lower_part + upper_part).reshape(
        date_count, height, breadth, channels
    ) + merge_bias.astype(jnp.float32)
    decode_in = merged.astype(jnp.bfloat16)
    decode_out, decode_stored = block_forward(decode_in, decode, sea_fine)
    result = decode_out.astype(jnp.bfloat16)
    grad_decode_in, decode_grads = block_backward(
        out_grad.astype(jnp.float32), decode, sea_fine, decode_stored
    )
    grad_merged = grad_decode_in.astype(jnp.bfloat16).reshape(-1, channels)
    coarse_grid = coarse_low.reshape(date_count, half_height, 1, half_breadth, 1, wide_channels)
    upsampled_rows = jnp.broadcast_to(
        coarse_grid, (date_count, half_height, 2, half_breadth, 2, wide_channels)
    ).reshape(-1, wide_channels)
    grad_merge_weight = jnp.concatenate(
        [cross_rows(upsampled_rows, grad_merged), cross_rows(skip_rows, grad_merged)], axis=0
    )
    grad_merge_bias = jnp.sum(grad_merged.astype(jnp.float32), axis=0)
    grad_upsampled = by_transpose(grad_merged, merge_upper)
    grad_coarse = jnp.sum(
        grad_upsampled.reshape(date_count, half_height, 2, half_breadth, 2, wide_channels),
        axis=(2, 4),
    )
    grad_skip_direct = by_transpose(grad_merged, merge_lower)
    grad_coarse_in, bottle_grads = block_backward(grad_coarse, bottle, sea_coarse, coarse_stored)
    grad_wide = grad_coarse_in.astype(jnp.bfloat16).reshape(-1, wide_channels)
    grad_widen_weight = cross_rows(pooled, grad_wide)
    grad_widen_bias = jnp.sum(grad_wide.astype(jnp.float32), axis=0)
    grad_pooled = (
        by_transpose(grad_wide, widen_weight).reshape(
            date_count, half_height, 1, half_breadth, 1, channels
        )
        * 0.25
    )
    grad_skip = (
        grad_skip_direct.reshape(date_count, half_height, 2, half_breadth, 2, channels)
        + grad_pooled
    )
    grad_skip = grad_skip.reshape(date_count, height, breadth, channels)
    grad_fine, encode_grads = block_backward(grad_skip, encode, sea_fine, encode_stored)
    fine_grad = grad_fine.astype(jnp.bfloat16)
    large_parts = [
        encode_grads[3],
        encode_grads[5],
        grad_widen_weight,
        bottle_grads[3],
        bottle_grads[5],
        grad_merge_weight,
        decode_grads[3],
        decode_grads[5],
    ]
    large_extents = [part_grad.shape for part_grad in large_parts]
    large_vector = jnp.concatenate([part_grad.reshape(-1) for part_grad in large_parts])
    share = lax.psum_scatter(large_vector, ("lat", "lon"), scatter_dimension=0, tiled=True)
    large_total = lax.all_gather(
        share.astype(jnp.bfloat16), ("lat", "lon"), axis=0, tiled=True
    ).astype(share.dtype)
    small_parts = [
        encode_grads[0],
        encode_grads[4],
        encode_grads[6],
        grad_widen_bias,
        bottle_grads[0],
        bottle_grads[4],
        bottle_grads[6],
        grad_merge_bias,
        decode_grads[0],
        decode_grads[4],
        decode_grads[6],
    ]
    small_extents = [part_grad.shape for part_grad in small_parts]
    small_vector = jnp.concatenate([part_grad.reshape(-1) for part_grad in small_parts])
    small_total = lax.psum(small_vector, ("lat", "lon"))
    (
        encode_up_sum,
        encode_down_sum,
        widen_w_sum,
        bottle_up_sum,
        bottle_down_sum,
        merge_w_sum,
        decode_up_sum,
        decode_down_sum,
    ) = unpack(large_total, large_extents)
    (
        encode_kernel_sum,
        encode_upb_sum,
        encode_downb_sum,
        widen_b_sum,
        bottle_kernel_sum,
        bottle_upb_sum,
        bottle_downb_sum,
        merge_b_sum,
        decode_kernel_sum,
        decode_upb_sum,
        decode_downb_sum,
    ) = unpack(small_total, small_extents)
    return (
        result,
        fine_grad,
        encode_kernel_sum,
        encode_grads[1],
        encode_grads[2],
        encode_up_sum,
        encode_upb_sum,
        encode_down_sum,
        encode_downb_sum,
        widen_w_sum,
        widen_b_sum,
        bottle_kernel_sum,
        bottle_grads[1],
        bottle_grads[2],
        bottle_up_sum,
        bottle_upb_sum,
        bottle_down_sum,
        bottle_downb_sum,
        merge_w_sum,
        merge_b_sum,
        decode_kernel_sum,
        decode_grads[1],
        decode_grads[2],
        decode_up_sum,
        decode_upb_sum,
        decode_down_sum,
        decode_downb_sum,
    )


def solution(mesh):
    placed = (
        P(None, "lat", "lon", None),
        P(None, "lat", "lon"),
        P(None, "lat", "lon", None),
        P(),
        P(),
        P(),
        P("lat", None),
        P(),
        P("lat", None),
        P(),
        P("lat", None),
        P(),
        P(),
        P(),
        P(),
        P("lat", None),
        P(),
        P("lat", None),
        P(),
        P("lat", None),
        P(),
        P(),
        P(),
        P(),
        P("lat", None),
        P(),
        P("lat", None),
        P(),
    )
    return jax.shard_map(
        shards,
        mesh=mesh,
        in_specs=placed,
        out_specs=(
            P(None, "lat", "lon", None),
            P(None, "lat", "lon", None),
            P(),
            P(),
            P(),
            P(),
            P(),
            P(),
            P(),
            P(),
            P(),
            P(),
            P(),
            P(),
            P(),
            P(),
            P(),
            P(),
            P(),
            P(),
            P(),
            P(),
            P(),
            P(),
            P(),
            P(),
            P(),
        ),
        check_vma=False,
    )
```

profile of v0, /device:TPU:0, one launch (start us, length us, event | category | flops | bytes accessed | tf_op | source)
XLA Modules:
  0.0 2299.5 jit_solution(13207212915180531190)
XLA Ops:
  32.2 21.0 all-gather.1
  53.2 15.3 all-gather.2
  125.4 26.5 %multiply_reduce_fusion.1 = (f32[400]{0:T(512)}, f32[400]{0:T(512)}, f32[4,12,32,400]{3,2,1,0:T(8,128)}) fusion(f32[4,12,32]{2,1,0:T(8,128)S(1)} %copy-done.50, bf16[4,15,38,400]{3,2,1,0:T(8,128)(2,1)S(1)} %get-tuple-element.441, f32[400]{0:T(512)} %bitcast.523, f32[400]{0:T(512)} %bitcast.522, f32[400]{0:T(512)} %bitcast.521, f32[400]{0:T(512)} %bitcast.520, ...), kind=kLoop, calls=%fused_computation.214 | loop fusion | flops 97688800 | bytes 59185344 | tf_op jit(solution)/shard_map/reduce_sum | solution.py:78
  151.9 43.4 %all-reduce.7 = (f32[400]{0:T(512)S(1)}, f32[]{:T(128)}, f32[400]{0:T(512)S(1)}) all-reduce(f32[400]{0:T(512)} %get-tuple-element.207, f32[]{:T(128)} %convert_reduce_fusion.9, f32[400]{0:T(512)} %get-tuple-element.206), channel_id=1, replica_groups=mesh['lat'=4,'lon'=8] {'lat','lon'}, use_global_device_ids=true, to_apply=%region_5.0 | all-reduce | flops 801 | bytes 6408 | tf_op jit(solution)/shard_map/psum | solution.py:82
  201.5 29.4 %multiply_convert_fusion.1 = (bf16[1536,1600]{0,1:T(8,128)(2,1)}, f32[1536,1600]{0,1:T(8,128)}, f32[1536,1600]{0,1:T(8,128)}) fusion(f32[1600]{0:T(1024)S(1)} %copy-done.321, bf16[1536,400]{1,0:T(8,128)(2,1)S(1)} %bitcast.461, bf16[400,1600]{1,0:T(8,128)(2,1)} %reshape.643), kind=kOutput, calls=%fused_computation.171 | convolution fusion | flops 2128281600 | bytes 27091200 | tf_op jit(solution)/shard_map/dot_general | solution.py:93
  269.2 12.7 collective-permute-done.6
  281.9 17.8 collective-permute-done.7
  301.6 11.4 multiply_reduce_fusion.4
  313.1 38.8 %all-reduce.6 = (f32[800]{0:T(1024)S(1)}, f32[]{:T(128)}, f32[800]{0:T(1024)S(1)}) all-reduce(f32[800]{0:T(1024)S(1)} %get-tuple-element.279, f32[]{:T(128)} %reduce_sum.1550, f32[800]{0:T(1024)S(1)} %get-tuple-element.278), channel_id=1, replica_groups=mesh['lat'=4,'lon'=8] {'lat','lon'}, use_global_device_ids=true, to_apply=%region_13.0 | all-reduce | flops 1601 | bytes 12808 | tf_op jit(solution)/shard_map/psum | solution.py:82
  352.9 16.4 multiply_convert_fusion.2
  369.4 7.7 multiply_convert_fusion.10
  407.6 12.8 collective-permute-done.11
  424.9 24.8 %multiply_reduce_fusion = (f32[400]{0:T(512)S(1)}, f32[400]{0:T(512)S(1)}, f32[4,12,32,400]{3,2,1,0:T(8,128)}) fusion(f32[4,12,32]{2,1,0:T(8,128)S(1)} %copy-done.52, bf16[4,15,38,400]{3,2,1,0:T(8,128)(2,1)S(1)} %get-tuple-element.437, f32[400]{0:T(512)} %bitcast.594, f32[400]{0:T(512)} %bitcast.593, f32[400]{0:T(512)} %bitcast.592, f32[400]{0:T(512)} %bitcast.591, ...), kind=kLoop, calls=%fused_computation.212 | loop fusion | flops 103218400 | bytes 55614144 | tf_op jit(solution)/shard_map/reduce_sum | solution.py:78
  449.8 38.6 %all-reduce.5 = (f32[400]{0:T(512)S(1)}, f32[400]{0:T(512)S(1)}) all-reduce(f32[400]{0:T(512)S(1)} %get-tuple-element.205, f32[400]{0:T(512)S(1)} %get-tuple-element.204), channel_id=1, replica_groups=mesh['lat'=4,'lon'=8] {'lat','lon'}, use_global_device_ids=true, to_apply=%region_17.0 | all-reduce | flops 800 | bytes 6400 | tf_op jit(solution)/shard_map/psum | solution.py:82
  492.7 30.1 %multiply_convert_fusion = (bf16[1536,1600]{0,1:T(8,128)(2,1)}, f32[1536,1600]{0,1:T(8,128)}, f32[1536,1600]{0,1:T(8,128)}) fusion(f32[1600]{0:T(1024)S(1)} %copy-done.320, bf16[1536,400]{1,0:T(8,128)(2,1)S(1)} %bitcast.463, bf16[400,1600]{1,0:T(8,128)(2,1)S(1)} %copy-done.62), kind=kOutput, calls=%fused_computation.158 | convolution fusion | flops 2128281600 | bytes 27091200 | tf_op jit(solution)/shard_map/dot_general | solution.py:93
  522.9 12.3 convert_reduce_fusion
  550.5 40.8 %all-reduce.4 = (f32[400]{0:T(512)S(1)}, f32[400]{0:T(512)S(1)}) all-reduce(f32[400]{0:T(512)S(1)} %multiply_reduce_fusion.3, f32[400]{0:T(512)S(1)} %get-tuple-element.689), channel_id=1, replica_groups=mesh['lat'=4,'lon'=8] {'lat','lon'}, use_global_device_ids=true, to_apply=%region_21.0 | all-reduce | flops 800 | bytes 6400 | tf_op jit(solution)/shard_map/psum | solution.py:122
  591.4 23.0 %fusion.193 = (f32[400]{0:T(512)S(1)}, f32[400]{0:T(512)S(1)}, f32[400]{0:T(512)S(1)}, f32[400]{0:T(512)S(1)}, f32[400]{0:T(512)S(1)}, /*index=5*/f32[400]{0:T(5...) fusion(bf16[4,15,38,400]{3,2,1,0:T(8,128)(2,1)} %copy-done.4, ...), kind=kLoop, calls=%fused_computation.486 | loop fusion | flops 39314400 | bytes 28305344 | tf_op jit(solution)/shard_map/reduce_sum | solution.py:51
  615.5 9.4 fusion.165
  654.6 13.3 fusion.192
  681.9 12.6 collective-permute-done.15
  698.4 25.1 %convert_reduce_fusion.4 = (f32[400]{0:T(512)}, bf16[4,12,32,400]{3,2,1,0:T(8,128)(2,1)S(1)}) fusion(bf16[4,15,38,400]{3,2,1,0:T(8,128)(2,1)S(1)} %get-tuple-element.433, f32[400]{0:T(512)S(1)} %bitcast.605, f32[400]{0:T(512)S(1)} %bitcast.604, f32[400]{0:T(512)S(1)} %bitcast.603, f32[400]{0:T(512)S(1)} %bitcast.602, f32[400]{0:T(512)S(1)} %bitcast.601, ...), kind=kLoop, calls=%fused_computation.567 | loop fusion | flops 104447600 | bytes 55612544 | tf_op jit(solution)/shard_map/reduce_sum | solution.py:271
  730.9 8.3 fusion.429
  739.3 9.3 convert_reduce_fusion.2
  764.0 39.2 %all-reduce.3 = (f32[800]{0:T(1024)S(1)}, f32[800]{0:T(1024)S(1)}) all-reduce(f32[800]{0:T(1024)S(1)} %multiply_reduce_fusion.5, f32[800]{0:T(1024)S(1)} %get-tuple-element.691), channel_id=1, replica_groups=mesh['lat'=4,'lon'=8] {'lat','lon'}, use_global_device_ids=true, to_apply=%region_26.0 | all-reduce | flops 1600 | bytes 12800 | tf_op jit(solution)/shard_map/psum | solution.py:122
  852.3 11.2 reshape.630
  863.6 14.2 reshape.631
  881.4 11.6 convert_reduce_fusion.8
  911.7 10.8 convert_reduce_fusion.1
  945.0 11.9 dynamic-update-slice.3
  956.9 87.2 %dynamic-update-slice.4 = f32[8480000]{0:T(1024)} dynamic-update-slice(f32[8480000]{0:T(1024)} %dynamic-update-slice.3, f32[2560000]{0:T(1024)} %reshape.630, s32[]{} %constant.210) | dynamic-update-slice | bytes 20480004
  1044.1 87.0 %dynamic-update-slice.5 = f32[8480000]{0:T(1024)} dynamic-update-slice(f32[8480000]{0:T(1024)} %dynamic-update-slice.4, f32[2560000]{0:T(1024)} %reshape.631, s32[]{} %constant.211) | dynamic-update-slice | bytes 20480004
  1131.1 17.6 dynamic-update-slice.6
  1148.7 21.8 dynamic-update-slice.7
  1170.5 22.7 dynamic-update-slice.8
  1199.2 553.9 %all-reduce.15 = (bf16[8480000]{0:T(1024)(128)(2,1)}, f32[400]{0:T(512)S(1)}, f32[400]{0:T(512)S(1)}) all-reduce(f32[8480000]{0:T(1024)} %dynamic-update-slice.8, f32[400]{0:T(512)S(1)} %multiply_reduce_fusion.2, f32[400]{0:T(512)S(1)} %get-tuple-element.693), channel_id=2, replica_groups=mesh['lat'=4,'lon'=8] {'lat','lon'}, use_global_device_ids=true, to_apply=%region_187.0.clone | all-reduce | flops 8480800 | bytes 50886400
  1753.1 10.9 fusion.267
  1764.1 8.8 fusion.239
  1773.0 8.4 fusion.266
  1781.9 8.8 concatenate.399
  1798.1 9.0 dynamic-update-slice
  1824.2 92.4 %all-reduce.12.cloned.1.call-done = f32[87600]{0:T(1024)} async-done(((f32[87600]{0:T(1024)}), f32[87600]{0:T(1024)}) %all-reduce.12.cloned.1.call-update) | async-done | bytes 350416 | tf_op jit(solution)/shard_map/psum | solution.py:326
  1930.6 25.4 %fusion.269 = bf16[4,12,32,400]{3,2,1,0:T(8,128)(2,1)} fusion(f32[4,12,32,400]{3,0,2,1:T(4,128)S(1)} %bitcast.451, bf16[4,12,32,400]{3,2,1,0:T(8,128)(2,1)S(1)} %copy-done.17, bf16[4,12,3,400]{3,2,1,0:T(4,128)(2,1)S(1)} %collective-permute-done.21, bf16[4,12,3,400]{3,2,1,0:T(4,128)(2,1)S(1)} %collective-permute-done.20, ...), kind=kLoop, calls=%fused_computation.563 | loop fusion | flops 102604800 | bytes 56839744 | tf_op jit(solution)/shard_map/convert_element_type | solution.py:294
  1956.1 249.6 %all-reduce.14.cloned.1.call-done = bf16[8480000]{0:T(1024)(128)(2,1)} async-done(((bf16[8480000]{0:T(1024)(128)(2,1)}), bf16[8480000]{0:T(1024)(128)(2,1)}) %all-reduce.14.cloned.1.call-update) | async-done | bytes 16960016
  2205.6 10.8 fusion.440
  2216.4 13.5 slice.3016
  2229.9 12.2 copy.181
  2242.1 11.7 slice.3013
  (1013 shorter events, 428.0 us)
Async XLA Ops:
  7.2 191.2 %all-gather.19.cloned.1.call-start = ((), (), s32[]{:S(2)}) async-start(), calls=%async_computation.6 | async-start | bytes 1730560 | tf_op jit(solution)/shard_map/all_gather | solution.py:190
  8.0 223.0 %all-gather.11.cloned.1.call-start = ((), (), s32[]{:S(2)}) async-start(), calls=%async_computation | async-start | bytes 2048000 | tf_op jit(solution)/shard_map/all_gather | solution.py:191
  8.7 344.1 %all-gather.13.cloned.1.call-start = ((), (), s32[]{:S(2)}) async-start(), calls=%async_computation.1 | async-start | bytes 6400000 | tf_op jit(solution)/shard_map/all_gather | solution.py:193
  9.4 359.9 %all-gather.15.cloned.1.call-start = ((), (), s32[]{:S(2)}) async-start(), calls=%async_computation.2 | async-start | bytes 7168000 | tf_op jit(solution)/shard_map/all_gather | solution.py:194
  10.0 388.6 %all-gather.21.cloned.1.call-start = ((), (), s32[]{:S(2)}) async-start(), calls=%async_computation.7 | async-start | bytes 1730560 | tf_op jit(solution)/shard_map/all_gather | solution.py:196
  10.6 512.2 %all-gather.17.cloned.1.call-start = ((), (), s32[]{:S(2)}) async-start(), calls=%async_computation.3 | async-start | bytes 2048000 | tf_op jit(solution)/shard_map/all_gather | solution.py:197
  11.6 57.0 %collective-permute-start = (bf16[4,12,3,400]{3,2,1,0:T(4,128)(2,1)}, bf16[4,12,3,400]{3,2,1,0:T(4,128)(2,1)}, u32[]{:S(2)}, u32[]{:S(2)}) collective-permute-start(bf16[4,12,3,400]{3,2,1,0:T(4,128)(2,1)} %get-tuple-element.451), channel_id=1, source_target_pairs={{0,1},{1,2},{2,3},{3,4},{4,5},{5,6},{6,7},{7,0},{8,9},{9,10},{10,1... | collective-permute-start | bytes 345608 | tf_op jit(solution)/shard_map/ppermute | solution.py:18
  12.0 56.6 %collective-permute-start.1 = (bf16[4,12,3,400]{3,2,1,0:T(4,128)(2,1)}, bf16[4,12,3,400]{3,2,1,0:T(4,128)(2,1)}, u32[]{:S(2)}, u32[]{:S(2)}) collective-permute-start(bf16[4,12,3,400]{3,2,1,0:T(4,128)(2,1)} %get-tuple-element.452), channel_id=1, source_target_pairs={{1,0},{2,1},{3,2},{4,3},{5,4},{6,5},{7,6},{0,7},{9,8},{10,9},{11,1... | collective-permute-start | bytes 345608 | tf_op jit(solution)/shard_map/ppermute | solution.py:21
  16.1 1900.5 %all-reduce.12.cloned.1.call-start = ((), (), s32[]{:S(2)}) async-start(), calls=%async_computation.4 | async-start | bytes 704512 | tf_op jit(solution)/shard_map/psum | solution.py:326
  29.7 45.7 %copy-start.84 = (s32[4,12,32]{2,0,1:T(4,128)S(1)}, s32[4,12,32]{2,0,1:T(4,128)}, u32[]{:S(2)}) copy-start(s32[4,12,32]{2,0,1:T(4,128)} %param.29) | copy-start | bytes 18436
  70.9 49.8 %collective-permute-start.2 = (bf16[4,3,38,400]{3,2,1,0:T(8,128)(2,1)}, bf16[4,3,38,400]{3,2,1,0:T(8,128)(2,1)}, u32[]{:S(2)}, u32[]{:S(2)}) collective-permute-start(bf16[4,3,38,400]{3,2,1,0:T(8,128)(2,1)} %get-tuple-element.442), channel_id=1, source_target_pairs={{0,8},{8,16},{16,24},{1,9},{9,17},{17,25},{2,10},{10,18},{18,26},{... | collective-permute-start | bytes 1094408 | tf_op jit(solution)/shard_map/ppermute | solution.py:18
  73.8 46.9 %collective-permute-start.3 = (bf16[4,3,38,400]{3,2,1,0:T(8,128)(2,1)}, bf16[4,3,38,400]{3,2,1,0:T(8,128)(2,1)}, u32[]{:S(2)}, u32[]{:S(2)}) collective-permute-start(bf16[4,3,38,400]{3,2,1,0:T(8,128)(2,1)} %get-tuple-element.443), channel_id=1, source_target_pairs={{8,0},{16,8},{24,16},{9,1},{17,9},{25,17},{10,2},{18,10},{26,18},{... | collective-permute-start | bytes 1094408 | tf_op jit(solution)/shard_map/ppermute | solution.py:21
  96.7 204.5 %copy-start.73 = (f32[4,6,16]{2,1,0:T(8,128)}, f32[4,6,16]{2,1,0:T(8,128)S(1)}, u32[]{:S(2)}) copy-start(f32[4,6,16]{2,1,0:T(8,128)S(1)} %copy.154) | copy-start | bytes 4612
  253.7 47.5 %copy-start.23 = (bf16[384,800]{1,0:T(8,128)(2,1)}, bf16[384,800]{1,0:T(8,128)(2,1)S(1)}, u32[]{:S(2)}) copy-start(bf16[384,800]{1,0:T(8,128)(2,1)S(1)} %copy.155) | copy-start | bytes 1843204
  253.8 7.8 collective-permute-start.4
  253.9 7.7 collective-permute-start.5
  262.7 19.2 collective-permute-start.6
  266.6 33.1 %collective-permute-start.7 = (bf16[4,3,22,800]{3,2,1,0:T(8,128)(2,1)S(1)}, bf16[4,3,22,800]{3,2,1,0:T(8,128)(2,1)S(1)}, u32[]{:S(2)}, u32[]{:S(2)}) collective-permute-start(bf16[4,3,22,800]{3,2,1,0:T(8,128)(2,1)S(1)} %get-tuple-element.460), channel_id=1, source_target_pairs={{8,0},{16,8},{24,16},{9,1},{17,9},{25,17},{10,2},{18,10},{26,18},{... | collective-permute-start | bytes 1267208 | tf_op jit(solution)/shard_map/ppermute | solution.py:21
  301.6 51.0 %copy-start.93 = (f32[800]{0:T(1024)S(1)}, f32[800]{0:T(1024)}, u32[]{:S(2)}) copy-start(f32[800]{0:T(1024)} %convert_element_type.1354) | copy-start | bytes 9604
  301.6 51.0 %copy-start.139 = (f32[800]{0:T(1024)S(1)}, f32[800]{0:T(1024)}, u32[]{:S(2)}) copy-start(f32[800]{0:T(1024)} %convert_element_type.1355) | copy-start | bytes 9604
  313.0 56.3 %copy-start.21 = (f32[4,6,16,800]{3,2,1,0:T(8,128)}, f32[4,6,16,800]{3,2,1,0:T(8,128)S(1)}, u32[]{:S(2)}) copy-start(f32[4,6,16,800]{3,2,1,0:T(8,128)S(1)} %get-tuple-element.418) | copy-start | bytes 3686404
  383.5 8.3 collective-permute-start.8
  383.6 8.3 collective-permute-start.9
  392.4 15.2 collective-permute-start.10
  396.6 23.7 %collective-permute-start.11 = (bf16[4,3,38,400]{3,2,1,0:T(8,128)(2,1)S(1)}, bf16[4,3,38,400]{3,2,1,0:T(8,128)(2,1)}, u32[]{:S(2)}, u32[]{:S(2)}) collective-permute-start(bf16[4,3,38,400]{3,2,1,0:T(8,128)(2,1)S(1)} %get-tuple-element.439), channel_id=1, source_target_pairs={{8,0},{16,8},{24,16},{9,1},{17,9},{25,17},{10,2},{18,10},{26,18},{... | collective-permute-start | bytes 1094408 | tf_op jit(solution)/shard_map/ppermute | solution.py:21
  398.6 192.8 %copy-start.81 = (f32[4,12,32]{2,1,0:T(8,128)}, f32[4,12,32]{2,1,0:T(8,128)S(1)}, u32[]{:S(2)}) copy-start(f32[4,12,32]{2,1,0:T(8,128)S(1)} %copy.162) | copy-start | bytes 18436
  424.9 64.2 %copy-start.100 = (f32[400]{0:T(512)S(1)}, f32[400]{0:T(512)}, u32[]{:S(2)}) copy-start(f32[400]{0:T(512)} %convert_element_type.1413) | copy-start | bytes 4804
  547.1 44.2 %copy-start.324 = (bf16[400]{0:T(512)(128)(2,1)S(1)}, bf16[400]{0:T(512)(128)(2,1)}, u32[]{:S(2)}) copy-start(bf16[400]{0:T(512)(128)(2,1)} %param.50) | copy-start | bytes 2404
  626.3 41.8 %collective-permute-start.12 = (bf16[4,12,3,400]{3,2,1,0:T(4,128)(2,1)}, bf16[4,12,3,400]{3,2,1,0:T(4,128)(2,1)S(1)}, u32[]{:S(2)}, u32[]{:S(2)}) collective-permute-start(bf16[4,12,3,400]{3,2,1,0:T(4,128)(2,1)} %get-tuple-element.447), channel_id=1, source_target_pairs={{0,1},{1,2},{2,3},{3,4},{4,5},{5,6},{6,7},{7,0},{8,9},{9,10},{10,1... | collective-permute-start | bytes 345608 | tf_op jit(solution)/shard_map/ppermute | solution.py:18
  626.4 41.7 %collective-permute-start.13 = (bf16[4,12,3,400]{3,2,1,0:T(4,128)(2,1)}, bf16[4,12,3,400]{3,2,1,0:T(4,128)(2,1)}, u32[]{:S(2)}, u32[]{:S(2)}) collective-permute-start(bf16[4,12,3,400]{3,2,1,0:T(4,128)(2,1)} %get-tuple-element.448), channel_id=1, source_target_pairs={{1,0},{2,1},{3,2},{4,3},{5,4},{6,5},{7,6},{0,7},{9,8},{10,9},{11,1... | collective-permute-start | bytes 345608 | tf_op jit(solution)/shard_map/ppermute | solution.py:21
  670.0 11.9 collective-permute-start.14
  674.2 20.3 collective-permute-start.15
  759.5 44.4 %copy-start.7 = (bf16[4,9,22,800]{3,2,1,0:T(8,128)(2,1)S(1)}, bf16[4,9,22,800]{3,2,1,0:T(8,128)(2,1)}, u32[]{:S(2)}) copy-start(bf16[4,9,22,800]{3,2,1,0:T(8,128)(2,1)} %copy-done.6) | copy-start | bytes 3801604
  759.5 44.4 %copy-start.87 = (f32[4,6,16]{2,1,0:T(8,128)S(1)}, f32[4,6,16]{2,1,0:T(8,128)}, u32[]{:S(2)}) copy-start(f32[4,6,16]{2,1,0:T(8,128)} %copy.168) | copy-start | bytes 4612
  759.5 44.4 %copy-start.94 = (f32[800]{0:T(1024)S(1)}, f32[800]{0:T(1024)}, u32[]{:S(2)}) copy-start(f32[800]{0:T(1024)} %convert_element_type.1354) | copy-start | bytes 9604
  827.9 9.8 collective-permute-start.16
  827.9 9.8 collective-permute-start.17
  839.3 39.3 %collective-permute-start.18 = (bf16[4,3,22,800]{3,2,1,0:T(8,128)(2,1)}, bf16[4,3,22,800]{3,2,1,0:T(8,128)(2,1)S(1)}, u32[]{:S(2)}, u32[]{:S(2)}) collective-permute-start(bf16[4,3,22,800]{3,2,1,0:T(8,128)(2,1)} %get-tuple-element.455), channel_id=1, source_target_pairs={{0,8},{8,16},{16,24},{1,9},{9,17},{17,25},{2,10},{10,18},{18,26},{... | collective-permute-start | bytes 1267208 | tf_op jit(solution)/shard_map/ppermute | solution.py:18
  843.6 35.1 %collective-permute-start.19 = (bf16[4,3,22,800]{3,2,1,0:T(8,128)(2,1)}, bf16[4,3,22,800]{3,2,1,0:T(8,128)(2,1)}, u32[]{:S(2)}, u32[]{:S(2)}) collective-permute-start(bf16[4,3,22,800]{3,2,1,0:T(8,128)(2,1)} %get-tuple-element.456), channel_id=1, source_target_pairs={{8,0},{16,8},{24,16},{9,1},{17,9},{25,17},{10,2},{18,10},{26,18},{... | collective-permute-start | bytes 1267208 | tf_op jit(solution)/shard_map/ppermute | solution.py:21
  1199.1 553.9 %copy-start.326 = (bf16[400]{0:T(512)(128)(2,1)S(1)}, bf16[400]{0:T(512)(128)(2,1)}, u32[]{:S(2)}) copy-start(bf16[400]{0:T(512)(128)(2,1)} %param.32) | copy-start | bytes 2404
  1199.1 553.9 %copy-start.3 = (bf16[4,15,38,400]{3,2,1,0:T(8,128)(2,1)S(1)}, bf16[4,15,38,400]{3,2,1,0:T(8,128)(2,1)}, u32[]{:S(2)}) copy-start(bf16[4,15,38,400]{3,2,1,0:T(8,128)(2,1)} %copy-done.2) | copy-start | bytes 5472004
  1199.1 553.9 %copy-start.82 = (f32[4,12,32]{2,1,0:T(8,128)S(1)}, f32[4,12,32]{2,1,0:T(8,128)}, u32[]{:S(2)}) copy-start(f32[4,12,32]{2,1,0:T(8,128)} %copy-done.81) | copy-start | bytes 18436
  1199.2 553.9 %copy-start.99 = (f32[400]{0:T(512)S(1)}, f32[400]{0:T(512)}, u32[]{:S(2)}) copy-start(f32[400]{0:T(512)} %convert_element_type.1291) | copy-start | bytes 4804
  1790.7 414.9 %all-reduce.14.cloned.1.call-start = ((), (), s32[]{:S(2)}) async-start(), calls=%async_computation.5 | async-start | bytes 33923072
  1808.7 9.2 collective-permute-start.20
  1808.8 9.2 collective-permute-start.21
  1818.5 107.9 %collective-permute-start.22 = (bf16[4,3,38,400]{3,2,1,0:T(8,128)(2,1)S(1)}, bf16[4,3,38,400]{3,2,1,0:T(8,128)(2,1)}, u32[]{:S(2)}, u32[]{:S(2)}) collective-permute-start(bf16[4,3,38,400]{3,2,1,0:T(8,128)(2,1)S(1)} %get-tuple-element.430), channel_id=1, source_target_pairs={{0,8},{8,16},{16,24},{1,9},{9,17},{17,25},{2,10},{10,18},{18,26},{... | collective-permute-start | bytes 1094408 | tf_op jit(solution)/shard_map/ppermute | solution.py:18
  1822.9 103.5 %collective-permute-start.23 = (bf16[4,3,38,400]{3,2,1,0:T(8,128)(2,1)S(1)}, bf16[4,3,38,400]{3,2,1,0:T(8,128)(2,1)}, u32[]{:S(2)}, u32[]{:S(2)}) collective-permute-start(bf16[4,3,38,400]{3,2,1,0:T(8,128)(2,1)S(1)} %get-tuple-element.431), channel_id=1, source_target_pairs={{8,0},{16,8},{24,16},{9,1},{17,9},{25,17},{10,2},{18,10},{26,18},{... | collective-permute-start | bytes 1094408 | tf_op jit(solution)/shard_map/ppermute | solution.py:21
  (325 other events, 4599.2 us)
Sparse Core Ops, SparseCore 0:
  9.9 34.9 all-gather.18
  46.7 43.4 all-gather.10
  92.1 60.4 all-gather.12
  154.3 66.2 all-gather.14
  222.3 29.3 all-gather.20
  253.4 41.2 all-gather.16
  1790.9 125.6 all-reduce.11
  1924.0 281.6 all-reduce.13
where the time goes:
time: 2330 us; the launch traced here: 2300 us
  blocking collectives  791 us (34%)
  local copies, waits for them, and re-layouts  543 us (23%)
  waiting for transfers between devices  413 us (18%)
  other arithmetic  286 us (12%)
  matrix products  191 us (8%)
  starting transfers between devices  54.5 us (2%)
    unnamed x1, blocking collectives  554 us
    unnamed x720, local copies, waits for them, and re-layouts  288 us
    unnamed x9, waiting for transfers between devices  253 us
    psum x3, blocking collectives, block_forward(): lax.psum((local_sums[0], local_sums[1], local_sums[2]), ('lat', 'lon'))  121 us
    psum x1, waiting for transfers between devices, shards(): small_total = lax.psum(small_vector, ('lat', 'lon'))  92.4 us
    reduce_sum x11, other arithmetic, kernel_terms(): row_terms.append(jnp.sum(window * upstream, axis=(0, 1, 2)))  88.1 us
    psum x2, blocking collectives, block_backward(): lax.psum((local_back[0], local_back[1]), ('lat', 'lon'))  80 us
    dot_general x3, matrix products, block_forward(): jnp.dot(normed, up_weight, preferred_element_type=jnp.float32)  75.9 us
  transfers between devices with their start and end apart: 32, of which 10 were waited for; matrix products, arithmetic and copies ran while one was open for 18% of the time, Pallas kernels for 0%

commit v1 on v0

v1 whole, which is shorter than its diff:
```python
import math

import jax
import jax.numpy as jnp
from jax import lax
from jax.sharding import PartitionSpec as P

epsilon = 1e-05
both = ("lat", "lon")
bf16 = jnp.bfloat16
f32 = jnp.float32


def exchange_pairs(count, group, step):
    return [(i, (i // group) * group + ((i % group) ^ step)) for i in range(count)]


def to_dates(tiles):
    dates, count = tiles.shape[0], lax.axis_size("lat")
    own = lax.axis_index("lat") % dates
    pieces = [lax.dynamic_index_in_dim(tiles, own, 0, keepdims=False)]
    for step in range(1, dates):
        pieces.append(
            lax.ppermute(
                lax.dynamic_index_in_dim(tiles, own ^ step, 0, keepdims=False),
                "lat",
                exchange_pairs(count, dates, step),
            )
        )
    stacked = jnp.stack(pieces)
    ordered = [lax.dynamic_index_in_dim(stacked, own ^ tile, 0, keepdims=False) for tile in range(dates)]
    return jnp.concatenate(ordered, axis=0)


def from_dates(band, dates):
    count = lax.axis_size("lat")
    own = lax.axis_index("lat") % dates
    tiles = band.reshape((dates, band.shape[0] // dates) + band.shape[1:])
    pieces = [lax.dynamic_index_in_dim(tiles, own, 0, keepdims=False)]
    for step in range(1, dates):
        pieces.append(
            lax.ppermute(
                lax.dynamic_index_in_dim(tiles, own ^ step, 0, keepdims=False),
                "lat",
                exchange_pairs(count, dates, step),
            )
        )
    stacked = jnp.stack(pieces)
    return jnp.stack([lax.dynamic_index_in_dim(stacked, own ^ date, 0, keepdims=False) for date in range(dates)])


def widen_map(source, dates):
    count = lax.axis_size("lon")
    forward = [(i, (i + 1) % count) for i in range(count)]
    backward = [(target, origin) for origin, target in forward]
    left = lax.ppermute(source[:, -3:], "lon", forward)
    right = lax.ppermute(source[:, :3], "lon", backward)
    wrapped = jnp.concatenate([left, source, right], axis=1)
    tiles = lax.axis_size("lat")
    if tiles == dates:
        return jnp.pad(wrapped, ((3, 3), (0, 0), (0, 0)))
    down = [(i, i + dates) for i in range(tiles - dates)]
    up = [(target, origin) for origin, target in down]
    above = lax.ppermute(wrapped[-3:], "lat", down)
    below = lax.ppermute(wrapped[:3], "lat", up)
    return jnp.concatenate([above, wrapped, below], axis=0)


def sum_all(local):
    count = lax.axis_size(both)
    copies = jnp.broadcast_to(local[None], (count,) + local.shape)
    return jnp.sum(lax.all_to_all(copies, both, 0, 0, tiled=False), axis=0)


def stencil(extended, kernel, height, breadth):
    taps = kernel.astype(f32)
    summed = jnp.zeros((height, breadth, extended.shape[2]), f32)
    for across in range(7):
        for column in range(7):
            summed = summed + taps[across, column] * extended[
                across : across + height, column : column + breadth, :
            ].astype(f32)
    return summed


def kernel_terms(extended, grad_mixed, height, breadth):
    upstream = grad_mixed.astype(f32)
    terms = []
    for across in range(7):
        for column in range(7):
            window = extended[across : across + height, column : column + breadth, :].astype(f32)
            terms.append(jnp.sum(window * upstream, axis=(0, 1)))
    return jnp.stack(terms)


def cross_rows(former, latter):
    return lax.dot_general(former, latter, (((0,), (0,)), ((), ())), preferred_element_type=f32)


def by_transpose(former, latter):
    return lax.dot_general(former, latter, (((1,), (1,)), ((), ())), preferred_element_type=f32)


def gelu_pair(hidden):
    phi = 0.5 * lax.erfc(hidden * (-math.sqrt(0.5)))
    density = jnp.exp(-0.5 * hidden * hidden) * (1.0 / math.sqrt(2.0 * math.pi))
    return hidden * phi, phi + hidden * density


def block_forward(source, params, sea, dates):
    kernel, gain, shift, up, up_bias, down, down_bias = params
    height, breadth, channels = source.shape
    extended = widen_map(source, dates)
    mixed = stencil(extended, kernel, height, breadth)
    masked = sea * mixed
    local = jnp.stack(
        [jnp.sum(masked, axis=(0, 1)), jnp.sum(masked * mixed, axis=(0, 1)), jnp.full((channels,), jnp.sum(sea))]
    )
    first, square, ocean = sum_all(local)
    ocean = ocean[0]
    mean = first / ocean
    factor = lax.rsqrt(square / ocean - mean * mean + epsilon)
    unit = (mixed - mean) * factor
    normed = (unit * gain.astype(f32) + shift.astype(f32)).astype(bf16).reshape(-1, channels)
    hidden = jnp.dot(normed, up, preferred_element_type=f32) + up_bias.astype(f32)
    active, slope = gelu_pair(hidden)
    active = active.astype(bf16)
    slope = slope.astype(bf16)
    branch = jnp.dot(active, down, preferred_element_type=f32) + down_bias.astype(f32)
    output = sea * (source.astype(f32) + branch.reshape(source.shape))
    return output, (extended, mixed, mean, factor, ocean, normed, slope, active)


def block_backward(grad_output, params, sea, stored, dates):
    kernel, gain, shift, up, up_bias, down, down_bias = params
    extended, mixed, mean, factor, ocean, normed, slope, active = stored
    height, breadth, channels = mixed.shape
    grad_branch = (sea * grad_output).astype(bf16).reshape(-1, channels)
    grad_hidden = (by_transpose(grad_branch, down) * slope.astype(f32)).astype(bf16)
    grad_normed = by_transpose(grad_hidden, up).reshape(mixed.shape)
    unit = (mixed - mean) * factor
    local = jnp.stack([jnp.sum(grad_normed, axis=(0, 1)), jnp.sum(grad_normed * unit, axis=(0, 1))])
    grad_shift, grad_gain = sum_all(local)
    gain = gain.astype(f32)
    grad_mixed = factor * (gain * grad_normed - sea / ocean * (gain * grad_shift + unit * (gain * grad_gain)))
    grad_mixed = grad_mixed.astype(bf16)
    grad_extended = widen_map(grad_mixed, dates)
    grad_source = sea * grad_output + stencil(grad_extended, kernel[::-1, ::-1], height, breadth)
    grad_down = cross_rows(active, grad_branch)
    grad_down_bias = jnp.sum(grad_branch.astype(f32), axis=0)
    grad_up = cross_rows(normed, grad_hidden)
    grad_up_bias = jnp.sum(grad_hidden.astype(f32), axis=0)
    grad_kernel = kernel_terms(extended, grad_mixed, height, breadth)
    return grad_source, (grad_kernel, grad_gain, grad_shift, grad_up, grad_up_bias, grad_down, grad_down_bias)


def shards(
    fine_map,
    ocean_mask,
    out_grad,
    encode_depth,
    encode_gain,
    encode_shift,
    encode_up,
    encode_up_bias,
    encode_down,
    encode_down_bias,
    widen_weight,
    widen_bias,
    bottle_depth,
    bottle_gain,
    bottle_shift,
    bottle_up,
    bottle_up_bias,
    bottle_down,
    bottle_down_bias,
    merge_weight,
    merge_bias,
    decode_depth,
    decode_gain,
    decode_shift,
    decode_up,
    decode_up_bias,
    decode_down,
    decode_down_bias,
):
    (encode_up, encode_down, widen_weight, bottle_up, bottle_down, merge_weight, decode_up, decode_down) = (
        lax.all_gather(weight, "lat", axis=0, tiled=True)
        for weight in (
            encode_up,
            encode_down,
            widen_weight,
            bottle_up,
            bottle_down,
            merge_weight,
            decode_up,
            decode_down,
        )
    )
    dates = fine_map.shape[0]
    fine = to_dates(fine_map)
    sea_fine = to_dates(ocean_mask).astype(f32)[..., None]
    upstream = to_dates(out_grad)
    height, breadth, channels = fine.shape
    half_height, half_breadth = height // 2, breadth // 2
    wide = widen_weight.shape[1]
    sea_coarse = jnp.max(sea_fine.reshape(half_height, 2, half_breadth, 2, 1), axis=(1, 3))
    encode = (encode_depth, encode_gain, encode_shift, encode_up, encode_up_bias, encode_down, encode_down_bias)
    bottle = (bottle_depth, bottle_gain, bottle_shift, bottle_up, bottle_up_bias, bottle_down, bottle_down_bias)
    decode = (decode_depth, decode_gain, decode_shift, decode_up, decode_up_bias, decode_down, decode_down_bias)
    merge_upper = merge_weight[:wide]
    merge_lower = merge_weight[wide:]

    encode_out, encode_stored = block_forward(fine, encode, sea_fine, dates)
    skip_map = encode_out.astype(bf16)
    skip_rows = skip_map.reshape(-1, channels)
    blocks = skip_map.reshape(half_height, 2, half_breadth, 2, channels).astype(f32)
    pooled = (jnp.sum(blocks, axis=(1, 3)) * 0.25).astype(bf16).reshape(-1, channels)
    coarse_in = jnp.dot(pooled, widen_weight, preferred_element_type=f32) + widen_bias.astype(f32)
    coarse_in = coarse_in.astype(bf16).reshape(half_height, half_breadth, wide)
    coarse_out, coarse_stored = block_forward(coarse_in, bottle, sea_coarse, dates)
    coarse_low = coarse_out.astype(bf16).reshape(-1, wide)
    upper = jnp.dot(coarse_low, merge_upper, preferred_element_type=f32)
    upper = upper.reshape(half_height, 1, half_breadth, 1, channels)
    lower = jnp.dot(skip_rows, merge_lower, preferred_element_type=f32)
    lower = lower.reshape(half_height, 2, half_breadth, 2, channels)
    merged = (lower + upper).reshape(height, breadth, channels) + merge_bias.astype(f32)
    decode_out, decode_stored = block_forward(merged.astype(bf16), decode, sea_fine, dates)
    result = from_dates(decode_out.astype(bf16), dates)

    grad_decode_in, decode_grads = block_backward(upstream.astype(f32), decode, sea_fine, decode_stored, dates)
    grad_merged = grad_decode_in.astype(bf16)
    grad_merged_rows = grad_merged.reshape(-1, channels)
    grad_block_sum = jnp.sum(
        grad_merged.astype(f32).reshape(half_height, 2, half_breadth, 2, channels), axis=(1, 3)
    ).reshape(-1, channels)
    grad_merge_bias = jnp.sum(grad_block_sum, axis=0)
    grad_block_low = grad_block_sum.astype(bf16)
    grad_block_rest = (grad_block_sum - grad_block_low.astype(f32)).astype(bf16)
    grad_merge_weight = jnp.concatenate(
        [
            cross_rows(coarse_low, grad_block_low) + cross_rows(coarse_low, grad_block_rest),
            cross_rows(skip_rows, grad_merged_rows),
        ],
        axis=0,
    )
    grad_coarse = (by_transpose(grad_block_low, merge_upper) + by_transpose(grad_block_rest, merge_upper)).reshape(
        half_height, half_breadth, wide
    )
    grad_skip_direct = by_transpose(grad_merged_rows, merge_lower)
    grad_coarse_in, bottle_grads = block_backward(grad_coarse, bottle, sea_coarse, coarse_stored, dates)
    grad_wide = grad_coarse_in.astype(bf16).reshape(-1, wide)
    grad_widen_weight = cross_rows(pooled, grad_wide)
    grad_widen_bias = jnp.sum(grad_wide.astype(f32), axis=0)
    grad_pooled = by_transpose(grad_wide, widen_weight).reshape(half_height, 1, half_breadth, 1, channels) * 0.25
    grad_skip = grad_skip_direct.reshape(half_height, 2, half_breadth, 2, channels) + grad_pooled
    grad_fine, encode_grads = block_backward(
        grad_skip.reshape(height, breadth, channels), encode, sea_fine, encode_stored, dates
    )
    fine_grad = from_dates(grad_fine.astype(bf16), dates)

    def summed(parts):
        return [total.astype(f32) for total in lax.psum([part.astype(bf16) for part in parts], both)]

    decode_up_sum, decode_down_sum, merge_sum = summed([decode_grads[3], decode_grads[5], grad_merge_weight])
    bottle_up_sum, bottle_down_sum, widen_sum = summed([bottle_grads[3], bottle_grads[5], grad_widen_weight])
    encode_up_sum, encode_down_sum = summed([encode_grads[3], encode_grads[5]])
    small_parts = [
        encode_grads[0],
        encode_grads[4],
        encode_grads[6],
        grad_widen_bias,
        bottle_grads[0],
        bottle_grads[4],
        bottle_grads[6],
        grad_merge_bias,
        decode_grads[0],
        decode_grads[4],
        decode_grads[6],
    ]
    small = lax.psum(small_parts, both)
    return (
        result,
        fine_grad,
        small[0].reshape(encode_depth.shape),
        encode_grads[1],
        encode_grads[2],
        encode_up_sum,
        small[1],
        encode_down_sum,
        small[2],
        widen_sum,
        small[3],
        small[4].reshape(bottle_depth.shape),
        bottle_grads[1],
        bottle_grads[2],
        bottle_up_sum,
        small[5],
        bottle_down_sum,
        small[6],
        merge_sum,
        small[7],
        small[8].reshape(decode_depth.shape),
        decode_grads[1],
        decode_grads[2],
        decode_up_sum,
        small[9],
        decode_down_sum,
        small[10],
    )


def solution(mesh):
    whole = P()
    rows = P("lat", None)
    tile = P(None, "lat", "lon", None)
    block = (whole, whole, whole, rows, whole, rows, whole)
    placed = (tile, P(None, "lat", "lon"), tile) + block + (rows, whole) + block + (rows, whole) + block
    return jax.shard_map(
        shards,
        mesh=mesh,
        in_specs=placed,
        out_specs=(tile, tile) + (whole,) * 25,
        check_vma=False,
    )
```

time: 2330 us -> 1130 us (0.48)
  blocking collectives: 791 us -> 84.6 us
  local copies, waits for them, and re-layouts: 543 us -> 144 us
  waiting for transfers between devices: 413 us -> 331 us
    unnamed x1 -> x0, blocking collectives: 554 us -> none
    unnamed x720 -> x844, local copies, waits for them, and re-layouts: 288 us -> 19.8 us
    unnamed x9 -> x8, waiting for transfers between devices: 253 us -> 3.16 us
    psum x1 -> x2, waiting for transfers between devices: 92.4 us -> 293 us  [the longest x1 181 us: summed(): lax.psum([part.astype(bf16) for part in parts], both)]
    psum x5 -> x1, blocking collectives: 201 us -> 43.9 us  [shards(): small = lax.psum(small_parts, both)]
    slice x26 -> x9, local copies, waits for them, and re-layouts: 78.4 us -> 4.77 us  [the longest x6 2.55 us: widen_map(): left = lax.ppermute(source[:, -3:], 'lon', forward)]
    ppermute x24 -> x27, waiting for transfers between devices: 67.7 us -> 31.8 us  [the longest x6 15.2 us: widen_map(): left = lax.ppermute(source[:, -3:], 'lon', forward)]
    concatenate x4, local copies, waits for them, and re-layouts: 35.8 us -> 2.39 us  [to_dates(): return jnp.concatenate(ordered, axis=0)]
  transfers between devices with their start and end apart: 32 -> 41, of which waited for: 10 -> 11; matrix products, arithmetic and copies ran while one was open for 18% -> 39% of each run, Pallas kernels for 0% -> 0%
where the time goes in v1:
time: 1130 us; the launch traced here: 1120 us
  waiting for transfers between devices  331 us (29%)
  other arithmetic  301 us (27%)
  matrix products  180 us (16%)
  local copies, waits for them, and re-layouts  144 us (13%)
  blocking collectives  84.6 us (7%)
  starting transfers between devices  58.8 us (5%)
  between operations  20.9 us (2%)
    psum x1, waiting for transfers between devices, summed(): lax.psum([part.astype(bf16) for part in parts], both)  181 us
    psum x1, waiting for transfers between devices, shards(): small = lax.psum(small_parts, both)  112 us
    dot_general x3, matrix products, block_forward(): jnp.dot(normed, up, preferred_element_type=f32) + up_bias.astype(f32)  76.4 us
    reduce_sum x3, other arithmetic, block_forward(): jnp.sum(masked, axis=(0, 1))  71 us
    reduce_sum x11, other arithmetic, kernel_terms(): terms.append(jnp.sum(window * upstream, axis=(0, 1)))  69.5 us
    dot_general x10, matrix products, by_transpose(): lax.dot_general(former, latter, (((1,), (1,)), ((), ())), preferred_eleme...  48.7 us
    psum x1, blocking collectives, shards(): small = lax.psum(small_parts, both)  43.9 us
    all_gather x2, blocking collectives, shards(): lax.all_gather(weight, 'lat', axis=0, tiled=True)  40.7 us
  transfers between devices with their start and end apart: 41, of which 11 were waited for; matrix products, arithmetic and copies ran while one was open for 39% of the time, Pallas kernels for 0%

profile of v1, /device:TPU:0, one launch (start us, length us, event | category | flops | bytes accessed | tf_op | source)
XLA Modules:
  0.0 1120.4 jit_solution(2642444557982647834)
XLA Ops:
  12.0 3.9 collective-permute-start.2
  30.6 28.6 %all-gather.1 = bf16[4,300,400]{1,2,0:T(8,128)(2,1)S(1)} all-gather(bf16[1,300,400]{1,2,0:T(8,128)(2,1)S(1)} %bitcast.513), channel_id=1, replica_groups=mesh['lat'=4,'lon'=8] {'lat'}, dimensions={0}, use_global_device_ids=true | all-gather | bytes 1200000 | tf_op jit(solution)/shard_map/all_gather | solution.py:188
  60.6 12.1 %all-gather.2 = bf16[4,100,800]{2,1,0:T(8,128)(2,1)S(1)} all-gather(bf16[1,100,800]{2,1,0:T(8,128)(2,1)S(1)} %bitcast.516), channel_id=1, replica_groups=mesh['lat'=4,'lon'=8] {'lat'}, dimensions={0}, use_global_device_ids=true | all-gather | bytes 800000 | tf_op jit(solution)/shard_map/all_gather | solution.py:188
  102.6 4.0 collective-permute-done.6
  110.3 28.1 %multiply_reduce_fusion.1 = (f32[400]{0:T(512)S(1)}, f32[400]{0:T(512)S(1)}, f32[48,32,400]{2,1,0:T(8,128)S(1)}) fusion(f32[48,32]{1,0:T(8,128)S(1)} %add_convert_fusion.9, bf16[54,38,400]{2,1,0:T(8,128)(2,1)S(1)} %select_maximum_fusion.6, f32[400]{0:T(512)S(1)} %bitcast.790, f32[400]{0:T(512)S(1)} %bitcast.789, f32[400]{0:T(512)S(1)} %bitcast.788, ...), kind=kLoop, calls=%fused_computation.236 | loop fusion | flops 94002400 | bytes 62756544 | tf_op jit(solution)/shard_map/reduce_sum | solution.py:117
  149.7 5.2 reshape.448
  164.8 29.0 %multiply_convert_fusion.3 = (bf16[1536,1600]{0,1:T(8,128)(2,1)}, f32[1536,1600]{0,1:T(8,128)}, f32[1536,1600]{0,1:T(8,128)}) fusion(f32[1600]{0:T(1024)S(1)} %copy-done.382, bf16[1536,400]{1,0:T(8,128)(2,1)} %bitcast.500, bf16[400,1600]{1,0:T(8,128)(2,1)} %reshape.451), kind=kOutput, calls=%fused_computation.185 | convolution fusion | flops 2125824000 | bytes 27091200 | tf_op jit(solution)/shard_map/dot_general | solution.py:125
  193.8 7.3 multiply_convert_fusion.13
  204.5 6.2 reshape.426
  226.7 12.0 %multiply_reduce_fusion.4 = (f32[800]{0:T(1024)S(1)}, f32[800]{0:T(1024)S(1)}, f32[24,16,800]{2,1,0:T(8,128)S(1)}) fusion(f32[24,16]{1,0:T(8,128)S(1)} %copy.196, bf16[30,22,800]{2,1,0:T(8,128)(2,1)S(1)} %select_maximum_fusion.10, f32[800]{0:T(1024)S(1)} %copy-done.181, f32[800]{0:T(1024)S(1)} %copy-done.182, f32[800]{0:T(1024)S(1)} %copy-done.183, ...), kind=kLoop, calls=%fused_computation.643 | loop fusion | flops 51608000 | bytes 28043136 | tf_op jit(solution)/shard_map/reduce_sum | solution.py:117
  259.4 16.4 %multiply_convert_fusion.4 = (bf16[384,3200]{1,0:T(8,128)(2,1)}, f32[384,3200]{1,0:T(8,128)}, f32[384,3200]{1,0:T(8,128)}) fusion(f32[3200]{0:T(1024)S(1)} %copy-done.219, bf16[384,800]{1,0:T(8,128)(2,1)S(1)} %bitcast.504, bf16[800,3200]{1,0:T(8,128)(2,1)} %all-gather.13.cloned.1.call-done), kind=kOutput, calls=%fused_computation.219 | convolution fusion | flops 2045952000 | bytes 18035200 | tf_op jit(solution)/shard_map/dot_general | solution.py:125
  275.9 6.5 fusion.440
  289.2 3.7 reshape.431
  305.1 30.9 %multiply_reduce_fusion = (f32[400]{0:T(512)S(1)}, f32[400]{0:T(512)S(1)}, f32[400]{0:T(512)}, f32[48,32,400]{2,1,0:T(8,128)}) fusion(f32[48,32]{1,0:T(8,128)S(1)} %copy-done.82, bf16[12,32,400]{2,1,0:T(8,128)(2,1)S(1)} %get-tuple-element.374, bf16[12,32,400]{2,1,0:T(8,128)(2,1)S(1)} %get-tuple-element.375, bf16[12,32,400]{2,1,0:T(8,128)(2,1)S(1)} %get-tuple-element.376, ...), kind=kLoop, calls=%fused_computation.234 | loop fusion | flops 110590800 | bytes 56844544 | tf_op jit(solution)/shard_map/reduce_sum | solution.py:117
  337.5 3.8 all-to-all-start.2
  351.9 5.3 reshape.430
  365.1 31.0 %multiply_convert_fusion.2 = (bf16[1536,1600]{0,1:T(8,128)(2,1)}, f32[1536,1600]{0,1:T(8,128)}, f32[1536,1600]{0,1:T(8,128)}) fusion(f32[1600]{0:T(1024)} %convert_element_type.1562, bf16[1536,400]{1,0:T(8,128)(2,1)S(1)} %bitcast.502, bf16[400,1600]{1,0:T(8,128)(2,1)S(1)} %reshape.457), kind=kOutput, calls=%fused_computation.172 | convolution fusion | flops 2125824000 | bytes 27091200 | tf_op jit(solution)/shard_map/dot_general | solution.py:125
  396.1 11.4 %convert_reduce_fusion = (f32[1600]{0:T(1024)}, bf16[1536,1600]{0,1:T(8,128)(2,1)S(1)}) fusion(f32[1536,1600]{0,1:T(8,128)} %get-tuple-element.328, f32[1536,1600]{0,1:T(8,128)} %get-tuple-element.609, bf16[1600,400]{1,0:T(8,128)(2,1)} %all-gather.17.cloned.1.call-done, f32[1536,400]{0,1:T(8,128)} %copy.210, f32[1536]{0:T(1024)S(1)} %copy-done.122), kind=kOutput, calls=%fused_computation.168 | convolution fusion | flops 1994340864 | bytes 28326144 | tf_op jit(solution)/shard_map/dot_general | solution.py:101
  407.5 4.4 fusion.488
  411.9 4.2 convolution_convert_fusion.3
  419.7 3.9 convolution_add_fusion.3
  434.7 5.9 all-to-all-start.3
  450.6 10.7 fusion.211
  462.4 9.0 fusion.212
  474.0 5.8 fusion.191
  491.9 28.8 %convert_reduce_fusion.8 = (f32[400]{0:T(512)}, bf16[48,32,400]{2,1,0:T(8,128)(2,1)S(1)}) fusion(bf16[54,38,400]{2,1,0:T(8,128)(2,1)S(1)} %select_maximum_fusion.2, f32[400]{0:T(512)S(1)} %bitcast.692, f32[400]{0:T(512)S(1)} %bitcast.691, f32[400]{0:T(512)S(1)} %bitcast.690, f32[400]{0:T(512)S(1)} %bitcast.689, f32[400]{0:T(512)S(1)} %bitcast.688, ...), kind=kLoop, calls=%fused_computation.909 | loop fusion | flops 108748400 | bytes 55612544 | tf_op jit(solution)/shard_map/reduce_sum | solution.py:237
  526.2 5.4 reduce_sum.1612
  537.5 9.6 convert_reduce_fusion.2
  547.1 5.2 convolution_convert_fusion.1
  559.5 5.9 all-to-all-start.4
  573.9 4.7 convolution_convert_fusion
  580.2 5.3 fusion.434
  586.3 3.9 fusion.435
  602.4 12.4 %convert_reduce_fusion.6 = (f32[800]{0:T(1024)}, bf16[24,16,800]{2,1,0:T(8,128)(2,1)S(1)}) fusion(bf16[30,22,800]{2,1,0:T(8,128)(2,1)S(1)} %select_maximum_fusion.8, f32[800]{0:T(1024)S(1)} %copy-done.146, f32[800]{0:T(1024)S(1)} %copy-done.147, f32[800]{0:T(1024)S(1)} %copy-done.148, f32[800]{0:T(1024)S(1)} %copy-done.149, f32[800]{0:T(1024)S(1)} %copy-done.150, ...), kind=kLoop, calls=%fused_computation.866 | loop fusion | flops 51916000 | bytes 28654336 | tf_op jit(solution)/shard_map/reduce_sum | solution.py:254
  627.4 10.6 convert_reduce_fusion.1
  638.1 3.8 fusion.490
  641.9 4.2 convolution_convert_fusion.5
  656.3 4.4 all-to-all-start.5
  667.8 43.9 %all-reduce.6 = (f32[1600]{0:T(1024)}, f32[400]{0:T(512)}, f32[800]{0:T(1024)}, f32[3200]{0:T(1024)}, f32[800]{0:T(1024)}, /*index=5*/f32[400]{0:T(512)}, f32[1600]{0:T(1024)}, f32[400]{0:T(512)}) all-reduce(f32[1600]{0:T(1024)S(1)} %get-tuple-element.617, ...), channel_id=1, replica_groups=mesh['lat'=4,'lon'=8] {'lat','lon'}, use_global_device_ids=true, to_apply=%region_75.76 | all-reduce | flops 9200 | bytes 73600 | tf_op jit(solution)/shard_map/psum | solution.py:281
  711.9 10.8 fusion.285
  724.6 9.0 fusion.286
  738.7 23.7 %add_convert_fusion = bf16[48,32,400]{2,1,0:T(8,128)(2,1)S(1)} fusion(f32[48,32,400]{2,1,0:T(8,128)S(1)} %copy-done.34, bf16[48,32,400]{2,1,0:T(8,128)(2,1)S(1)} %get-tuple-element.324, bf16[48,3,400]{2,1,0:T(4,128)(2,1)S(1)} %collective-permute-done.23, bf16[48,3,400]{2,1,0:T(4,128)(2,1)S(1)} %collective-permute-done.22, ...), kind=kLoop, calls=%fused_computation.590 | loop fusion | flops 102604800 | bytes 56839744 | tf_op jit(solution)/shard_map/convert_element_type | solution.py:260
  767.0 7.9 fusion.284
  777.9 10.0 collective-permute-done.25
  793.7 181.1 %all-reduce.14.cloned.1.call-done = (bf16[400,1600]{1,0:T(8,128)(2,1)}, bf16[1600,400]{0,1:T(8,128)(2,1)}, bf16[400,800]{1,0:T(8,128)(2,1)}, bf16[800,3200]{1,0:...) async-done(((bf16[400,1600]{1,0:T(8,128)(2,1)}, bf16[1600,400]{0,1:T(8,128)(2,1)}, ...) | async-done | bytes 16960016 | tf_op jit(solution)/shard_map/psum | solution.py:263
  981.9 4.7 convert_element_type.1752
  986.6 4.7 convert_element_type.1755
  996.6 112.0 %all-reduce.12.cloned.1.call-done = (f32[7,7,400]{2,1,0:T(8,128)}, f32[7,7,800]{2,1,0:T(8,128)}, f32[7,7,400]{2,1,0:T(8,128)}) async-done(((f32[7,7,400]{2,1,0:T(8,128)}, f32[7,7,800]{2,1,0:T(8,128)}, f32[7,7,400]{2,1,0:T(8,128)}), (f32[7,7,400]{2,1,0:T(8,128)}, f32[7,7,800]{2,1,0:T(8,128)}, f32[7,7,400]{2,1,0:T(8,128)})) %all-reduce.12.cloned.1.call-update) | async-done | bytes 313616 | tf_op jit(solution)/shard_map/psum | solution.py:281
  (1167 shorter events, 298.4 us)
Async XLA Ops:
  7.2 155.0 %all-gather.19.cloned.1.call-start = ((), (), s32[]{:S(2)}) async-start(), calls=%async_computation.10 | async-start | bytes 1730560 | tf_op jit(solution)/shard_map/all_gather | solution.py:188
  8.0 185.8 %all-gather.11.cloned.1.call-start = ((), (), s32[]{:S(2)}) async-start(), calls=%async_computation.6 | async-start | bytes 2048000 | tf_op jit(solution)/shard_map/all_gather | solution.py:188
  8.7 250.7 %all-gather.13.cloned.1.call-start = ((), (), s32[]{:S(2)}) async-start(), calls=%async_computation.7 | async-start | bytes 6400000 | tf_op jit(solution)/shard_map/all_gather | solution.py:188
  9.5 266.4 %all-gather.15.cloned.1.call-start = ((), (), s32[]{:S(2)}) async-start(), calls=%async_computation.8 | async-start | bytes 7168000 | tf_op jit(solution)/shard_map/all_gather | solution.py:188
  10.1 337.6 %all-gather.21.cloned.1.call-start = ((), (), s32[]{:S(2)}) async-start(), calls=%async_computation.11 | async-start | bytes 1730560 | tf_op jit(solution)/shard_map/all_gather | solution.py:188
  10.6 385.4 %all-gather.17.cloned.1.call-start = ((), (), s32[]{:S(2)}) async-start(), calls=%async_computation.9 | async-start | bytes 2048000 | tf_op jit(solution)/shard_map/all_gather | solution.py:188
  12.0 63.7 %collective-permute-start.2 = (s32[12,32]{1,0:T(8,128)}, s32[12,32]{1,0:T(8,128)}, u32[]{:S(2)}, u32[]{:S(2)}) collective-permute-start(s32[12,32]{1,0:T(8,128)} %bitcast.479), channel_id=1, source_target_pairs={{0,24},{8,16},{16,8},{24,0},{1,25},{9,17},{17,9},{25,1},{2,26},{10... | collective-permute-start | bytes 4616 | tf_op jit(solution)/shard_map/ppermute | solution.py:24
  16.5 70.1 %collective-permute-start.1 = (s32[12,32]{1,0:T(8,128)}, s32[12,32]{1,0:T(8,128)}, u32[]{:S(2)}, u32[]{:S(2)}) collective-permute-start(s32[12,32]{1,0:T(8,128)} %bitcast.480), channel_id=1, source_target_pairs={{0,16},{8,24},{16,0},{24,8},{1,17},{9,25},{17,1},{25,9},{2,18},{10... | collective-permute-start | bytes 4616 | tf_op jit(solution)/shard_map/ppermute | solution.py:24
  18.1 74.1 %collective-permute-start.5 = (bf16[12,32,400]{2,1,0:T(8,128)(2,1)}, bf16[12,32,400]{2,1,0:T(8,128)(2,1)}, u32[]{:S(2)}, u32[]{:S(2)}) collective-permute-start(bf16[12,32,400]{2,1,0:T(8,128)(2,1)} %get-tuple-element.371), channel_id=1, source_target_pairs={{0,24},{8,16},{16,8},{24,0},{1,25},{9,17},{17,9},{25,1},{2,26},{10... | collective-permute-start | bytes 921608 | tf_op jit(solution)/shard_map/ppermute | solution.py:24
  19.6 73.6 %collective-permute-start.4 = (bf16[12,32,400]{2,1,0:T(8,128)(2,1)}, bf16[12,32,400]{2,1,0:T(8,128)(2,1)}, u32[]{:S(2)}, u32[]{:S(2)}) collective-permute-start(bf16[12,32,400]{2,1,0:T(8,128)(2,1)} %get-tuple-element.372), channel_id=1, source_target_pairs={{0,16},{8,24},{16,0},{24,8},{1,17},{9,25},{17,1},{25,9},{2,18},{10... | collective-permute-start | bytes 921608 | tf_op jit(solution)/shard_map/ppermute | solution.py:24
  19.7 73.5 %collective-permute-start.3 = (bf16[12,32,400]{2,1,0:T(8,128)(2,1)}, bf16[12,32,400]{2,1,0:T(8,128)(2,1)}, u32[]{:S(2)}, u32[]{:S(2)}) collective-permute-start(bf16[12,32,400]{2,1,0:T(8,128)(2,1)} %get-tuple-element.370), channel_id=1, source_target_pairs={{0,8},{8,0},{16,24},{24,16},{1,9},{9,1},{17,25},{25,17},{2,10},{10... | collective-permute-start | bytes 921608 | tf_op jit(solution)/shard_map/ppermute | solution.py:24
  29.7 48.2 %copy-start.403 = (bf16[400]{0:T(512)(128)(2,1)S(1)}, bf16[400]{0:T(512)(128)(2,1)}, u32[]{:S(2)}) copy-start(bf16[400]{0:T(512)(128)(2,1)} %param.33) | copy-start | bytes 2404
  29.7 48.8 %copy-start.391 = (bf16[400]{0:T(512)(128)(2,1)S(1)}, bf16[400]{0:T(512)(128)(2,1)}, u32[]{:S(2)}) copy-start(bf16[400]{0:T(512)(128)(2,1)} %param.32) | copy-start | bytes 2404
  29.7 49.3 %copy-start.379 = (bf16[3200]{0:T(1024)(128)(2,1)S(1)}, bf16[3200]{0:T(1024)(128)(2,1)}, u32[]{:S(2)}) copy-start(bf16[3200]{0:T(1024)(128)(2,1)} %param.44) | copy-start | bytes 19204
  29.7 49.9 %copy-start.395 = (bf16[800]{0:T(1024)(128)(2,1)S(1)}, bf16[800]{0:T(1024)(128)(2,1)}, u32[]{:S(2)}) copy-start(bf16[800]{0:T(1024)(128)(2,1)} %param.39) | copy-start | bytes 4804
  29.7 50.5 %copy-start.396 = (bf16[800]{0:T(1024)(128)(2,1)S(1)}, bf16[800]{0:T(1024)(128)(2,1)}, u32[]{:S(2)}) copy-start(bf16[800]{0:T(1024)(128)(2,1)} %param.42) | copy-start | bytes 4804
  29.8 51.1 %copy-start.380 = (bf16[800]{0:T(1024)(128)(2,1)S(1)}, bf16[800]{0:T(1024)(128)(2,1)}, u32[]{:S(2)}) copy-start(bf16[800]{0:T(1024)(128)(2,1)} %param.41) | copy-start | bytes 4804
  29.8 51.7 %copy-start.397 = (bf16[800]{0:T(1024)(128)(2,1)S(1)}, bf16[800]{0:T(1024)(128)(2,1)}, u32[]{:S(2)}) copy-start(bf16[800]{0:T(1024)(128)(2,1)} %param.46) | copy-start | bytes 4804
  75.7 11.7 %collective-permute-start = (s32[12,32]{1,0:T(8,128)S(1)}, s32[12,32]{1,0:T(8,128)S(1)}, u32[]{:S(2)}, u32[]{:S(2)}) collective-permute-start(s32[12,32]{1,0:T(8,128)S(1)} %bitcast.835), channel_id=1, source_target_pairs={{0,8},{8,0},{16,24},{24,16},{1,9},{9,1},{17,25},{25,17},{2,10},{10... | collective-permute-start | bytes 4616 | tf_op jit(solution)/shard_map/ppermute | solution.py:24
  86.5 161.6 %collective-permute-start.17 = (bf16[12,32,400]{2,1,0:T(8,128)(2,1)}, bf16[12,32,400]{2,1,0:T(8,128)(2,1)}, u32[]{:S(2)}, u32[]{:S(2)}) collective-permute-start(bf16[12,32,400]{2,1,0:T(8,128)(2,1)} %get-tuple-element.379), channel_id=1, source_target_pairs={{0,24},{8,16},{16,8},{24,0},{1,25},{9,17},{17,9},{25,1},{2,26},{10... | collective-permute-start | bytes 921608 | tf_op jit(solution)/shard_map/ppermute | solution.py:24
  87.4 160.8 %collective-permute-start.16 = (bf16[12,32,400]{2,1,0:T(8,128)(2,1)}, bf16[12,32,400]{2,1,0:T(8,128)(2,1)}, u32[]{:S(2)}, u32[]{:S(2)}) collective-permute-start(bf16[12,32,400]{2,1,0:T(8,128)(2,1)} %get-tuple-element.380), channel_id=1, source_target_pairs={{0,16},{8,24},{16,0},{24,8},{1,17},{9,25},{17,1},{25,9},{2,18},{10... | collective-permute-start | bytes 921608 | tf_op jit(solution)/shard_map/ppermute | solution.py:24
  92.3 155.9 %collective-permute-start.15 = (bf16[12,32,400]{2,1,0:T(8,128)(2,1)}, bf16[12,32,400]{2,1,0:T(8,128)(2,1)}, u32[]{:S(2)}, u32[]{:S(2)}) collective-permute-start(bf16[12,32,400]{2,1,0:T(8,128)(2,1)} %get-tuple-element.378), channel_id=1, source_target_pairs={{0,8},{8,0},{16,24},{24,16},{1,9},{9,1},{17,25},{25,17},{2,10},{10... | collective-permute-start | bytes 921608 | tf_op jit(solution)/shard_map/ppermute | solution.py:24
  97.2 5.3 collective-permute-start.7
  97.3 9.2 collective-permute-start.6
  139.4 18.8 %all-to-all-start = ((f32[32,3,400]{2,1,0:T(4,128)}), f32[32,3,400]{2,1,0:T(4,128)}, u32[]{:S(2)}, u32[]{:S(2)}) async-start(f32[32,3,400]{2,1,0:T(4,128)} %broadcast_in_dim.12), calls=%async_computation | async-start | bytes 524288 | tf_op jit(solution)/shard_map/all_to_all | solution.py:72
  215.6 6.5 collective-permute-start.9
  219.1 6.6 collective-permute-start.8
  239.9 17.9 %all-to-all-start.1 = ((f32[32,3,800]{2,1,0:T(4,128)}), f32[32,3,800]{2,1,0:T(4,128)S(1)}, u32[]{:S(2)}, u32[]{:S(2)}) async-start(f32[32,3,800]{2,1,0:T(4,128)} %broadcast_in_dim.13), calls=%async_computation.1 | async-start | bytes 917504 | tf_op jit(solution)/shard_map/all_to_all | solution.py:72
  295.6 4.8 collective-permute-start.11
  296.5 6.9 collective-permute-start.10
  337.5 19.8 %all-to-all-start.2 = ((f32[32,3,400]{2,1,0:T(4,128)}), f32[32,3,400]{2,1,0:T(4,128)}, u32[]{:S(2)}, u32[]{:S(2)}) async-start(f32[32,3,400]{2,1,0:T(4,128)} %broadcast_in_dim.14), calls=%async_computation.2 | async-start | bytes 524288 | tf_op jit(solution)/shard_map/all_to_all | solution.py:72
  434.7 15.8 %all-to-all-start.3 = ((f32[32,2,400]{2,1,0:T(2,128)}), f32[32,2,400]{2,1,0:T(2,128)S(1)}, u32[]{:S(2)}, u32[]{:S(2)}) async-start(f32[32,2,400]{2,1,0:T(2,128)} %broadcast_in_dim.15), calls=%async_computation.3 | async-start | bytes 262144 | tf_op jit(solution)/shard_map/all_to_all | solution.py:72
  445.0 42.1 %collective-permute-start.14 = (bf16[12,32,400]{2,1,0:T(8,128)(2,1)}, bf16[12,32,400]{2,1,0:T(8,128)(2,1)S(1)}, u32[]{:S(2)}, u32[]{:S(2)}) collective-permute-start(bf16[12,32,400]{2,1,0:T(8,128)(2,1)} %get-tuple-element.354), channel_id=1, source_target_pairs={{0,24},{8,16},{16,8},{24,0},{1,25},{9,17},{17,9},{25,1},{2,26},{10... | collective-permute-start | bytes 921608 | tf_op jit(solution)/shard_map/ppermute | solution.py:42
  447.7 39.4 %collective-permute-start.13 = (bf16[12,32,400]{2,1,0:T(8,128)(2,1)}, bf16[12,32,400]{2,1,0:T(8,128)(2,1)}, u32[]{:S(2)}, u32[]{:S(2)}) collective-permute-start(bf16[12,32,400]{2,1,0:T(8,128)(2,1)} %get-tuple-element.355), channel_id=1, source_target_pairs={{0,16},{8,24},{16,0},{24,8},{1,17},{9,25},{17,1},{25,9},{2,18},{10... | collective-permute-start | bytes 921608 | tf_op jit(solution)/shard_map/ppermute | solution.py:42
  448.3 38.8 %collective-permute-start.12 = (bf16[12,32,400]{2,1,0:T(8,128)(2,1)}, bf16[12,32,400]{2,1,0:T(8,128)(2,1)}, u32[]{:S(2)}, u32[]{:S(2)}) collective-permute-start(bf16[12,32,400]{2,1,0:T(8,128)(2,1)} %get-tuple-element.356), channel_id=1, source_target_pairs={{0,8},{8,0},{16,24},{24,16},{1,9},{9,1},{17,25},{25,17},{2,10},{10... | collective-permute-start | bytes 921608 | tf_op jit(solution)/shard_map/ppermute | solution.py:42
  471.4 19.0 %collective-permute-start.19 = (bf16[48,3,400]{2,1,0:T(4,128)(2,1)}, bf16[48,3,400]{2,1,0:T(4,128)(2,1)S(1)}, u32[]{:S(2)}, u32[]{:S(2)}) collective-permute-start(bf16[48,3,400]{2,1,0:T(4,128)(2,1)} %get-tuple-element.348), channel_id=1, source_target_pairs={{1,0},{2,1},{3,2},{4,3},{5,4},{6,5},{7,6},{0,7},{9,8},{10,9},{11,1... | collective-permute-start | bytes 345608 | tf_op jit(solution)/shard_map/ppermute | solution.py:57
  474.0 16.4 %collective-permute-start.18 = (bf16[48,3,400]{2,1,0:T(4,128)(2,1)}, bf16[48,3,400]{2,1,0:T(4,128)(2,1)S(1)}, u32[]{:S(2)}, u32[]{:S(2)}) collective-permute-start(bf16[48,3,400]{2,1,0:T(4,128)(2,1)} %get-tuple-element.347), channel_id=1, source_target_pairs={{0,1},{1,2},{2,3},{3,4},{4,5},{5,6},{6,7},{7,0},{8,9},{9,10},{10,1... | collective-permute-start | bytes 345608 | tf_op jit(solution)/shard_map/ppermute | solution.py:56
  559.5 19.0 %all-to-all-start.4 = ((f32[32,2,800]{2,1,0:T(2,128)}), f32[32,2,800]{2,1,0:T(2,128)}, u32[]{:S(2)}, u32[]{:S(2)}) async-start(f32[32,2,800]{2,1,0:T(2,128)} %broadcast_in_dim.16), calls=%async_computation.4 | async-start | bytes 458752 | tf_op jit(solution)/shard_map/all_to_all | solution.py:72
  590.2 9.0 collective-permute-start.21
  593.6 6.9 collective-permute-start.20
  656.3 55.4 %all-to-all-start.5 = ((f32[32,2,400]{2,1,0:T(2,128)}), f32[32,2,400]{2,1,0:T(2,128)S(1)}, u32[]{:S(2)}, u32[]{:S(2)}) async-start(f32[32,2,400]{2,1,0:T(2,128)} %broadcast_in_dim.17), calls=%async_computation.5 | async-start | bytes 262144 | tf_op jit(solution)/shard_map/all_to_all | solution.py:72
  660.7 314.1 %all-reduce.14.cloned.1.call-start = ((), (), s32[]{:S(2)}) async-start(), calls=%async_computation.13 | async-start | bytes 34611200 | tf_op jit(solution)/shard_map/psum | solution.py:263
  667.2 441.4 %all-reduce.12.cloned.1.call-start = ((), (), s32[]{:S(2)}) async-start(), calls=%async_computation.12 | async-start | bytes 860160 | tf_op jit(solution)/shard_map/psum | solution.py:281
  722.8 11.1 collective-permute-start.23
  724.6 12.6 %collective-permute-start.22 = (bf16[48,3,400]{2,1,0:T(4,128)(2,1)S(1)}, bf16[48,3,400]{2,1,0:T(4,128)(2,1)S(1)}, u32[]{:S(2)}, u32[]{:S(2)}) collective-permute-start(bf16[48,3,400]{2,1,0:T(4,128)(2,1)S(1)} %get-tuple-element.345), channel_id=1, source_target_pairs={{0,1},{1,2},{2,3},{3,4},{4,5},{5,6},{6,7},{7,0},{8,9},{9,10},{10,1... | collective-permute-start | bytes 345608 | tf_op jit(solution)/shard_map/ppermute | solution.py:56
  763.5 14.4 %collective-permute-start.26 = (bf16[12,32,400]{2,1,0:T(8,128)(2,1)}, bf16[12,32,400]{2,1,0:T(8,128)(2,1)S(1)}, u32[]{:S(2)}, u32[]{:S(2)}) collective-permute-start(bf16[12,32,400]{2,1,0:T(8,128)(2,1)} %get-tuple-element.342), channel_id=1, source_target_pairs={{0,24},{8,16},{16,8},{24,0},{1,25},{9,17},{17,9},{25,1},{2,26},{10... | collective-permute-start | bytes 921608 | tf_op jit(solution)/shard_map/ppermute | solution.py:42
  764.9 23.1 %collective-permute-start.25 = (bf16[12,32,400]{2,1,0:T(8,128)(2,1)}, bf16[12,32,400]{2,1,0:T(8,128)(2,1)S(1)}, u32[]{:S(2)}, u32[]{:S(2)}) collective-permute-start(bf16[12,32,400]{2,1,0:T(8,128)(2,1)} %get-tuple-element.343), channel_id=1, source_target_pairs={{0,16},{8,24},{16,0},{24,8},{1,17},{9,25},{17,1},{25,9},{2,18},{10... | collective-permute-start | bytes 921608 | tf_op jit(solution)/shard_map/ppermute | solution.py:42
  765.8 25.1 %collective-permute-start.24 = (bf16[12,32,400]{2,1,0:T(8,128)(2,1)}, bf16[12,32,400]{2,1,0:T(8,128)(2,1)}, u32[]{:S(2)}, u32[]{:S(2)}) collective-permute-start(bf16[12,32,400]{2,1,0:T(8,128)(2,1)} %get-tuple-element.344), channel_id=1, source_target_pairs={{0,8},{8,0},{16,24},{24,16},{1,9},{9,1},{17,25},{25,17},{2,10},{10... | collective-permute-start | bytes 921608 | tf_op jit(solution)/shard_map/ppermute | solution.py:42
  (409 other events, 3634.7 us)
Sparse Core Ops, SparseCore 0:
  9.9 49.1 all-gather.18
  61.0 45.4 all-gather.10
  108.3 63.1 all-gather.12
  173.2 65.5 all-gather.14
  240.4 30.6 all-gather.20
  272.8 31.5 all-gather.16
  669.7 305.0 all-reduce.13
  982.3 126.1 all-reduce.11

commit v2 on v1

v2 whole, which is shorter than its diff:
```python
import functools
import math

import jax
import jax.numpy as jnp
from jax import lax
from jax.experimental import pallas as pl
from jax.experimental.pallas import tpu as pltpu
from jax.sharding import PartitionSpec as P

epsilon = 1e-05
both = ("lat", "lon")
bf16 = jnp.bfloat16
f32 = jnp.float32
lanes = 128
strip = 12
room = pltpu.CompilerParams(vmem_limit_bytes=56 << 20)


def exchange_pairs(count, group, step):
    return [(i, (i // group) * group + ((i % group) ^ step)) for i in range(count)]


def to_dates(tiles):
    dates, count = tiles.shape[0], lax.axis_size("lat")
    own = lax.axis_index("lat") % dates
    pieces = [lax.dynamic_index_in_dim(tiles, own, 0, keepdims=False)]
    for step in range(1, dates):
        pieces.append(
            lax.ppermute(
                lax.dynamic_index_in_dim(tiles, own ^ step, 0, keepdims=False),
                "lat",
                exchange_pairs(count, dates, step),
            )
        )
    stacked = jnp.stack(pieces)
    ordered = [lax.dynamic_index_in_dim(stacked, own ^ tile, 0, keepdims=False) for tile in range(dates)]
    return jnp.concatenate(ordered, axis=0)


def from_dates(band, dates):
    count = lax.axis_size("lat")
    own = lax.axis_index("lat") % dates
    tiles = band.reshape((dates, band.shape[0] // dates) + band.shape[1:])
    pieces = [lax.dynamic_index_in_dim(tiles, own, 0, keepdims=False)]
    for step in range(1, dates):
        pieces.append(
            lax.ppermute(
                lax.dynamic_index_in_dim(tiles, own ^ step, 0, keepdims=False),
                "lat",
                exchange_pairs(count, dates, step),
            )
        )
    stacked = jnp.stack(pieces)
    return jnp.stack([lax.dynamic_index_in_dim(stacked, own ^ date, 0, keepdims=False) for date in range(dates)])


def borders(source, dates):
    count = lax.axis_size("lon")
    forward = [(i, (i + 1) % count) for i in range(count)]
    backward = [(target, origin) for origin, target in forward]
    left = lax.ppermute(source[:, -3:], "lon", forward)
    right = lax.ppermute(source[:, :3], "lon", backward)
    tiles = lax.axis_size("lat")
    if tiles == dates:
        return left, right
    down = [(i, i + dates) for i in range(tiles - dates)]
    up = [(target, origin) for origin, target in down]
    last = jnp.concatenate([left[-3:], source[-3:], right[-3:]], axis=1)
    first = jnp.concatenate([left[:3], source[:3], right[:3]], axis=1)
    return left, right, lax.ppermute(last, "lat", down), lax.ppermute(first, "lat", up)


def sum_all(local):
    count = lax.axis_size(both)
    copies = jnp.broadcast_to(local[None], (count,) + local.shape)
    return jnp.sum(lax.all_to_all(copies, both, 0, 0, tiled=False), axis=0)


def fill_extended(wide_ref, centre, edges):
    rows, columns = centre.shape[0], centre.shape[1]
    blank = jnp.zeros((3, columns + 16, lanes), f32)
    wide_ref[0:3] = blank
    wide_ref[rows + 3 :] = blank
    wide_ref[3 : rows + 3, 8 : columns + 8] = centre[...].astype(f32)
    wide_ref[3 : rows + 3, 5:8] = edges[0][...].astype(f32)
    wide_ref[3 : rows + 3, columns + 8 : columns + 11] = edges[1][...].astype(f32)
    if len(edges) > 2:
        wide_ref[0:3, 5 : columns + 11] = edges[2][...].astype(f32)
        wide_ref[rows + 3 :, 5 : columns + 11] = edges[3][...].astype(f32)


def strip_sum(wide_ref, taps, top, start, flipped):
    total = None
    for column in range(7):
        window = wide_ref[pl.ds(top, strip + 6), start + 5 + column : start + 13 + column, :]
        for across in range(7):
            place = 7 * across + column
            tap = taps[pl.ds(48 - place if flipped else place, 8, stride=0), :]
            term = window[across : across + strip] * tap[None]
            total = term if total is None else total + term
    return total


def stencil_forward_kernel(edge_count, source, *refs):
    edges = refs[:edge_count]
    taps, sea, mixed, sums, wide_ref = refs[edge_count:]
    rows, columns = source.shape[0], source.shape[1]
    fill_extended(wide_ref, source, edges)

    def step(index, carry):
        first, square = carry
        top = index * strip
        for start in range(0, columns, 8):
            here = (pl.ds(top, strip), slice(start, start + 8))
            total = strip_sum(wide_ref, taps, top, start, False)
            mixed[here] = total
            masked = total * sea[here]
            first = first + jnp.sum(masked, axis=0)
            square = square + jnp.sum(masked * total, axis=0)
        return first, square

    zero = jnp.zeros((8, lanes), f32)
    first, square = lax.fori_loop(0, rows // strip, step, (zero, zero))
    sums[0:1] = jnp.sum(first, axis=0, keepdims=True)
    sums[1:2] = jnp.sum(square, axis=0, keepdims=True)


def stencil_backward_kernel(edge_count, grad, *refs):
    edges = refs[:edge_count]
    taps, sea, upstream, out, sums, wide_ref = refs[edge_count:]
    rows, columns = grad.shape[0], grad.shape[1]
    fill_extended(wide_ref, grad, edges)

    def step(index, first):
        top = index * strip
        for start in range(0, columns, 8):
            here = (pl.ds(top, strip), slice(start, start + 8))
            total = strip_sum(wide_ref, taps, top, start, True)
            low = (total + upstream[here].astype(f32) * sea[here]).astype(bf16)
            out[here] = low
            first = first + jnp.sum(low.astype(f32), axis=0)
        return first

    first = lax.fori_loop(0, rows // strip, step, jnp.zeros((8, lanes), f32))
    sums[...] = jnp.sum(first, axis=0, keepdims=True)


def kernel_grad_kernel(edge_count, source, *refs):
    edges = refs[:edge_count]
    grad, out, wide_ref, sums_ref = refs[edge_count:]
    rows, columns = source.shape[0], source.shape[1]
    fill_extended(wide_ref, source, edges)
    sums_ref[...] = jnp.zeros_like(sums_ref)

    def step(index, carry):
        top = index * strip
        for start in range(0, columns, 8):
            upstream = grad[pl.ds(top, strip), start : start + 8, :].astype(f32)
            for column in range(7):
                window = wide_ref[pl.ds(top, strip + 6), start + 5 + column : start + 13 + column, :]
                for across in range(7):
                    sums_ref[7 * across + column] += jnp.sum(window[across : across + strip] * upstream, axis=0)
        return carry

    lax.fori_loop(0, rows // strip, step, 0)
    out[...] = jnp.sum(sums_ref[...], axis=1)


def by_channel(array):
    rest = array.shape[:-1]
    return pl.BlockSpec(rest + (lanes,), lambda tile: (0,) * len(rest) + (tile,))


def same_block(array):
    return pl.BlockSpec(array.shape, lambda tile: (0,) * array.ndim)


def wide_scratch(rows, columns):
    return pltpu.VMEM((rows + 6, columns + 16, lanes), f32)


def stencil_forward(source, edges, taps, sea):
    rows, columns, channels = source.shape
    sums = jax.ShapeDtypeStruct((2, channels), f32)
    mixed = jax.ShapeDtypeStruct(source.shape, f32)
    return pl.pallas_call(
        functools.partial(stencil_forward_kernel, len(edges)),
        grid=(pl.cdiv(channels, lanes),),
        in_specs=[by_channel(array) for array in (source, *edges, taps)] + [same_block(sea)],
        out_specs=[by_channel(mixed), by_channel(sums)],
        out_shape=[mixed, sums],
        scratch_shapes=[wide_scratch(rows, columns)],
        compiler_params=room,
        name="stencil_forward",
    )(source, *edges, taps, sea)


def stencil_backward(grad, edges, taps, sea, upstream):
    rows, columns, channels = grad.shape
    out = jax.ShapeDtypeStruct(grad.shape, bf16)
    sums = jax.ShapeDtypeStruct((1, channels), f32)
    return pl.pallas_call(
        functools.partial(stencil_backward_kernel, len(edges)),
        grid=(pl.cdiv(channels, lanes),),
        in_specs=[by_channel(array) for array in (grad, *edges, taps)] + [same_block(sea), by_channel(upstream)],
        out_specs=[by_channel(out), by_channel(sums)],
        out_shape=[out, sums],
        scratch_shapes=[wide_scratch(rows, columns)],
        compiler_params=room,
        name="stencil_backward",
    )(grad, *edges, taps, sea, upstream)


def kernel_grad(source, edges, grad):
    rows, columns, channels = source.shape
    out = jax.ShapeDtypeStruct((49, channels), f32)
    return pl.pallas_call(
        functools.partial(kernel_grad_kernel, len(edges)),
        grid=(pl.cdiv(channels, lanes),),
        in_specs=[by_channel(array) for array in (source, *edges, grad)],
        out_specs=by_channel(out),
        out_shape=out,
        scratch_shapes=[wide_scratch(rows, columns), pltpu.VMEM((49, 8, lanes), f32)],
        compiler_params=room,
        name="kernel_grad",
    )(source, *edges, grad)


def chunks_of(width, size):
    edges = list(range(0, width, size))
    if len(edges) > 1 and width - edges[-1] < size // 2:
        edges.pop()
    return list(zip(edges, edges[1:] + [width]))


def spread(sea, channels):
    return jnp.concatenate([sea] * pl.cdiv(channels, lanes), axis=1)[:, :channels]


def gelu_pair(hidden):
    below = 0.5 + 0.5 * lax.erf(hidden * math.sqrt(0.5))
    density = jnp.exp(-0.5 * hidden * hidden) * (1.0 / math.sqrt(2.0 * math.pi))
    return hidden * below, below + hidden * density


def mlp_forward_kernel(
    size, mixed, source, sea, scales, up, up_bias, down, down_bias, out, active, slope, normed
):
    unit = (mixed[...] - scales[0:1]) * scales[1:2]
    low = (unit * scales[2:3] + scales[3:4]).astype(bf16)
    normed[...] = low
    branch = down_bias[...]
    for a, b in chunks_of(up.shape[1], size):
        hidden = jnp.dot(low, up[:, a:b], preferred_element_type=f32) + up_bias[:, a:b]
        value, rise = gelu_pair(hidden)
        value = value.astype(bf16)
        active[:, a:b] = value
        slope[:, a:b] = rise.astype(bf16)
        branch = branch + jnp.dot(value, down[a:b, :], preferred_element_type=f32)
    mask = spread(sea[...], out.shape[1])
    out[...] = (mask * (source[...].astype(f32) + branch)).astype(bf16)


def mlp_backward_kernel(
    size,
    upstream,
    mixed,
    slope,
    sea,
    scales,
    up,
    down,
    grad_branch,
    grad_hidden,
    grad_normed,
    sums,
    down_sums,
    up_sums,
):
    @pl.when(pl.program_id(0) == 0)
    def _():
        sums[...] = jnp.zeros_like(sums)
        down_sums[...] = jnp.zeros_like(down_sums)
        up_sums[...] = jnp.zeros_like(up_sums)

    mask = spread(sea[...], upstream.shape[1])
    low = (mask * upstream[...].astype(f32)).astype(bf16)
    grad_branch[...] = low
    down_sums[...] += jnp.sum(low.astype(f32), axis=0, keepdims=True)
    normed = None
    for a, b in chunks_of(up.shape[1], size):
        grad_active = lax.dot_general(low, down[a:b, :], (((1,), (1,)), ((), ())), preferred_element_type=f32)
        hidden = (grad_active * slope[:, a:b].astype(f32)).astype(bf16)
        grad_hidden[:, a:b] = hidden
        up_sums[:, a:b] += jnp.sum(hidden.astype(f32), axis=0, keepdims=True)
        part = lax.dot_general(hidden, up[:, a:b], (((1,), (1,)), ((), ())), preferred_element_type=f32)
        normed = part if normed is None else normed + part
    grad_normed[...] = normed
    unit = (mixed[...] - scales[0:1]) * scales[1:2]
    sums[0:1] += jnp.sum(normed, axis=0, keepdims=True)
    sums[1:2] += jnp.sum(normed * unit, axis=0, keepdims=True)


def tall(rows, width):
    return pl.BlockSpec((rows, width), lambda i: (i, 0))


def fixed(array):
    return pl.BlockSpec(array.shape, lambda i: (0, 0), pipeline_mode=pl.Buffered(1))


def mlp_forward(mixed, source, sea, scales, up, up_bias, down, down_bias):
    pixels, channels = mixed.shape
    wide = up.shape[1]
    rows = math.gcd(pixels, 384)
    return pl.pallas_call(
        functools.partial(mlp_forward_kernel, 512),
        grid=(pixels // rows,),
        in_specs=[tall(rows, channels), tall(rows, channels), tall(rows, lanes)]
        + [fixed(array) for array in (scales, up, up_bias, down, down_bias)],
        out_specs=[tall(rows, channels), tall(rows, wide), tall(rows, wide), tall(rows, channels)],
        out_shape=[jax.ShapeDtypeStruct((pixels, width), bf16) for width in (channels, wide, wide, channels)],
        compiler_params=room,
        name="mlp_forward",
    )(mixed, source, sea, scales, up, up_bias, down, down_bias)


def mlp_backward(upstream, mixed, slope, sea, scales, up, down):
    pixels, channels = mixed.shape
    wide = up.shape[1]
    rows = math.gcd(pixels, 384)
    sums = [jax.ShapeDtypeStruct(shape, f32) for shape in ((2, channels), (1, channels), (1, wide))]
    return pl.pallas_call(
        functools.partial(mlp_backward_kernel, 512),
        grid=(pixels // rows,),
        in_specs=[tall(rows, channels), tall(rows, channels), tall(rows, wide), tall(rows, lanes)]
        + [fixed(array) for array in (scales, up, down)],
        out_specs=[tall(rows, channels), tall(rows, wide), tall(rows, channels)]
        + [pl.BlockSpec(array.shape, lambda i: (0, 0)) for array in sums],
        out_shape=[
            jax.ShapeDtypeStruct((pixels, channels), bf16),
            jax.ShapeDtypeStruct((pixels, wide), bf16),
            jax.ShapeDtypeStruct((pixels, channels), f32),
        ]
        + sums,
        compiler_params=room,
        name="mlp_backward",
    )(upstream, mixed, slope, sea, scales, up, down)


def cross_rows(former, latter):
    return lax.dot_general(former, latter, (((0,), (0,)), ((), ())), preferred_element_type=f32)


def by_transpose(former, latter):
    return lax.dot_general(former, latter, (((1,), (1,)), ((), ())), preferred_element_type=f32)


def block_forward(source, params, sea, ocean, dates):
    kernel, gain, shift, up, up_bias, down, down_bias = params
    height, breadth, channels = source.shape
    taps = kernel.astype(f32).reshape(49, channels)
    edges = borders(source, dates)
    mixed, local = stencil_forward(source, edges, taps, sea)
    first, square, ocean = sum_all(jnp.concatenate([local, jnp.broadcast_to(ocean, (1, channels))]))
    mean = first / ocean
    factor = lax.rsqrt(square / ocean - mean * mean + epsilon)
    scales = jnp.stack([mean, factor, gain.astype(f32), shift.astype(f32)])
    mixed = mixed.reshape(-1, channels)
    output, active, slope, normed = mlp_forward(
        mixed,
        source.reshape(-1, channels),
        sea.reshape(-1, lanes),
        scales,
        up,
        up_bias.astype(f32)[None],
        down,
        down_bias.astype(f32)[None],
    )
    return output, (source, edges, taps, mixed, scales, ocean, normed, slope, active)


def block_backward(upstream, params, sea, stored, dates):
    kernel, gain, shift, up, up_bias, down, down_bias = params
    source, edges, taps, mixed, scales, ocean, normed, slope, active = stored
    channels = source.shape[2]
    grad_branch, grad_hidden, grad_normed, local, down_sums, up_sums = mlp_backward(
        upstream, mixed, slope, sea.reshape(-1, lanes), scales, up, down
    )
    grad_shift, grad_gain = sum_all(local)
    mean, factor, gain = scales[0], scales[1], scales[2]
    unit = (mixed - mean) * factor
    weight = spread(sea.reshape(-1, lanes), channels) / ocean
    grad_mixed = factor * (gain * grad_normed - weight * (gain * grad_shift + unit * (gain * grad_gain)))
    grad_mixed = grad_mixed.astype(bf16).reshape(source.shape)
    grad_edges = borders(grad_mixed, dates)
    grad_kernel = kernel_grad(source, edges, grad_mixed)
    grad_source, source_sums = stencil_backward(grad_mixed, grad_edges, taps, sea, upstream.reshape(source.shape))
    grad_down = cross_rows(active, grad_branch)
    grad_up = cross_rows(normed, grad_hidden)
    return (
        grad_source.reshape(-1, channels),
        source_sums[0],
        (grad_kernel, grad_gain, grad_shift, grad_up, up_sums[0], grad_down, down_sums[0]),
    )


def shards(
    fine_map,
    ocean_mask,
    out_grad,
    encode_depth,
    encode_gain,
    encode_shift,
    encode_up,
    encode_up_bias,
    encode_down,
    encode_down_bias,
    widen_weight,
    widen_bias,
    bottle_depth,
    bottle_gain,
    bottle_shift,
    bottle_up,
    bottle_up_bias,
    bottle_down,
    bottle_down_bias,
    merge_weight,
    merge_bias,
    decode_depth,
    decode_gain,
    decode_shift,
    decode_up,
    decode_up_bias,
    decode_down,
    decode_down_bias,
):
    (encode_up, encode_down, widen_weight, bottle_up, bottle_down, merge_weight, decode_up, decode_down) = (
        lax.all_gather(weight, "lat", axis=0, tiled=True)
        for weight in (
            encode_up,
            encode_down,
            widen_weight,
            bottle_up,
            bottle_down,
            merge_weight,
            decode_up,
            decode_down,
        )
    )
    dates = fine_map.shape[0]
    fine = to_dates(fine_map)
    ocean_band = to_dates(ocean_mask).astype(f32)
    upstream = to_dates(out_grad)
    height, breadth, channels = fine.shape
    half_height, half_breadth = height // 2, breadth // 2
    wide = widen_weight.shape[1]
    coarse_band = jnp.max(ocean_band.reshape(half_height, 2, half_breadth, 2), axis=(1, 3))
    sea_fine = jnp.broadcast_to(ocean_band[..., None], (height, breadth, lanes))
    sea_coarse = jnp.broadcast_to(coarse_band[..., None], (half_height, half_breadth, lanes))
    encode = (encode_depth, encode_gain, encode_shift, encode_up, encode_up_bias, encode_down, encode_down_bias)
    bottle = (bottle_depth, bottle_gain, bottle_shift, bottle_up, bottle_up_bias, bottle_down, bottle_down_bias)
    decode = (decode_depth, decode_gain, decode_shift, decode_up, decode_up_bias, decode_down, decode_down_bias)
    merge_upper = merge_weight[:wide]
    merge_lower = merge_weight[wide:]
    ocean_fine = jnp.sum(ocean_band)
    ocean_coarse = jnp.sum(coarse_band)

    skip_rows, encode_stored = block_forward(fine, encode, sea_fine, ocean_fine, dates)
    blocks = skip_rows.reshape(half_height, 2, half_breadth, 2, channels).astype(f32)
    pooled = (jnp.sum(blocks, axis=(1, 3)) * 0.25).astype(bf16).reshape(-1, channels)
    coarse_in = jnp.dot(pooled, widen_weight, preferred_element_type=f32) + widen_bias.astype(f32)
    coarse_in = coarse_in.astype(bf16).reshape(half_height, half_breadth, wide)
    coarse_low, coarse_stored = block_forward(coarse_in, bottle, sea_coarse, ocean_coarse, dates)
    upper = jnp.dot(coarse_low, merge_upper, preferred_element_type=f32)
    upper = upper.reshape(half_height, 1, half_breadth, 1, channels)
    lower = jnp.dot(skip_rows, merge_lower, preferred_element_type=f32)
    lower = lower.reshape(half_height, 2, half_breadth, 2, channels)
    merged = (lower + upper).reshape(height, breadth, channels) + merge_bias.astype(f32)
    decode_rows, decode_stored = block_forward(merged.astype(bf16), decode, sea_fine, ocean_fine, dates)
    result = from_dates(decode_rows.reshape(fine.shape), dates)

    grad_merged, grad_merge_bias, decode_grads = block_backward(
        upstream.reshape(-1, channels), decode, sea_fine, decode_stored, dates
    )
    grad_block_sum = jnp.sum(
        grad_merged.astype(f32).reshape(half_height, 2, half_breadth, 2, channels), axis=(1, 3)
    ).reshape(-1, channels)
    grad_block_low = grad_block_sum.astype(bf16)
    grad_block_rest = (grad_block_sum - grad_block_low.astype(f32)).astype(bf16)
    grad_merge_weight = jnp.concatenate(
        [
            cross_rows(coarse_low, grad_block_low) + cross_rows(coarse_low, grad_block_rest),
            cross_rows(skip_rows, grad_merged),
        ],
        axis=0,
    )
    grad_coarse = by_transpose(grad_block_low, merge_upper) + by_transpose(grad_block_rest, merge_upper)
    grad_skip_direct = by_transpose(grad_merged, merge_lower)
    grad_wide, grad_widen_bias, bottle_grads = block_backward(grad_coarse, bottle, sea_coarse, coarse_stored, dates)
    grad_widen_weight = cross_rows(pooled, grad_wide)
    grad_pooled = by_transpose(grad_wide, widen_weight).reshape(half_height, 1, half_breadth, 1, channels) * 0.25
    grad_skip = grad_skip_direct.reshape(half_height, 2, half_breadth, 2, channels) + grad_pooled
    grad_fine, _, encode_grads = block_backward(
        grad_skip.reshape(-1, channels), encode, sea_fine, encode_stored, dates
    )
    fine_grad = from_dates(grad_fine.reshape(fine.shape), dates)

    def summed(parts):
        return [total.astype(f32) for total in lax.psum([part.astype(bf16) for part in parts], both)]

    decode_up_sum, decode_down_sum, merge_sum = summed([decode_grads[3], decode_grads[5], grad_merge_weight])
    bottle_up_sum, bottle_down_sum, widen_sum = summed([bottle_grads[3], bottle_grads[5], grad_widen_weight])
    encode_up_sum, encode_down_sum = summed([encode_grads[3], encode_grads[5]])
    small_parts = [
        encode_grads[0],
        encode_grads[4],
        encode_grads[6],
        grad_widen_bias,
        bottle_grads[0],
        bottle_grads[4],
        bottle_grads[6],
        grad_merge_bias,
        decode_grads[0],
        decode_grads[4],
        decode_grads[6],
    ]
    small = lax.psum(small_parts, both)
    return (
        result,
        fine_grad,
        small[0].reshape(encode_depth.shape),
        encode_grads[1],
        encode_grads[2],
        encode_up_sum,
        small[1],
        encode_down_sum,
        small[2],
        widen_sum,
        small[3],
        small[4].reshape(bottle_depth.shape),
        bottle_grads[1],
        bottle_grads[2],
        bottle_up_sum,
        small[5],
        bottle_down_sum,
        small[6],
        merge_sum,
        small[7],
        small[8].reshape(decode_depth.shape),
        decode_grads[1],
        decode_grads[2],
        decode_up_sum,
        small[9],
        decode_down_sum,
        small[10],
    )


def solution(mesh):
    whole = P()
    rows = P("lat", None)
    tile = P(None, "lat", "lon", None)
    block = (whole, whole, whole, rows, whole, rows, whole)
    placed = (tile, P(None, "lat", "lon"), tile) + block + (rows, whole) + block + (rows, whole) + block
    return jax.shard_map(
        shards,
        mesh=mesh,
        in_specs=placed,
        out_specs=(tile, tile) + (whole,) * 25,
        check_vma=False,
    )
```

time: 1130 us -> 924 us (0.82)
  other arithmetic: 301 us -> 58.5 us
  Pallas kernels: 0 us -> 187 us
  matrix products: 180 us -> 50.5 us
  local copies, waits for them, and re-layouts: 144 us -> 82.8 us
  waiting for transfers between devices: 331 us -> 373 us
    reduce_sum x20 -> x2, other arithmetic: 190 us -> 1.22 us  [the longest x1 0.61 us: shards(): ocean_fine = jnp.sum(ocean_band)]
    pallas_call x0 -> x15, Pallas kernels: none -> 187 us  [the longest x3 39.6 us: stencil_backward(): pl.pallas_call(functools.partial(stencil_backward_kernel, len(edges)), gr...]
    dot_general x6 -> x0, matrix products: 94.1 us -> none  [the longest x3 76.4 us: block_forward(): jnp.dot(normed, up, preferred_element_type=f32) + up_bias.astype(f32)]
    dot_general x10 -> x4, matrix products: 48.7 us -> 3.9 us  [by_transpose(): lax.dot_general(former, latter, (((1,), (1,)), ((), ())), preferred_eleme...]
    all_gather x6, waiting for transfers between devices: 0.09 us -> 37.7 us  [shards(): lax.all_gather(weight, 'lat', axis=0, tiled=True)]
    convert_element_type x22 -> x7, other arithmetic: 44.8 us -> 10.3 us  [the longest x3 9.14 us: block_backward(): grad_mixed = grad_mixed.astype(bf16).reshape(source.shape)]
    all_to_all x6, waiting for transfers between devices: 3.18 us -> 34.5 us  [sum_all(): return jnp.sum(lax.all_to_all(copies, both, 0, 0, tiled=False), axis=0)]
    reshape x7 -> x4, local copies, waits for them, and re-layouts: 29 us -> 5.82 us  [the longest x1 3.75 us: shards(): grad_skip.reshape(-1, channels)]
  transfers between devices with their start and end apart: 41 -> 41, of which waited for: 11 -> 14; matrix products, arithmetic and copies ran while one was open for 39% -> 15% of each run, Pallas kernels for 0% -> 12%
where the time goes in v2:
time: 924 us; the launch traced here: 916 us
  waiting for transfers between devices  373 us (40%)
  Pallas kernels  187 us (20%)
  local copies, waits for them, and re-layouts  82.8 us (9%)
  blocking collectives  80.9 us (9%)
  starting transfers between devices  67.4 us (7%)
  other arithmetic  58.5 us (6%)
  matrix products  50.5 us (5%)
  between operations  16.1 us (2%)
    psum x1, waiting for transfers between devices, summed(): lax.psum([part.astype(bf16) for part in parts], both)  162 us
    psum x1, waiting for transfers between devices, shards(): small = lax.psum(small_parts, both)  111 us
    psum x1, blocking collectives, shards(): small = lax.psum(small_parts, both)  49.2 us
    pallas_call x3, Pallas kernels, stencil_backward(): pl.pallas_call(functools.partial(stencil_backward_kernel, len(edges)), gr...  39.6 us
    pallas_call x3, Pallas kernels, mlp_forward(): pl.pallas_call(functools.partial(mlp_forward_kernel, 512), grid=(pixels /...  38.8 us
    pallas_call x3, Pallas kernels, stencil_forward(): pl.pallas_call(functools.partial(stencil_forward_kernel, len(edges)), gri...  38.7 us
    dot_general x10, matrix products, cross_rows(): lax.dot_general(former, latter, (((0,), (0,)), ((), ())), preferred_eleme...  38.2 us
    all_gather x6, waiting for transfers between devices, shards(): lax.all_gather(weight, 'lat', axis=0, tiled=True)  37.7 us
  transfers between devices with their start and end apart: 41, of which 14 were waited for; matrix products, arithmetic and copies ran while one was open for 15% of the time, Pallas kernels for 12%

profile of v2, /device:TPU:0, one launch (start us, length us, event | category | flops | bytes accessed | tf_op | source)
XLA Modules:
  0.0 916.3 jit_solution(14500909154380276972)
XLA Ops:
  21.2 15.8 %all-gather.2 = bf16[4,100,800]{2,1,0:T(8,128)(2,1)S(1)} all-gather(bf16[1,100,800]{2,1,0:T(8,128)(2,1)S(1)} %bitcast.206), channel_id=1, replica_groups=mesh['lat'=4,'lon'=8] {'lat'}, dimensions={0}, use_global_device_ids=true | all-gather | bytes 800000 | tf_op jit(solution)/shard_map/all_gather | solution.py:440
  40.0 15.9 %all-gather.1 = bf16[4,300,400]{1,2,0:T(8,128)(2,1)S(1)} all-gather(bf16[1,300,400]{1,2,0:T(8,128)(2,1)S(1)} %bitcast.205), channel_id=1, replica_groups=mesh['lat'=4,'lon'=8] {'lat'}, dimensions={0}, use_global_device_ids=true | all-gather | bytes 1200000 | tf_op jit(solution)/shard_map/all_gather | solution.py:440
  74.2 12.4 %collective-permute-done.2 = bf16[12,32,400]{2,1,0:T(8,128)(2,1)S(1)} collective-permute-done((bf16[12,32,400]{2,1,0:T(8,128)(2,1)}, bf16[12,32,400]{2,1,0:T(8,128)(2,1)S(1)}, u32[]{:S(2)}, u32[]{:S(2)}) %collective-permute-start.2) | collective-permute-done | bytes 307232 | tf_op jit(solution)/shard_map/ppermute | solution.py:30
  88.6 3.5 collective-permute-start.4
  96.8 15.0 %stencil_forward.3 = (f32[48,32,400]{2,1,0:T(8,128)}, f32[2,400]{1,0:T(2,128)}) custom-call(bf16[48,32,400]{2,1,0:T(8,128)(2,1)} %copy-done.2, bf16[48,3,400]{2,1,0:T(4,128)(2,1)} %copy-done.30, bf16[48,3,400]{2,1,0:T(4,128)(2,1)} %copy-done.31, f32[49,400]{1,0:T(8,128)} %reshape.239.refs_2_, f32[48,32,128]{2,1,0:T(8,128)} %broadcast_in_dim.46.refs_3_), custom_call_target="tpu_custom_call" | custom-call | tf_op jit(solution)/shard_map/stencil_forward/pallas_call | solution.py:187
  113.9 6.6 all-to-all-start
  121.4 9.5 %all-to-all-done = f32[32,3,400]{2,1,0:T(4,128)S(1)} async-done(((f32[32,3,400]{2,1,0:T(4,128)}), f32[32,3,400]{2,1,0:T(4,128)S(1)}, u32[]{:S(2)}, u32[]{:S(2)}) %all-to-all-start) | async-done | bytes 153632 | tf_op jit(solution)/shard_map/all_to_all | solution.py:77
  136.2 12.6 %mlp_forward.3 = (bf16[1536,400]{1,0:T(8,128)(2,1)}, bf16[1536,1600]{1,0:T(8,128)(2,1)}, bf16[1536,1600]{1,0:T(8,128)(2,1)}, bf16[1536,400]{1,0:T(8,128)(2,1)}) custom-call(f32[1536,400]{1,0:T(8,128)} %bitcast.173, bf16[1536,400]{1,0:T(8,128)(2,1)} %bitcast.172, f32[1536,128]{1,0:T(8,128)} %broadcast_in_dim.47.sea, f32[4,400]{1,0:T(4,128)} %pad_maximum_fusion.13.scales, ...), custom_call_target="tpu_custom_call" | custom-call | tf_op jit(solution)/shard_map/mlp_forward/pallas_call | solution.py:317
  148.9 3.4 reshape.243
  152.3 3.8 reduce_sum.92
  167.8 8.5 stencil_forward.4
  184.0 12.5 %all-to-all-done.1 = f32[32,3,800]{2,1,0:T(4,128)S(1)} async-done(((f32[32,3,800]{2,1,0:T(4,128)}), f32[32,3,800]{2,1,0:T(4,128)S(1)}, u32[]{:S(2)}, u32[]{:S(2)}) %all-to-all-start.1) | async-done | bytes 307232 | tf_op jit(solution)/shard_map/all_to_all | solution.py:77
  197.3 37.7 %all-gather.15.cloned.1.call-done.down = bf16[3200,800]{1,0:T(8,128)(2,1)} async-done(((bf16[800,800]{1,0:T(8,128)(2,1)}), bf16[3200,800]{1,0:T(8,128)(2,1)}) %all-gather.15.cloned.1.call-update) | async-done | bytes 5120016 | tf_op jit(solution)/shard_map/all_gather | solution.py:440
  235.8 13.5 %mlp_forward.4 = (bf16[384,800]{1,0:T(8,128)(2,1)}, bf16[384,3200]{1,0:T(8,128)(2,1)}, bf16[384,3200]{1,0:T(8,128)(2,1)}, bf16[384,800]{1,0:T(8,128)(2,1)}) custom-call(f32[384,800]{1,0:T(8,128)} %bitcast.185, bf16[384,800]{1,0:T(8,128)(2,1)} %copy-done.11, f32[384,128]{1,0:T(8,128)} %broadcast_in_dim.104.sea, f32[4,800]{1,0:T(4,128)} %pad_maximum_fusion.12.scales, ...), custom_call_target="tpu_custom_call" | custom-call | tf_op jit(solution)/shard_map/mlp_forward/pallas_call | solution.py:317
  252.5 3.5 add.210
  256.0 3.4 add.206
  259.5 4.9 add_convert_fusion
  265.4 3.7 collective-permute-start.11
  273.8 15.1 %stencil_forward.5 = (f32[48,32,400]{2,1,0:T(8,128)}, f32[2,400]{1,0:T(2,128)}) custom-call(bf16[48,32,400]{2,1,0:T(8,128)(2,1)} %copy-done.7, bf16[48,3,400]{2,1,0:T(4,128)(2,1)} %copy-done.32, bf16[48,3,400]{2,1,0:T(4,128)(2,1)} %copy-done.33, f32[49,400]{1,0:T(8,128)} %reshape.250.refs_2_, f32[48,32,128]{2,1,0:T(8,128)} %broadcast_in_dim.46.refs_3_), custom_call_target="tpu_custom_call" | custom-call | tf_op jit(solution)/shard_map/stencil_forward/pallas_call | solution.py:187
  291.0 4.2 all-to-all-start.2
  299.3 6.3 all-to-all-done.2
  306.3 12.6 %mlp_forward.5 = (bf16[1536,400]{1,0:T(8,128)(2,1)}, bf16[1536,1600]{1,0:T(8,128)(2,1)}, bf16[1536,1600]{1,0:T(8,128)(2,1)}, bf16[1536,400]{1,0:T(8,128)(2,1)}) custom-call(f32[1536,400]{1,0:T(8,128)} %bitcast.175, bf16[1536,400]{1,0:T(8,128)(2,1)} %get-tuple-element.210.source, f32[1536,128]{1,0:T(8,128)} %broadcast_in_dim.47.sea, ...), custom_call_target="tpu_custom_call" | custom-call | tf_op jit(solution)/shard_map/mlp_forward/pallas_call | solution.py:317
  318.9 11.9 %mlp_backward.3 = (bf16[1536,400]{1,0:T(8,128)(2,1)}, bf16[1536,1600]{1,0:T(8,128)(2,1)}, f32[1536,400]{1,0:T(8,128)}, f32[2,400]{1,0:T(2,128)}, f32[1,400]{1,0:T(1,128)}, /*index=5*/f32[1,1600]{1,0:T(1,128)}) custom-call(bf16[1536,400]{1,0:T(8,128)(2,1)} %bitcast.183, f32[1536,400]{1,0:T(8,128)} %bitcast.176, bf16[1536,1600]{1,0:T(8,128)(2,1)} %get-tuple-element.77.slope, ...), custom_call_target="tpu_custom_call" | custom-call | tf_op jit(solution)/shard_map/mlp_backward/pallas_call | solution.py:334
  334.9 6.5 convolution_convert_fusion.2
  343.2 3.5 multiply_convert_fusion.1
  350.5 3.5 convolution_convert_fusion.3
  356.9 15.4 %stencil_backward.3 = (bf16[48,32,400]{2,1,0:T(8,128)(2,1)}, f32[1,400]{1,0:T(1,128)}) custom-call(bf16[48,32,400]{2,1,0:T(8,128)(2,1)} %bitcast.178, bf16[48,3,400]{2,1,0:T(4,128)(2,1)} %copy-done.42, bf16[48,3,400]{2,1,0:T(4,128)(2,1)} %copy-done.43, f32[49,400]{1,0:T(8,128)} %reshape.250.refs_2_, f32[48,32,128]{2,1,0:T(8,128)} %broadcast_in_dim.46.refs_3_, ...), custom_call_target="tpu_custom_call" | custom-call | tf_op jit(solution)/shard_map/stencil_backward/pallas_call | solution.py:203
  384.3 12.9 %mlp_backward.4 = (bf16[384,800]{1,0:T(8,128)(2,1)}, bf16[384,3200]{1,0:T(8,128)(2,1)}, f32[384,800]{1,0:T(8,128)}, f32[2,800]{1,0:T(2,128)}, f32[1,800]{1,0:T(1,128)}, /*index=5*/f32[1,3200]{1,0:T(1,128)}) custom-call(f32[384,800]{1,0:T(8,128)} %convolution_add_fusion.2.upstream, f32[384,800]{1,0:T(8,128)} %bitcast.186, ...), custom_call_target="tpu_custom_call" | custom-call | tf_op jit(solution)/shard_map/mlp_backward/pallas_call | solution.py:334
  401.4 7.2 convolution_convert_fusion
  408.7 5.3 convolution_convert_fusion.1
  416.7 3.6 collective-permute-start.21
  424.1 8.8 stencil_backward.4
  440.9 3.8 reshape.232.upstream
  444.6 12.3 %mlp_backward.5 = (bf16[1536,400]{1,0:T(8,128)(2,1)}, bf16[1536,1600]{1,0:T(8,128)(2,1)}, f32[1536,400]{1,0:T(8,128)}, f32[2,400]{1,0:T(2,128)}, f32[1,400]{1,0:T(1,128)}, /*index=5*/f32[1,1600]{1,0:T(1,128)}) custom-call(f32[1536,400]{1,0:T(8,128)} %reshape.232.upstream, f32[1536,400]{1,0:T(8,128)} %bitcast.174, ...), custom_call_target="tpu_custom_call" | custom-call | tf_op jit(solution)/shard_map/mlp_backward/pallas_call | solution.py:334
  456.9 6.6 convolution_convert_fusion.4
  463.5 3.6 convolution_convert_fusion.5
  468.5 5.9 all-to-all-start.5
  479.1 4.5 all-to-all-done.5
  492.9 12.8 %kernel_grad.5 = f32[49,400]{1,0:T(8,128)} custom-call(bf16[48,32,400]{2,1,0:T(8,128)(2,1)} %copy-done.7, bf16[48,3,400]{2,1,0:T(4,128)(2,1)} %copy-done.32, bf16[48,3,400]{2,1,0:T(4,128)(2,1)} %copy-done.33, bf16[48,32,400]{2,1,0:T(8,128)(2,1)} %bitcast.179), custom_call_target="tpu_custom_call" | custom-call | tf_op jit(solution)/shard_map/kernel_grad/pallas_call | solution.py:218
  507.2 3.5 reshape_reshape.7.refs_4_
  510.8 15.4 %stencil_backward.5 = (bf16[48,32,400]{2,1,0:T(8,128)(2,1)}, f32[1,400]{1,0:T(1,128)}) custom-call(bf16[48,32,400]{2,1,0:T(8,128)(2,1)} %bitcast.181, bf16[48,3,400]{2,1,0:T(4,128)(2,1)} %collective-permute-done.22.refs_0_, bf16[48,3,400]{2,1,0:T(4,128)(2,1)} %collective-permute-done.23.refs_1_, f32[49,400]{1,0:T(8,128)} %reshape.239.refs_2_, ...), custom_call_target="tpu_custom_call" | custom-call | tf_op jit(solution)/shard_map/stencil_backward/pallas_call | solution.py:203
  534.5 7.6 kernel_grad.4
  543.8 49.2 %all-reduce.3 = (f32[1600]{0:T(1024)}, f32[400]{0:T(512)}, f32[800]{0:T(1024)}, f32[3200]{0:T(1024)}, f32[800]{0:T(1024)}, /*index=5*/f32[400]{0:T(512)}, f32[1600]{0:T(1024)}, f32[400]{0:T(512)}) all-reduce(f32[1600]{0:T(1024)S(1)} %reduce.5, f32[400]{0:T(512)S(1)} %bitcast.234, ...), channel_id=1, replica_groups=mesh['lat'=4,'lon'=8] {'lat','lon'}, use_global_device_ids=true, to_apply=%region_13.14 | all-reduce | flops 9200 | bytes 73600 | tf_op jit(solution)/shard_map/psum | solution.py:529
  593.0 12.7 %kernel_grad.3 = f32[49,400]{1,0:T(8,128)} custom-call(bf16[48,32,400]{2,1,0:T(8,128)(2,1)} %copy-done.2, bf16[48,3,400]{2,1,0:T(4,128)(2,1)} %copy-done.30, bf16[48,3,400]{2,1,0:T(4,128)(2,1)} %copy-done.31, bf16[48,32,400]{2,1,0:T(8,128)(2,1)} %bitcast.182), custom_call_target="tpu_custom_call" | custom-call | tf_op jit(solution)/shard_map/kernel_grad/pallas_call | solution.py:218
  609.2 162.4 %all-reduce.11.cloned.1.call-done = (bf16[400,1600]{1,0:T(8,128)(2,1)}, bf16[1600,400]{0,1:T(8,128)(2,1)}, bf16[400,800]{1,0:T(8,128)(2,1)}, bf16[800,3200]{1,0:...) async-done(((bf16[400,1600]{1,0:T(8,128)(2,1)}, bf16[1600,400]{0,1:T(8,128)(2,1)}, ...) | async-done | bytes 16960016 | tf_op jit(solution)/shard_map/psum | solution.py:511
  771.6 7.3 convert_element_type.163
  778.9 4.7 convert_element_type.165
  793.4 110.8 %all-reduce.9.cloned.1.call-done = (f32[7,7,400]{2,1,0:T(8,128)}, f32[7,7,800]{2,1,0:T(8,128)}, f32[7,7,400]{2,1,0:T(8,128)}) async-done(((f32[7,7,400]{2,1,0:T(8,128)}, f32[7,7,800]{2,1,0:T(8,128)}, f32[7,7,400]{2,1,0:T(8,128)}), (f32[7,7,400]{2,1,0:T(8,128)}, f32[7,7,800]{2,1,0:T(8,128)}, f32[7,7,400]{2,1,0:T(8,128)})) %all-reduce.9.cloned.1.call-update) | async-done | bytes 313616 | tf_op jit(solution)/shard_map/psum | solution.py:529
  (420 shorter events, 173.9 us)
Async XLA Ops:
  7.2 125.0 %all-gather.19.cloned.1.call-start = ((), (), s32[]{:S(2)}) async-start(), calls=%async_computation.10 | async-start | bytes 1730560 | tf_op jit(solution)/shard_map/all_gather | solution.py:440
  7.9 127.1 %all-gather.11.cloned.1.call-start = ((), (), s32[]{:S(2)}) async-start(), calls=%async_computation.6 | async-start | bytes 2048000 | tf_op jit(solution)/shard_map/all_gather | solution.py:440
  8.7 188.6 %all-gather.13.cloned.1.call-start = ((), (), s32[]{:S(2)}) async-start(), calls=%async_computation.7 | async-start | bytes 6400000 | tf_op jit(solution)/shard_map/all_gather | solution.py:440
  9.4 225.6 %all-gather.15.cloned.1.call-start = ((), (), s32[]{:S(2)}) async-start(), calls=%async_computation.8 | async-start | bytes 7168000 | tf_op jit(solution)/shard_map/all_gather | solution.py:440
  10.0 286.8 %all-gather.21.cloned.1.call-start = ((), (), s32[]{:S(2)}) async-start(), calls=%async_computation.11 | async-start | bytes 1730560 | tf_op jit(solution)/shard_map/all_gather | solution.py:440
  10.6 295.7 %all-gather.17.cloned.1.call-start = ((), (), s32[]{:S(2)}) async-start(), calls=%async_computation.9 | async-start | bytes 2048000 | tf_op jit(solution)/shard_map/all_gather | solution.py:440
  11.9 60.8 %collective-permute-start = (bf16[12,32,400]{2,1,0:T(8,128)(2,1)}, bf16[12,32,400]{2,1,0:T(8,128)(2,1)}, u32[]{:S(2)}, u32[]{:S(2)}) collective-permute-start(bf16[12,32,400]{2,1,0:T(8,128)(2,1)} %get-tuple-element.178), channel_id=1, source_target_pairs={{0,8},{8,0},{16,24},{24,16},{1,9},{9,1},{17,25},{25,17},{2,10},{10... | collective-permute-start | bytes 921608 | tf_op jit(solution)/shard_map/ppermute | solution.py:30
  14.8 59.4 %collective-permute-start.1 = (bf16[12,32,400]{2,1,0:T(8,128)(2,1)}, bf16[12,32,400]{2,1,0:T(8,128)(2,1)}, u32[]{:S(2)}, u32[]{:S(2)}) collective-permute-start(bf16[12,32,400]{2,1,0:T(8,128)(2,1)} %get-tuple-element.180), channel_id=1, source_target_pairs={{0,16},{8,24},{16,0},{24,8},{1,17},{9,25},{17,1},{25,9},{2,18},{10... | collective-permute-start | bytes 921608 | tf_op jit(solution)/shard_map/ppermute | solution.py:30
  16.4 50.8 %collective-permute-start.5 = (s32[12,32]{1,0:T(8,128)S(1)}, s32[12,32]{1,0:T(8,128)S(1)}, u32[]{:S(2)}, u32[]{:S(2)}) collective-permute-start(s32[12,32]{1,0:T(8,128)S(1)} %bitcast.217), channel_id=1, source_target_pairs={{0,8},{8,0},{16,24},{24,16},{1,9},{9,1},{17,25},{25,17},{2,10},{10... | collective-permute-start | bytes 4616 | tf_op jit(solution)/shard_map/ppermute | solution.py:30
  17.0 51.7 %collective-permute-start.6 = (s32[12,32]{1,0:T(8,128)S(1)}, s32[12,32]{1,0:T(8,128)S(1)}, u32[]{:S(2)}, u32[]{:S(2)}) collective-permute-start(s32[12,32]{1,0:T(8,128)S(1)} %bitcast.216), channel_id=1, source_target_pairs={{0,16},{8,24},{16,0},{24,8},{1,17},{9,25},{17,1},{25,9},{2,18},{10... | collective-permute-start | bytes 4616 | tf_op jit(solution)/shard_map/ppermute | solution.py:30
  17.1 53.0 %collective-permute-start.7 = (s32[12,32]{1,0:T(8,128)S(1)}, s32[12,32]{1,0:T(8,128)}, u32[]{:S(2)}, u32[]{:S(2)}) collective-permute-start(s32[12,32]{1,0:T(8,128)S(1)} %bitcast.215), channel_id=1, source_target_pairs={{0,24},{8,16},{16,8},{24,0},{1,25},{9,17},{17,9},{25,1},{2,26},{10... | collective-permute-start | bytes 4616 | tf_op jit(solution)/shard_map/ppermute | solution.py:30
  38.1 17.7 %copy-start.22 = (bf16[4,12,32,400]{3,2,1,0:T(8,128)(2,1)S(1)}, bf16[4,12,32,400]{3,2,1,0:T(8,128)(2,1)}, u32[]{:S(2)}) copy-start(bf16[4,12,32,400]{3,2,1,0:T(8,128)(2,1)} %param.30) | copy-start | bytes 3686404
  57.0 74.6 %copy-start.51 = (f32[400]{0:T(512)}, f32[400]{0:T(512)S(1)}, u32[]{:S(2)}) copy-start(f32[400]{0:T(512)S(1)} %convert_element_type.136) | copy-start | bytes 4804
  61.9 24.7 %copy-start.24 = (bf16[1,12,32,400]{3,2,1,0:T(8,128)(2,1)S(1)}, bf16[1,12,32,400]{3,2,1,0:T(8,128)(2,1)}, u32[]{:S(2)}) copy-start(bf16[1,12,32,400]{3,2,1,0:T(8,128)(2,1)} %get-tuple-element.177) | copy-start | bytes 921604
  67.2 19.4 %collective-permute-start.2 = (bf16[12,32,400]{2,1,0:T(8,128)(2,1)}, bf16[12,32,400]{2,1,0:T(8,128)(2,1)S(1)}, u32[]{:S(2)}, u32[]{:S(2)}) collective-permute-start(bf16[12,32,400]{2,1,0:T(8,128)(2,1)} %get-tuple-element.179), channel_id=1, source_target_pairs={{0,24},{8,16},{16,8},{24,0},{1,25},{9,17},{17,9},{25,1},{2,26},{10... | collective-permute-start | bytes 921608 | tf_op jit(solution)/shard_map/ppermute | solution.py:30
  68.7 200.5 %collective-permute-start.15 = (bf16[12,32,400]{2,1,0:T(8,128)(2,1)}, bf16[12,32,400]{2,1,0:T(8,128)(2,1)}, u32[]{:S(2)}, u32[]{:S(2)}) collective-permute-start(bf16[12,32,400]{2,1,0:T(8,128)(2,1)} %get-tuple-element.158), channel_id=1, source_target_pairs={{0,8},{8,0},{16,24},{24,16},{1,9},{9,1},{17,25},{25,17},{2,10},{10... | collective-permute-start | bytes 921608 | tf_op jit(solution)/shard_map/ppermute | solution.py:30
  70.1 199.1 %collective-permute-start.16 = (bf16[12,32,400]{2,1,0:T(8,128)(2,1)}, bf16[12,32,400]{2,1,0:T(8,128)(2,1)}, u32[]{:S(2)}, u32[]{:S(2)}) collective-permute-start(bf16[12,32,400]{2,1,0:T(8,128)(2,1)} %get-tuple-element.160), channel_id=1, source_target_pairs={{0,16},{8,24},{16,0},{24,8},{1,17},{9,25},{17,1},{25,9},{2,18},{10... | collective-permute-start | bytes 921608 | tf_op jit(solution)/shard_map/ppermute | solution.py:30
  72.7 196.5 %collective-permute-start.17 = (bf16[12,32,400]{2,1,0:T(8,128)(2,1)}, bf16[12,32,400]{2,1,0:T(8,128)(2,1)}, u32[]{:S(2)}, u32[]{:S(2)}) collective-permute-start(bf16[12,32,400]{2,1,0:T(8,128)(2,1)} %get-tuple-element.159), channel_id=1, source_target_pairs={{0,24},{8,16},{16,8},{24,0},{1,25},{9,17},{17,9},{25,1},{2,26},{10... | collective-permute-start | bytes 921608 | tf_op jit(solution)/shard_map/ppermute | solution.py:30
  88.5 7.1 collective-permute-start.3
  88.6 7.0 collective-permute-start.4
  113.9 17.0 %all-to-all-start = ((f32[32,3,400]{2,1,0:T(4,128)}), f32[32,3,400]{2,1,0:T(4,128)S(1)}, u32[]{:S(2)}, u32[]{:S(2)}) async-start(f32[32,3,400]{2,1,0:T(4,128)} %broadcast_in_dim.48), calls=%async_computation | async-start | bytes 524288 | tf_op jit(solution)/shard_map/all_to_all | solution.py:77
  121.4 14.8 %copy-start.19 = (f32[384,896]{1,0:T(8,128)}, f32[384,896]{1,0:T(8,128)S(1)}, u32[]{:S(2)}) copy-start(f32[384,896]{1,0:T(8,128)S(1)} %broadcast_dynamic-update-slice_fusion.3) | copy-start | bytes 4128772
  159.3 7.7 collective-permute-start.8
  159.7 7.2 collective-permute-start.9
  176.3 20.4 %copy-start.64 = (f32[1,800]{1,0:T(1,128)S(1)}, f32[1,800]{1,0:T(1,128)}, u32[]{:S(2)}) copy-start(f32[1,800]{1,0:T(1,128)} %stack.133) | copy-start | bytes 9604
  176.3 20.4 %copy-start.65 = (f32[1,800]{1,0:T(1,128)S(1)}, f32[1,800]{1,0:T(1,128)}, u32[]{:S(2)}) copy-start(f32[1,800]{1,0:T(1,128)} %reshape.246) | copy-start | bytes 9604
  178.5 18.0 %all-to-all-start.1 = ((f32[32,3,800]{2,1,0:T(4,128)}), f32[32,3,800]{2,1,0:T(4,128)S(1)}, u32[]{:S(2)}, u32[]{:S(2)}) async-start(f32[32,3,800]{2,1,0:T(4,128)} %broadcast_in_dim.105), calls=%async_computation.1 | async-start | bytes 917504 | tf_op jit(solution)/shard_map/all_to_all | solution.py:77
  265.4 7.1 collective-permute-start.10
  265.4 7.0 collective-permute-start.11
  291.0 14.6 %all-to-all-start.2 = ((f32[32,3,400]{2,1,0:T(4,128)}), f32[32,3,400]{2,1,0:T(4,128)S(1)}, u32[]{:S(2)}, u32[]{:S(2)}) async-start(f32[32,3,400]{2,1,0:T(4,128)} %broadcast_in_dim.110), calls=%async_computation.2 | async-start | bytes 524288 | tf_op jit(solution)/shard_map/all_to_all | solution.py:77
  332.2 10.8 %all-to-all-start.3 = ((f32[32,2,400]{2,1,0:T(2,128)}), f32[32,2,400]{2,1,0:T(2,128)S(1)}, u32[]{:S(2)}, u32[]{:S(2)}) async-start(f32[32,2,400]{2,1,0:T(2,128)} %broadcast_in_dim.115), calls=%async_computation.3 | async-start | bytes 262144 | tf_op jit(solution)/shard_map/all_to_all | solution.py:77
  346.9 8.6 collective-permute-start.18
  347.2 8.3 collective-permute-start.19
  398.6 15.3 %all-to-all-start.4 = ((f32[32,2,800]{2,1,0:T(2,128)}), f32[32,2,800]{2,1,0:T(2,128)S(1)}, u32[]{:S(2)}, u32[]{:S(2)}) async-start(f32[32,2,800]{2,1,0:T(2,128)} %broadcast_in_dim.116), calls=%async_computation.4 | async-start | bytes 458752 | tf_op jit(solution)/shard_map/all_to_all | solution.py:77
  401.2 370.4 %all-reduce.11.cloned.1.call-start = ((), (), s32[]{:S(2)}) async-start(), calls=%async_computation.13 | async-start | bytes 34611200 | tf_op jit(solution)/shard_map/psum | solution.py:511
  416.6 6.8 collective-permute-start.20
  416.7 6.6 collective-permute-start.21
  468.5 15.2 %all-to-all-start.5 = ((f32[32,2,400]{2,1,0:T(2,128)}), f32[32,2,400]{2,1,0:T(2,128)S(1)}, u32[]{:S(2)}, u32[]{:S(2)}) async-start(f32[32,2,400]{2,1,0:T(2,128)} %broadcast_in_dim.117), calls=%async_computation.5 | async-start | bytes 262144 | tf_op jit(solution)/shard_map/all_to_all | solution.py:77
  474.4 429.8 %all-reduce.9.cloned.1.call-start = ((), (), s32[]{:S(2)}) async-start(), calls=%async_computation.12 | async-start | bytes 860160 | tf_op jit(solution)/shard_map/psum | solution.py:529
  475.6 54.9 %collective-permute-start.12 = (bf16[12,32,400]{2,1,0:T(8,128)(2,1)}, bf16[12,32,400]{2,1,0:T(8,128)(2,1)}, u32[]{:S(2)}, u32[]{:S(2)}) collective-permute-start(bf16[12,32,400]{2,1,0:T(8,128)(2,1)} %get-tuple-element.168), channel_id=1, source_target_pairs={{0,8},{8,0},{16,24},{24,16},{1,9},{9,1},{17,25},{25,17},{2,10},{10... | collective-permute-start | bytes 921608 | tf_op jit(solution)/shard_map/ppermute | solution.py:48
  477.4 53.8 %collective-permute-start.13 = (bf16[12,32,400]{2,1,0:T(8,128)(2,1)}, bf16[12,32,400]{2,1,0:T(8,128)(2,1)}, u32[]{:S(2)}, u32[]{:S(2)}) collective-permute-start(bf16[12,32,400]{2,1,0:T(8,128)(2,1)} %get-tuple-element.167), channel_id=1, source_target_pairs={{0,16},{8,24},{16,0},{24,8},{1,17},{9,25},{17,1},{25,9},{2,18},{10... | collective-permute-start | bytes 921608 | tf_op jit(solution)/shard_map/ppermute | solution.py:48
  478.9 52.4 %collective-permute-start.14 = (bf16[12,32,400]{2,1,0:T(8,128)(2,1)}, bf16[12,32,400]{2,1,0:T(8,128)(2,1)}, u32[]{:S(2)}, u32[]{:S(2)}) collective-permute-start(bf16[12,32,400]{2,1,0:T(8,128)(2,1)} %get-tuple-element.166), channel_id=1, source_target_pairs={{0,24},{8,16},{16,8},{24,0},{1,25},{9,17},{17,9},{25,1},{2,26},{10... | collective-permute-start | bytes 921608 | tf_op jit(solution)/shard_map/ppermute | solution.py:48
  489.3 21.5 %collective-permute-start.22 = (bf16[48,3,400]{2,1,0:T(4,128)(2,1)}, bf16[48,3,400]{2,1,0:T(4,128)(2,1)}, u32[]{:S(2)}, u32[]{:S(2)}) collective-permute-start(bf16[48,3,400]{2,1,0:T(4,128)(2,1)} %get-tuple-element.150), channel_id=1, source_target_pairs={{0,1},{1,2},{2,3},{3,4},{4,5},{5,6},{6,7},{7,0},{8,9},{9,10},{10,1... | collective-permute-start | bytes 345608 | tf_op jit(solution)/shard_map/ppermute | solution.py:62
  490.8 19.9 %collective-permute-start.23 = (bf16[48,3,400]{2,1,0:T(4,128)(2,1)}, bf16[48,3,400]{2,1,0:T(4,128)(2,1)}, u32[]{:S(2)}, u32[]{:S(2)}) collective-permute-start(bf16[48,3,400]{2,1,0:T(4,128)(2,1)} %get-tuple-element.149), channel_id=1, source_target_pairs={{1,0},{2,1},{3,2},{4,3},{5,4},{6,5},{7,6},{0,7},{9,8},{10,9},{11,1... | collective-permute-start | bytes 345608 | tf_op jit(solution)/shard_map/ppermute | solution.py:63
  492.9 14.4 %copy-start.4 = (f32[24,2,16,2,400]{4,3,2,1,0:T(2,128)S(1)}, f32[24,2,16,2,400]{4,3,2,1,0:T(2,128)}, u32[]{:S(2)}) copy-start(f32[24,2,16,2,400]{4,3,2,1,0:T(2,128)} %copy-done.3) | copy-start | bytes 7372804
  527.7 79.6 %collective-permute-start.24 = (bf16[12,32,400]{2,1,0:T(8,128)(2,1)S(1)}, bf16[12,32,400]{2,1,0:T(8,128)(2,1)S(1)}, u32[]{:S(2)}, u32[]{:S(2)}) collective-permute-start(bf16[12,32,400]{2,1,0:T(8,128)(2,1)S(1)} %get-tuple-element.148), channel_id=1, source_target_pairs={{0,8},{8,0},{16,24},{24,16},{1,9},{9,1},{17,25},{25,17},{2,10},{10... | collective-permute-start | bytes 921608 | tf_op jit(solution)/shard_map/ppermute | solution.py:48
  529.4 77.9 %collective-permute-start.25 = (bf16[12,32,400]{2,1,0:T(8,128)(2,1)S(1)}, bf16[12,32,400]{2,1,0:T(8,128)(2,1)S(1)}, u32[]{:S(2)}, u32[]{:S(2)}) collective-permute-start(bf16[12,32,400]{2,1,0:T(8,128)(2,1)S(1)} %get-tuple-element.147), channel_id=1, source_target_pairs={{0,16},{8,24},{16,0},{24,8},{1,17},{9,25},{17,1},{25,9},{2,18},{10... | collective-permute-start | bytes 921608 | tf_op jit(solution)/shard_map/ppermute | solution.py:48
  530.6 76.7 %collective-permute-start.26 = (bf16[12,32,400]{2,1,0:T(8,128)(2,1)S(1)}, bf16[12,32,400]{2,1,0:T(8,128)(2,1)S(1)}, u32[]{:S(2)}, u32[]{:S(2)}) collective-permute-start(bf16[12,32,400]{2,1,0:T(8,128)(2,1)S(1)} %get-tuple-element.146), channel_id=1, source_target_pairs={{0,24},{8,16},{16,8},{24,0},{1,25},{9,17},{17,9},{25,1},{2,26},{10... | collective-permute-start | bytes 921608 | tf_op jit(solution)/shard_map/ppermute | solution.py:48
  (96 other events, 448.3 us)
Sparse Core Ops, SparseCore 0:
  9.9 38.5 all-gather.18
  50.3 47.4 all-gather.10
  99.7 63.0 all-gather.12
  164.5 70.4 all-gather.14
  236.7 29.4 all-gather.20
  267.9 32.8 all-gather.16
  467.2 304.3 all-reduce.10
  777.9 126.2 all-reduce.8

commit v3 on v2

--- a/solution.py
+++ b/solution.py
@@ -164,7 +164,8 @@
         return carry
 
     lax.fori_loop(0, rows // strip, step, 0)
-    out[...] = jnp.sum(sums_ref[...], axis=1)
+    out[0, 0:49] = jnp.sum(sums_ref[...], axis=1)
+    out[0, 49:56] = jnp.zeros((7, lanes), f32)
 
 
 def by_channel(array):
@@ -214,12 +215,13 @@
 
 def kernel_grad(source, edges, grad):
     rows, columns, channels = source.shape
-    out = jax.ShapeDtypeStruct((49, channels), f32)
+    tiles = pl.cdiv(channels, lanes)
+    out = jax.ShapeDtypeStruct((tiles, 56, lanes), f32)
     return pl.pallas_call(
         functools.partial(kernel_grad_kernel, len(edges)),
-        grid=(pl.cdiv(channels, lanes),),
+        grid=(tiles,),
         in_specs=[by_channel(array) for array in (source, *edges, grad)],
-        out_specs=by_channel(out),
+        out_specs=pl.BlockSpec((1, 56, lanes), lambda tile: (tile, 0, 0)),
         out_shape=out,
         scratch_shapes=[wide_scratch(rows, columns), pltpu.VMEM((49, 8, lanes), f32)],
         compiler_params=room,
@@ -349,6 +351,114 @@
     )(upstream, mixed, slope, sea, scales, up, down)
 
 
+def weight_grads_kernel(grad_branch, normed, active, grad_hidden, out, branch_ref, normed_ref):
+    @pl.when(pl.program_id(0) == 0)
+    def _():
+        branch_ref[...] = grad_branch[...].T
+        normed_ref[...] = normed[...].T
+
+    up = jnp.dot(normed_ref[...], grad_hidden[...], preferred_element_type=f32).astype(bf16)
+    down = jnp.dot(branch_ref[...], active[...], preferred_element_type=f32).astype(bf16)
+    for part in range(out.shape[1]):
+        out[0, part] = up[:, part * lanes : (part + 1) * lanes]
+        out[1, part] = down[:, part * lanes : (part + 1) * lanes]
+
+
+def weight_grads(grad_branch, normed, active, grad_hidden):
+    pixels, channels = normed.shape
+    hidden = active.shape[1]
+    tiles = pl.cdiv(hidden, lanes)
+    parts = next(count for count in (5, 4, 3, 2, 1) if count == 2 or tiles % count == 0)
+    return pl.pallas_call(
+        weight_grads_kernel,
+        grid=(pl.cdiv(tiles, parts),),
+        in_specs=[fixed(grad_branch), fixed(normed)]
+        + [pl.BlockSpec((pixels, parts * lanes), lambda tile: (0, tile))] * 2,
+        out_specs=pl.BlockSpec((2, parts, channels, lanes), lambda tile: (0, tile, 0, 0)),
+        out_shape=jax.ShapeDtypeStruct((2, tiles, channels, lanes), bf16),
+        scratch_shapes=[pltpu.VMEM((channels, pixels), bf16)] * 2,
+        compiler_params=room,
+        name="weight_grads",
+    )(grad_branch, normed, active, grad_hidden)
+
+
+def unpack_kernel(core, own, other, up, down):
+    mine, theirs = own[...].astype(f32), other[...].astype(f32)
+    first = core[0] == 0
+    up[...] = jnp.where(first, mine, theirs)
+    down[...] = jnp.where(first, theirs, mine).T
+
+
+def unpack(core, own, other, channels, hidden):
+    block = pl.BlockSpec((channels, lanes), lambda tile, core: (tile, 0))
+    return pl.pallas_call(
+        unpack_kernel,
+        grid_spec=pltpu.PrefetchScalarGridSpec(
+            num_scalar_prefetch=1,
+            grid=(pl.cdiv(hidden, lanes),),
+            in_specs=[block, block],
+            out_specs=[
+                pl.BlockSpec((channels, lanes), lambda tile, core: (0, tile)),
+                pl.BlockSpec((lanes, channels), lambda tile, core: (tile, 0)),
+            ],
+        ),
+        out_shape=[
+            jax.ShapeDtypeStruct((channels, hidden), f32),
+            jax.ShapeDtypeStruct((hidden, channels), f32),
+        ],
+        compiler_params=room,
+        name="unpack",
+    )(core, own, other)
+
+
+def swap(array, axis, step):
+    return lax.ppermute(array, axis, [(i, i ^ step) for i in range(lax.axis_size(axis))])
+
+
+def take(stacked, index):
+    return lax.dynamic_index_in_dim(stacked, index, 0, keepdims=False)
+
+
+def exchange_add(stacked, axis, own, scale):
+    count = stacked.shape[0]
+    got = [swap(take(stacked, own ^ step), axis, scale * step) for step in range(1, count)]
+    total = take(stacked, own).astype(f32)
+    for piece in got:
+        total = total + piece.astype(f32)
+    return total.astype(bf16)
+
+
+def exchange_all(piece, axis, own, scale, count):
+    got = jnp.stack([piece] + [swap(piece, axis, scale * step) for step in range(1, count)])
+    return jnp.concatenate([take(got, own ^ place) for place in range(count)], axis=0)
+
+
+def sum_group(pair):
+    tiles, columns = lax.axis_size("lat"), lax.axis_size("lon") // 2
+    tile, place = lax.axis_index("lat"), lax.axis_index("lon")
+    core, column = place % 2, place // 2
+    rows = pair.shape[1]
+    padded = -(-rows // (8 * tiles * columns)) * 8 * tiles * columns
+    pair = jnp.pad(pair, ((0, 0), (0, padded - rows), (0, 0)))
+    got = swap(take(pair, 1 - core), "lon", 1)
+    half = (take(pair, core).astype(f32) + got.astype(f32)).astype(bf16)
+    share = exchange_add(half.reshape(tiles, -1, lanes), "lat", tile, 1)
+    share = exchange_add(share.reshape(columns, -1, lanes), "lon", column, 2)
+    share = exchange_all(share, "lon", column, 2, columns)
+    half = exchange_all(share, "lat", tile, 1, tiles)
+    return half, swap(half, "lon", 1)
+
+
+def sum_small(flat):
+    count = lax.axis_size(both)
+    rows = flat.shape[0]
+    padded = -(-rows // (8 * count)) * 8 * count
+    pieces = jnp.pad(flat, ((0, padded - rows), (0, 0))).reshape(count, -1, lanes)
+    share = jnp.sum(lax.all_to_all(pieces, both, 0, 0, tiled=False), axis=0)
+    copies = jnp.broadcast_to(share[None], pieces.shape)
+    return lax.all_to_all(copies, both, 0, 0, tiled=False).reshape(padded, lanes)[:rows]
+
+
 def cross_rows(former, latter):
     return lax.dot_general(former, latter, (((0,), (0,)), ((), ())), preferred_element_type=f32)
 
@@ -397,12 +507,11 @@
     grad_edges = borders(grad_mixed, dates)
     grad_kernel = kernel_grad(source, edges, grad_mixed)
     grad_source, source_sums = stencil_backward(grad_mixed, grad_edges, taps, sea, upstream.reshape(source.shape))
-    grad_down = cross_rows(active, grad_branch)
-    grad_up = cross_rows(normed, grad_hidden)
     return (
         grad_source.reshape(-1, channels),
-        source_sums[0],
-        (grad_kernel, grad_gain, grad_shift, grad_up, up_sums[0], grad_down, down_sums[0]),
+        source_sums,
+        (grad_gain, grad_shift, (grad_branch, normed, active, grad_hidden)),
+        (grad_kernel, down_sums, up_sums),
     )
 
 
@@ -481,7 +590,7 @@
     decode_rows, decode_stored = block_forward(merged.astype(bf16), decode, sea_fine, ocean_fine, dates)
     result = from_dates(decode_rows.reshape(fine.shape), dates)
 
-    grad_merged, grad_merge_bias, decode_grads = block_backward(
+    grad_merged, merge_sums, decode_grads, decode_small = block_backward(
         upstream.reshape(-1, channels), decode, sea_fine, decode_stored, dates
     )
     grad_block_sum = jnp.sum(
@@ -496,65 +605,94 @@
         ],
         axis=0,
     )
+    grad_branch, normed, active, grad_hidden = decode_grads[2]
+    decode_parts = [cross_rows(normed, grad_hidden), cross_rows(active, grad_branch), grad_merge_weight]
+    decode_sums = lax.psum([part.astype(bf16) for part in decode_parts], both)
+    decode_up_sum, decode_down_sum, merge_sum = [total.astype(f32) for total in decode_sums]
+
     grad_coarse = by_transpose(grad_block_low, merge_upper) + by_transpose(grad_block_rest, merge_upper)
     grad_skip_direct = by_transpose(grad_merged, merge_lower)
-    grad_wide, grad_widen_bias, bottle_grads = block_backward(grad_coarse, bottle, sea_coarse, coarse_stored, dates)
-    grad_widen_weight = cross_rows(pooled, grad_wide)
+    grad_wide, widen_sums, bottle_grads, bottle_small = block_backward(
+        grad_coarse, bottle, sea_coarse, coarse_stored, dates
+    )
+    core = (lax.axis_index("lon") % 2).astype(jnp.int32)[None]
+    bottle_pair = weight_grads(*bottle_grads[2]).reshape(2, -1, lanes)
+    bottle_up_sum, bottle_down_sum = unpack(core, *sum_group(bottle_pair), wide, bottle_up.shape[1])
+
+    grad_widen = cross_rows(pooled, grad_wide).astype(bf16)
+    widen_tiles = pl.cdiv(wide, 2 * lanes)
+    grad_widen = jnp.pad(grad_widen, ((0, 0), (0, 2 * widen_tiles * lanes - wide)))
+    grad_widen = grad_widen.reshape(channels, 2, widen_tiles, lanes).transpose(1, 2, 0, 3).reshape(2, -1, lanes)
     grad_pooled = by_transpose(grad_wide, widen_weight).reshape(half_height, 1, half_breadth, 1, channels) * 0.25
     grad_skip = grad_skip_direct.reshape(half_height, 2, half_breadth, 2, channels) + grad_pooled
-    grad_fine, _, encode_grads = block_backward(
+    grad_fine, _, encode_grads, encode_small = block_backward(
         grad_skip.reshape(-1, channels), encode, sea_fine, encode_stored, dates
     )
     fine_grad = from_dates(grad_fine.reshape(fine.shape), dates)
-
-    def summed(parts):
-        return [total.astype(f32) for total in lax.psum([part.astype(bf16) for part in parts], both)]
-
-    decode_up_sum, decode_down_sum, merge_sum = summed([decode_grads[3], decode_grads[5], grad_merge_weight])
-    bottle_up_sum, bottle_down_sum, widen_sum = summed([bottle_grads[3], bottle_grads[5], grad_widen_weight])
-    encode_up_sum, encode_down_sum = summed([encode_grads[3], encode_grads[5]])
-    small_parts = [
-        encode_grads[0],
-        encode_grads[4],
-        encode_grads[6],
-        grad_widen_bias,
-        bottle_grads[0],
-        bottle_grads[4],
-        bottle_grads[6],
-        grad_merge_bias,
-        decode_grads[0],
-        decode_grads[4],
-        decode_grads[6],
-    ]
-    small = lax.psum(small_parts, both)
+    encode_pair = weight_grads(*encode_grads[2]).reshape(2, -1, lanes)
+    own, other = sum_group(jnp.concatenate([encode_pair, grad_widen], axis=1))
+    encode_up_sum, encode_down_sum = unpack(core, own, other, channels, encode_up.shape[1])
+    start = encode_pair.shape[1]
+    lower = jnp.where(core == 0, own[start : start + grad_widen.shape[1]], other[start : start + grad_widen.shape[1]])
+    upper = jnp.where(core == 0, other[start : start + grad_widen.shape[1]], own[start : start + grad_widen.shape[1]])
+    widen_sum = jnp.stack([lower, upper]).reshape(2 * widen_tiles, channels, lanes).astype(f32)
+    widen_sum = widen_sum.transpose(1, 0, 2).reshape(channels, -1)[:, :wide]
+
+    kernels = [encode_small[0], bottle_small[0], decode_small[0]]
+    rows = [encode_small[1:], (widen_sums,), bottle_small[1:], (merge_sums,), decode_small[1:]]
+    rows = [row for group in rows for row in group]
+    padded = [jnp.pad(row, ((0, 0), (0, -row.shape[1] % lanes))) for row in rows]
+    line = jnp.concatenate(padded, axis=1)
+    small = sum_small(jnp.concatenate([array.reshape(-1, lanes) for array in kernels] + [line.reshape(-1, lanes)]))
+    kernel_sums, at = [], 0
+    for array, shape in zip(kernels, (encode_depth.shape, bottle_depth.shape, decode_depth.shape)):
+        count = array.shape[0] * 56
+        total = small[at : at + count].reshape(array.shape)[:, :49].transpose(1, 0, 2).reshape(49, -1)
+        kernel_sums.append(total[:, : shape[2]].reshape(shape))
+        at += count
+    line = small[at:].reshape(-1)
+    row_sums, at = [], 0
+    for row, wider in zip(rows, padded):
+        row_sums.append(line[at : at + row.shape[1]])
+        at += wider.shape[1]
+    (encode_upb, encode_downb, widen_b, bottle_upb, bottle_downb, bottle_merge_b, decode_upb, decode_downb) = (
+        row_sums[1],
+        row_sums[0],
+        row_sums[2],
+        row_sums[4],
+        row_sums[3],
+        row_sums[5],
+        row_sums[7],
+        row_sums[6],
+    )
     return (
         result,
         fine_grad,
-        small[0].reshape(encode_depth.shape),
+        kernel_sums[0],
+        encode_grads[0],
         encode_grads[1],
-        encode_grads[2],
         encode_up_sum,
-        small[1],
+        encode_upb,
         encode_down_sum,
-        small[2],
+        encode_downb,
         widen_sum,
-        small[3],
-        small[4].reshape(bottle_depth.shape),
+        widen_b,
+        kernel_sums[1],
+        bottle_grads[0],
         bottle_grads[1],
-        bottle_grads[2],
         bottle_up_sum,
-        small[5],
+        bottle_upb,
         bottle_down_sum,
-        small[6],
+        bottle_downb,
         merge_sum,
-        small[7],
-        small[8].reshape(decode_depth.shape),
+        bottle_merge_b,
+        kernel_sums[2],
+        decode_grads[0],
         decode_grads[1],
-        decode_grads[2],
         decode_up_sum,
-        small[9],
+        decode_upb,
         decode_down_sum,
-        small[10],
+        decode_downb,
     )
 
 

time: 924 us -> 985 us (1.066)
  waiting for transfers between devices: 373 us -> 304 us
  starting transfers between devices: 67.4 us -> 134 us
  Pallas kernels: 187 us -> 239 us
  other arithmetic: 58.5 us -> 108 us
  blocking collectives: 80.9 us -> 31.8 us
  local copies, waits for them, and re-layouts: 82.8 us -> 112 us
  matrix products: 50.5 us -> 30.1 us
    psum x2 -> x1, waiting for transfers between devices: 273 us -> 85.3 us  [shards(): decode_sums = lax.psum([part.astype(bf16) for part in decode_parts], both)]
    ppermute x0 -> x28, waiting for transfers between devices: none -> 70.1 us  [swap(): lax.ppermute(array, axis, [(i, i ^ step) for i in range(lax.axis_size(axi...]
    ppermute x0 -> x28, starting transfers between devices: none -> 65.9 us  [swap(): lax.ppermute(array, axis, [(i, i ^ step) for i in range(lax.axis_size(axi...]
    ppermute x6, waiting for transfers between devices: 0.02 us -> 57.1 us  [from_dates(): lax.ppermute(lax.dynamic_index_in_dim(tiles, own ^ step, 0, keepdims=Fals...]
    pallas_call x3 -> x7, Pallas kernels: 33.1 us -> 84.9 us  [the longest x3 32.9 us: kernel_grad(): pl.pallas_call(functools.partial(kernel_grad_kernel, len(edges)), grid=(t...]
    psum x1 -> x0, blocking collectives: 49.2 us -> none  [shards(): small = lax.psum(small_parts, both)]
    concatenate x0 -> x5, other arithmetic: none -> 42.5 us  [the longest x2 38.8 us: exchange_all(): jnp.concatenate([take(got, own ^ place) for place in range(count)], axis=0)]
    dot_general x10 -> x6, matrix products: 38.2 us -> 16.7 us  [cross_rows(): lax.dot_general(former, latter, (((0,), (0,)), ((), ())), preferred_eleme...]
  transfers between devices with their start and end apart: 41 -> 70, of which waited for: 14 -> 18; matrix products, arithmetic and copies ran while one was open for 15% -> 23% of each run, Pallas kernels for 12% -> 17%
where the time goes in v3:
time: 985 us; the launch traced here: 976 us
  waiting for transfers between devices  304 us (31%)
  Pallas kernels  239 us (24%)
  starting transfers between devices  134 us (14%)
  local copies, waits for them, and re-layouts  112 us (11%)
  other arithmetic  108 us (11%)
  blocking collectives  31.8 us (3%)
  matrix products  30.1 us (3%)
  between operations  16.3 us (2%)
    psum x1, waiting for transfers between devices, shards(): decode_sums = lax.psum([part.astype(bf16) for part in decode_parts], both)  85.3 us
    ppermute x28, waiting for transfers between devices, swap(): lax.ppermute(array, axis, [(i, i ^ step) for i in range(lax.axis_size(axi...  70.1 us
    ppermute x28, starting transfers between devices, swap(): lax.ppermute(array, axis, [(i, i ^ step) for i in range(lax.axis_size(axi...  65.9 us
    ppermute x6, waiting for transfers between devices, from_dates(): lax.ppermute(lax.dynamic_index_in_dim(tiles, own ^ step, 0, keepdims=Fals...  57.1 us
    pallas_call x3, Pallas kernels, stencil_backward(): pl.pallas_call(functools.partial(stencil_backward_kernel, len(edges)), gr...  39.3 us
    pallas_call x3, Pallas kernels, mlp_forward(): pl.pallas_call(functools.partial(mlp_forward_kernel, 512), grid=(pixels /...  38.8 us
    concatenate x2, other arithmetic, exchange_all(): jnp.concatenate([take(got, own ^ place) for place in range(count)], axis=0)  38.8 us
    pallas_call x3, Pallas kernels, stencil_forward(): pl.pallas_call(functools.partial(stencil_forward_kernel, len(edges)), gri...  38.7 us
  transfers between devices with their start and end apart: 70, of which 18 were waited for; matrix products, arithmetic and copies ran while one was open for 23% of the time, Pallas kernels for 17%

profile of v3, /device:TPU:0, one launch (start us, length us, event | category | flops | bytes accessed | tf_op | source)
XLA Modules:
  0.0 975.7 jit_solution(10741950168487068215)
XLA Ops:
  22.2 14.8 %all-gather.2 = bf16[4,100,800]{2,1,0:T(8,128)(2,1)S(1)} all-gather(bf16[1,100,800]{2,1,0:T(8,128)(2,1)S(1)} %bitcast.391), channel_id=1, replica_groups=mesh['lat'=4,'lon'=8] {'lat'}, dimensions={0}, use_global_device_ids=true | all-gather | bytes 800000 | tf_op jit(solution)/shard_map/all_gather | solution.py:549
  48.4 17.0 %all-gather.1 = bf16[4,300,400]{1,2,0:T(8,128)(2,1)S(1)} all-gather(bf16[1,300,400]{1,2,0:T(8,128)(2,1)S(1)} %bitcast.390), channel_id=1, replica_groups=mesh['lat'=4,'lon'=8] {'lat'}, dimensions={0}, use_global_device_ids=true | all-gather | bytes 1200000 | tf_op jit(solution)/shard_map/all_gather | solution.py:549
  80.6 11.5 %collective-permute-done.2 = bf16[12,32,400]{2,1,0:T(8,128)(2,1)S(1)} collective-permute-done((bf16[12,32,400]{2,1,0:T(8,128)(2,1)S(1)}, bf16[12,32,400]{2,1,0:T(8,128)(2,1)S(1)}, u32[]{:S(2)}, u32[]{:S(2)}) %collective-permute-start.2) | collective-permute-done | bytes 307232 | tf_op jit(solution)/shard_map/ppermute | solution.py:30
  102.3 15.1 %stencil_forward.3 = (f32[48,32,400]{2,1,0:T(8,128)}, f32[2,400]{1,0:T(2,128)}) custom-call(bf16[48,32,400]{2,1,0:T(8,128)(2,1)} %copy-done.2, bf16[48,3,400]{2,1,0:T(4,128)(2,1)} %copy-done.33, bf16[48,3,400]{2,1,0:T(4,128)(2,1)} %copy-done.34, f32[49,400]{1,0:T(8,128)} %reshape.349.refs_2_, f32[48,32,128]{2,1,0:T(8,128)} %broadcast_in_dim.115.refs_3_), custom_call_target="tpu_custom_call" | custom-call | tf_op jit(solution)/shard_map/stencil_forward/pallas_call | solution.py:188
  119.4 4.4 all-to-all-start
  124.7 9.5 all-to-all-done
  139.1 12.6 %mlp_forward.3 = (bf16[1536,400]{1,0:T(8,128)(2,1)}, bf16[1536,1600]{1,0:T(8,128)(2,1)}, bf16[1536,1600]{1,0:T(8,128)(2,1)}, bf16[1536,400]{1,0:T(8,128)(2,1)}) custom-call(f32[1536,400]{1,0:T(8,128)} %bitcast.320, bf16[1536,400]{1,0:T(8,128)(2,1)} %bitcast.319, f32[1536,128]{1,0:T(8,128)} %broadcast_in_dim.116.sea, f32[4,400]{1,0:T(4,128)} %pad_maximum_fusion.22.scales, ...), custom_call_target="tpu_custom_call" | custom-call | tf_op jit(solution)/shard_map/mlp_forward/pallas_call | solution.py:319
  170.4 8.5 stencil_forward.4
  181.1 4.0 all-to-all-start.1
  187.6 12.5 %all-to-all-done.1 = f32[32,3,800]{2,1,0:T(4,128)S(1)} async-done(((f32[32,3,800]{2,1,0:T(4,128)}), f32[32,3,800]{2,1,0:T(4,128)S(1)}, u32[]{:S(2)}, u32[]{:S(2)}) %all-to-all-start.1) | async-done | bytes 307232 | tf_op jit(solution)/shard_map/all_to_all | solution.py:77
  200.8 30.0 %all-gather.15.cloned.1.call-done.down = bf16[3200,800]{1,0:T(8,128)(2,1)} async-done(((bf16[800,800]{1,0:T(8,128)(2,1)}), bf16[3200,800]{1,0:T(8,128)(2,1)}) %all-gather.15.cloned.1.call-update) | async-done | bytes 5120016 | tf_op jit(solution)/shard_map/all_gather | solution.py:549
  231.6 13.6 %mlp_forward.4 = (bf16[384,800]{1,0:T(8,128)(2,1)}, bf16[384,3200]{1,0:T(8,128)(2,1)}, bf16[384,3200]{1,0:T(8,128)(2,1)}, bf16[384,800]{1,0:T(8,128)(2,1)}) custom-call(f32[384,800]{1,0:T(8,128)} %bitcast.334, bf16[384,800]{1,0:T(8,128)(2,1)} %copy-done.12, f32[384,128]{1,0:T(8,128)} %broadcast_in_dim.124.sea, f32[4,800]{1,0:T(4,128)} %pad_maximum_fusion.21.scales, ...), custom_call_target="tpu_custom_call" | custom-call | tf_op jit(solution)/shard_map/mlp_forward/pallas_call | solution.py:319
  255.3 4.9 add_convert_fusion
  270.0 15.1 %stencil_forward.5 = (f32[48,32,400]{2,1,0:T(8,128)}, f32[2,400]{1,0:T(2,128)}) custom-call(bf16[48,32,400]{2,1,0:T(8,128)(2,1)} %copy-done.6, bf16[48,3,400]{2,1,0:T(4,128)(2,1)} %copy-done.35, bf16[48,3,400]{2,1,0:T(4,128)(2,1)} %copy-done.36, f32[49,400]{1,0:T(8,128)} %reshape.360.refs_2_, f32[48,32,128]{2,1,0:T(8,128)} %broadcast_in_dim.115.refs_3_), custom_call_target="tpu_custom_call" | custom-call | tf_op jit(solution)/shard_map/stencil_forward/pallas_call | solution.py:188
  294.9 6.4 all-to-all-done.2
  302.0 12.6 %mlp_forward.5 = (bf16[1536,400]{1,0:T(8,128)(2,1)}, bf16[1536,1600]{1,0:T(8,128)(2,1)}, bf16[1536,1600]{1,0:T(8,128)(2,1)}, bf16[1536,400]{1,0:T(8,128)(2,1)}) custom-call(f32[1536,400]{1,0:T(8,128)} %bitcast.322, bf16[1536,400]{1,0:T(8,128)(2,1)} %get-tuple-element.405.source, f32[1536,128]{1,0:T(8,128)} %broadcast_in_dim.116.sea, ...), custom_call_target="tpu_custom_call" | custom-call | tf_op jit(solution)/shard_map/mlp_forward/pallas_call | solution.py:319
  314.6 12.0 %mlp_backward.3 = (bf16[1536,400]{1,0:T(8,128)(2,1)}, bf16[1536,1600]{1,0:T(8,128)(2,1)}, f32[1536,400]{1,0:T(8,128)}, f32[2,400]{1,0:T(2,128)}, f32[1,400]{1,0:T(1,128)}, /*index=5*/f32[1,1600]{1,0:T(1,128)}) custom-call(bf16[1536,400]{1,0:T(8,128)(2,1)} %bitcast.332, f32[1536,400]{1,0:T(8,128)} %bitcast.323, bf16[1536,1600]{1,0:T(8,128)(2,1)} %get-tuple-element.81.slope, ...), custom_call_target="tpu_custom_call" | custom-call | tf_op jit(solution)/shard_map/mlp_backward/pallas_call | solution.py:336
  335.1 6.6 convolution_convert_fusion
  353.0 12.6 %kernel_grad.5 = f32[4,56,128]{2,1,0:T(8,128)} custom-call(bf16[48,32,400]{2,1,0:T(8,128)(2,1)} %copy-done.6, bf16[48,3,400]{2,1,0:T(4,128)(2,1)} %copy-done.35, bf16[48,3,400]{2,1,0:T(4,128)(2,1)} %copy-done.36, bf16[48,32,400]{2,1,0:T(8,128)(2,1)} %bitcast.327), custom_call_target="tpu_custom_call" | custom-call | tf_op jit(solution)/shard_map/kernel_grad/pallas_call | solution.py:220
  368.8 15.0 %stencil_backward.3 = (bf16[48,32,400]{2,1,0:T(8,128)(2,1)}, f32[1,400]{1,0:T(1,128)}) custom-call(bf16[48,32,400]{2,1,0:T(8,128)(2,1)} %bitcast.328, bf16[48,3,400]{2,1,0:T(4,128)(2,1)} %copy-done.50, bf16[48,3,400]{2,1,0:T(4,128)(2,1)} %copy-done.51, f32[49,400]{1,0:T(8,128)} %reshape.360.refs_2_, f32[48,32,128]{2,1,0:T(8,128)} %broadcast_in_dim.115.refs_3_, ...), custom_call_target="tpu_custom_call" | custom-call | tf_op jit(solution)/shard_map/stencil_backward/pallas_call | solution.py:204
  387.6 4.1 convert_reduce_fusion
  394.0 12.9 %mlp_backward.4 = (bf16[384,800]{1,0:T(8,128)(2,1)}, bf16[384,3200]{1,0:T(8,128)(2,1)}, f32[384,800]{1,0:T(8,128)}, f32[2,800]{1,0:T(2,128)}, f32[1,800]{1,0:T(1,128)}, /*index=5*/f32[1,3200]{1,0:T(1,128)}) custom-call(f32[384,800]{1,0:T(8,128)} %convolution_add_fusion.2.upstream, f32[384,800]{1,0:T(8,128)} %bitcast.335, ...), custom_call_target="tpu_custom_call" | custom-call | tf_op jit(solution)/shard_map/mlp_backward/pallas_call | solution.py:336
  408.3 4.1 all-to-all-start.4
  412.5 11.2 %weight_grads.3 = bf16[2,25,800,128]{3,2,1,0:T(8,128)(2,1)} custom-call(bf16[384,800]{1,0:T(8,128)(2,1)} %get-tuple-element.107.grad_branch, bf16[384,800]{1,0:T(8,128)(2,1)} %get-tuple-element.108.normed, bf16[384,3200]{1,0:T(8,128)(2,1)} %get-tuple-element.109.active, bf16[384,3200]{1,0:T(8,128)(2,1)} %get-tuple-element.110.grad_hidden), custom_call_target="tpu_custom_call" | custom-call | tf_op jit(solution)/shard_map/weight_grads/pallas_call | solution.py:372
  423.7 5.8 fusion.4
  442.0 7.6 kernel_grad.4
  450.2 8.8 stencil_backward.4
  474.3 12.1 %mlp_backward.5 = (bf16[1536,400]{1,0:T(8,128)(2,1)}, bf16[1536,1600]{1,0:T(8,128)(2,1)}, f32[1536,400]{1,0:T(8,128)}, f32[2,400]{1,0:T(2,128)}, f32[1,400]{1,0:T(1,128)}, /*index=5*/f32[1,1600]{1,0:T(1,128)}) custom-call(f32[1536,400]{1,0:T(8,128)} %reshape.320.upstream, f32[1536,400]{1,0:T(8,128)} %bitcast.321, ...), custom_call_target="tpu_custom_call" | custom-call | tf_op jit(solution)/shard_map/mlp_backward/pallas_call | solution.py:336
  486.4 11.7 %weight_grads.2 = bf16[2,13,400,128]{3,2,1,0:T(8,128)(2,1)} custom-call(bf16[1536,400]{1,0:T(8,128)(2,1)} %get-tuple-element.101.grad_branch, bf16[1536,400]{1,0:T(8,128)(2,1)} %get-tuple-element.102.normed, bf16[1536,1600]{1,0:T(8,128)(2,1)} %get-tuple-element.103.active, bf16[1536,1600]{1,0:T(8,128)(2,1)} %get-tuple-element.104.grad_hidden), custom_call_target="tpu_custom_call" | custom-call | tf_op jit(solution)/shard_map/weight_grads/pallas_call | solution.py:372
  503.0 4.0 all-to-all-start.5
  507.2 8.0 all-to-all-done.5
  515.3 5.0 fusion
  526.4 25.4 %collective-permute-done.42 = bf16[5024,128]{1,0:T(8,128)(2,1)S(1)} collective-permute-done((bf16[5024,128]{1,0:T(8,128)(2,1)S(1)}, bf16[5024,128]{1,0:T(8,128)(2,1)S(1)}, u32[]{:S(2)}, u32[]{:S(2)}) %collective-permute-start.42) | collective-permute-done | bytes 1286176 | tf_op jit(solution)/shard_map/ppermute | solution.py:415
  551.8 27.0 %collective-permute-done.43 = bf16[5024,128]{1,0:T(8,128)(2,1)S(1)} collective-permute-done((bf16[5024,128]{1,0:T(8,128)(2,1)S(1)}, bf16[5024,128]{1,0:T(8,128)(2,1)S(1)}, u32[]{:S(2)}, u32[]{:S(2)}) %collective-permute-start.43) | collective-permute-done | bytes 1286176 | tf_op jit(solution)/shard_map/ppermute | solution.py:415
  584.9 12.7 %kernel_grad.3 = f32[4,56,128]{2,1,0:T(8,128)} custom-call(bf16[48,32,400]{2,1,0:T(8,128)(2,1)} %copy-done.2, bf16[48,3,400]{2,1,0:T(4,128)(2,1)} %copy-done.33, bf16[48,3,400]{2,1,0:T(4,128)(2,1)} %copy-done.34, bf16[48,32,400]{2,1,0:T(8,128)(2,1)} %bitcast.330), custom_call_target="tpu_custom_call" | custom-call | tf_op jit(solution)/shard_map/kernel_grad/pallas_call | solution.py:220
  604.3 15.5 %stencil_backward.5 = (bf16[48,32,400]{2,1,0:T(8,128)(2,1)}, f32[1,400]{1,0:T(1,128)}) custom-call(bf16[48,32,400]{2,1,0:T(8,128)(2,1)} %bitcast.331, bf16[48,3,400]{2,1,0:T(4,128)(2,1)} %copy-done.49, bf16[48,3,400]{2,1,0:T(4,128)(2,1)} %collective-permute-done.23.refs_1_, f32[49,400]{1,0:T(8,128)} %reshape.349.refs_2_, ...), custom_call_target="tpu_custom_call" | custom-call | tf_op jit(solution)/shard_map/stencil_backward/pallas_call | solution.py:204
  624.3 14.0 %collective-permute-start.49 = (bf16[1256,128]{1,0:T(8,128)(2,1)S(1)}, bf16[1256,128]{1,0:T(8,128)(2,1)S(1)}, u32[]{:S(2)}, u32[]{:S(2)}) collective-permute-start(bf16[1256,128]{1,0:T(8,128)(2,1)S(1)} %fusion.30), channel_id=1, source_target_pairs={{0,4},{1,5},{2,6},{3,7},{4,0},{5,1},{6,2},{7,3},{8,12},{9,13},{10,... | collective-permute-start | bytes 964616 | tf_op jit(solution)/shard_map/ppermute | solution.py:415
  646.7 11.7 %collective-permute-done.50 = bf16[1256,128]{1,0:T(8,128)(2,1)S(1)} collective-permute-done((bf16[1256,128]{1,0:T(8,128)(2,1)S(1)}, bf16[1256,128]{1,0:T(8,128)(2,1)S(1)}, u32[]{:S(2)}, u32[]{:S(2)}) %collective-permute-start.50) | collective-permute-done | bytes 321568 | tf_op jit(solution)/shard_map/ppermute | solution.py:415
  667.7 57.1 %collective-permute-done.24 = bf16[12,32,400]{2,1,0:T(8,128)(2,1)S(1)} collective-permute-done((bf16[12,32,400]{2,1,0:T(8,128)(2,1)S(1)}, bf16[12,32,400]{2,1,0:T(8,128)(2,1)S(1)}, u32[]{:S(2)}, u32[]{:S(2)}) %collective-permute-start.24) | collective-permute-done | bytes 307232 | tf_op jit(solution)/shard_map/ppermute | solution.py:48
  727.0 10.8 %collective-permute-start.31 = (bf16[432,128]{1,0:T(8,128)(2,1)S(1)}, bf16[432,128]{1,0:T(8,128)(2,1)S(1)}, u32[]{:S(2)}, u32[]{:S(2)}) collective-permute-start(bf16[432,128]{1,0:T(8,128)(2,1)S(1)} %get-tuple-element.370), channel_id=1, source_target_pairs={{0,2},{1,3},{2,0},{3,1},{4,6},{5,7},{6,4},{7,5},{8,10},{9,11},{10,... | collective-permute-start | bytes 331784 | tf_op jit(solution)/shard_map/ppermute | solution.py:415
  739.1 6.1 collective-permute-start.32
  745.2 5.2 collective-permute-start.33
  770.9 38.7 %pad_maximum_fusion.1.own = bf16[20096,128]{1,0:T(8,128)(2,1)} fusion(bf16[5024,128]{1,0:T(8,128)(2,1)S(1)} %get-tuple-element.296, bf16[5024,128]{1,0:T(8,128)(2,1)S(1)} %get-tuple-element.297, bf16[5024,128]{1,0:T(8,128)(2,1)S(1)} %get-tuple-element.298, bf16[5024,128]{1,0:T(8,128)(2,1)S(1)} %get-tuple-element.295), kind=kLoop, calls=%fused_computation.10 | loop fusion | flops 20578304 | bytes 10289152 | tf_op jit(solution)/shard_map/concatenate | solution.py:433
  815.6 85.3 %all-reduce.17.cloned.1.call-done = (bf16[1200,400]{0,1:T(8,128)(2,1)}, bf16[400,1600]{1,0:T(8,128)(2,1)}, bf16[1600,400]{0,1:T(8,128)(2,1)}) async-done(((bf16[1200,400]{0,1:T(8,128)(2,1)}, bf16[400,1600]{1,0:T(8,128)(2,1)}, bf16[1600,400]{0,1:T(8,128)(2,1)}), (bf16[1200,400]{0,1:T(8,128)(2,1)}, bf16[400,1600]{1,0:T(8,128)(2,1)}, bf16[1600,400]{0,1:T(8,128)(2,1)})) %all-reduce.17.cloned.1.call-update) | async-done | bytes 3520016 | tf_op jit(solution)/shard_map/psum | solution.py:610
  921.7 9.2 unpack.2
  930.9 4.4 copy.195
  936.5 19.9 %unpack.3 = (f32[800,3200]{1,0:T(8,128)}, f32[3200,800]{1,0:T(8,128)}) custom-call(s32[1]{0:T(128)} %bitcast.90.core, bf16[20096,128]{1,0:T(8,128)(2,1)} %pad_maximum_fusion.1.own, bf16[20096,128]{1,0:T(8,128)(2,1)} %collective-permute-done.54.other), custom_call_target="tpu_custom_call" | custom-call | tf_op jit(solution)/shard_map/unpack/pallas_call | solution.py:394
  956.5 12.2 %copy.196 = f32[3200,800]{0,1:T(8,128)} copy(f32[3200,800]{1,0:T(8,128)} %get-tuple-element.268) | data formatting | bytes 20480000
  (538 shorter events, 270.1 us)
Async XLA Ops:
  7.2 128.3 %all-gather.19.cloned.1.call-start = ((), (), s32[]{:S(2)}) async-start(), calls=%async_computation.12 | async-start | bytes 1730560 | tf_op jit(solution)/shard_map/all_gather | solution.py:549
  7.9 130.0 %all-gather.11.cloned.1.call-start = ((), (), s32[]{:S(2)}) async-start(), calls=%async_computation.8 | async-start | bytes 2048000 | tf_op jit(solution)/shard_map/all_gather | solution.py:549
  8.7 192.2 %all-gather.13.cloned.1.call-start = ((), (), s32[]{:S(2)}) async-start(), calls=%async_computation.9 | async-start | bytes 6400000 | tf_op jit(solution)/shard_map/all_gather | solution.py:549
  9.4 221.4 %all-gather.15.cloned.1.call-start = ((), (), s32[]{:S(2)}) async-start(), calls=%async_computation.10 | async-start | bytes 7168000 | tf_op jit(solution)/shard_map/all_gather | solution.py:549
  10.0 282.4 %all-gather.21.cloned.1.call-start = ((), (), s32[]{:S(2)}) async-start(), calls=%async_computation.13 | async-start | bytes 1730560 | tf_op jit(solution)/shard_map/all_gather | solution.py:549
  10.6 291.4 %all-gather.17.cloned.1.call-start = ((), (), s32[]{:S(2)}) async-start(), calls=%async_computation.11 | async-start | bytes 2048000 | tf_op jit(solution)/shard_map/all_gather | solution.py:549
  11.8 67.4 %collective-permute-start = (bf16[12,32,400]{2,1,0:T(8,128)(2,1)}, bf16[12,32,400]{2,1,0:T(8,128)(2,1)S(1)}, u32[]{:S(2)}, u32[]{:S(2)}) collective-permute-start(bf16[12,32,400]{2,1,0:T(8,128)(2,1)} %get-tuple-element.348), channel_id=1, source_target_pairs={{0,8},{8,0},{16,24},{24,16},{1,9},{9,1},{17,25},{25,17},{2,10},{10... | collective-permute-start | bytes 921608 | tf_op jit(solution)/shard_map/ppermute | solution.py:30
  14.7 65.9 %collective-permute-start.1 = (bf16[12,32,400]{2,1,0:T(8,128)(2,1)}, bf16[12,32,400]{2,1,0:T(8,128)(2,1)}, u32[]{:S(2)}, u32[]{:S(2)}) collective-permute-start(bf16[12,32,400]{2,1,0:T(8,128)(2,1)} %get-tuple-element.350), channel_id=1, source_target_pairs={{0,16},{8,24},{16,0},{24,8},{1,17},{9,25},{17,1},{25,9},{2,18},{10... | collective-permute-start | bytes 921608 | tf_op jit(solution)/shard_map/ppermute | solution.py:30
  16.9 56.1 %collective-permute-start.5 = (s32[12,32]{1,0:T(8,128)}, s32[12,32]{1,0:T(8,128)}, u32[]{:S(2)}, u32[]{:S(2)}) collective-permute-start(s32[12,32]{1,0:T(8,128)} %bitcast.313), channel_id=1, source_target_pairs={{0,8},{8,0},{16,24},{24,16},{1,9},{9,1},{17,25},{25,17},{2,10},{10... | collective-permute-start | bytes 4616 | tf_op jit(solution)/shard_map/ppermute | solution.py:30
  18.0 56.4 %collective-permute-start.6 = (s32[12,32]{1,0:T(8,128)}, s32[12,32]{1,0:T(8,128)}, u32[]{:S(2)}, u32[]{:S(2)}) collective-permute-start(s32[12,32]{1,0:T(8,128)} %bitcast.312), channel_id=1, source_target_pairs={{0,16},{8,24},{16,0},{24,8},{1,17},{9,25},{17,1},{25,9},{2,18},{10... | collective-permute-start | bytes 4616 | tf_op jit(solution)/shard_map/ppermute | solution.py:30
  18.0 58.0 %collective-permute-start.7 = (s32[12,32]{1,0:T(8,128)S(1)}, s32[12,32]{1,0:T(8,128)}, u32[]{:S(2)}, u32[]{:S(2)}) collective-permute-start(s32[12,32]{1,0:T(8,128)S(1)} %bitcast.404), channel_id=1, source_target_pairs={{0,24},{8,16},{16,8},{24,0},{1,25},{9,17},{17,9},{25,1},{2,26},{10... | collective-permute-start | bytes 4616 | tf_op jit(solution)/shard_map/ppermute | solution.py:30
  74.4 190.6 %collective-permute-start.15 = (bf16[12,32,400]{2,1,0:T(8,128)(2,1)}, bf16[12,32,400]{2,1,0:T(8,128)(2,1)}, u32[]{:S(2)}, u32[]{:S(2)}) collective-permute-start(bf16[12,32,400]{2,1,0:T(8,128)(2,1)} %get-tuple-element.328), channel_id=1, source_target_pairs={{0,8},{8,0},{16,24},{24,16},{1,9},{9,1},{17,25},{25,17},{2,10},{10... | collective-permute-start | bytes 921608 | tf_op jit(solution)/shard_map/ppermute | solution.py:30
  76.0 188.9 %collective-permute-start.16 = (bf16[12,32,400]{2,1,0:T(8,128)(2,1)}, bf16[12,32,400]{2,1,0:T(8,128)(2,1)}, u32[]{:S(2)}, u32[]{:S(2)}) collective-permute-start(bf16[12,32,400]{2,1,0:T(8,128)(2,1)} %get-tuple-element.330), channel_id=1, source_target_pairs={{0,16},{8,24},{16,0},{24,8},{1,17},{9,25},{17,1},{25,9},{2,18},{10... | collective-permute-start | bytes 921608 | tf_op jit(solution)/shard_map/ppermute | solution.py:30
  79.1 185.9 %collective-permute-start.17 = (bf16[12,32,400]{2,1,0:T(8,128)(2,1)}, bf16[12,32,400]{2,1,0:T(8,128)(2,1)}, u32[]{:S(2)}, u32[]{:S(2)}) collective-permute-start(bf16[12,32,400]{2,1,0:T(8,128)(2,1)} %get-tuple-element.329), channel_id=1, source_target_pairs={{0,24},{8,16},{16,8},{24,0},{1,25},{9,17},{17,9},{25,1},{2,26},{10... | collective-permute-start | bytes 921608 | tf_op jit(solution)/shard_map/ppermute | solution.py:30
  331.6 34.0 %collective-permute-start.12 = (bf16[12,32,400]{2,1,0:T(8,128)(2,1)}, bf16[12,32,400]{2,1,0:T(8,128)(2,1)S(1)}, u32[]{:S(2)}, u32[]{:S(2)}) collective-permute-start(bf16[12,32,400]{2,1,0:T(8,128)(2,1)} %get-tuple-element.338), channel_id=1, source_target_pairs={{0,8},{8,0},{16,24},{24,16},{1,9},{9,1},{17,25},{25,17},{2,10},{10... | collective-permute-start | bytes 921608 | tf_op jit(solution)/shard_map/ppermute | solution.py:48
  333.3 32.3 %collective-permute-start.13 = (bf16[12,32,400]{2,1,0:T(8,128)(2,1)S(1)}, bf16[12,32,400]{2,1,0:T(8,128)(2,1)S(1)}, u32[]{:S(2)}, u32[]{:S(2)}) collective-permute-start(bf16[12,32,400]{2,1,0:T(8,128)(2,1)S(1)} %get-tuple-element.337), channel_id=1, source_target_pairs={{0,16},{8,24},{16,0},{24,8},{1,17},{9,25},{17,1},{25,9},{2,18},{10... | collective-permute-start | bytes 921608 | tf_op jit(solution)/shard_map/ppermute | solution.py:48
  334.7 30.9 %collective-permute-start.14 = (bf16[12,32,400]{2,1,0:T(8,128)(2,1)S(1)}, bf16[12,32,400]{2,1,0:T(8,128)(2,1)S(1)}, u32[]{:S(2)}, u32[]{:S(2)}) collective-permute-start(bf16[12,32,400]{2,1,0:T(8,128)(2,1)S(1)} %get-tuple-element.336), channel_id=1, source_target_pairs={{0,24},{8,16},{16,8},{24,0},{1,25},{9,17},{17,9},{25,1},{2,26},{10... | collective-permute-start | bytes 921608 | tf_op jit(solution)/shard_map/ppermute | solution.py:48
  408.3 24.8 %all-to-all-start.4 = ((f32[32,2,800]{2,1,0:T(2,128)}), f32[32,2,800]{2,1,0:T(2,128)}, u32[]{:S(2)}, u32[]{:S(2)}) async-start(f32[32,2,800]{2,1,0:T(2,128)} %broadcast_in_dim.136), calls=%async_computation.4 | async-start | bytes 458752 | tf_op jit(solution)/shard_map/all_to_all | solution.py:77
  431.3 84.0 %collective-permute-start.41 = (bf16[20096,128]{1,0:T(8,128)(2,1)}, bf16[20096,128]{1,0:T(8,128)(2,1)}, u32[]{:S(2)}, u32[]{:S(2)}) collective-permute-start(bf16[20096,128]{1,0:T(8,128)(2,1)} %fusion.4), channel_id=1, source_target_pairs={{0,1},{1,0},{2,3},{3,2},{4,5},{5,4},{6,7},{7,6},{8,9},{9,8},{10,11... | collective-permute-start | bytes 15433736 | tf_op jit(solution)/shard_map/ppermute | solution.py:415
  502.3 137.3 %collective-permute-start.27 = (bf16[6912,128]{1,0:T(8,128)(2,1)}, bf16[6912,128]{1,0:T(8,128)(2,1)}, u32[]{:S(2)}, u32[]{:S(2)}) collective-permute-start(bf16[6912,128]{1,0:T(8,128)(2,1)} %dynamic-slice_bitcast_fusion), channel_id=1, source_target_pairs={{0,1},{1,0},{2,3},{3,2},{4,5},{5,4},{6,7},{7,6},{8,9},{9,8},{10,11... | collective-permute-start | bytes 5308424 | tf_op jit(solution)/shard_map/ppermute | solution.py:415
  520.7 31.1 %collective-permute-start.42 = (bf16[5024,128]{1,0:T(8,128)(2,1)S(1)}, bf16[5024,128]{1,0:T(8,128)(2,1)S(1)}, u32[]{:S(2)}, u32[]{:S(2)}) collective-permute-start(bf16[5024,128]{1,0:T(8,128)(2,1)S(1)} %get-tuple-element.299), channel_id=1, source_target_pairs={{0,8},{8,0},{16,24},{24,16},{1,9},{9,1},{17,25},{25,17},{2,10},{10... | collective-permute-start | bytes 3858440 | tf_op jit(solution)/shard_map/ppermute | solution.py:415
  521.5 57.3 %collective-permute-start.43 = (bf16[5024,128]{1,0:T(8,128)(2,1)S(1)}, bf16[5024,128]{1,0:T(8,128)(2,1)S(1)}, u32[]{:S(2)}, u32[]{:S(2)}) collective-permute-start(bf16[5024,128]{1,0:T(8,128)(2,1)S(1)} %get-tuple-element.301), channel_id=1, source_target_pairs={{0,16},{8,24},{16,0},{24,8},{1,17},{9,25},{17,1},{25,9},{2,18},{10... | collective-permute-start | bytes 3858440 | tf_op jit(solution)/shard_map/ppermute | solution.py:415
  522.3 56.6 %collective-permute-start.44 = (bf16[5024,128]{1,0:T(8,128)(2,1)S(1)}, bf16[5024,128]{1,0:T(8,128)(2,1)S(1)}, u32[]{:S(2)}, u32[]{:S(2)}) collective-permute-start(bf16[5024,128]{1,0:T(8,128)(2,1)S(1)} %get-tuple-element.300), channel_id=1, source_target_pairs={{0,24},{8,16},{16,8},{24,0},{1,25},{9,17},{17,9},{25,1},{2,26},{10... | collective-permute-start | bytes 3858440 | tf_op jit(solution)/shard_map/ppermute | solution.py:415
  526.4 71.2 %collective-permute-start.22 = (bf16[48,3,400]{2,1,0:T(4,128)(2,1)S(1)}, bf16[48,3,400]{2,1,0:T(4,128)(2,1)S(1)}, u32[]{:S(2)}, u32[]{:S(2)}) collective-permute-start(bf16[48,3,400]{2,1,0:T(4,128)(2,1)S(1)} %get-tuple-element.320), channel_id=1, source_target_pairs={{0,1},{1,2},{2,3},{3,4},{4,5},{5,6},{6,7},{7,0},{8,9},{9,10},{10,1... | collective-permute-start | bytes 345608 | tf_op jit(solution)/shard_map/ppermute | solution.py:62
  580.4 39.4 %collective-permute-start.45 = (bf16[1256,128]{1,0:T(8,128)(2,1)}, bf16[1256,128]{1,0:T(8,128)(2,1)S(1)}, u32[]{:S(2)}, u32[]{:S(2)}) collective-permute-start(bf16[1256,128]{1,0:T(8,128)(2,1)} %get-tuple-element.357), channel_id=1, source_target_pairs={{0,2},{1,3},{2,0},{3,1},{4,6},{5,7},{6,4},{7,5},{8,10},{9,11},{10,... | collective-permute-start | bytes 964616 | tf_op jit(solution)/shard_map/ppermute | solution.py:415
  581.1 38.7 %collective-permute-start.46 = (bf16[1256,128]{1,0:T(8,128)(2,1)S(1)}, bf16[1256,128]{1,0:T(8,128)(2,1)S(1)}, u32[]{:S(2)}, u32[]{:S(2)}) collective-permute-start(bf16[1256,128]{1,0:T(8,128)(2,1)S(1)} %get-tuple-element.359), channel_id=1, source_target_pairs={{0,4},{1,5},{2,6},{3,7},{4,0},{5,1},{6,2},{7,3},{8,12},{9,13},{10,... | collective-permute-start | bytes 964616 | tf_op jit(solution)/shard_map/ppermute | solution.py:415
  582.3 37.6 %collective-permute-start.47 = (bf16[1256,128]{1,0:T(8,128)(2,1)S(1)}, bf16[1256,128]{1,0:T(8,128)(2,1)}, u32[]{:S(2)}, u32[]{:S(2)}) collective-permute-start(bf16[1256,128]{1,0:T(8,128)(2,1)S(1)} %get-tuple-element.358), channel_id=1, source_target_pairs={{0,6},{1,7},{2,4},{3,5},{4,2},{5,3},{6,0},{7,1},{8,14},{9,15},{10,... | collective-permute-start | bytes 964616 | tf_op jit(solution)/shard_map/ppermute | solution.py:415
  599.4 152.6 %all-to-all-start.6 = ((f32[32,32,128]{2,1,0:T(8,128)}), f32[32,32,128]{2,1,0:T(8,128)S(1)}, u32[]{:S(2)}, u32[]{:S(2)}) async-start(f32[32,32,128]{2,1,0:T(8,128)} %bitcast.87), calls=%async_computation.6 | async-start | bytes 1048576 | tf_op jit(solution)/shard_map/all_to_all | solution.py:457
  602.1 298.9 %all-reduce.17.cloned.1.call-start = ((), (), s32[]{:S(2)}) async-start(), calls=%async_computation.14 | async-start | bytes 7372800 | tf_op jit(solution)/shard_map/psum | solution.py:610
  621.0 22.8 %collective-permute-start.48 = (bf16[1256,128]{1,0:T(8,128)(2,1)S(1)}, bf16[1256,128]{1,0:T(8,128)(2,1)S(1)}, u32[]{:S(2)}, u32[]{:S(2)}) collective-permute-start(bf16[1256,128]{1,0:T(8,128)(2,1)S(1)} %fusion.30), channel_id=1, source_target_pairs={{0,2},{1,3},{2,0},{3,1},{4,6},{5,7},{6,4},{7,5},{8,10},{9,11},{10,... | collective-permute-start | bytes 964616 | tf_op jit(solution)/shard_map/ppermute | solution.py:415
  624.3 22.4 %collective-permute-start.49 = (bf16[1256,128]{1,0:T(8,128)(2,1)S(1)}, bf16[1256,128]{1,0:T(8,128)(2,1)S(1)}, u32[]{:S(2)}, u32[]{:S(2)}) collective-permute-start(bf16[1256,128]{1,0:T(8,128)(2,1)S(1)} %fusion.30), channel_id=1, source_target_pairs={{0,4},{1,5},{2,6},{3,7},{4,0},{5,1},{6,2},{7,3},{8,12},{9,13},{10,... | collective-permute-start | bytes 964616 | tf_op jit(solution)/shard_map/ppermute | solution.py:415
  638.2 20.2 %collective-permute-start.50 = (bf16[1256,128]{1,0:T(8,128)(2,1)S(1)}, bf16[1256,128]{1,0:T(8,128)(2,1)S(1)}, u32[]{:S(2)}, u32[]{:S(2)}) collective-permute-start(bf16[1256,128]{1,0:T(8,128)(2,1)S(1)} %fusion.30), channel_id=1, source_target_pairs={{0,6},{1,7},{2,4},{3,5},{4,2},{5,3},{6,0},{7,1},{8,14},{9,15},{10,... | collective-permute-start | bytes 964616 | tf_op jit(solution)/shard_map/ppermute | solution.py:415
  641.7 20.3 %collective-permute-start.28 = (bf16[1728,128]{1,0:T(8,128)(2,1)S(1)}, bf16[1728,128]{1,0:T(8,128)(2,1)S(1)}, u32[]{:S(2)}, u32[]{:S(2)}) collective-permute-start(bf16[1728,128]{1,0:T(8,128)(2,1)S(1)} %get-tuple-element.308), channel_id=1, source_target_pairs={{0,8},{8,0},{16,24},{24,16},{1,9},{9,1},{17,25},{25,17},{2,10},{10... | collective-permute-start | bytes 1327112 | tf_op jit(solution)/shard_map/ppermute | solution.py:415
  642.9 22.5 %collective-permute-start.29 = (bf16[1728,128]{1,0:T(8,128)(2,1)S(1)}, bf16[1728,128]{1,0:T(8,128)(2,1)S(1)}, u32[]{:S(2)}, u32[]{:S(2)}) collective-permute-start(bf16[1728,128]{1,0:T(8,128)(2,1)S(1)} %get-tuple-element.310), channel_id=1, source_target_pairs={{0,16},{8,24},{16,0},{24,8},{1,17},{9,25},{17,1},{25,9},{2,18},{10... | collective-permute-start | bytes 1327112 | tf_op jit(solution)/shard_map/ppermute | solution.py:415
  643.8 22.5 %collective-permute-start.30 = (bf16[1728,128]{1,0:T(8,128)(2,1)S(1)}, bf16[1728,128]{1,0:T(8,128)(2,1)S(1)}, u32[]{:S(2)}, u32[]{:S(2)}) collective-permute-start(bf16[1728,128]{1,0:T(8,128)(2,1)S(1)} %get-tuple-element.309), channel_id=1, source_target_pairs={{0,24},{8,16},{16,8},{24,0},{1,25},{9,17},{17,9},{25,1},{2,26},{10... | collective-permute-start | bytes 1327112 | tf_op jit(solution)/shard_map/ppermute | solution.py:415
  659.9 106.2 %collective-permute-start.51 = (bf16[5024,128]{1,0:T(8,128)(2,1)}, bf16[5024,128]{1,0:T(8,128)(2,1)}, u32[]{:S(2)}, u32[]{:S(2)}) collective-permute-start(bf16[5024,128]{1,0:T(8,128)(2,1)} %get-tuple-element.352), channel_id=1, source_target_pairs={{0,8},{8,0},{16,24},{24,16},{1,9},{9,1},{17,25},{25,17},{2,10},{10... | collective-permute-start | bytes 3858440 | tf_op jit(solution)/shard_map/ppermute | solution.py:415
  661.0 106.5 %collective-permute-start.52 = (bf16[5024,128]{1,0:T(8,128)(2,1)}, bf16[5024,128]{1,0:T(8,128)(2,1)}, u32[]{:S(2)}, u32[]{:S(2)}) collective-permute-start(bf16[5024,128]{1,0:T(8,128)(2,1)} %get-tuple-element.352), channel_id=1, source_target_pairs={{0,16},{8,24},{16,0},{24,8},{1,17},{9,25},{17,1},{25,9},{2,18},{10... | collective-permute-start | bytes 3858440 | tf_op jit(solution)/shard_map/ppermute | solution.py:415
  661.9 105.6 %collective-permute-start.53 = (bf16[5024,128]{1,0:T(8,128)(2,1)}, bf16[5024,128]{1,0:T(8,128)(2,1)}, u32[]{:S(2)}, u32[]{:S(2)}) collective-permute-start(bf16[5024,128]{1,0:T(8,128)(2,1)} %get-tuple-element.352), channel_id=1, source_target_pairs={{0,24},{8,16},{16,8},{24,0},{1,25},{9,17},{17,9},{25,1},{2,26},{10... | collective-permute-start | bytes 3858440 | tf_op jit(solution)/shard_map/ppermute | solution.py:415
  665.4 59.5 %collective-permute-start.24 = (bf16[12,32,400]{2,1,0:T(8,128)(2,1)S(1)}, bf16[12,32,400]{2,1,0:T(8,128)(2,1)S(1)}, u32[]{:S(2)}, u32[]{:S(2)}) collective-permute-start(bf16[12,32,400]{2,1,0:T(8,128)(2,1)S(1)} %get-tuple-element.318), channel_id=1, source_target_pairs={{0,8},{8,0},{16,24},{24,16},{1,9},{9,1},{17,25},{25,17},{2,10},{10... | collective-permute-start | bytes 921608 | tf_op jit(solution)/shard_map/ppermute | solution.py:48
  666.3 60.8 %collective-permute-start.25 = (bf16[12,32,400]{2,1,0:T(8,128)(2,1)S(1)}, bf16[12,32,400]{2,1,0:T(8,128)(2,1)S(1)}, u32[]{:S(2)}, u32[]{:S(2)}) collective-permute-start(bf16[12,32,400]{2,1,0:T(8,128)(2,1)S(1)} %get-tuple-element.317), channel_id=1, source_target_pairs={{0,16},{8,24},{16,0},{24,8},{1,17},{9,25},{17,1},{25,9},{2,18},{10... | collective-permute-start | bytes 921608 | tf_op jit(solution)/shard_map/ppermute | solution.py:48
  752.9 154.2 %all-to-all-start.7 = ((f32[32,32,128]{2,1,0:T(8,128)}), f32[32,32,128]{2,1,0:T(8,128)S(1)}, u32[]{:S(2)}, u32[]{:S(2)}) async-start(f32[32,32,128]{2,1,0:T(8,128)} %broadcast_in_dim.138), calls=%async_computation.7 | async-start | bytes 1048576 | tf_op jit(solution)/shard_map/all_to_all | solution.py:459
  761.1 48.5 %collective-permute-start.34 = (bf16[432,128]{1,0:T(8,128)(2,1)S(1)}, bf16[432,128]{1,0:T(8,128)(2,1)S(1)}, u32[]{:S(2)}, u32[]{:S(2)}) collective-permute-start(bf16[432,128]{1,0:T(8,128)(2,1)S(1)} %fusion.42), channel_id=1, source_target_pairs={{0,2},{1,3},{2,0},{3,1},{4,6},{5,7},{6,4},{7,5},{8,10},{9,11},{10,... | collective-permute-start | bytes 331784 | tf_op jit(solution)/shard_map/ppermute | solution.py:415
  763.0 46.6 %collective-permute-start.35 = (bf16[432,128]{1,0:T(8,128)(2,1)S(1)}, bf16[432,128]{1,0:T(8,128)(2,1)S(1)}, u32[]{:S(2)}, u32[]{:S(2)}) collective-permute-start(bf16[432,128]{1,0:T(8,128)(2,1)S(1)} %fusion.42), channel_id=1, source_target_pairs={{0,4},{1,5},{2,6},{3,7},{4,0},{5,1},{6,2},{7,3},{8,12},{9,13},{10,... | collective-permute-start | bytes 331784 | tf_op jit(solution)/shard_map/ppermute | solution.py:415
  766.1 43.6 %collective-permute-start.36 = (bf16[432,128]{1,0:T(8,128)(2,1)S(1)}, bf16[432,128]{1,0:T(8,128)(2,1)S(1)}, u32[]{:S(2)}, u32[]{:S(2)}) collective-permute-start(bf16[432,128]{1,0:T(8,128)(2,1)S(1)} %fusion.42), channel_id=1, source_target_pairs={{0,6},{1,7},{2,4},{3,5},{4,2},{5,3},{6,0},{7,1},{8,14},{9,15},{10,... | collective-permute-start | bytes 331784 | tf_op jit(solution)/shard_map/ppermute | solution.py:415
  809.6 126.9 %collective-permute-start.54 = (bf16[20096,128]{1,0:T(8,128)(2,1)}, bf16[20096,128]{1,0:T(8,128)(2,1)}, u32[]{:S(2)}, u32[]{:S(2)}) collective-permute-start(bf16[20096,128]{1,0:T(8,128)(2,1)} %pad_maximum_fusion.1.own), channel_id=1, source_target_pairs={{0,1},{1,0},{2,3},{3,2},{4,5},{5,4},{6,7},{7,6},{8,9},{9,8},{10,11... | collective-permute-start | bytes 15433736 | tf_op jit(solution)/shard_map/ppermute | solution.py:415
  810.6 98.1 %collective-permute-start.37 = (bf16[1728,128]{1,0:T(8,128)(2,1)}, bf16[1728,128]{1,0:T(8,128)(2,1)}, u32[]{:S(2)}, u32[]{:S(2)}) collective-permute-start(bf16[1728,128]{1,0:T(8,128)(2,1)} %get-tuple-element.365), channel_id=1, source_target_pairs={{0,8},{8,0},{16,24},{24,16},{1,9},{9,1},{17,25},{25,17},{2,10},{10... | collective-permute-start | bytes 1327112 | tf_op jit(solution)/shard_map/ppermute | solution.py:415
  811.1 97.7 %collective-permute-start.38 = (bf16[1728,128]{1,0:T(8,128)(2,1)}, bf16[1728,128]{1,0:T(8,128)(2,1)}, u32[]{:S(2)}, u32[]{:S(2)}) collective-permute-start(bf16[1728,128]{1,0:T(8,128)(2,1)} %get-tuple-element.365), channel_id=1, source_target_pairs={{0,16},{8,24},{16,0},{24,8},{1,17},{9,25},{17,1},{25,9},{2,18},{10... | collective-permute-start | bytes 1327112 | tf_op jit(solution)/shard_map/ppermute | solution.py:415
  812.9 95.9 %collective-permute-start.39 = (bf16[1728,128]{1,0:T(8,128)(2,1)}, bf16[1728,128]{1,0:T(8,128)(2,1)}, u32[]{:S(2)}, u32[]{:S(2)}) collective-permute-start(bf16[1728,128]{1,0:T(8,128)(2,1)} %get-tuple-element.365), channel_id=1, source_target_pairs={{0,24},{8,16},{16,8},{24,0},{1,25},{9,17},{17,9},{25,1},{2,26},{10... | collective-permute-start | bytes 1327112 | tf_op jit(solution)/shard_map/ppermute | solution.py:415
  (129 other events, 1311.0 us)
Sparse Core Ops, SparseCore 0:
  9.9 35.9 all-gather.18
  47.7 49.6 all-gather.10
  99.2 61.4 all-gather.12
  162.4 68.3 all-gather.14
  232.5 29.0 all-gather.20
  263.3 32.6 all-gather.16
  739.2 161.7 all-reduce.16

commit v4 on v3

--- a/solution.py
+++ b/solution.py
@@ -386,7 +386,7 @@
     mine, theirs = own[...].astype(f32), other[...].astype(f32)
     first = core[0] == 0
     up[...] = jnp.where(first, mine, theirs)
-    down[...] = jnp.where(first, theirs, mine).T
+    down[...] = jnp.where(first, theirs, mine)
 
 
 def unpack(core, own, other, channels, hidden):
@@ -397,15 +397,9 @@
             num_scalar_prefetch=1,
             grid=(pl.cdiv(hidden, lanes),),
             in_specs=[block, block],
-            out_specs=[
-                pl.BlockSpec((channels, lanes), lambda tile, core: (0, tile)),
-                pl.BlockSpec((lanes, channels), lambda tile, core: (tile, 0)),
-            ],
+            out_specs=[pl.BlockSpec((channels, lanes), lambda tile, core: (0, tile))] * 2,
         ),
-        out_shape=[
-            jax.ShapeDtypeStruct((channels, hidden), f32),
-            jax.ShapeDtypeStruct((hidden, channels), f32),
-        ],
+        out_shape=[jax.ShapeDtypeStruct((channels, hidden), f32)] * 2,
         compiler_params=room,
         name="unpack",
     )(core, own, other)
@@ -597,28 +591,21 @@
         grad_merged.astype(f32).reshape(half_height, 2, half_breadth, 2, channels), axis=(1, 3)
     ).reshape(-1, channels)
     grad_block_low = grad_block_sum.astype(bf16)
-    grad_block_rest = (grad_block_sum - grad_block_low.astype(f32)).astype(bf16)
-    grad_merge_weight = jnp.concatenate(
-        [
-            cross_rows(coarse_low, grad_block_low) + cross_rows(coarse_low, grad_block_rest),
-            cross_rows(skip_rows, grad_merged),
-        ],
-        axis=0,
-    )
-    grad_branch, normed, active, grad_hidden = decode_grads[2]
-    decode_parts = [cross_rows(normed, grad_hidden), cross_rows(active, grad_branch), grad_merge_weight]
-    decode_sums = lax.psum([part.astype(bf16) for part in decode_parts], both)
-    decode_up_sum, decode_down_sum, merge_sum = [total.astype(f32) for total in decode_sums]
-
-    grad_coarse = by_transpose(grad_block_low, merge_upper) + by_transpose(grad_block_rest, merge_upper)
+    grad_merge_upper = cross_rows(grad_block_low, coarse_low)
+    grad_merge_lower = cross_rows(grad_merged, skip_rows)
+    grad_coarse = by_transpose(grad_block_low, merge_upper)
     grad_skip_direct = by_transpose(grad_merged, merge_lower)
     grad_wide, widen_sums, bottle_grads, bottle_small = block_backward(
         grad_coarse, bottle, sea_coarse, coarse_stored, dates
     )
+    early = [grad_merge_upper, grad_merge_lower]
+    for grad_branch, normed, active, grad_hidden in (decode_grads[2], bottle_grads[2]):
+        early += [cross_rows(normed, grad_hidden), cross_rows(grad_branch, active)]
+    early = lax.psum([part.astype(bf16) for part in early], both)
+    early = [total.astype(f32) for total in early]
+    merge_sum = jnp.concatenate(early[:2], axis=1).T
+    decode_up_sum, decode_down_sum, bottle_up_sum, bottle_down_sum = early[2], early[3].T, early[4], early[5].T
     core = (lax.axis_index("lon") % 2).astype(jnp.int32)[None]
-    bottle_pair = weight_grads(*bottle_grads[2]).reshape(2, -1, lanes)
-    bottle_up_sum, bottle_down_sum = unpack(core, *sum_group(bottle_pair), wide, bottle_up.shape[1])
-
     grad_widen = cross_rows(pooled, grad_wide).astype(bf16)
     widen_tiles = pl.cdiv(wide, 2 * lanes)
     grad_widen = jnp.pad(grad_widen, ((0, 0), (0, 2 * widen_tiles * lanes - wide)))
@@ -632,6 +619,7 @@
     encode_pair = weight_grads(*encode_grads[2]).reshape(2, -1, lanes)
     own, other = sum_group(jnp.concatenate([encode_pair, grad_widen], axis=1))
     encode_up_sum, encode_down_sum = unpack(core, own, other, channels, encode_up.shape[1])
+    encode_down_sum = encode_down_sum.T
     start = encode_pair.shape[1]
     lower = jnp.where(core == 0, own[start : start + grad_widen.shape[1]], other[start : start + grad_widen.shape[1]])
     upper = jnp.where(core == 0, other[start : start + grad_widen.shape[1]], own[start : start + grad_widen.shape[1]])

time: 985 us -> 752 us (0.76)
  waiting for transfers between devices: 304 us -> 183 us
  other arithmetic: 108 us -> 69.2 us
  starting transfers between devices: 134 us -> 95.6 us
  Pallas kernels: 239 us -> 209 us
  local copies, waits for them, and re-layouts: 112 us -> 96 us
  matrix products: 30.1 us -> 42.2 us
    ppermute x6, waiting for transfers between devices: 57.1 us -> 0.02 us  [from_dates(): lax.ppermute(lax.dynamic_index_in_dim(tiles, own ^ step, 0, keepdims=Fals...]
    psum x1, waiting for transfers between devices: 85.3 us -> 31.8 us  [shards(): early = lax.psum([part.astype(bf16) for part in early], both)]
    ppermute x28 -> x14, starting transfers between devices: 65.9 us -> 20.6 us  [swap(): lax.ppermute(array, axis, [(i, i ^ step) for i in range(lax.axis_size(axi...]
    concatenate x2 -> x1, other arithmetic: 38.8 us -> 0.12 us  [exchange_all(): jnp.concatenate([take(got, own ^ place) for place in range(count)], axis=0)]
    pallas_call x2 -> x1, Pallas kernels: 29.1 us -> 8.99 us  [unpack(): pl.pallas_call(unpack_kernel, grid_spec=pltpu.PrefetchScalarGridSpec(num_...]
    ppermute x28 -> x14, waiting for transfers between devices: 70.1 us -> 52.7 us  [swap(): lax.ppermute(array, axis, [(i, i ^ step) for i in range(lax.axis_size(axi...]
    unnamed x244 -> x250, local copies, waits for them, and re-layouts: 36.1 us -> 20.6 us
    dot_general x6 -> x7, matrix products: 16.7 us -> 28.3 us  [cross_rows(): lax.dot_general(former, latter, (((0,), (0,)), ((), ())), preferred_eleme...]
  transfers between devices with their start and end apart: 70 -> 56, of which waited for: 18 -> 18; matrix products, arithmetic and copies ran while one was open for 23% -> 23% of each run, Pallas kernels for 17% -> 21%
where the time goes in v4:
time: 752 us; the launch traced here: 743 us
  Pallas kernels  209 us (28%)
  waiting for transfers between devices  183 us (24%)
  local copies, waits for them, and re-layouts  96 us (13%)
  starting transfers between devices  95.6 us (13%)
  other arithmetic  69.2 us (9%)
  matrix products  42.2 us (6%)
  blocking collectives  31.9 us (4%)
  between operations  16.3 us (2%)
    ppermute x14, waiting for transfers between devices, swap(): lax.ppermute(array, axis, [(i, i ^ step) for i in range(lax.axis_size(axi...  52.7 us
    pallas_call x3, Pallas kernels, stencil_backward(): pl.pallas_call(functools.partial(stencil_backward_kernel, len(edges)), gr...  39.2 us
    pallas_call x3, Pallas kernels, mlp_forward(): pl.pallas_call(functools.partial(mlp_forward_kernel, 512), grid=(pixels /...  38.8 us
    pallas_call x3, Pallas kernels, stencil_forward(): pl.pallas_call(functools.partial(stencil_forward_kernel, len(edges)), gri...  38.6 us
    pallas_call x3, Pallas kernels, mlp_backward(): pl.pallas_call(functools.partial(mlp_backward_kernel, 512), grid=(pixels...  38.1 us
    all_to_all x6, waiting for transfers between devices, sum_all(): return jnp.sum(lax.all_to_all(copies, both, 0, 0, tiled=False), axis=0)  36.8 us
    pallas_call x3, Pallas kernels, kernel_grad(): pl.pallas_call(functools.partial(kernel_grad_kernel, len(edges)), grid=(t...  33.1 us
    all_gather x2, blocking collectives, shards(): lax.all_gather(weight, 'lat', axis=0, tiled=True)  31.9 us
  transfers between devices with their start and end apart: 56, of which 18 were waited for; matrix products, arithmetic and copies ran while one was open for 23% of the time, Pallas kernels for 21%

profile of v4, /device:TPU:0, one launch (start us, length us, event | category | flops | bytes accessed | tf_op | source)
XLA Modules:
  0.0 742.9 jit_solution(153481587802519199)
XLA Ops:
  22.2 14.8 %all-gather.2 = bf16[4,100,800]{2,1,0:T(8,128)(2,1)S(1)} all-gather(bf16[1,100,800]{2,1,0:T(8,128)(2,1)S(1)} %bitcast.334), channel_id=1, replica_groups=mesh['lat'=4,'lon'=8] {'lat'}, dimensions={0}, use_global_device_ids=true | all-gather | bytes 800000 | tf_op jit(solution)/shard_map/all_gather | solution.py:543
  48.4 17.0 %all-gather.1 = bf16[4,300,400]{1,2,0:T(8,128)(2,1)S(1)} all-gather(bf16[1,300,400]{1,2,0:T(8,128)(2,1)S(1)} %bitcast.333), channel_id=1, replica_groups=mesh['lat'=4,'lon'=8] {'lat'}, dimensions={0}, use_global_device_ids=true | all-gather | bytes 1200000 | tf_op jit(solution)/shard_map/all_gather | solution.py:543
  80.6 11.5 %collective-permute-done.2 = bf16[12,32,400]{2,1,0:T(8,128)(2,1)S(1)} collective-permute-done((bf16[12,32,400]{2,1,0:T(8,128)(2,1)S(1)}, bf16[12,32,400]{2,1,0:T(8,128)(2,1)S(1)}, u32[]{:S(2)}, u32[]{:S(2)}) %collective-permute-start.2) | collective-permute-done | bytes 307232 | tf_op jit(solution)/shard_map/ppermute | solution.py:30
  102.2 15.0 %stencil_forward.3 = (f32[48,32,400]{2,1,0:T(8,128)}, f32[2,400]{1,0:T(2,128)}) custom-call(bf16[48,32,400]{2,1,0:T(8,128)(2,1)} %copy-done.2, bf16[48,3,400]{2,1,0:T(4,128)(2,1)} %copy-done.33, bf16[48,3,400]{2,1,0:T(4,128)(2,1)} %copy-done.34, f32[49,400]{1,0:T(8,128)} %reshape.329.refs_2_, f32[48,32,128]{2,1,0:T(8,128)} %broadcast_in_dim.115.refs_3_), custom_call_target="tpu_custom_call" | custom-call | tf_op jit(solution)/shard_map/stencil_forward/pallas_call | solution.py:188
  119.4 4.6 all-to-all-start
  124.8 9.5 %all-to-all-done = f32[32,3,400]{2,1,0:T(4,128)S(1)} async-done(((f32[32,3,400]{2,1,0:T(4,128)}), f32[32,3,400]{2,1,0:T(4,128)S(1)}, u32[]{:S(2)}, u32[]{:S(2)}) %all-to-all-start) | async-done | bytes 153632 | tf_op jit(solution)/shard_map/all_to_all | solution.py:77
  139.3 12.6 %mlp_forward.3 = (bf16[1536,400]{1,0:T(8,128)(2,1)}, bf16[1536,1600]{1,0:T(8,128)(2,1)}, bf16[1536,1600]{1,0:T(8,128)(2,1)}, bf16[1536,400]{1,0:T(8,128)(2,1)}) custom-call(f32[1536,400]{1,0:T(8,128)} %bitcast.268, bf16[1536,400]{1,0:T(8,128)(2,1)} %bitcast.267, f32[1536,128]{1,0:T(8,128)} %broadcast_in_dim.116.sea, f32[4,400]{1,0:T(4,128)} %pad_maximum_fusion.17.scales, ...), custom_call_target="tpu_custom_call" | custom-call | tf_op jit(solution)/shard_map/mlp_forward/pallas_call | solution.py:319
  155.3 3.8 reduce_sum.104
  170.6 8.5 %stencil_forward.4 = (f32[24,16,800]{2,1,0:T(8,128)}, f32[2,800]{1,0:T(2,128)}) custom-call(bf16[24,16,800]{2,1,0:T(8,128)(2,1)} %bitcast.288, bf16[24,3,800]{2,1,0:T(4,128)(2,1)} %copy-done.40, bf16[24,3,800]{2,1,0:T(4,128)(2,1)} %copy-done.41, f32[49,800]{1,0:T(8,128)} %reshape.335.refs_2_, f32[24,16,128]{2,1,0:T(8,128)} %broadcast_in_dim.122.refs_3_), custom_call_target="tpu_custom_call" | custom-call | tf_op jit(solution)/shard_map/stencil_forward/pallas_call | solution.py:188
  187.4 12.5 %all-to-all-done.1 = f32[32,3,800]{2,1,0:T(4,128)S(1)} async-done(((f32[32,3,800]{2,1,0:T(4,128)}), f32[32,3,800]{2,1,0:T(4,128)S(1)}, u32[]{:S(2)}, u32[]{:S(2)}) %all-to-all-start.1) | async-done | bytes 307232 | tf_op jit(solution)/shard_map/all_to_all | solution.py:77
  200.6 30.4 %all-gather.15.cloned.1.call-done.down = bf16[3200,800]{1,0:T(8,128)(2,1)} async-done(((bf16[800,800]{1,0:T(8,128)(2,1)}), bf16[3200,800]{1,0:T(8,128)(2,1)}) %all-gather.15.cloned.1.call-update) | async-done | bytes 5120016 | tf_op jit(solution)/shard_map/all_gather | solution.py:543
  231.8 13.5 %mlp_forward.4 = (bf16[384,800]{1,0:T(8,128)(2,1)}, bf16[384,3200]{1,0:T(8,128)(2,1)}, bf16[384,3200]{1,0:T(8,128)(2,1)}, bf16[384,800]{1,0:T(8,128)(2,1)}) custom-call(f32[384,800]{1,0:T(8,128)} %bitcast.280, bf16[384,800]{1,0:T(8,128)(2,1)} %copy-done.13, f32[384,128]{1,0:T(8,128)} %broadcast_in_dim.124.sea, f32[4,800]{1,0:T(4,128)} %pad_maximum_fusion.16.scales, ...), custom_call_target="tpu_custom_call" | custom-call | tf_op jit(solution)/shard_map/mlp_forward/pallas_call | solution.py:319
  255.5 4.9 add_convert_fusion
  261.5 3.7 collective-permute-start.11
  269.9 15.1 %stencil_forward.5 = (f32[48,32,400]{2,1,0:T(8,128)}, f32[2,400]{1,0:T(2,128)}) custom-call(bf16[48,32,400]{2,1,0:T(8,128)(2,1)} %copy-done.6, bf16[48,3,400]{2,1,0:T(4,128)(2,1)} %copy-done.35, bf16[48,3,400]{2,1,0:T(4,128)(2,1)} %copy-done.36, f32[49,400]{1,0:T(8,128)} %reshape.340.refs_2_, f32[48,32,128]{2,1,0:T(8,128)} %broadcast_in_dim.115.refs_3_), custom_call_target="tpu_custom_call" | custom-call | tf_op jit(solution)/shard_map/stencil_forward/pallas_call | solution.py:188
  287.0 4.2 all-to-all-start.2
  295.8 5.7 all-to-all-done.2
  302.3 12.6 %mlp_forward.5 = (bf16[1536,400]{1,0:T(8,128)(2,1)}, bf16[1536,1600]{1,0:T(8,128)(2,1)}, bf16[1536,1600]{1,0:T(8,128)(2,1)}, bf16[1536,400]{1,0:T(8,128)(2,1)}) custom-call(f32[1536,400]{1,0:T(8,128)} %bitcast.270, bf16[1536,400]{1,0:T(8,128)(2,1)} %get-tuple-element.224.source, f32[1536,128]{1,0:T(8,128)} %broadcast_in_dim.116.sea, ...), custom_call_target="tpu_custom_call" | custom-call | tf_op jit(solution)/shard_map/mlp_forward/pallas_call | solution.py:319
  314.9 12.0 %mlp_backward.3 = (bf16[1536,400]{1,0:T(8,128)(2,1)}, bf16[1536,1600]{1,0:T(8,128)(2,1)}, f32[1536,400]{1,0:T(8,128)}, f32[2,400]{1,0:T(2,128)}, f32[1,400]{1,0:T(1,128)}, /*index=5*/f32[1,1600]{1,0:T(1,128)}) custom-call(bf16[1536,400]{1,0:T(8,128)(2,1)} %bitcast.278, f32[1536,400]{1,0:T(8,128)} %bitcast.271, bf16[1536,1600]{1,0:T(8,128)(2,1)} %get-tuple-element.79.slope, ...), custom_call_target="tpu_custom_call" | custom-call | tf_op jit(solution)/shard_map/mlp_backward/pallas_call | solution.py:336
  335.3 6.6 convolution_convert_fusion.3
  349.3 3.9 collective-permute-start.19
  353.2 12.6 %kernel_grad.5 = f32[4,56,128]{2,1,0:T(8,128)} custom-call(bf16[48,32,400]{2,1,0:T(8,128)(2,1)} %copy-done.6, bf16[48,3,400]{2,1,0:T(4,128)(2,1)} %copy-done.35, bf16[48,3,400]{2,1,0:T(4,128)(2,1)} %copy-done.36, bf16[48,32,400]{2,1,0:T(8,128)(2,1)} %bitcast.273), custom_call_target="tpu_custom_call" | custom-call | tf_op jit(solution)/shard_map/kernel_grad/pallas_call | solution.py:220
  368.6 15.0 %stencil_backward.3 = (bf16[48,32,400]{2,1,0:T(8,128)(2,1)}, f32[1,400]{1,0:T(1,128)}) custom-call(bf16[48,32,400]{2,1,0:T(8,128)(2,1)} %bitcast.274, bf16[48,3,400]{2,1,0:T(4,128)(2,1)} %copy-done.49, bf16[48,3,400]{2,1,0:T(4,128)(2,1)} %copy-done.50, f32[49,400]{1,0:T(8,128)} %reshape.340.refs_2_, f32[48,32,128]{2,1,0:T(8,128)} %broadcast_in_dim.115.refs_3_, ...), custom_call_target="tpu_custom_call" | custom-call | tf_op jit(solution)/shard_map/stencil_backward/pallas_call | solution.py:204
  393.8 12.9 %mlp_backward.4 = (bf16[384,800]{1,0:T(8,128)(2,1)}, bf16[384,3200]{1,0:T(8,128)(2,1)}, f32[384,800]{1,0:T(8,128)}, f32[2,800]{1,0:T(2,128)}, f32[1,800]{1,0:T(1,128)}, /*index=5*/f32[1,3200]{1,0:T(1,128)}) custom-call(f32[384,800]{1,0:T(8,128)} %fusion.22.upstream, f32[384,800]{1,0:T(8,128)} %bitcast.281, bf16[384,3200]{1,0:T(8,128)(2,1)} %get-tuple-element.83.slope, ...), custom_call_target="tpu_custom_call" | custom-call | tf_op jit(solution)/shard_map/mlp_backward/pallas_call | solution.py:336
  408.1 4.0 all-to-all-start.4
  412.4 7.1 convolution_convert_fusion.1
  419.5 5.3 fusion.2
  432.8 7.7 %kernel_grad.4 = f32[7,56,128]{2,1,0:T(8,128)} custom-call(bf16[24,16,800]{2,1,0:T(8,128)(2,1)} %bitcast.289, bf16[24,3,800]{2,1,0:T(4,128)(2,1)} %copy-done.40, bf16[24,3,800]{2,1,0:T(4,128)(2,1)} %copy-done.41, bf16[24,16,800]{2,1,0:T(8,128)(2,1)} %bitcast.285), custom_call_target="tpu_custom_call" | custom-call | tf_op jit(solution)/shard_map/kernel_grad/pallas_call | solution.py:220
  441.1 8.8 %stencil_backward.4 = (bf16[24,16,800]{2,1,0:T(8,128)(2,1)}, f32[1,800]{1,0:T(1,128)}) custom-call(bf16[24,16,800]{2,1,0:T(8,128)(2,1)} %bitcast.286, bf16[24,3,800]{2,1,0:T(4,128)(2,1)} %copy-done.52, bf16[24,3,800]{2,1,0:T(4,128)(2,1)} %copy-done.53, f32[49,800]{1,0:T(8,128)} %reshape.335.refs_2_, f32[24,16,128]{2,1,0:T(8,128)} %broadcast_in_dim.122.refs_3_, ...), custom_call_target="tpu_custom_call" | custom-call | tf_op jit(solution)/shard_map/stencil_backward/pallas_call | solution.py:204
  459.1 3.7 reshape.303.upstream
  467.0 13.2 %mlp_backward.5 = (bf16[1536,400]{1,0:T(8,128)(2,1)}, bf16[1536,1600]{1,0:T(8,128)(2,1)}, f32[1536,400]{1,0:T(8,128)}, f32[2,400]{1,0:T(2,128)}, f32[1,400]{1,0:T(1,128)}, /*index=5*/f32[1,1600]{1,0:T(1,128)}) custom-call(f32[1536,400]{1,0:T(8,128)} %reshape.303.upstream, f32[1536,400]{1,0:T(8,128)} %bitcast.269, ...), custom_call_target="tpu_custom_call" | custom-call | tf_op jit(solution)/shard_map/mlp_backward/pallas_call | solution.py:336
  480.2 11.9 %weight_grads.1 = bf16[2,13,400,128]{3,2,1,0:T(8,128)(2,1)} custom-call(bf16[1536,400]{1,0:T(8,128)(2,1)} %get-tuple-element.99.grad_branch, bf16[1536,400]{1,0:T(8,128)(2,1)} %get-tuple-element.100.normed, bf16[1536,1600]{1,0:T(8,128)(2,1)} %get-tuple-element.101.active, bf16[1536,1600]{1,0:T(8,128)(2,1)} %get-tuple-element.102.grad_hidden), custom_call_target="tpu_custom_call" | custom-call | tf_op jit(solution)/shard_map/weight_grads/pallas_call | solution.py:372
  497.1 4.4 all-to-all-start.5
  501.8 9.1 %all-to-all-done.5 = f32[32,2,400]{2,1,0:T(2,128)S(1)} async-done(((f32[32,2,400]{2,1,0:T(2,128)}), f32[32,2,400]{2,1,0:T(2,128)S(1)}, u32[]{:S(2)}, u32[]{:S(2)}) %all-to-all-start.5) | async-done | bytes 102432 | tf_op jit(solution)/shard_map/all_to_all | solution.py:77
  511.0 4.2 multiply_convert_fusion
  515.3 12.9 %kernel_grad.3 = f32[4,56,128]{2,1,0:T(8,128)} custom-call(bf16[48,32,400]{2,1,0:T(8,128)(2,1)} %copy-done.2, bf16[48,3,400]{2,1,0:T(4,128)(2,1)} %copy-done.33, bf16[48,3,400]{2,1,0:T(4,128)(2,1)} %copy-done.34, bf16[48,32,400]{2,1,0:T(8,128)(2,1)} %bitcast.275), custom_call_target="tpu_custom_call" | custom-call | tf_op jit(solution)/shard_map/kernel_grad/pallas_call | solution.py:220
  548.9 8.3 %collective-permute-done.22.refs_0_ = bf16[48,3,400]{2,1,0:T(4,128)(2,1)} collective-permute-done((bf16[48,3,400]{2,1,0:T(4,128)(2,1)}, bf16[48,3,400]{2,1,0:T(4,128)(2,1)}, u32[]{:S(2)}, u32[]{:S(2)}) %collective-permute-start.22) | collective-permute-done | bytes 115232 | tf_op jit(solution)/shard_map/ppermute | solution.py:62
  557.2 15.4 %stencil_backward.5 = (bf16[48,32,400]{2,1,0:T(8,128)(2,1)}, f32[1,400]{1,0:T(1,128)}) custom-call(bf16[48,32,400]{2,1,0:T(8,128)(2,1)} %bitcast.277, bf16[48,3,400]{2,1,0:T(4,128)(2,1)} %collective-permute-done.22.refs_0_, bf16[48,3,400]{2,1,0:T(4,128)(2,1)} %collective-permute-done.23.refs_1_, f32[49,400]{1,0:T(8,128)} %reshape.329.refs_2_, ...), custom_call_target="tpu_custom_call" | custom-call | tf_op jit(solution)/shard_map/stencil_backward/pallas_call | solution.py:204
  587.4 5.7 all-to-all-start.7
  596.2 5.2 collective-permute-start.34
  610.0 18.3 %collective-permute-done.35 = bf16[432,128]{1,0:T(8,128)(2,1)S(1)} collective-permute-done((bf16[432,128]{1,0:T(8,128)(2,1)S(1)}, bf16[432,128]{1,0:T(8,128)(2,1)S(1)}, u32[]{:S(2)}, u32[]{:S(2)}) %collective-permute-start.35) | collective-permute-done | bytes 110624 | tf_op jit(solution)/shard_map/ppermute | solution.py:409
  636.1 6.8 collective-permute-done.37
  642.9 7.1 collective-permute-done.38
  650.1 14.8 %collective-permute-done.39 = bf16[1728,128]{1,0:T(8,128)(2,1)S(1)} collective-permute-done((bf16[1728,128]{1,0:T(8,128)(2,1)}, bf16[1728,128]{1,0:T(8,128)(2,1)S(1)}, u32[]{:S(2)}, u32[]{:S(2)}) %collective-permute-start.39) | collective-permute-done | bytes 442400 | tf_op jit(solution)/shard_map/ppermute | solution.py:409
  676.6 9.0 %unpack.1 = (f32[400,1600]{1,0:T(8,128)}, f32[400,1600]{1,0:T(8,128)}) custom-call(s32[1]{0:T(128)} %bitcast.90.core, bf16[6912,128]{1,0:T(8,128)(2,1)} %copy-done.15, bf16[6912,128]{1,0:T(8,128)(2,1)} %collective-permute-done.40.other), custom_call_target="tpu_custom_call" | custom-call | tf_op jit(solution)/shard_map/unpack/pallas_call | solution.py:394
  686.7 31.8 %all-reduce.16.cloned.1.call-done = (bf16[800,3200]{1,0:T(8,128)(2,1)}, bf16[3200,800]{0,1:T(8,128)(2,1)}, bf16[400,400]{1,0:T(8,128)(2,1)}, bf16[400,800]{1,0:T...) async-done(((bf16[800,3200]{1,0:T(8,128)(2,1)}, bf16[3200,800]{0,1:T(8,128)(2,1)}, bf16[400,400]{1,0:T(8,128)(2,1)}, bf16[400,800]{1,0:T(8,128)(2,1)}, ...) | async-done | bytes 13760016 | tf_op jit(solution)/shard_map/psum | solution.py:604
  718.6 7.3 convert_element_type.218
  725.9 4.7 transpose.77
  (502 shorter events, 237.0 us)
Async XLA Ops:
  7.2 128.4 %all-gather.19.cloned.1.call-start = ((), (), s32[]{:S(2)}) async-start(), calls=%async_computation.12 | async-start | bytes 1730560 | tf_op jit(solution)/shard_map/all_gather | solution.py:543
  7.9 130.2 %all-gather.11.cloned.1.call-start = ((), (), s32[]{:S(2)}) async-start(), calls=%async_computation.8 | async-start | bytes 2048000 | tf_op jit(solution)/shard_map/all_gather | solution.py:543
  8.7 191.9 %all-gather.13.cloned.1.call-start = ((), (), s32[]{:S(2)}) async-start(), calls=%async_computation.9 | async-start | bytes 6400000 | tf_op jit(solution)/shard_map/all_gather | solution.py:543
  9.4 221.6 %all-gather.15.cloned.1.call-start = ((), (), s32[]{:S(2)}) async-start(), calls=%async_computation.10 | async-start | bytes 7168000 | tf_op jit(solution)/shard_map/all_gather | solution.py:543
  10.0 282.7 %all-gather.21.cloned.1.call-start = ((), (), s32[]{:S(2)}) async-start(), calls=%async_computation.13 | async-start | bytes 1730560 | tf_op jit(solution)/shard_map/all_gather | solution.py:543
  10.6 291.7 %all-gather.17.cloned.1.call-start = ((), (), s32[]{:S(2)}) async-start(), calls=%async_computation.11 | async-start | bytes 2048000 | tf_op jit(solution)/shard_map/all_gather | solution.py:543
  11.8 67.3 %collective-permute-start = (bf16[12,32,400]{2,1,0:T(8,128)(2,1)}, bf16[12,32,400]{2,1,0:T(8,128)(2,1)S(1)}, u32[]{:S(2)}, u32[]{:S(2)}) collective-permute-start(bf16[12,32,400]{2,1,0:T(8,128)(2,1)} %get-tuple-element.176), channel_id=1, source_target_pairs={{0,8},{8,0},{16,24},{24,16},{1,9},{9,1},{17,25},{25,17},{2,10},{10... | collective-permute-start | bytes 921608 | tf_op jit(solution)/shard_map/ppermute | solution.py:30
  14.7 65.9 %collective-permute-start.1 = (bf16[12,32,400]{2,1,0:T(8,128)(2,1)}, bf16[12,32,400]{2,1,0:T(8,128)(2,1)}, u32[]{:S(2)}, u32[]{:S(2)}) collective-permute-start(bf16[12,32,400]{2,1,0:T(8,128)(2,1)} %get-tuple-element.178), channel_id=1, source_target_pairs={{0,16},{8,24},{16,0},{24,8},{1,17},{9,25},{17,1},{25,9},{2,18},{10... | collective-permute-start | bytes 921608 | tf_op jit(solution)/shard_map/ppermute | solution.py:30
  16.9 56.1 %collective-permute-start.5 = (s32[12,32]{1,0:T(8,128)}, s32[12,32]{1,0:T(8,128)}, u32[]{:S(2)}, u32[]{:S(2)}) collective-permute-start(s32[12,32]{1,0:T(8,128)} %bitcast.263), channel_id=1, source_target_pairs={{0,8},{8,0},{16,24},{24,16},{1,9},{9,1},{17,25},{25,17},{2,10},{10... | collective-permute-start | bytes 4616 | tf_op jit(solution)/shard_map/ppermute | solution.py:30
  18.0 56.4 %collective-permute-start.6 = (s32[12,32]{1,0:T(8,128)}, s32[12,32]{1,0:T(8,128)}, u32[]{:S(2)}, u32[]{:S(2)}) collective-permute-start(s32[12,32]{1,0:T(8,128)} %bitcast.262), channel_id=1, source_target_pairs={{0,16},{8,24},{16,0},{24,8},{1,17},{9,25},{17,1},{25,9},{2,18},{10... | collective-permute-start | bytes 4616 | tf_op jit(solution)/shard_map/ppermute | solution.py:30
  18.0 58.0 %collective-permute-start.7 = (s32[12,32]{1,0:T(8,128)S(1)}, s32[12,32]{1,0:T(8,128)}, u32[]{:S(2)}, u32[]{:S(2)}) collective-permute-start(s32[12,32]{1,0:T(8,128)S(1)} %bitcast.347), channel_id=1, source_target_pairs={{0,24},{8,16},{16,8},{24,0},{1,25},{9,17},{17,9},{25,1},{2,26},{10... | collective-permute-start | bytes 4616 | tf_op jit(solution)/shard_map/ppermute | solution.py:30
  73.0 19.1 %collective-permute-start.2 = (bf16[12,32,400]{2,1,0:T(8,128)(2,1)S(1)}, bf16[12,32,400]{2,1,0:T(8,128)(2,1)S(1)}, u32[]{:S(2)}, u32[]{:S(2)}) collective-permute-start(bf16[12,32,400]{2,1,0:T(8,128)(2,1)S(1)} %copy-done.47), channel_id=1, source_target_pairs={{0,24},{8,16},{16,8},{24,0},{1,25},{9,17},{17,9},{25,1},{2,26},{10... | collective-permute-start | bytes 921608 | tf_op jit(solution)/shard_map/ppermute | solution.py:30
  74.4 190.8 %collective-permute-start.15 = (bf16[12,32,400]{2,1,0:T(8,128)(2,1)}, bf16[12,32,400]{2,1,0:T(8,128)(2,1)}, u32[]{:S(2)}, u32[]{:S(2)}) collective-permute-start(bf16[12,32,400]{2,1,0:T(8,128)(2,1)} %get-tuple-element.156), channel_id=1, source_target_pairs={{0,8},{8,0},{16,24},{24,16},{1,9},{9,1},{17,25},{25,17},{2,10},{10... | collective-permute-start | bytes 921608 | tf_op jit(solution)/shard_map/ppermute | solution.py:30
  76.0 189.2 %collective-permute-start.16 = (bf16[12,32,400]{2,1,0:T(8,128)(2,1)}, bf16[12,32,400]{2,1,0:T(8,128)(2,1)}, u32[]{:S(2)}, u32[]{:S(2)}) collective-permute-start(bf16[12,32,400]{2,1,0:T(8,128)(2,1)} %get-tuple-element.158), channel_id=1, source_target_pairs={{0,16},{8,24},{16,0},{24,8},{1,17},{9,25},{17,1},{25,9},{2,18},{10... | collective-permute-start | bytes 921608 | tf_op jit(solution)/shard_map/ppermute | solution.py:30
  79.1 186.1 %collective-permute-start.17 = (bf16[12,32,400]{2,1,0:T(8,128)(2,1)}, bf16[12,32,400]{2,1,0:T(8,128)(2,1)}, u32[]{:S(2)}, u32[]{:S(2)}) collective-permute-start(bf16[12,32,400]{2,1,0:T(8,128)(2,1)} %get-tuple-element.157), channel_id=1, source_target_pairs={{0,24},{8,16},{16,8},{24,0},{1,25},{9,17},{17,9},{25,1},{2,26},{10... | collective-permute-start | bytes 921608 | tf_op jit(solution)/shard_map/ppermute | solution.py:30
  119.4 15.0 %all-to-all-start = ((f32[32,3,400]{2,1,0:T(4,128)}), f32[32,3,400]{2,1,0:T(4,128)S(1)}, u32[]{:S(2)}, u32[]{:S(2)}) async-start(f32[32,3,400]{2,1,0:T(4,128)} %broadcast_in_dim.117), calls=%async_computation | async-start | bytes 524288 | tf_op jit(solution)/shard_map/all_to_all | solution.py:77
  181.3 18.5 %all-to-all-start.1 = ((f32[32,3,800]{2,1,0:T(4,128)}), f32[32,3,800]{2,1,0:T(4,128)S(1)}, u32[]{:S(2)}, u32[]{:S(2)}) async-start(f32[32,3,800]{2,1,0:T(4,128)} %broadcast_in_dim.125), calls=%async_computation.1 | async-start | bytes 917504 | tf_op jit(solution)/shard_map/all_to_all | solution.py:77
  287.0 14.6 %all-to-all-start.2 = ((f32[32,3,400]{2,1,0:T(4,128)}), f32[32,3,400]{2,1,0:T(4,128)S(1)}, u32[]{:S(2)}, u32[]{:S(2)}) async-start(f32[32,3,400]{2,1,0:T(4,128)} %broadcast_in_dim.130), calls=%async_computation.2 | async-start | bytes 524288 | tf_op jit(solution)/shard_map/all_to_all | solution.py:77
  328.3 17.2 %all-to-all-start.3 = ((f32[32,2,400]{2,1,0:T(2,128)}), f32[32,2,400]{2,1,0:T(2,128)S(1)}, u32[]{:S(2)}, u32[]{:S(2)}) async-start(f32[32,2,400]{2,1,0:T(2,128)} %broadcast_in_dim.135), calls=%async_computation.3 | async-start | bytes 262144 | tf_op jit(solution)/shard_map/all_to_all | solution.py:77
  331.8 34.0 %collective-permute-start.12 = (bf16[12,32,400]{2,1,0:T(8,128)(2,1)}, bf16[12,32,400]{2,1,0:T(8,128)(2,1)S(1)}, u32[]{:S(2)}, u32[]{:S(2)}) collective-permute-start(bf16[12,32,400]{2,1,0:T(8,128)(2,1)} %get-tuple-element.166), channel_id=1, source_target_pairs={{0,8},{8,0},{16,24},{24,16},{1,9},{9,1},{17,25},{25,17},{2,10},{10... | collective-permute-start | bytes 921608 | tf_op jit(solution)/shard_map/ppermute | solution.py:48
  333.6 32.3 %collective-permute-start.13 = (bf16[12,32,400]{2,1,0:T(8,128)(2,1)S(1)}, bf16[12,32,400]{2,1,0:T(8,128)(2,1)S(1)}, u32[]{:S(2)}, u32[]{:S(2)}) collective-permute-start(bf16[12,32,400]{2,1,0:T(8,128)(2,1)S(1)} %get-tuple-element.165), channel_id=1, source_target_pairs={{0,16},{8,24},{16,0},{24,8},{1,17},{9,25},{17,1},{25,9},{2,18},{10... | collective-permute-start | bytes 921608 | tf_op jit(solution)/shard_map/ppermute | solution.py:48
  335.0 30.8 %collective-permute-start.14 = (bf16[12,32,400]{2,1,0:T(8,128)(2,1)S(1)}, bf16[12,32,400]{2,1,0:T(8,128)(2,1)S(1)}, u32[]{:S(2)}, u32[]{:S(2)}) collective-permute-start(bf16[12,32,400]{2,1,0:T(8,128)(2,1)S(1)} %get-tuple-element.164), channel_id=1, source_target_pairs={{0,24},{8,16},{16,8},{24,0},{1,25},{9,17},{17,9},{25,1},{2,26},{10... | collective-permute-start | bytes 921608 | tf_op jit(solution)/shard_map/ppermute | solution.py:48
  349.2 18.0 %collective-permute-start.18 = (bf16[48,3,400]{2,1,0:T(4,128)(2,1)S(1)}, bf16[48,3,400]{2,1,0:T(4,128)(2,1)S(1)}, u32[]{:S(2)}, u32[]{:S(2)}) collective-permute-start(bf16[48,3,400]{2,1,0:T(4,128)(2,1)S(1)} %get-tuple-element.150), channel_id=1, source_target_pairs={{0,1},{1,2},{2,3},{3,4},{4,5},{5,6},{6,7},{7,0},{8,9},{9,10},{10,1... | collective-permute-start | bytes 345608 | tf_op jit(solution)/shard_map/ppermute | solution.py:62
  349.3 18.0 %collective-permute-start.19 = (bf16[48,3,400]{2,1,0:T(4,128)(2,1)S(1)}, bf16[48,3,400]{2,1,0:T(4,128)(2,1)S(1)}, u32[]{:S(2)}, u32[]{:S(2)}) collective-permute-start(bf16[48,3,400]{2,1,0:T(4,128)(2,1)S(1)} %get-tuple-element.149), channel_id=1, source_target_pairs={{1,0},{2,1},{3,2},{4,3},{5,4},{6,5},{7,6},{0,7},{9,8},{10,9},{11,1... | collective-permute-start | bytes 345608 | tf_op jit(solution)/shard_map/ppermute | solution.py:63
  408.1 16.7 %all-to-all-start.4 = ((f32[32,2,800]{2,1,0:T(2,128)}), f32[32,2,800]{2,1,0:T(2,128)S(1)}, u32[]{:S(2)}, u32[]{:S(2)}) async-start(f32[32,2,800]{2,1,0:T(2,128)} %broadcast_in_dim.136), calls=%async_computation.4 | async-start | bytes 458752 | tf_op jit(solution)/shard_map/all_to_all | solution.py:77
  412.2 306.4 %all-reduce.16.cloned.1.call-start = ((), (), s32[]{:S(2)}) async-start(), calls=%async_computation.14 | async-start | bytes 28057600 | tf_op jit(solution)/shard_map/psum | solution.py:604
  427.5 13.0 %collective-permute-start.20 = (bf16[24,3,800]{2,1,0:T(4,128)(2,1)S(1)}, bf16[24,3,800]{2,1,0:T(4,128)(2,1)S(1)}, u32[]{:S(2)}, u32[]{:S(2)}) collective-permute-start(bf16[24,3,800]{2,1,0:T(4,128)(2,1)S(1)} %get-tuple-element.180), channel_id=1, source_target_pairs={{0,1},{1,2},{2,3},{3,4},{4,5},{5,6},{6,7},{7,0},{8,9},{9,10},{10,1... | collective-permute-start | bytes 345608 | tf_op jit(solution)/shard_map/ppermute | solution.py:62
  427.8 12.7 %collective-permute-start.21 = (bf16[24,3,800]{2,1,0:T(4,128)(2,1)S(1)}, bf16[24,3,800]{2,1,0:T(4,128)(2,1)S(1)}, u32[]{:S(2)}, u32[]{:S(2)}) collective-permute-start(bf16[24,3,800]{2,1,0:T(4,128)(2,1)S(1)} %get-tuple-element.179), channel_id=1, source_target_pairs={{1,0},{2,1},{3,2},{4,3},{5,4},{6,5},{7,6},{0,7},{9,8},{10,9},{11,1... | collective-permute-start | bytes 345608 | tf_op jit(solution)/shard_map/ppermute | solution.py:63
  496.4 31.7 %collective-permute-start.27 = (bf16[6912,128]{1,0:T(8,128)(2,1)}, bf16[6912,128]{1,0:T(8,128)(2,1)S(1)}, u32[]{:S(2)}, u32[]{:S(2)}) collective-permute-start(bf16[6912,128]{1,0:T(8,128)(2,1)} %dynamic-slice_bitcast_fusion), channel_id=1, source_target_pairs={{0,1},{1,0},{2,3},{3,2},{4,5},{5,4},{6,7},{7,6},{8,9},{9,8},{10,11... | collective-permute-start | bytes 5308424 | tf_op jit(solution)/shard_map/ppermute | solution.py:409
  497.1 13.7 %all-to-all-start.5 = ((f32[32,2,400]{2,1,0:T(2,128)}), f32[32,2,400]{2,1,0:T(2,128)S(1)}, u32[]{:S(2)}, u32[]{:S(2)}) async-start(f32[32,2,400]{2,1,0:T(2,128)} %broadcast_in_dim.137), calls=%async_computation.5 | async-start | bytes 262144 | tf_op jit(solution)/shard_map/all_to_all | solution.py:77
  529.8 42.8 %collective-permute-start.28 = (bf16[1728,128]{1,0:T(8,128)(2,1)}, bf16[1728,128]{1,0:T(8,128)(2,1)}, u32[]{:S(2)}, u32[]{:S(2)}) collective-permute-start(bf16[1728,128]{1,0:T(8,128)(2,1)} %get-tuple-element.136), channel_id=1, source_target_pairs={{0,8},{8,0},{16,24},{24,16},{1,9},{9,1},{17,25},{25,17},{2,10},{10... | collective-permute-start | bytes 1327112 | tf_op jit(solution)/shard_map/ppermute | solution.py:409
  531.4 41.2 %collective-permute-start.29 = (bf16[1728,128]{1,0:T(8,128)(2,1)}, bf16[1728,128]{1,0:T(8,128)(2,1)}, u32[]{:S(2)}, u32[]{:S(2)}) collective-permute-start(bf16[1728,128]{1,0:T(8,128)(2,1)} %get-tuple-element.138), channel_id=1, source_target_pairs={{0,16},{8,24},{16,0},{24,8},{1,17},{9,25},{17,1},{25,9},{2,18},{10... | collective-permute-start | bytes 1327112 | tf_op jit(solution)/shard_map/ppermute | solution.py:409
  532.5 40.0 %collective-permute-start.30 = (bf16[1728,128]{1,0:T(8,128)(2,1)}, bf16[1728,128]{1,0:T(8,128)(2,1)}, u32[]{:S(2)}, u32[]{:S(2)}) collective-permute-start(bf16[1728,128]{1,0:T(8,128)(2,1)} %get-tuple-element.137), channel_id=1, source_target_pairs={{0,24},{8,16},{16,8},{24,0},{1,25},{9,17},{17,9},{25,1},{2,26},{10... | collective-permute-start | bytes 1327112 | tf_op jit(solution)/shard_map/ppermute | solution.py:409
  534.1 51.4 %all-to-all-start.6 = ((f32[32,32,128]{2,1,0:T(8,128)}), f32[32,32,128]{2,1,0:T(8,128)}, u32[]{:S(2)}, u32[]{:S(2)}) async-start(f32[32,32,128]{2,1,0:T(8,128)} %bitcast.87), calls=%async_computation.6 | async-start | bytes 1048576 | tf_op jit(solution)/shard_map/all_to_all | solution.py:451
  539.5 17.7 %collective-permute-start.22 = (bf16[48,3,400]{2,1,0:T(4,128)(2,1)}, bf16[48,3,400]{2,1,0:T(4,128)(2,1)}, u32[]{:S(2)}, u32[]{:S(2)}) collective-permute-start(bf16[48,3,400]{2,1,0:T(4,128)(2,1)} %get-tuple-element.148), channel_id=1, source_target_pairs={{0,1},{1,2},{2,3},{3,4},{4,5},{5,6},{6,7},{7,0},{8,9},{9,10},{10,1... | collective-permute-start | bytes 345608 | tf_op jit(solution)/shard_map/ppermute | solution.py:62
  539.7 17.5 %collective-permute-start.23 = (bf16[48,3,400]{2,1,0:T(4,128)(2,1)}, bf16[48,3,400]{2,1,0:T(4,128)(2,1)}, u32[]{:S(2)}, u32[]{:S(2)}) collective-permute-start(bf16[48,3,400]{2,1,0:T(4,128)(2,1)} %get-tuple-element.147), channel_id=1, source_target_pairs={{1,0},{2,1},{3,2},{4,3},{5,4},{6,5},{7,6},{0,7},{9,8},{10,9},{11,1... | collective-permute-start | bytes 345608 | tf_op jit(solution)/shard_map/ppermute | solution.py:63
  576.1 28.1 %collective-permute-start.24 = (bf16[12,32,400]{2,1,0:T(8,128)(2,1)}, bf16[12,32,400]{2,1,0:T(8,128)(2,1)S(1)}, u32[]{:S(2)}, u32[]{:S(2)}) collective-permute-start(bf16[12,32,400]{2,1,0:T(8,128)(2,1)} %get-tuple-element.146), channel_id=1, source_target_pairs={{0,8},{8,0},{16,24},{24,16},{1,9},{9,1},{17,25},{25,17},{2,10},{10... | collective-permute-start | bytes 921608 | tf_op jit(solution)/shard_map/ppermute | solution.py:48
  577.6 28.0 %collective-permute-start.25 = (bf16[12,32,400]{2,1,0:T(8,128)(2,1)}, bf16[12,32,400]{2,1,0:T(8,128)(2,1)}, u32[]{:S(2)}, u32[]{:S(2)}) collective-permute-start(bf16[12,32,400]{2,1,0:T(8,128)(2,1)} %get-tuple-element.145), channel_id=1, source_target_pairs={{0,16},{8,24},{16,0},{24,8},{1,17},{9,25},{17,1},{25,9},{2,18},{10... | collective-permute-start | bytes 921608 | tf_op jit(solution)/shard_map/ppermute | solution.py:48
  579.1 26.5 %collective-permute-start.26 = (bf16[12,32,400]{2,1,0:T(8,128)(2,1)}, bf16[12,32,400]{2,1,0:T(8,128)(2,1)}, u32[]{:S(2)}, u32[]{:S(2)}) collective-permute-start(bf16[12,32,400]{2,1,0:T(8,128)(2,1)} %get-tuple-element.144), channel_id=1, source_target_pairs={{0,24},{8,16},{16,8},{24,0},{1,25},{9,17},{17,9},{25,1},{2,26},{10... | collective-permute-start | bytes 921608 | tf_op jit(solution)/shard_map/ppermute | solution.py:48
  579.7 15.5 %collective-permute-start.32 = (bf16[432,128]{1,0:T(8,128)(2,1)}, bf16[432,128]{1,0:T(8,128)(2,1)}, u32[]{:S(2)}, u32[]{:S(2)}) collective-permute-start(bf16[432,128]{1,0:T(8,128)(2,1)} %get-tuple-element.191), channel_id=1, source_target_pairs={{0,4},{1,5},{2,6},{3,7},{4,0},{5,1},{6,2},{7,3},{8,12},{9,13},{10,... | collective-permute-start | bytes 331784 | tf_op jit(solution)/shard_map/ppermute | solution.py:409
  583.1 12.1 %collective-permute-start.33 = (bf16[432,128]{1,0:T(8,128)(2,1)}, bf16[432,128]{1,0:T(8,128)(2,1)}, u32[]{:S(2)}, u32[]{:S(2)}) collective-permute-start(bf16[432,128]{1,0:T(8,128)(2,1)} %get-tuple-element.190), channel_id=1, source_target_pairs={{0,6},{1,7},{2,4},{3,5},{4,2},{5,3},{6,0},{7,1},{8,14},{9,15},{10,... | collective-permute-start | bytes 331784 | tf_op jit(solution)/shard_map/ppermute | solution.py:409
  587.4 47.1 %all-to-all-start.7 = ((f32[32,32,128]{2,1,0:T(8,128)}), f32[32,32,128]{2,1,0:T(8,128)S(1)}, u32[]{:S(2)}, u32[]{:S(2)}) async-start(f32[32,32,128]{2,1,0:T(8,128)} %broadcast_in_dim.138), calls=%async_computation.7 | async-start | bytes 1048576 | tf_op jit(solution)/shard_map/all_to_all | solution.py:453
  596.2 13.7 %collective-permute-start.34 = (bf16[432,128]{1,0:T(8,128)(2,1)S(1)}, bf16[432,128]{1,0:T(8,128)(2,1)S(1)}, u32[]{:S(2)}, u32[]{:S(2)}) collective-permute-start(bf16[432,128]{1,0:T(8,128)(2,1)S(1)} %fusion.32), channel_id=1, source_target_pairs={{0,2},{1,3},{2,0},{3,1},{4,6},{5,7},{6,4},{7,5},{8,10},{9,11},{10,... | collective-permute-start | bytes 331784 | tf_op jit(solution)/shard_map/ppermute | solution.py:409
  601.5 26.8 %collective-permute-start.35 = (bf16[432,128]{1,0:T(8,128)(2,1)S(1)}, bf16[432,128]{1,0:T(8,128)(2,1)S(1)}, u32[]{:S(2)}, u32[]{:S(2)}) collective-permute-start(bf16[432,128]{1,0:T(8,128)(2,1)S(1)} %fusion.32), channel_id=1, source_target_pairs={{0,4},{1,5},{2,6},{3,7},{4,0},{5,1},{6,2},{7,3},{8,12},{9,13},{10,... | collective-permute-start | bytes 331784 | tf_op jit(solution)/shard_map/ppermute | solution.py:409
  604.3 24.0 %collective-permute-start.36 = (bf16[432,128]{1,0:T(8,128)(2,1)S(1)}, bf16[432,128]{1,0:T(8,128)(2,1)S(1)}, u32[]{:S(2)}, u32[]{:S(2)}) collective-permute-start(bf16[432,128]{1,0:T(8,128)(2,1)S(1)} %fusion.32), channel_id=1, source_target_pairs={{0,6},{1,7},{2,4},{3,5},{4,2},{5,3},{6,0},{7,1},{8,14},{9,15},{10,... | collective-permute-start | bytes 331784 | tf_op jit(solution)/shard_map/ppermute | solution.py:409
  629.2 13.7 %collective-permute-start.37 = (bf16[1728,128]{1,0:T(8,128)(2,1)}, bf16[1728,128]{1,0:T(8,128)(2,1)S(1)}, u32[]{:S(2)}, u32[]{:S(2)}) collective-permute-start(bf16[1728,128]{1,0:T(8,128)(2,1)} %get-tuple-element.184), channel_id=1, source_target_pairs={{0,8},{8,0},{16,24},{24,16},{1,9},{9,1},{17,25},{25,17},{2,10},{10... | collective-permute-start | bytes 1327112 | tf_op jit(solution)/shard_map/ppermute | solution.py:409
  630.4 19.7 %collective-permute-start.38 = (bf16[1728,128]{1,0:T(8,128)(2,1)}, bf16[1728,128]{1,0:T(8,128)(2,1)S(1)}, u32[]{:S(2)}, u32[]{:S(2)}) collective-permute-start(bf16[1728,128]{1,0:T(8,128)(2,1)} %get-tuple-element.184), channel_id=1, source_target_pairs={{0,16},{8,24},{16,0},{24,8},{1,17},{9,25},{17,1},{25,9},{2,18},{10... | collective-permute-start | bytes 1327112 | tf_op jit(solution)/shard_map/ppermute | solution.py:409
  632.2 32.7 %collective-permute-start.39 = (bf16[1728,128]{1,0:T(8,128)(2,1)}, bf16[1728,128]{1,0:T(8,128)(2,1)S(1)}, u32[]{:S(2)}, u32[]{:S(2)}) collective-permute-start(bf16[1728,128]{1,0:T(8,128)(2,1)} %get-tuple-element.184), channel_id=1, source_target_pairs={{0,24},{8,16},{16,8},{24,0},{1,25},{9,17},{17,9},{25,1},{2,26},{10... | collective-permute-start | bytes 1327112 | tf_op jit(solution)/shard_map/ppermute | solution.py:409
  (119 other events, 939.1 us)
Sparse Core Ops, SparseCore 0:
  9.9 35.9 all-gather.18
  47.7 49.6 all-gather.10
  99.2 61.4 all-gather.12
  162.4 68.5 all-gather.14
  232.7 29.4 all-gather.20
  263.9 32.8 all-gather.16
  432.9 285.6 all-reduce.15

commit v5 on v4

--- a/solution.py
+++ b/solution.py
@@ -53,6 +53,39 @@
         )
     stacked = jnp.stack(pieces)
     return jnp.stack([lax.dynamic_index_in_dim(stacked, own ^ date, 0, keepdims=False) for date in range(dates)])
+
+
+def after(array, event):
+    return lax.optimization_barrier((array, event))[0]
+
+
+def gathered(shard):
+    return exchange_all(shard, "lat", lax.axis_index("lat"), 1, lax.axis_size("lat"))
+
+
+def both_halves(half):
+    other = swap(half, "lon", 1)
+    first = lax.axis_index("lon") % 2 == 0
+    return jnp.where(first, half, other), jnp.where(first, other, half)
+
+
+def gathered_by_columns(shard):
+    columns = shard.shape[1]
+    start = columns // 2 // lanes * lanes
+    width = columns - start
+    core = lax.axis_index("lon") % 2
+    half = lax.dynamic_slice_in_dim(shard, core * start, width, axis=1)
+    low, high = both_halves(lax.all_gather(half, "lat", axis=0, tiled=True))
+    return jnp.concatenate([low[:, :start], high], axis=1)
+
+
+def gathered_by_rows(shard):
+    rows, columns = shard.shape
+    core = lax.axis_index("lon") % 2
+    half = lax.dynamic_slice_in_dim(shard, core * (rows // 2), rows // 2, axis=0)
+    low, high = both_halves(lax.all_gather(half, "lat", axis=0, tiled=True))
+    pieces = [piece.reshape(-1, 1, rows // 2, columns) for piece in (low, high)]
+    return jnp.concatenate(pieces, axis=1).reshape(-1, columns)
 
 
 def borders(source, dates):
@@ -539,43 +572,36 @@
     decode_down,
     decode_down_bias,
 ):
-    (encode_up, encode_down, widen_weight, bottle_up, bottle_down, merge_weight, decode_up, decode_down) = (
-        lax.all_gather(weight, "lat", axis=0, tiled=True)
-        for weight in (
-            encode_up,
-            encode_down,
-            widen_weight,
-            bottle_up,
-            bottle_down,
-            merge_weight,
-            decode_up,
-            decode_down,
-        )
-    )
     dates = fine_map.shape[0]
     fine = to_dates(fine_map)
-    ocean_band = to_dates(ocean_mask).astype(f32)
-    upstream = to_dates(out_grad)
+    encode_up, encode_down = (gathered(after(weight, fine)) for weight in (encode_up, encode_down))
+    bottle_up, bottle_down = gathered_by_columns(bottle_up), gathered_by_rows(bottle_down)
+    decode_up = lax.all_gather(decode_up, "lat", axis=0, tiled=True)
+    decode_down = lax.all_gather(decode_down, "lat", axis=0, tiled=True)
+    ocean_band = to_dates(after(ocean_mask, fine)).astype(f32)
     height, breadth, channels = fine.shape
     half_height, half_breadth = height // 2, breadth // 2
-    wide = widen_weight.shape[1]
+    wide = bottle_depth.shape[2]
     coarse_band = jnp.max(ocean_band.reshape(half_height, 2, half_breadth, 2), axis=(1, 3))
     sea_fine = jnp.broadcast_to(ocean_band[..., None], (height, breadth, lanes))
     sea_coarse = jnp.broadcast_to(coarse_band[..., None], (half_height, half_breadth, lanes))
     encode = (encode_depth, encode_gain, encode_shift, encode_up, encode_up_bias, encode_down, encode_down_bias)
     bottle = (bottle_depth, bottle_gain, bottle_shift, bottle_up, bottle_up_bias, bottle_down, bottle_down_bias)
     decode = (decode_depth, decode_gain, decode_shift, decode_up, decode_up_bias, decode_down, decode_down_bias)
-    merge_upper = merge_weight[:wide]
-    merge_lower = merge_weight[wide:]
     ocean_fine = jnp.sum(ocean_band)
     ocean_coarse = jnp.sum(coarse_band)
 
     skip_rows, encode_stored = block_forward(fine, encode, sea_fine, ocean_fine, dates)
+    widen_weight = gathered(after(widen_weight, encode_stored[3]))
     blocks = skip_rows.reshape(half_height, 2, half_breadth, 2, channels).astype(f32)
     pooled = (jnp.sum(blocks, axis=(1, 3)) * 0.25).astype(bf16).reshape(-1, channels)
     coarse_in = jnp.dot(pooled, widen_weight, preferred_element_type=f32) + widen_bias.astype(f32)
     coarse_in = coarse_in.astype(bf16).reshape(half_height, half_breadth, wide)
     coarse_low, coarse_stored = block_forward(coarse_in, bottle, sea_coarse, ocean_coarse, dates)
+    merge_weight = gathered(after(merge_weight, coarse_stored[3]))
+    merge_upper = merge_weight[:wide]
+    merge_lower = merge_weight[wide:]
+    upstream = to_dates(after(out_grad, coarse_stored[3]))
     upper = jnp.dot(coarse_low, merge_upper, preferred_element_type=f32)
     upper = upper.reshape(half_height, 1, half_breadth, 1, channels)
     lower = jnp.dot(skip_rows, merge_lower, preferred_element_type=f32)

time: 752 us -> 742 us (0.987)
  blocking collectives: 31.9 us -> 0 us
  waiting for transfers between devices: 183 us -> 168 us
  other arithmetic: 69.2 us -> 83.4 us
  local copies, waits for them, and re-layouts: 96 us -> 110 us
  starting transfers between devices: 95.6 us -> 108 us
    ppermute x14 -> x28, waiting for transfers between devices: 52.7 us -> 91.7 us  [swap(): lax.ppermute(array, axis, [(i, i ^ step) for i in range(lax.axis_size(axi...]
    all_gather x2 -> x0, blocking collectives: 31.9 us -> none  [shards(): lax.all_gather(weight, 'lat', axis=0, tiled=True)]
    all_gather x6 -> x4, waiting for transfers between devices: 30.4 us -> 0.06 us  [the longest x1 0.02 us: gathered_by_rows(): low, high = both_halves(lax.all_gather(half, 'lat', axis=0, tiled=True))]
    all_to_all x6, waiting for transfers between devices: 36.8 us -> 15.4 us  [sum_all(): return jnp.sum(lax.all_to_all(copies, both, 0, 0, tiled=False), axis=0)]
    ppermute x14 -> x28, starting transfers between devices: 20.6 us -> 38.7 us  [swap(): lax.ppermute(array, axis, [(i, i ^ step) for i in range(lax.axis_size(axi...]
    unnamed x250 -> x278, local copies, waits for them, and re-layouts: 20.6 us -> 16.5 us
  transfers between devices with their start and end apart: 56 -> 68, of which waited for: 18 -> 22; matrix products, arithmetic and copies ran while one was open for 23% -> 26% of each run, Pallas kernels for 21% -> 21%
where the time goes in v5:
time: 742 us; the launch traced here: 735 us
  Pallas kernels  208 us (28%)
  waiting for transfers between devices  168 us (23%)
  local copies, waits for them, and re-layouts  110 us (15%)
  starting transfers between devices  108 us (15%)
  other arithmetic  83.4 us (11%)
  matrix products  40.8 us (5%)
  between operations  16 us (2%)
    ppermute x28, waiting for transfers between devices, swap(): lax.ppermute(array, axis, [(i, i ^ step) for i in range(lax.axis_size(axi...  91.7 us
    pallas_call x3, Pallas kernels, stencil_backward(): pl.pallas_call(functools.partial(stencil_backward_kernel, len(edges)), gr...  39.3 us
    pallas_call x3, Pallas kernels, mlp_forward(): pl.pallas_call(functools.partial(mlp_forward_kernel, 512), grid=(pixels /...  38.7 us
    ppermute x28, starting transfers between devices, swap(): lax.ppermute(array, axis, [(i, i ^ step) for i in range(lax.axis_size(axi...  38.7 us
    pallas_call x3, Pallas kernels, stencil_forward(): pl.pallas_call(functools.partial(stencil_forward_kernel, len(edges)), gri...  38.5 us
    pallas_call x3, Pallas kernels, mlp_backward(): pl.pallas_call(functools.partial(mlp_backward_kernel, 512), grid=(pixels...  37.4 us
    psum x1, waiting for transfers between devices, shards(): early = lax.psum([part.astype(bf16) for part in early], both)  35.2 us
    pallas_call x3, Pallas kernels, kernel_grad(): pl.pallas_call(functools.partial(kernel_grad_kernel, len(edges)), grid=(t...  33.2 us
  transfers between devices with their start and end apart: 68, of which 22 were waited for; matrix products, arithmetic and copies ran while one was open for 26% of the time, Pallas kernels for 21%

profile of v5, /device:TPU:0, one launch (start us, length us, event | category | flops | bytes accessed | tf_op | source)
XLA Modules:
  0.0 734.7 jit_solution(10693645294330752132)
XLA Ops:
  27.3 5.5 collective-permute-done.1
  32.7 8.5 %collective-permute-done.2 = bf16[12,32,400]{2,1,0:T(8,128)(2,1)S(1)} collective-permute-done((bf16[12,32,400]{2,1,0:T(8,128)(2,1)S(1)}, bf16[12,32,400]{2,1,0:T(8,128)(2,1)S(1)}, u32[]{:S(2)}, u32[]{:S(2)}) %collective-permute-start.2) | collective-permute-done | bytes 307232 | tf_op jit(solution)/shard_map/ppermute | solution.py:30
  58.7 15.1 %stencil_forward.3 = (f32[48,32,400]{2,1,0:T(8,128)}, f32[2,400]{1,0:T(2,128)}) custom-call(bf16[48,32,400]{2,1,0:T(8,128)(2,1)} %copy-done.4, bf16[48,3,400]{2,1,0:T(4,128)(2,1)} %copy-done.37, bf16[48,3,400]{2,1,0:T(4,128)(2,1)} %copy-done.38, f32[49,400]{1,0:T(8,128)} %reshape.341.refs_2_, f32[48,32,128]{2,1,0:T(8,128)} %broadcast_in_dim.115.refs_3_), custom_call_target="tpu_custom_call" | custom-call | tf_op jit(solution)/shard_map/stencil_forward/pallas_call | solution.py:221
  93.8 10.5 %collective-permute-done.13 = bf16[400,400]{1,0:T(8,128)(2,1)S(1)} collective-permute-done((bf16[400,400]{1,0:T(8,128)(2,1)S(1)}, bf16[400,400]{1,0:T(8,128)(2,1)S(1)}, u32[]{:S(2)}, u32[]{:S(2)}) %collective-permute-start.13) | collective-permute-done | bytes 320032 | tf_op jit(solution)/shard_map/ppermute | solution.py:442
  107.1 4.5 collective-permute-done.8
  112.4 10.5 %collective-permute-done.10 = bf16[100,1600]{1,0:T(8,128)(2,1)S(1)} collective-permute-done((bf16[100,1600]{1,0:T(8,128)(2,1)S(1)}, bf16[100,1600]{1,0:T(8,128)(2,1)S(1)}, u32[]{:S(2)}, u32[]{:S(2)}) %collective-permute-start.10) | collective-permute-done | bytes 320032 | tf_op jit(solution)/shard_map/ppermute | solution.py:442
  123.2 5.1 copy.222
  132.2 12.6 %mlp_forward.3 = (bf16[1536,400]{1,0:T(8,128)(2,1)}, bf16[1536,1600]{1,0:T(8,128)(2,1)}, bf16[1536,1600]{1,0:T(8,128)(2,1)}, bf16[1536,400]{1,0:T(8,128)(2,1)}) custom-call(f32[1536,400]{1,0:T(8,128)} %bitcast.309, bf16[1536,400]{1,0:T(8,128)(2,1)} %bitcast.308, f32[1536,128]{1,0:T(8,128)} %broadcast_in_dim.116.sea, f32[4,400]{1,0:T(4,128)} %pad_maximum_fusion.35.scales, ...), custom_call_target="tpu_custom_call" | custom-call | tf_op jit(solution)/shard_map/mlp_forward/pallas_call | solution.py:352
  148.3 3.8 reduce_sum.104
  163.8 8.4 %stencil_forward.4 = (f32[24,16,800]{2,1,0:T(8,128)}, f32[2,800]{1,0:T(2,128)}) custom-call(bf16[24,16,800]{2,1,0:T(8,128)(2,1)} %bitcast.330, bf16[24,3,800]{2,1,0:T(4,128)(2,1)} %copy-done.43, bf16[24,3,800]{2,1,0:T(4,128)(2,1)} %copy-done.44, f32[49,800]{1,0:T(8,128)} %reshape.347.refs_2_, f32[24,16,128]{2,1,0:T(8,128)} %broadcast_in_dim.122.refs_3_), custom_call_target="tpu_custom_call" | custom-call | tf_op jit(solution)/shard_map/stencil_forward/pallas_call | solution.py:221
  183.9 4.6 collective-permute-done.19
  188.5 6.8 collective-permute-done.20
  204.2 5.4 copy.223
  223.3 13.5 %mlp_forward.4 = (bf16[384,800]{1,0:T(8,128)(2,1)}, bf16[384,3200]{1,0:T(8,128)(2,1)}, bf16[384,3200]{1,0:T(8,128)(2,1)}, bf16[384,800]{1,0:T(8,128)(2,1)}) custom-call(f32[384,800]{1,0:T(8,128)} %bitcast.321, bf16[384,800]{1,0:T(8,128)(2,1)} %copy-done.17, f32[384,128]{1,0:T(8,128)} %broadcast_in_dim.124.sea, f32[4,800]{1,0:T(4,128)} %pad_maximum_fusion.34.scales, ...), custom_call_target="tpu_custom_call" | custom-call | tf_op jit(solution)/shard_map/mlp_forward/pallas_call | solution.py:352
  240.0 3.7 add.303
  247.1 4.8 add_convert_fusion
  261.2 15.0 %stencil_forward.5 = (f32[48,32,400]{2,1,0:T(8,128)}, f32[2,400]{1,0:T(2,128)}) custom-call(bf16[48,32,400]{2,1,0:T(8,128)(2,1)} %copy-done.8, bf16[48,3,400]{2,1,0:T(4,128)(2,1)} %copy-done.39, bf16[48,3,400]{2,1,0:T(4,128)(2,1)} %copy-done.40, f32[49,400]{1,0:T(8,128)} %reshape.352.refs_2_, f32[48,32,128]{2,1,0:T(8,128)} %broadcast_in_dim.115.refs_3_), custom_call_target="tpu_custom_call" | custom-call | tf_op jit(solution)/shard_map/stencil_forward/pallas_call | solution.py:221
  285.9 6.2 all-to-all-done.2
  293.8 12.6 %mlp_forward.5 = (bf16[1536,400]{1,0:T(8,128)(2,1)}, bf16[1536,1600]{1,0:T(8,128)(2,1)}, bf16[1536,1600]{1,0:T(8,128)(2,1)}, bf16[1536,400]{1,0:T(8,128)(2,1)}) custom-call(f32[1536,400]{1,0:T(8,128)} %bitcast.311, bf16[1536,400]{1,0:T(8,128)(2,1)} %get-tuple-element.254.source, f32[1536,128]{1,0:T(8,128)} %broadcast_in_dim.116.sea, ...), custom_call_target="tpu_custom_call" | custom-call | tf_op jit(solution)/shard_map/mlp_forward/pallas_call | solution.py:352
  306.5 12.0 %mlp_backward.3 = (bf16[1536,400]{1,0:T(8,128)(2,1)}, bf16[1536,1600]{1,0:T(8,128)(2,1)}, f32[1536,400]{1,0:T(8,128)}, f32[2,400]{1,0:T(2,128)}, f32[1,400]{1,0:T(1,128)}, /*index=5*/f32[1,1600]{1,0:T(1,128)}) custom-call(bf16[1536,400]{1,0:T(8,128)(2,1)} %bitcast.319, f32[1536,400]{1,0:T(8,128)} %bitcast.312, bf16[1536,1600]{1,0:T(8,128)(2,1)} %get-tuple-element.91.slope, ...), custom_call_target="tpu_custom_call" | custom-call | tf_op jit(solution)/shard_map/mlp_backward/pallas_call | solution.py:369
  327.0 6.1 fusion.11
  343.9 12.8 %kernel_grad.5 = f32[4,56,128]{2,1,0:T(8,128)} custom-call(bf16[48,32,400]{2,1,0:T(8,128)(2,1)} %copy-done.8, bf16[48,3,400]{2,1,0:T(4,128)(2,1)} %copy-done.39, bf16[48,3,400]{2,1,0:T(4,128)(2,1)} %copy-done.40, bf16[48,32,400]{2,1,0:T(8,128)(2,1)} %bitcast.314), custom_call_target="tpu_custom_call" | custom-call | tf_op jit(solution)/shard_map/kernel_grad/pallas_call | solution.py:253
  359.5 15.1 %stencil_backward.3 = (bf16[48,32,400]{2,1,0:T(8,128)(2,1)}, f32[1,400]{1,0:T(1,128)}) custom-call(bf16[48,32,400]{2,1,0:T(8,128)(2,1)} %bitcast.315, bf16[48,3,400]{2,1,0:T(4,128)(2,1)} %copy-done.56, bf16[48,3,400]{2,1,0:T(4,128)(2,1)} %copy-done.57, f32[49,400]{1,0:T(8,128)} %reshape.352.refs_2_, f32[48,32,128]{2,1,0:T(8,128)} %broadcast_in_dim.115.refs_3_, ...), custom_call_target="tpu_custom_call" | custom-call | tf_op jit(solution)/shard_map/stencil_backward/pallas_call | solution.py:237
  377.2 3.8 reduce_sum.109
  385.6 12.8 %mlp_backward.4 = (bf16[384,800]{1,0:T(8,128)(2,1)}, bf16[384,3200]{1,0:T(8,128)(2,1)}, f32[384,800]{1,0:T(8,128)}, f32[2,800]{1,0:T(2,128)}, f32[1,800]{1,0:T(1,128)}, /*index=5*/f32[1,3200]{1,0:T(1,128)}) custom-call(f32[384,800]{1,0:T(8,128)} %fusion.25.upstream, f32[384,800]{1,0:T(8,128)} %bitcast.322, bf16[384,3200]{1,0:T(8,128)(2,1)} %get-tuple-element.95.slope, ...), custom_call_target="tpu_custom_call" | custom-call | tf_op jit(solution)/shard_map/mlp_backward/pallas_call | solution.py:369
  399.9 4.2 all-to-all-start.4
  404.5 7.3 fusion.2
  411.9 5.3 convolution_convert_fusion.1
  426.8 7.6 %kernel_grad.4 = f32[7,56,128]{2,1,0:T(8,128)} custom-call(bf16[24,16,800]{2,1,0:T(8,128)(2,1)} %bitcast.331, bf16[24,3,800]{2,1,0:T(4,128)(2,1)} %copy-done.43, bf16[24,3,800]{2,1,0:T(4,128)(2,1)} %copy-done.44, bf16[24,16,800]{2,1,0:T(8,128)(2,1)} %bitcast.327), custom_call_target="tpu_custom_call" | custom-call | tf_op jit(solution)/shard_map/kernel_grad/pallas_call | solution.py:253
  435.2 8.8 %stencil_backward.4 = (bf16[24,16,800]{2,1,0:T(8,128)(2,1)}, f32[1,800]{1,0:T(1,128)}) custom-call(bf16[24,16,800]{2,1,0:T(8,128)(2,1)} %bitcast.328, bf16[24,3,800]{2,1,0:T(4,128)(2,1)} %copy-done.63, bf16[24,3,800]{2,1,0:T(4,128)(2,1)} %copy-done.64, f32[49,800]{1,0:T(8,128)} %reshape.347.refs_2_, f32[24,16,128]{2,1,0:T(8,128)} %broadcast_in_dim.122.refs_3_, ...), custom_call_target="tpu_custom_call" | custom-call | tf_op jit(solution)/shard_map/stencil_backward/pallas_call | solution.py:237
  459.1 12.6 %mlp_backward.5 = (bf16[1536,400]{1,0:T(8,128)(2,1)}, bf16[1536,1600]{1,0:T(8,128)(2,1)}, f32[1536,400]{1,0:T(8,128)}, f32[2,400]{1,0:T(2,128)}, f32[1,400]{1,0:T(1,128)}, /*index=5*/f32[1,1600]{1,0:T(1,128)}) custom-call(f32[1536,400]{1,0:T(8,128)} %reshape.315.upstream, f32[1536,400]{1,0:T(8,128)} %bitcast.310, ...), custom_call_target="tpu_custom_call" | custom-call | tf_op jit(solution)/shard_map/mlp_backward/pallas_call | solution.py:369
  471.7 11.9 %weight_grads.1 = bf16[2,13,400,128]{3,2,1,0:T(8,128)(2,1)} custom-call(bf16[1536,400]{1,0:T(8,128)(2,1)} %get-tuple-element.111.grad_branch, bf16[1536,400]{1,0:T(8,128)(2,1)} %get-tuple-element.112.normed, bf16[1536,1600]{1,0:T(8,128)(2,1)} %get-tuple-element.113.active, bf16[1536,1600]{1,0:T(8,128)(2,1)} %get-tuple-element.114.grad_hidden), custom_call_target="tpu_custom_call" | custom-call | tf_op jit(solution)/shard_map/weight_grads/pallas_call | solution.py:405
  488.5 4.2 all-to-all-start.5
  493.0 9.2 %all-to-all-done.5 = f32[32,2,400]{2,1,0:T(2,128)S(1)} async-done(((f32[32,2,400]{2,1,0:T(2,128)}), f32[32,2,400]{2,1,0:T(2,128)S(1)}, u32[]{:S(2)}, u32[]{:S(2)}) %all-to-all-start.5) | async-done | bytes 102432 | tf_op jit(solution)/shard_map/all_to_all | solution.py:110
  502.4 4.3 multiply_convert_fusion
  506.7 12.8 %kernel_grad.3 = f32[4,56,128]{2,1,0:T(8,128)} custom-call(bf16[48,32,400]{2,1,0:T(8,128)(2,1)} %copy-done.4, bf16[48,3,400]{2,1,0:T(4,128)(2,1)} %copy-done.37, bf16[48,3,400]{2,1,0:T(4,128)(2,1)} %copy-done.38, bf16[48,32,400]{2,1,0:T(8,128)(2,1)} %bitcast.316), custom_call_target="tpu_custom_call" | custom-call | tf_op jit(solution)/shard_map/kernel_grad/pallas_call | solution.py:253
  540.2 7.7 %collective-permute-done.36.refs_0_ = bf16[48,3,400]{2,1,0:T(4,128)(2,1)} collective-permute-done((bf16[48,3,400]{2,1,0:T(4,128)(2,1)}, bf16[48,3,400]{2,1,0:T(4,128)(2,1)}, u32[]{:S(2)}, u32[]{:S(2)}) %collective-permute-start.36) | collective-permute-done | bytes 115232 | tf_op jit(solution)/shard_map/ppermute | solution.py:95
  547.9 15.4 %stencil_backward.5 = (bf16[48,32,400]{2,1,0:T(8,128)(2,1)}, f32[1,400]{1,0:T(1,128)}) custom-call(bf16[48,32,400]{2,1,0:T(8,128)(2,1)} %bitcast.318, bf16[48,3,400]{2,1,0:T(4,128)(2,1)} %collective-permute-done.36.refs_0_, bf16[48,3,400]{2,1,0:T(4,128)(2,1)} %collective-permute-done.37.refs_1_, f32[49,400]{1,0:T(8,128)} %reshape.341.refs_2_, ...), custom_call_target="tpu_custom_call" | custom-call | tf_op jit(solution)/shard_map/stencil_backward/pallas_call | solution.py:237
  579.0 5.2 all-to-all-start.7
  587.2 5.6 collective-permute-start.48
  600.8 17.2 %collective-permute-done.49 = bf16[432,128]{1,0:T(8,128)(2,1)S(1)} collective-permute-done((bf16[432,128]{1,0:T(8,128)(2,1)S(1)}, bf16[432,128]{1,0:T(8,128)(2,1)S(1)}, u32[]{:S(2)}, u32[]{:S(2)}) %collective-permute-start.49) | collective-permute-done | bytes 110624 | tf_op jit(solution)/shard_map/ppermute | solution.py:442
  626.0 4.0 collective-permute-done.51
  630.0 6.7 collective-permute-done.52
  636.7 16.0 %collective-permute-done.53 = bf16[1728,128]{1,0:T(8,128)(2,1)S(1)} collective-permute-done((bf16[1728,128]{1,0:T(8,128)(2,1)}, bf16[1728,128]{1,0:T(8,128)(2,1)S(1)}, u32[]{:S(2)}, u32[]{:S(2)}) %collective-permute-start.53) | collective-permute-done | bytes 442400 | tf_op jit(solution)/shard_map/ppermute | solution.py:442
  665.6 8.9 %unpack.1 = (f32[400,1600]{1,0:T(8,128)}, f32[400,1600]{1,0:T(8,128)}) custom-call(s32[1]{0:T(128)} %bitcast.123.core, bf16[6912,128]{1,0:T(8,128)(2,1)} %copy-done.19, bf16[6912,128]{1,0:T(8,128)(2,1)} %collective-permute-done.54.other), custom_call_target="tpu_custom_call" | custom-call | tf_op jit(solution)/shard_map/unpack/pallas_call | solution.py:427
  675.7 35.2 %all-reduce.16.cloned.1.call-done = (bf16[800,3200]{1,0:T(8,128)(2,1)}, bf16[3200,800]{0,1:T(8,128)(2,1)}, bf16[400,400]{1,0:T(8,128)(2,1)}, bf16[400,800]{1,0:T...) async-done(((bf16[800,3200]{1,0:T(8,128)(2,1)}, bf16[3200,800]{0,1:T(8,128)(2,1)}, bf16[400,400]{1,0:T(8,128)(2,1)}, bf16[400,800]{1,0:T(8,128)(2,1)}, ...) | async-done | bytes 13760016 | tf_op jit(solution)/shard_map/psum | solution.py:630
  710.9 7.3 convert_element_type.218
  718.2 4.7 transpose.77
  (574 shorter events, 277.1 us)
Async XLA Ops:
  7.2 116.0 %all-gather.8.cloned.1.call-start = ((), (), s32[]{:S(2)}) async-start(), calls=%async_computation.9 | async-start | bytes 3584000 | tf_op jit(solution)/shard_map/all_gather | solution.py:86
  9.5 143.8 %all-gather.6.cloned.1.call-start = ((), (), s32[]{:S(2)}) async-start(), calls=%async_computation.8 | async-start | bytes 3328000 | tf_op jit(solution)/shard_map/all_gather | solution.py:78
  10.5 273.0 %all-gather.12.cloned.1.call-start = ((), (), s32[]{:S(2)}) async-start(), calls=%async_computation.11 | async-start | bytes 1730560 | tf_op jit(solution)/shard_map/all_gather | solution.py:579
  11.2 282.6 %all-gather.10.cloned.1.call-start = ((), (), s32[]{:S(2)}) async-start(), calls=%async_computation.10 | async-start | bytes 2048000 | tf_op jit(solution)/shard_map/all_gather | solution.py:580
  11.7 15.6 %collective-permute-start = (bf16[12,32,400]{2,1,0:T(8,128)(2,1)S(1)}, bf16[12,32,400]{2,1,0:T(8,128)(2,1)S(1)}, u32[]{:S(2)}, u32[]{:S(2)}) collective-permute-start(bf16[12,32,400]{2,1,0:T(8,128)(2,1)S(1)} %get-tuple-element.194), channel_id=1, source_target_pairs={{0,8},{8,0},{16,24},{24,16},{1,9},{9,1},{17,25},{25,17},{2,10},{10... | collective-permute-start | bytes 921608 | tf_op jit(solution)/shard_map/ppermute | solution.py:30
  14.7 18.0 %collective-permute-start.1 = (bf16[12,32,400]{2,1,0:T(8,128)(2,1)S(1)}, bf16[12,32,400]{2,1,0:T(8,128)(2,1)S(1)}, u32[]{:S(2)}, u32[]{:S(2)}) collective-permute-start(bf16[12,32,400]{2,1,0:T(8,128)(2,1)S(1)} %get-tuple-element.196), channel_id=1, source_target_pairs={{0,16},{8,24},{16,0},{24,8},{1,17},{9,25},{17,1},{25,9},{2,18},{10... | collective-permute-start | bytes 921608 | tf_op jit(solution)/shard_map/ppermute | solution.py:30
  16.2 25.0 %collective-permute-start.2 = (bf16[12,32,400]{2,1,0:T(8,128)(2,1)S(1)}, bf16[12,32,400]{2,1,0:T(8,128)(2,1)S(1)}, u32[]{:S(2)}, u32[]{:S(2)}) collective-permute-start(bf16[12,32,400]{2,1,0:T(8,128)(2,1)S(1)} %get-tuple-element.195), channel_id=1, source_target_pairs={{0,24},{8,16},{16,8},{24,0},{1,25},{9,17},{17,9},{25,1},{2,26},{10... | collective-permute-start | bytes 921608 | tf_op jit(solution)/shard_map/ppermute | solution.py:30
  46.8 47.0 %collective-permute-start.11 = (bf16[400,400]{1,0:T(8,128)(2,1)S(1)}, bf16[400,400]{1,0:T(8,128)(2,1)S(1)}, u32[]{:S(2)}, u32[]{:S(2)}) collective-permute-start(bf16[400,400]{1,0:T(8,128)(2,1)S(1)} %copy-done.47), channel_id=1, source_target_pairs={{0,8},{8,0},{16,24},{24,16},{1,9},{9,1},{17,25},{25,17},{2,10},{10... | collective-permute-start | bytes 960008 | tf_op jit(solution)/shard_map/ppermute | solution.py:442
  48.2 45.6 %collective-permute-start.12 = (bf16[400,400]{1,0:T(8,128)(2,1)S(1)}, bf16[400,400]{1,0:T(8,128)(2,1)}, u32[]{:S(2)}, u32[]{:S(2)}) collective-permute-start(bf16[400,400]{1,0:T(8,128)(2,1)S(1)} %copy-done.47), channel_id=1, source_target_pairs={{0,16},{8,24},{16,0},{24,8},{1,17},{9,25},{17,1},{25,9},{2,18},{10... | collective-permute-start | bytes 960008 | tf_op jit(solution)/shard_map/ppermute | solution.py:442
  76.0 15.0 %collective-permute-start.16 = (bf16[100,800]{1,0:T(8,128)(2,1)S(1)}, bf16[100,800]{1,0:T(8,128)(2,1)S(1)}, u32[]{:S(2)}, u32[]{:S(2)}) collective-permute-start(bf16[100,800]{1,0:T(8,128)(2,1)S(1)} %copy-done.58), channel_id=1, source_target_pairs={{0,24},{8,16},{16,8},{24,0},{1,25},{9,17},{17,9},{25,1},{2,26},{10... | collective-permute-start | bytes 480008 | tf_op jit(solution)/shard_map/ppermute | solution.py:442
  81.4 22.9 %collective-permute-start.13 = (bf16[400,400]{1,0:T(8,128)(2,1)S(1)}, bf16[400,400]{1,0:T(8,128)(2,1)S(1)}, u32[]{:S(2)}, u32[]{:S(2)}) collective-permute-start(bf16[400,400]{1,0:T(8,128)(2,1)S(1)} %copy-done.47), channel_id=1, source_target_pairs={{0,24},{8,16},{16,8},{24,0},{1,25},{9,17},{17,9},{25,1},{2,26},{10... | collective-permute-start | bytes 960008 | tf_op jit(solution)/shard_map/ppermute | solution.py:442
  85.7 44.1 %all-to-all-start = ((f32[32,3,400]{2,1,0:T(4,128)}), f32[32,3,400]{2,1,0:T(4,128)S(1)}, u32[]{:S(2)}, u32[]{:S(2)}) async-start(f32[32,3,400]{2,1,0:T(4,128)} %broadcast_in_dim.117), calls=%async_computation | async-start | bytes 524288 | tf_op jit(solution)/shard_map/all_to_all | solution.py:110
  89.0 22.6 %collective-permute-start.8 = (bf16[100,1600]{1,0:T(8,128)(2,1)S(1)}, bf16[100,1600]{1,0:T(8,128)(2,1)S(1)}, u32[]{:S(2)}, u32[]{:S(2)}) collective-permute-start(bf16[100,1600]{1,0:T(8,128)(2,1)S(1)} %copy-done.52), channel_id=1, source_target_pairs={{0,8},{8,0},{16,24},{24,16},{1,9},{9,1},{17,25},{25,17},{2,10},{10... | collective-permute-start | bytes 960008 | tf_op jit(solution)/shard_map/ppermute | solution.py:442
  91.0 21.5 %collective-permute-start.9 = (bf16[100,1600]{1,0:T(8,128)(2,1)S(1)}, bf16[100,1600]{1,0:T(8,128)(2,1)S(1)}, u32[]{:S(2)}, u32[]{:S(2)}) collective-permute-start(bf16[100,1600]{1,0:T(8,128)(2,1)S(1)} %copy-done.52), channel_id=1, source_target_pairs={{0,16},{8,24},{16,0},{24,8},{1,17},{9,25},{17,1},{25,9},{2,18},{10... | collective-permute-start | bytes 960008 | tf_op jit(solution)/shard_map/ppermute | solution.py:442
  93.8 29.1 %collective-permute-start.10 = (bf16[100,1600]{1,0:T(8,128)(2,1)S(1)}, bf16[100,1600]{1,0:T(8,128)(2,1)S(1)}, u32[]{:S(2)}, u32[]{:S(2)}) collective-permute-start(bf16[100,1600]{1,0:T(8,128)(2,1)S(1)} %copy-done.52), channel_id=1, source_target_pairs={{0,24},{8,16},{16,8},{24,0},{1,25},{9,17},{17,9},{25,1},{2,26},{10... | collective-permute-start | bytes 960008 | tf_op jit(solution)/shard_map/ppermute | solution.py:442
  128.3 75.9 %collective-permute-start.23 = (bf16[1600,800]{0,1:T(8,128)(2,1)}, bf16[1600,800]{0,1:T(8,128)(2,1)}, u32[]{:S(2)}, u32[]{:S(2)}) collective-permute-start(bf16[1600,800]{0,1:T(8,128)(2,1)} %copy.222), channel_id=1, source_target_pairs={{0,1},{1,0},{2,3},{3,2},{4,5},{5,4},{6,7},{7,6},{8,9},{9,8},{10,11... | collective-permute-start | bytes 7680008 | tf_op jit(solution)/shard_map/ppermute | solution.py:442
  153.3 62.4 %collective-permute-start.22 = (bf16[800,1664]{1,0:T(8,128)(2,1)}, bf16[800,1664]{1,0:T(8,128)(2,1)}, u32[]{:S(2)}, u32[]{:S(2)}) collective-permute-start(bf16[800,1664]{1,0:T(8,128)(2,1)} %all-gather.6.cloned.1.call-done), channel_id=1, source_target_pairs={{0,1},{1,0},{2,3},{3,2},{4,5},{5,4},{6,7},{7,6},{8,9},{9,8},{10,11... | collective-permute-start | bytes 7987208 | tf_op jit(solution)/shard_map/ppermute | solution.py:442
  172.3 16.2 %collective-permute-start.19 = (bf16[300,400]{0,1:T(8,128)(2,1)S(1)}, bf16[300,400]{0,1:T(8,128)(2,1)S(1)}, u32[]{:S(2)}, u32[]{:S(2)}) collective-permute-start(bf16[300,400]{0,1:T(8,128)(2,1)S(1)} %copy-done.55), channel_id=1, source_target_pairs={{0,8},{8,0},{16,24},{24,16},{1,9},{9,1},{17,25},{25,17},{2,10},{10... | collective-permute-start | bytes 720008 | tf_op jit(solution)/shard_map/ppermute | solution.py:442
  173.2 22.1 %collective-permute-start.20 = (bf16[300,400]{0,1:T(8,128)(2,1)S(1)}, bf16[300,400]{0,1:T(8,128)(2,1)S(1)}, u32[]{:S(2)}, u32[]{:S(2)}) collective-permute-start(bf16[300,400]{0,1:T(8,128)(2,1)S(1)} %copy-done.55), channel_id=1, source_target_pairs={{0,16},{8,24},{16,0},{24,8},{1,17},{9,25},{17,1},{25,9},{2,18},{10... | collective-permute-start | bytes 720008 | tf_op jit(solution)/shard_map/ppermute | solution.py:442
  174.1 23.8 %collective-permute-start.21 = (bf16[300,400]{0,1:T(8,128)(2,1)S(1)}, bf16[300,400]{0,1:T(8,128)(2,1)S(1)}, u32[]{:S(2)}, u32[]{:S(2)}) collective-permute-start(bf16[300,400]{0,1:T(8,128)(2,1)S(1)} %copy-done.55), channel_id=1, source_target_pairs={{0,24},{8,16},{16,8},{24,0},{1,25},{9,17},{17,9},{25,1},{2,26},{10... | collective-permute-start | bytes 720008 | tf_op jit(solution)/shard_map/ppermute | solution.py:442
  178.0 25.5 %all-to-all-start.1 = ((f32[32,3,800]{2,1,0:T(4,128)}), f32[32,3,800]{2,1,0:T(4,128)S(1)}, u32[]{:S(2)}, u32[]{:S(2)}) async-start(f32[32,3,800]{2,1,0:T(4,128)} %broadcast_in_dim.125), calls=%async_computation.1 | async-start | bytes 917504 | tf_op jit(solution)/shard_map/all_to_all | solution.py:110
  188.5 68.0 %collective-permute-start.29 = (bf16[12,32,400]{2,1,0:T(8,128)(2,1)}, bf16[12,32,400]{2,1,0:T(8,128)(2,1)}, u32[]{:S(2)}, u32[]{:S(2)}) collective-permute-start(bf16[12,32,400]{2,1,0:T(8,128)(2,1)} %get-tuple-element.176), channel_id=1, source_target_pairs={{0,8},{8,0},{16,24},{24,16},{1,9},{9,1},{17,25},{25,17},{2,10},{10... | collective-permute-start | bytes 921608 | tf_op jit(solution)/shard_map/ppermute | solution.py:30
  195.3 61.2 %collective-permute-start.30 = (bf16[12,32,400]{2,1,0:T(8,128)(2,1)}, bf16[12,32,400]{2,1,0:T(8,128)(2,1)}, u32[]{:S(2)}, u32[]{:S(2)}) collective-permute-start(bf16[12,32,400]{2,1,0:T(8,128)(2,1)} %get-tuple-element.175), channel_id=1, source_target_pairs={{0,16},{8,24},{16,0},{24,8},{1,17},{9,25},{17,1},{25,9},{2,18},{10... | collective-permute-start | bytes 921608 | tf_op jit(solution)/shard_map/ppermute | solution.py:30
  197.8 58.7 %collective-permute-start.31 = (bf16[12,32,400]{2,1,0:T(8,128)(2,1)}, bf16[12,32,400]{2,1,0:T(8,128)(2,1)}, u32[]{:S(2)}, u32[]{:S(2)}) collective-permute-start(bf16[12,32,400]{2,1,0:T(8,128)(2,1)} %get-tuple-element.174), channel_id=1, source_target_pairs={{0,24},{8,16},{16,8},{24,0},{1,25},{9,17},{17,9},{25,1},{2,26},{10... | collective-permute-start | bytes 921608 | tf_op jit(solution)/shard_map/ppermute | solution.py:30
  319.8 16.8 %all-to-all-start.3 = ((f32[32,2,400]{2,1,0:T(2,128)}), f32[32,2,400]{2,1,0:T(2,128)S(1)}, u32[]{:S(2)}, u32[]{:S(2)}) async-start(f32[32,2,400]{2,1,0:T(2,128)} %broadcast_in_dim.135), calls=%async_computation.3 | async-start | bytes 262144 | tf_op jit(solution)/shard_map/all_to_all | solution.py:110
  323.5 33.3 %collective-permute-start.26 = (bf16[12,32,400]{2,1,0:T(8,128)(2,1)}, bf16[12,32,400]{2,1,0:T(8,128)(2,1)S(1)}, u32[]{:S(2)}, u32[]{:S(2)}) collective-permute-start(bf16[12,32,400]{2,1,0:T(8,128)(2,1)} %get-tuple-element.184), channel_id=1, source_target_pairs={{0,8},{8,0},{16,24},{24,16},{1,9},{9,1},{17,25},{25,17},{2,10},{10... | collective-permute-start | bytes 921608 | tf_op jit(solution)/shard_map/ppermute | solution.py:48
  325.2 31.6 %collective-permute-start.27 = (bf16[12,32,400]{2,1,0:T(8,128)(2,1)}, bf16[12,32,400]{2,1,0:T(8,128)(2,1)S(1)}, u32[]{:S(2)}, u32[]{:S(2)}) collective-permute-start(bf16[12,32,400]{2,1,0:T(8,128)(2,1)} %get-tuple-element.183), channel_id=1, source_target_pairs={{0,16},{8,24},{16,0},{24,8},{1,17},{9,25},{17,1},{25,9},{2,18},{10... | collective-permute-start | bytes 921608 | tf_op jit(solution)/shard_map/ppermute | solution.py:48
  326.7 30.1 %collective-permute-start.28 = (bf16[12,32,400]{2,1,0:T(8,128)(2,1)S(1)}, bf16[12,32,400]{2,1,0:T(8,128)(2,1)S(1)}, u32[]{:S(2)}, u32[]{:S(2)}) collective-permute-start(bf16[12,32,400]{2,1,0:T(8,128)(2,1)S(1)} %get-tuple-element.182), channel_id=1, source_target_pairs={{0,24},{8,16},{16,8},{24,0},{1,25},{9,17},{17,9},{25,1},{2,26},{10... | collective-permute-start | bytes 921608 | tf_op jit(solution)/shard_map/ppermute | solution.py:48
  340.3 17.9 %collective-permute-start.32 = (bf16[48,3,400]{2,1,0:T(4,128)(2,1)S(1)}, bf16[48,3,400]{2,1,0:T(4,128)(2,1)S(1)}, u32[]{:S(2)}, u32[]{:S(2)}) collective-permute-start(bf16[48,3,400]{2,1,0:T(4,128)(2,1)S(1)} %get-tuple-element.168), channel_id=1, source_target_pairs={{0,1},{1,2},{2,3},{3,4},{4,5},{5,6},{6,7},{7,0},{8,9},{9,10},{10,1... | collective-permute-start | bytes 345608 | tf_op jit(solution)/shard_map/ppermute | solution.py:95
  340.4 17.8 %collective-permute-start.33 = (bf16[48,3,400]{2,1,0:T(4,128)(2,1)S(1)}, bf16[48,3,400]{2,1,0:T(4,128)(2,1)S(1)}, u32[]{:S(2)}, u32[]{:S(2)}) collective-permute-start(bf16[48,3,400]{2,1,0:T(4,128)(2,1)S(1)} %get-tuple-element.167), channel_id=1, source_target_pairs={{1,0},{2,1},{3,2},{4,3},{5,4},{6,5},{7,6},{0,7},{9,8},{10,9},{11,1... | collective-permute-start | bytes 345608 | tf_op jit(solution)/shard_map/ppermute | solution.py:96
  399.9 17.2 %all-to-all-start.4 = ((f32[32,2,800]{2,1,0:T(2,128)}), f32[32,2,800]{2,1,0:T(2,128)}, u32[]{:S(2)}, u32[]{:S(2)}) async-start(f32[32,2,800]{2,1,0:T(2,128)} %broadcast_in_dim.136), calls=%async_computation.4 | async-start | bytes 458752 | tf_op jit(solution)/shard_map/all_to_all | solution.py:110
  404.1 306.8 %all-reduce.16.cloned.1.call-start = ((), (), s32[]{:S(2)}) async-start(), calls=%async_computation.12 | async-start | bytes 28057600 | tf_op jit(solution)/shard_map/psum | solution.py:630
  487.8 31.7 %collective-permute-start.41 = (bf16[6912,128]{1,0:T(8,128)(2,1)}, bf16[6912,128]{1,0:T(8,128)(2,1)S(1)}, u32[]{:S(2)}, u32[]{:S(2)}) collective-permute-start(bf16[6912,128]{1,0:T(8,128)(2,1)} %dynamic-slice_bitcast_fusion), channel_id=1, source_target_pairs={{0,1},{1,0},{2,3},{3,2},{4,5},{5,4},{6,7},{7,6},{8,9},{9,8},{10,11... | collective-permute-start | bytes 5308424 | tf_op jit(solution)/shard_map/ppermute | solution.py:442
  521.1 42.2 %collective-permute-start.42 = (bf16[1728,128]{1,0:T(8,128)(2,1)}, bf16[1728,128]{1,0:T(8,128)(2,1)}, u32[]{:S(2)}, u32[]{:S(2)}) collective-permute-start(bf16[1728,128]{1,0:T(8,128)(2,1)} %get-tuple-element.150), channel_id=1, source_target_pairs={{0,8},{8,0},{16,24},{24,16},{1,9},{9,1},{17,25},{25,17},{2,10},{10... | collective-permute-start | bytes 1327112 | tf_op jit(solution)/shard_map/ppermute | solution.py:442
  522.6 40.7 %collective-permute-start.43 = (bf16[1728,128]{1,0:T(8,128)(2,1)}, bf16[1728,128]{1,0:T(8,128)(2,1)}, u32[]{:S(2)}, u32[]{:S(2)}) collective-permute-start(bf16[1728,128]{1,0:T(8,128)(2,1)} %get-tuple-element.152), channel_id=1, source_target_pairs={{0,16},{8,24},{16,0},{24,8},{1,17},{9,25},{17,1},{25,9},{2,18},{10... | collective-permute-start | bytes 1327112 | tf_op jit(solution)/shard_map/ppermute | solution.py:442
  523.6 39.7 %collective-permute-start.44 = (bf16[1728,128]{1,0:T(8,128)(2,1)}, bf16[1728,128]{1,0:T(8,128)(2,1)}, u32[]{:S(2)}, u32[]{:S(2)}) collective-permute-start(bf16[1728,128]{1,0:T(8,128)(2,1)} %get-tuple-element.151), channel_id=1, source_target_pairs={{0,24},{8,16},{16,8},{24,0},{1,25},{9,17},{17,9},{25,1},{2,26},{10... | collective-permute-start | bytes 1327112 | tf_op jit(solution)/shard_map/ppermute | solution.py:442
  525.4 51.6 %all-to-all-start.6 = ((f32[32,32,128]{2,1,0:T(8,128)}), f32[32,32,128]{2,1,0:T(8,128)}, u32[]{:S(2)}, u32[]{:S(2)}) async-start(f32[32,32,128]{2,1,0:T(8,128)} %bitcast.120), calls=%async_computation.6 | async-start | bytes 1048576 | tf_op jit(solution)/shard_map/all_to_all | solution.py:484
  530.8 17.1 %collective-permute-start.36 = (bf16[48,3,400]{2,1,0:T(4,128)(2,1)}, bf16[48,3,400]{2,1,0:T(4,128)(2,1)}, u32[]{:S(2)}, u32[]{:S(2)}) collective-permute-start(bf16[48,3,400]{2,1,0:T(4,128)(2,1)} %get-tuple-element.166), channel_id=1, source_target_pairs={{0,1},{1,2},{2,3},{3,4},{4,5},{5,6},{6,7},{7,0},{8,9},{9,10},{10,1... | collective-permute-start | bytes 345608 | tf_op jit(solution)/shard_map/ppermute | solution.py:95
  531.1 16.8 %collective-permute-start.37 = (bf16[48,3,400]{2,1,0:T(4,128)(2,1)}, bf16[48,3,400]{2,1,0:T(4,128)(2,1)}, u32[]{:S(2)}, u32[]{:S(2)}) collective-permute-start(bf16[48,3,400]{2,1,0:T(4,128)(2,1)} %get-tuple-element.165), channel_id=1, source_target_pairs={{1,0},{2,1},{3,2},{4,3},{5,4},{6,5},{7,6},{0,7},{9,8},{10,9},{11,1... | collective-permute-start | bytes 345608 | tf_op jit(solution)/shard_map/ppermute | solution.py:96
  566.9 28.5 %collective-permute-start.38 = (bf16[12,32,400]{2,1,0:T(8,128)(2,1)}, bf16[12,32,400]{2,1,0:T(8,128)(2,1)S(1)}, u32[]{:S(2)}, u32[]{:S(2)}) collective-permute-start(bf16[12,32,400]{2,1,0:T(8,128)(2,1)} %get-tuple-element.164), channel_id=1, source_target_pairs={{0,8},{8,0},{16,24},{24,16},{1,9},{9,1},{17,25},{25,17},{2,10},{10... | collective-permute-start | bytes 921608 | tf_op jit(solution)/shard_map/ppermute | solution.py:48
  568.4 28.4 %collective-permute-start.39 = (bf16[12,32,400]{2,1,0:T(8,128)(2,1)}, bf16[12,32,400]{2,1,0:T(8,128)(2,1)}, u32[]{:S(2)}, u32[]{:S(2)}) collective-permute-start(bf16[12,32,400]{2,1,0:T(8,128)(2,1)} %get-tuple-element.163), channel_id=1, source_target_pairs={{0,16},{8,24},{16,0},{24,8},{1,17},{9,25},{17,1},{25,9},{2,18},{10... | collective-permute-start | bytes 921608 | tf_op jit(solution)/shard_map/ppermute | solution.py:48
  570.5 26.3 %collective-permute-start.40 = (bf16[12,32,400]{2,1,0:T(8,128)(2,1)}, bf16[12,32,400]{2,1,0:T(8,128)(2,1)}, u32[]{:S(2)}, u32[]{:S(2)}) collective-permute-start(bf16[12,32,400]{2,1,0:T(8,128)(2,1)} %get-tuple-element.162), channel_id=1, source_target_pairs={{0,24},{8,16},{16,8},{24,0},{1,25},{9,17},{17,9},{25,1},{2,26},{10... | collective-permute-start | bytes 921608 | tf_op jit(solution)/shard_map/ppermute | solution.py:48
  570.5 15.6 %collective-permute-start.46 = (bf16[432,128]{1,0:T(8,128)(2,1)}, bf16[432,128]{1,0:T(8,128)(2,1)}, u32[]{:S(2)}, u32[]{:S(2)}) collective-permute-start(bf16[432,128]{1,0:T(8,128)(2,1)} %get-tuple-element.221), channel_id=1, source_target_pairs={{0,4},{1,5},{2,6},{3,7},{4,0},{5,1},{6,2},{7,3},{8,12},{9,13},{10,... | collective-permute-start | bytes 331784 | tf_op jit(solution)/shard_map/ppermute | solution.py:442
  579.0 45.5 %all-to-all-start.7 = ((f32[32,32,128]{2,1,0:T(8,128)}), f32[32,32,128]{2,1,0:T(8,128)S(1)}, u32[]{:S(2)}, u32[]{:S(2)}) async-start(f32[32,32,128]{2,1,0:T(8,128)} %broadcast_in_dim.138), calls=%async_computation.7 | async-start | bytes 1048576 | tf_op jit(solution)/shard_map/all_to_all | solution.py:486
  592.8 25.2 %collective-permute-start.49 = (bf16[432,128]{1,0:T(8,128)(2,1)S(1)}, bf16[432,128]{1,0:T(8,128)(2,1)S(1)}, u32[]{:S(2)}, u32[]{:S(2)}) collective-permute-start(bf16[432,128]{1,0:T(8,128)(2,1)S(1)} %fusion.28), channel_id=1, source_target_pairs={{0,4},{1,5},{2,6},{3,7},{4,0},{5,1},{6,2},{7,3},{8,12},{9,13},{10,... | collective-permute-start | bytes 331784 | tf_op jit(solution)/shard_map/ppermute | solution.py:442
  595.4 22.5 %collective-permute-start.50 = (bf16[432,128]{1,0:T(8,128)(2,1)S(1)}, bf16[432,128]{1,0:T(8,128)(2,1)S(1)}, u32[]{:S(2)}, u32[]{:S(2)}) collective-permute-start(bf16[432,128]{1,0:T(8,128)(2,1)S(1)} %fusion.28), channel_id=1, source_target_pairs={{0,6},{1,7},{2,4},{3,5},{4,2},{5,3},{6,0},{7,1},{8,14},{9,15},{10,... | collective-permute-start | bytes 331784 | tf_op jit(solution)/shard_map/ppermute | solution.py:442
  620.1 16.6 %collective-permute-start.52 = (bf16[1728,128]{1,0:T(8,128)(2,1)}, bf16[1728,128]{1,0:T(8,128)(2,1)S(1)}, u32[]{:S(2)}, u32[]{:S(2)}) collective-permute-start(bf16[1728,128]{1,0:T(8,128)(2,1)} %get-tuple-element.214), channel_id=1, source_target_pairs={{0,16},{8,24},{16,0},{24,8},{1,17},{9,25},{17,1},{25,9},{2,18},{10... | collective-permute-start | bytes 1327112 | tf_op jit(solution)/shard_map/ppermute | solution.py:442
  622.4 30.2 %collective-permute-start.53 = (bf16[1728,128]{1,0:T(8,128)(2,1)}, bf16[1728,128]{1,0:T(8,128)(2,1)S(1)}, u32[]{:S(2)}, u32[]{:S(2)}) collective-permute-start(bf16[1728,128]{1,0:T(8,128)(2,1)} %get-tuple-element.214), channel_id=1, source_target_pairs={{0,24},{8,16},{16,8},{24,0},{1,25},{9,17},{17,9},{25,1},{2,26},{10... | collective-permute-start | bytes 1327112 | tf_op jit(solution)/shard_map/ppermute | solution.py:442
  (149 other events, 1205.4 us)
Sparse Core Ops, SparseCore 0:
  10.5 62.7 all-gather.7
  75.6 58.4 all-gather.5
  136.0 27.9 all-gather.11
  165.6 56.7 all-gather.9
  426.9 283.9 all-reduce.15

commit v6 on v4

--- a/solution.py
+++ b/solution.py
@@ -3,6 +3,7 @@
 
 import jax
 import jax.numpy as jnp
+import numpy as np
 from jax import lax
 from jax.experimental import pallas as pl
 from jax.experimental.pallas import tpu as pltpu
@@ -55,6 +56,14 @@
     return jnp.stack([lax.dynamic_index_in_dim(stacked, own ^ date, 0, keepdims=False) for date in range(dates)])
 
 
+def after(array, event):
+    return lax.optimization_barrier((array, event))[0]
+
+
+def gathered(shard):
+    return exchange_all(shard, "lat", lax.axis_index("lat"), 1, lax.axis_size("lat"))
+
+
 def borders(source, dates):
     count = lax.axis_size("lon")
     forward = [(i, (i + 1) % count) for i in range(count)]
@@ -247,10 +256,11 @@
 
 
 def mlp_forward_kernel(
-    size, mixed, source, sea, scales, up, up_bias, down, down_bias, out, active, slope, normed
+    size, mixed, source, sea, scales, up, up_bias, down, down_bias, *refs
 ):
     unit = (mixed[...] - scales[0:1]) * scales[1:2]
     low = (unit * scales[2:3] + scales[3:4]).astype(bf16)
+    out, active, slope, normed = refs[-4:] if len(refs) == 4 else refs[3:7]
     normed[...] = low
     branch = down_bias[...]
     for a, b in chunks_of(up.shape[1], size):
@@ -261,7 +271,46 @@
         slope[:, a:b] = rise.astype(bf16)
         branch = branch + jnp.dot(value, down[a:b, :], preferred_element_type=f32)
     mask = spread(sea[...], out.shape[1])
-    out[...] = (mask * (source[...].astype(f32) + branch)).astype(bf16)
+    result = (mask * (source[...].astype(f32) + branch)).astype(bf16)
+    out[...] = result
+    if len(refs) > 4:
+        blocks, widen, widen_bias = refs[:3]
+        pooled, coarse = refs[7:]
+        mean = (0.25 * jnp.dot(blocks[...], result, preferred_element_type=f32)).astype(bf16)
+        pooled[...] = mean
+        coarse[...] = (jnp.dot(mean, widen[...], preferred_element_type=f32) + widen_bias[...]).astype(bf16)
+
+
+def merge_forward_kernel(coarse, skip, merge, bias, members, merged):
+    wide = coarse.shape[1]
+    upper = jnp.dot(coarse[...], merge[:wide, :], preferred_element_type=f32)
+    high = upper.astype(bf16)
+    rest = (upper - high.astype(f32)).astype(bf16)
+    total = jnp.dot(members[...], high, preferred_element_type=f32)
+    total = total + jnp.dot(members[...], rest, preferred_element_type=f32)
+    total = total + jnp.dot(skip[...], merge[wide:, :], preferred_element_type=f32)
+    merged[...] = (total + bias[...]).astype(bf16)
+
+
+def merge_backward_kernel(grad, merge, blocks, block_sums, grad_coarse):
+    wide = grad_coarse.shape[1]
+    low = jnp.dot(blocks[...], grad[...], preferred_element_type=f32).astype(bf16)
+    block_sums[...] = low
+    grad_coarse[...] = lax.dot_general(
+        low, merge[:wide, :], (((1,), (1,)), ((), ())), preferred_element_type=f32
+    )
+
+
+def skip_backward_kernel(grad, grad_wide, merge, widen, members, grad_skip):
+    wide = grad_wide.shape[1]
+    pooled = 0.25 * lax.dot_general(
+        grad_wide[...], widen[...], (((1,), (1,)), ((), ())), preferred_element_type=f32
+    )
+    high = pooled.astype(bf16)
+    rest = (pooled - high.astype(f32)).astype(bf16)
+    total = lax.dot_general(grad[...], merge[wide:, :], (((1,), (1,)), ((), ())), preferred_element_type=f32)
+    total = total + jnp.dot(members[...], high, preferred_element_type=f32)
+    grad_skip[...] = total + jnp.dot(members[...], rest, preferred_element_type=f32)
 
 
 def mlp_backward_kernel(
@@ -312,20 +361,72 @@
     return pl.BlockSpec(array.shape, lambda i: (0, 0), pipeline_mode=pl.Buffered(1))
 
 
-def mlp_forward(mixed, source, sea, scales, up, up_bias, down, down_bias):
+def by_rows(parts, array):
+    return tall(array.shape[0] // parts, array.shape[1])
+
+
+def mlp_forward(mixed, source, sea, scales, up, up_bias, down, down_bias, pooling=()):
     pixels, channels = mixed.shape
     wide = up.shape[1]
     rows = math.gcd(pixels, 384)
+    parts = pixels // rows
+    shapes = [(pixels, width) for width in (channels, wide, wide, channels)]
+    if pooling:
+        shapes += [(pixels // 4, channels), (pixels // 4, pooling[1].shape[1])]
+    outs = [jax.ShapeDtypeStruct(shape, bf16) for shape in shapes]
     return pl.pallas_call(
         functools.partial(mlp_forward_kernel, 512),
-        grid=(pixels // rows,),
-        in_specs=[tall(rows, channels), tall(rows, channels), tall(rows, lanes)]
-        + [fixed(array) for array in (scales, up, up_bias, down, down_bias)],
-        out_specs=[tall(rows, channels), tall(rows, wide), tall(rows, wide), tall(rows, channels)],
-        out_shape=[jax.ShapeDtypeStruct((pixels, width), bf16) for width in (channels, wide, wide, channels)],
+        grid=(parts,),
+        in_specs=[by_rows(parts, array) for array in (mixed, source, sea)]
+        + [fixed(array) for array in (scales, up, up_bias, down, down_bias, *pooling)],
+        out_specs=[by_rows(parts, out) for out in outs],
+        out_shape=outs,
         compiler_params=room,
         name="mlp_forward",
-    )(mixed, source, sea, scales, up, up_bias, down, down_bias)
+    )(mixed, source, sea, scales, up, up_bias, down, down_bias, *pooling)
+
+
+def merge_forward(coarse, skip, merge, bias, members, parts):
+    merged = jax.ShapeDtypeStruct(skip.shape, bf16)
+    return pl.pallas_call(
+        merge_forward_kernel,
+        grid=(parts,),
+        in_specs=[by_rows(parts, array) for array in (coarse, skip)]
+        + [fixed(array) for array in (merge, bias, members)],
+        out_specs=by_rows(parts, merged),
+        out_shape=merged,
+        compiler_params=room,
+        name="merge_forward",
+    )(coarse, skip, merge, bias, members)
+
+
+def merge_backward(grad, merge, blocks, wide, parts):
+    pixels, channels = grad.shape
+    block_sums = jax.ShapeDtypeStruct((pixels // 4, channels), bf16)
+    grad_coarse = jax.ShapeDtypeStruct((pixels // 4, wide), f32)
+    return pl.pallas_call(
+        merge_backward_kernel,
+        grid=(parts,),
+        in_specs=[by_rows(parts, grad), fixed(merge), fixed(blocks)],
+        out_specs=[by_rows(parts, block_sums), by_rows(parts, grad_coarse)],
+        out_shape=[block_sums, grad_coarse],
+        compiler_params=room,
+        name="merge_backward",
+    )(grad, merge, blocks)
+
+
+def skip_backward(grad, grad_wide, merge, widen, members, parts):
+    grad_skip = jax.ShapeDtypeStruct(grad.shape, f32)
+    return pl.pallas_call(
+        skip_backward_kernel,
+        grid=(parts,),
+        in_specs=[by_rows(parts, array) for array in (grad, grad_wide)]
+        + [fixed(array) for array in (merge, widen, members)],
+        out_specs=by_rows(parts, grad_skip),
+        out_shape=grad_skip,
+        compiler_params=room,
+        name="skip_backward",
+    )(grad, grad_wide, merge, widen, members)
 
 
 def mlp_backward(upstream, mixed, slope, sea, scales, up, down):
@@ -427,20 +528,93 @@
     return jnp.concatenate([take(got, own ^ place) for place in range(count)], axis=0)
 
 
-def sum_group(pair):
-    tiles, columns = lax.axis_size("lat"), lax.axis_size("lon") // 2
-    tile, place = lax.axis_index("lat"), lax.axis_index("lon")
-    core, column = place % 2, place // 2
+def kept_and_sent(array, bit):
+    pieces = array.reshape(2, -1, lanes)
+    return take(pieces, bit), take(pieces, 1 - bit)
+
+
+def low_sum(kept, got):
+    return (kept.astype(f32) + got.astype(f32)).astype(bf16)
+
+
+def in_order(bit, own, other):
+    return jnp.where(bit == 0, jnp.concatenate([own, other]), jnp.concatenate([other, own]))
+
+
+def reduce_over_cores(pair):
+    unit = 16 * lax.axis_size("lat") * lax.axis_size("lon") // 2
     rows = pair.shape[1]
-    padded = -(-rows // (8 * tiles * columns)) * 8 * tiles * columns
-    pair = jnp.pad(pair, ((0, 0), (0, padded - rows), (0, 0)))
-    got = swap(take(pair, 1 - core), "lon", 1)
-    half = (take(pair, core).astype(f32) + got.astype(f32)).astype(bf16)
-    share = exchange_add(half.reshape(tiles, -1, lanes), "lat", tile, 1)
-    share = exchange_add(share.reshape(columns, -1, lanes), "lon", column, 2)
-    share = exchange_all(share, "lon", column, 2, columns)
-    half = exchange_all(share, "lat", tile, 1, tiles)
-    return half, swap(half, "lon", 1)
+    pair = jnp.pad(pair, ((0, 0), (0, -rows % unit), (0, 0)))
+    core = lax.axis_index("lon") % 2
+    return low_sum(take(pair, core), swap(take(pair, 1 - core), "lon", 1))
+
+
+def reduce_first(half):
+    tile = lax.axis_index("lat")
+    parts = []
+    for share, step in zip((half[: half.shape[0] // 2], half[half.shape[0] // 2 :]), (1, 2)):
+        kept, sent = kept_and_sent(share, tile // step % 2)
+        parts.append((kept, swap(sent, "lat", step)))
+    return [low_sum(kept, got) for kept, got in parts]
+
+
+def reduce_second(shares):
+    tile = lax.axis_index("lat")
+    parts = []
+    for share, step in zip(shares, (2, 1)):
+        kept, sent = kept_and_sent(share, tile // step % 2)
+        parts.append((kept, swap(sent, "lat", step)))
+    return jnp.stack([low_sum(kept, got) for kept, got in parts])
+
+
+def reduce_columns(shares):
+    columns = lax.axis_size("lon") // 2
+    column = lax.axis_index("lon") // 2
+    pieces = shares.reshape(shares.shape[0], columns, -1, lanes).swapaxes(0, 1)
+    return exchange_add(pieces, "lon", column, 2)
+
+
+def spread_columns(share):
+    columns = lax.axis_size("lon") // 2
+    column = lax.axis_index("lon") // 2
+    got = jnp.stack([share] + [swap(share, "lon", 2 * step) for step in range(1, columns)])
+    whole = jnp.stack([take(got, column ^ place) for place in range(columns)], axis=1)
+    return whole.reshape(share.shape[0], -1, lanes)
+
+
+def spread_second(shares):
+    tile = lax.axis_index("lat")
+    return [
+        in_order(tile // step % 2, share, swap(share, "lat", step)) for share, step in zip(shares, (2, 1))
+    ]
+
+
+def spread_first(shares):
+    tile = lax.axis_index("lat")
+    parts = [
+        in_order(tile // step % 2, share, swap(share, "lat", step)) for share, step in zip(shares, (1, 2))
+    ]
+    return jnp.concatenate(parts)
+
+
+def reduce_tiles(half):
+    tiles = lax.axis_size("lat")
+    return exchange_add(half.reshape(tiles, -1, lanes), "lat", lax.axis_index("lat"), 1)[None]
+
+
+def spread_tiles(share):
+    return exchange_all(share[0], "lat", lax.axis_index("lat"), 1, lax.axis_size("lat"))
+
+
+def group_stages():
+    two_by_two = lax.axis_size("lat") == 4
+    return (
+        [reduce_over_cores]
+        + ([reduce_first, reduce_second] if two_by_two else [reduce_tiles])
+        + [reduce_columns, spread_columns]
+        + ([spread_second, spread_first] if two_by_two else [spread_tiles])
+        + [lambda half: (half, swap(half, "lon", 1))]
+    )
 
 
 def sum_small(flat):
@@ -461,9 +635,9 @@
     return lax.dot_general(former, latter, (((1,), (1,)), ((), ())), preferred_element_type=f32)
 
 
-def block_forward(source, params, sea, ocean, dates):
-    kernel, gain, shift, up, up_bias, down, down_bias = params
-    height, breadth, channels = source.shape
+def block_mix(source, params, sea, ocean, dates):
+    kernel, gain, shift = params[:3]
+    channels = source.shape[2]
     taps = kernel.astype(f32).reshape(49, channels)
     edges = borders(source, dates)
     mixed, local = stencil_forward(source, edges, taps, sea)
@@ -471,8 +645,14 @@
     mean = first / ocean
     factor = lax.rsqrt(square / ocean - mean * mean + epsilon)
     scales = jnp.stack([mean, factor, gain.astype(f32), shift.astype(f32)])
-    mixed = mixed.reshape(-1, channels)
-    output, active, slope, normed = mlp_forward(
+    return source, edges, taps, mixed.reshape(-1, channels), scales, ocean
+
+
+def block_forward(mix, params, sea, pooling=()):
+    source, edges, taps, mixed, scales, ocean = mix
+    up, up_bias, down, down_bias = params[3:]
+    channels = source.shape[2]
+    output, active, slope, normed, *coarse = mlp_forward(
         mixed,
         source.reshape(-1, channels),
         sea.reshape(-1, lanes),
@@ -481,32 +661,32 @@
         up_bias.astype(f32)[None],
         down,
         down_bias.astype(f32)[None],
+        pooling,
     )
-    return output, (source, edges, taps, mixed, scales, ocean, normed, slope, active)
-
-
-def block_backward(upstream, params, sea, stored, dates):
-    kernel, gain, shift, up, up_bias, down, down_bias = params
-    source, edges, taps, mixed, scales, ocean, normed, slope, active = stored
+    return output, coarse, mix + (normed, slope, active)
+
+
+def block_hidden(upstream, params, sea, stored):
+    scales, mixed, slope = stored[4], stored[3], stored[7]
+    return mlp_backward(upstream, mixed, slope, sea.reshape(-1, lanes), scales, params[3], params[5])
+
+
+def block_norm(grad_normed, local, sea, stored, dates):
+    source, edges, taps, mixed, scales, ocean = stored[:6]
     channels = source.shape[2]
-    grad_branch, grad_hidden, grad_normed, local, down_sums, up_sums = mlp_backward(
-        upstream, mixed, slope, sea.reshape(-1, lanes), scales, up, down
-    )
     grad_shift, grad_gain = sum_all(local)
     mean, factor, gain = scales[0], scales[1], scales[2]
     unit = (mixed - mean) * factor
     weight = spread(sea.reshape(-1, lanes), channels) / ocean
     grad_mixed = factor * (gain * grad_normed - weight * (gain * grad_shift + unit * (gain * grad_gain)))
     grad_mixed = grad_mixed.astype(bf16).reshape(source.shape)
-    grad_edges = borders(grad_mixed, dates)
-    grad_kernel = kernel_grad(source, edges, grad_mixed)
-    grad_source, source_sums = stencil_backward(grad_mixed, grad_edges, taps, sea, upstream.reshape(source.shape))
-    return (
-        grad_source.reshape(-1, channels),
-        source_sums,
-        (grad_gain, grad_shift, (grad_branch, normed, active, grad_hidden)),
-        (grad_kernel, down_sums, up_sums),
-    )
+    return grad_mixed, borders(grad_mixed, dates), grad_gain, grad_shift
+
+
+def block_source(grad_mixed, grad_edges, upstream, sea, stored):
+    source, taps = stored[0], stored[2]
+    grad_source, sums = stencil_backward(grad_mixed, grad_edges, taps, sea, upstream.reshape(source.shape))
+    return grad_source.reshape(-1, source.shape[2]), sums
 
 
 def shards(
@@ -539,85 +719,112 @@
     decode_down,
     decode_down_bias,
 ):
-    (encode_up, encode_down, widen_weight, bottle_up, bottle_down, merge_weight, decode_up, decode_down) = (
-        lax.all_gather(weight, "lat", axis=0, tiled=True)
-        for weight in (
-            encode_up,
-            encode_down,
-            widen_weight,
-            bottle_up,
-            bottle_down,
-            merge_weight,
-            decode_up,
-            decode_down,
-        )
-    )
-    dates = fine_map.shape[0]
-    fine = to_dates(fine_map)
-    ocean_band = to_dates(ocean_mask).astype(f32)
-    upstream = to_dates(out_grad)
-    height, breadth, channels = fine.shape
+    dates, tile_rows, breadth, channels = fine_map.shape
+    wide = bottle_depth.shape[2]
+    extra = jnp.swapaxes(ocean_mask, 1, 2).astype(bf16)[:, None]
+    extra = jnp.pad(extra, ((0, 0), (0, 0), (0, 0), (0, channels - tile_rows)))
+    packed = to_dates(jnp.concatenate([fine_map, extra], axis=1)).reshape(dates, tile_rows + 1, breadth, channels)
+    fine = packed[:, :tile_rows].reshape(-1, breadth, channels)
+    ocean_band = jnp.swapaxes(packed[:, tile_rows, :, :tile_rows], 1, 2).reshape(-1, breadth).astype(f32)
+    height = fine.shape[0]
     half_height, half_breadth = height // 2, breadth // 2
-    wide = widen_weight.shape[1]
+
+    encode_rows = encode_up.size // channels
+    encode_pack = jnp.concatenate([encode_up.reshape(-1, channels), encode_down])
+    encode_pack = gathered(encode_pack).reshape(lax.axis_size("lat"), -1, channels)
+    encode_up = encode_pack[:, :encode_rows].reshape(channels, -1)
+    encode_down = encode_pack[:, encode_rows:].reshape(-1, channels)
+    bottle_up = lax.all_gather(bottle_up, "lat", axis=0, tiled=True)
+    bottle_down = lax.all_gather(bottle_down, "lat", axis=0, tiled=True)
+    decode_rows = decode_down.shape[0]
+    decode_pack = lax.all_gather(jnp.concatenate([decode_down, merge_weight]), "lat", axis=0, tiled=False)
+    decode_down = decode_pack[:, :decode_rows].reshape(-1, channels)
+    merge_weight = decode_pack[:, decode_rows:].reshape(-1, channels)
+    decode_up = lax.all_gather(decode_up, "lat", axis=0, tiled=True)
+
     coarse_band = jnp.max(ocean_band.reshape(half_height, 2, half_breadth, 2), axis=(1, 3))
     sea_fine = jnp.broadcast_to(ocean_band[..., None], (height, breadth, lanes))
     sea_coarse = jnp.broadcast_to(coarse_band[..., None], (half_height, half_breadth, lanes))
     encode = (encode_depth, encode_gain, encode_shift, encode_up, encode_up_bias, encode_down, encode_down_bias)
     bottle = (bottle_depth, bottle_gain, bottle_shift, bottle_up, bottle_up_bias, bottle_down, bottle_down_bias)
     decode = (decode_depth, decode_gain, decode_shift, decode_up, decode_up_bias, decode_down, decode_down_bias)
-    merge_upper = merge_weight[:wide]
-    merge_lower = merge_weight[wide:]
     ocean_fine = jnp.sum(ocean_band)
     ocean_coarse = jnp.sum(coarse_band)
-
-    skip_rows, encode_stored = block_forward(fine, encode, sea_fine, ocean_fine, dates)
-    blocks = skip_rows.reshape(half_height, 2, half_breadth, 2, channels).astype(f32)
-    pooled = (jnp.sum(blocks, axis=(1, 3)) * 0.25).astype(bf16).reshape(-1, channels)
-    coarse_in = jnp.dot(pooled, widen_weight, preferred_element_type=f32) + widen_bias.astype(f32)
-    coarse_in = coarse_in.astype(bf16).reshape(half_height, half_breadth, wide)
-    coarse_low, coarse_stored = block_forward(coarse_in, bottle, sea_coarse, ocean_coarse, dates)
-    upper = jnp.dot(coarse_low, merge_upper, preferred_element_type=f32)
-    upper = upper.reshape(half_height, 1, half_breadth, 1, channels)
-    lower = jnp.dot(skip_rows, merge_lower, preferred_element_type=f32)
-    lower = lower.reshape(half_height, 2, half_breadth, 2, channels)
-    merged = (lower + upper).reshape(height, breadth, channels) + merge_bias.astype(f32)
-    decode_rows, decode_stored = block_forward(merged.astype(bf16), decode, sea_fine, ocean_fine, dates)
+    parts = height * breadth // math.gcd(height * breadth, 384)
+    pixel = np.arange(height * breadth // parts)
+    block = pixel // breadth // 2 * half_breadth + pixel % breadth // 2
+    members = jnp.asarray(block[:, None] == np.arange(pixel.size // 4), dtype=bf16)
+    blocks = jnp.asarray(np.arange(pixel.size // 4)[:, None] == block, dtype=bf16)
+
+    mix = block_mix(fine, encode, sea_fine, ocean_fine, dates)
+    widen_weight = gathered(after(widen_weight, mix[3]))
+    skip_rows, (pooled, coarse_in), encode_stored = block_forward(
+        mix, encode, sea_fine, (blocks, widen_weight, widen_bias.astype(f32)[None])
+    )
+    coarse_in = coarse_in.reshape(half_height, half_breadth, wide)
+    mix = block_mix(coarse_in, bottle, sea_coarse, ocean_coarse, dates)
+    coarse_low, _, coarse_stored = block_forward(mix, bottle, sea_coarse)
+    upstream = to_dates(after(out_grad, mix[3])).reshape(-1, channels)
+    merged = merge_forward(coarse_low, skip_rows, merge_weight, merge_bias.astype(f32)[None], members, parts)
+    mix = block_mix(merged.reshape(fine.shape), decode, sea_fine, ocean_fine, dates)
+    decode_rows, _, decode_stored = block_forward(mix, decode, sea_fine)
     result = from_dates(decode_rows.reshape(fine.shape), dates)
 
-    grad_merged, merge_sums, decode_grads, decode_small = block_backward(
-        upstream.reshape(-1, channels), decode, sea_fine, decode_stored, dates
-    )
-    grad_block_sum = jnp.sum(
-        grad_merged.astype(f32).reshape(half_height, 2, half_breadth, 2, channels), axis=(1, 3)
-    ).reshape(-1, channels)
-    grad_block_low = grad_block_sum.astype(bf16)
-    grad_merge_upper = cross_rows(grad_block_low, coarse_low)
-    grad_merge_lower = cross_rows(grad_merged, skip_rows)
-    grad_coarse = by_transpose(grad_block_low, merge_upper)
-    grad_skip_direct = by_transpose(grad_merged, merge_lower)
-    grad_wide, widen_sums, bottle_grads, bottle_small = block_backward(
-        grad_coarse, bottle, sea_coarse, coarse_stored, dates
-    )
-    early = [grad_merge_upper, grad_merge_lower]
-    for grad_branch, normed, active, grad_hidden in (decode_grads[2], bottle_grads[2]):
-        early += [cross_rows(normed, grad_hidden), cross_rows(grad_branch, active)]
+    grad_branch, grad_hidden, grad_normed, local, *decode_small = block_hidden(upstream, decode, sea_fine, decode_stored)
+    early = [
+        cross_rows(decode_stored[6], grad_hidden),
+        cross_rows(grad_branch, decode_stored[8]),
+    ]
+    grad_mixed, grad_edges, *decode_norm = block_norm(grad_normed, local, sea_fine, decode_stored, dates)
+    decode_kernel = kernel_grad(*decode_stored[:2], grad_mixed)
+    grad_merged, merge_sums = block_source(grad_mixed, grad_edges, upstream, sea_fine, decode_stored)
+
+    block_sums, grad_coarse = merge_backward(grad_merged, merge_weight, blocks, wide, parts)
+    early += [cross_rows(block_sums, coarse_low), cross_rows(grad_merged, skip_rows)]
     early = lax.psum([part.astype(bf16) for part in early], both)
     early = [total.astype(f32) for total in early]
-    merge_sum = jnp.concatenate(early[:2], axis=1).T
-    decode_up_sum, decode_down_sum, bottle_up_sum, bottle_down_sum = early[2], early[3].T, early[4], early[5].T
+    decode_up_sum, decode_down_sum = early[0], early[1].T
+    merge_sum = jnp.concatenate(early[2:], axis=1).T
+
+    stages = group_stages()
+    grad_branch, grad_hidden, grad_normed, local, *bottle_small = block_hidden(
+        grad_coarse, bottle, sea_coarse, coarse_stored
+    )
+    pair = weight_grads(grad_branch, coarse_stored[6], coarse_stored[8], grad_hidden).reshape(2, -1, lanes)
+    grad_mixed, grad_edges, *bottle_norm = block_norm(grad_normed, local, sea_coarse, coarse_stored, dates)
+    bottle_kernel = kernel_grad(*coarse_stored[:2], grad_mixed)
+    state = stages[0](pair)
+    grad_mixed = after(grad_mixed, state)
+    grad_wide, widen_sums = block_source(grad_mixed, grad_edges, grad_coarse, sea_coarse, coarse_stored)
+    grad_skip = skip_backward(grad_merged, grad_wide, merge_weight, widen_weight, members, parts)
+
+    grad_branch, grad_hidden, grad_normed, local, *encode_small = block_hidden(
+        grad_skip, encode, sea_fine, encode_stored
+    )
+    state = stages[1](state)
+    grad_hidden = after(grad_hidden, state)
+    encode_pair = weight_grads(grad_branch, encode_stored[6], encode_stored[8], grad_hidden).reshape(2, -1, lanes)
+    grad_mixed, grad_edges, *encode_norm = block_norm(grad_normed, local, sea_fine, encode_stored, dates)
+    if len(stages) > 6:
+        state = stages[2](state)
+        grad_mixed = after(grad_mixed, state)
+    encode_kernel = kernel_grad(*encode_stored[:2], grad_mixed)
+    grad_fine, _ = block_source(grad_mixed, grad_edges, grad_skip, sea_fine, encode_stored)
+    for stage in stages[-5:]:
+        state = stage(state)
     core = (lax.axis_index("lon") % 2).astype(jnp.int32)[None]
+    bottle_up_sum, bottle_down_sum = unpack(core, *state, wide, bottle_up.shape[1])
+    bottle_down_sum = bottle_down_sum.T
+
     grad_widen = cross_rows(pooled, grad_wide).astype(bf16)
     widen_tiles = pl.cdiv(wide, 2 * lanes)
     grad_widen = jnp.pad(grad_widen, ((0, 0), (0, 2 * widen_tiles * lanes - wide)))
     grad_widen = grad_widen.reshape(channels, 2, widen_tiles, lanes).transpose(1, 2, 0, 3).reshape(2, -1, lanes)
-    grad_pooled = by_transpose(grad_wide, widen_weight).reshape(half_height, 1, half_breadth, 1, channels) * 0.25
-    grad_skip = grad_skip_direct.reshape(half_height, 2, half_breadth, 2, channels) + grad_pooled
-    grad_fine, _, encode_grads, encode_small = block_backward(
-        grad_skip.reshape(-1, channels), encode, sea_fine, encode_stored, dates
-    )
     fine_grad = from_dates(grad_fine.reshape(fine.shape), dates)
-    encode_pair = weight_grads(*encode_grads[2]).reshape(2, -1, lanes)
-    own, other = sum_group(jnp.concatenate([encode_pair, grad_widen], axis=1))
+    state = jnp.concatenate([encode_pair, grad_widen], axis=1)
+    for stage in stages:
+        state = stage(state)
+    own, other = state
     encode_up_sum, encode_down_sum = unpack(core, own, other, channels, encode_up.shape[1])
     encode_down_sum = encode_down_sum.T
     start = encode_pair.shape[1]
@@ -626,8 +833,8 @@
     widen_sum = jnp.stack([lower, upper]).reshape(2 * widen_tiles, channels, lanes).astype(f32)
     widen_sum = widen_sum.transpose(1, 0, 2).reshape(channels, -1)[:, :wide]
 
-    kernels = [encode_small[0], bottle_small[0], decode_small[0]]
-    rows = [encode_small[1:], (widen_sums,), bottle_small[1:], (merge_sums,), decode_small[1:]]
+    kernels = [encode_kernel, bottle_kernel, decode_kernel]
+    rows = [encode_small, (widen_sums,), bottle_small, (merge_sums,), decode_small]
     rows = [row for group in rows for row in group]
     padded = [jnp.pad(row, ((0, 0), (0, -row.shape[1] % lanes))) for row in rows]
     line = jnp.concatenate(padded, axis=1)
@@ -657,8 +864,8 @@
         result,
         fine_grad,
         kernel_sums[0],
-        encode_grads[0],
-        encode_grads[1],
+        encode_norm[0],
+        encode_norm[1],
         encode_up_sum,
         encode_upb,
         encode_down_sum,
@@ -666,8 +873,8 @@
         widen_sum,
         widen_b,
         kernel_sums[1],
-        bottle_grads[0],
-        bottle_grads[1],
+        bottle_norm[0],
+        bottle_norm[1],
         bottle_up_sum,
         bottle_upb,
         bottle_down_sum,
@@ -675,8 +882,8 @@
         merge_sum,
         bottle_merge_b,
         kernel_sums[2],
-        decode_grads[0],
-        decode_grads[1],
+        decode_norm[0],
+        decode_norm[1],
         decode_up_sum,
         decode_upb,
         decode_down_sum,

time: 752 us -> 885 us (1.18)
  waiting for transfers between devices: 183 us -> 236 us
  Pallas kernels: 209 us -> 258 us
  other arithmetic: 69.2 us -> 103 us
  starting transfers between devices: 95.6 us -> 128 us
  matrix products: 42.2 us -> 16 us
  blocking collectives: 31.9 us -> 11.2 us
  local copies, waits for them, and re-layouts: 96 us -> 107 us
    ppermute x14 -> x38, waiting for transfers between devices: 52.7 us -> 134 us  [swap(): lax.ppermute(array, axis, [(i, i ^ step) for i in range(lax.axis_size(axi...]
    all_gather x2 -> x0, blocking collectives: 31.9 us -> none  [shards(): lax.all_gather(weight, 'lat', axis=0, tiled=True)]
    psum x1, waiting for transfers between devices: 31.8 us -> 0.01 us  [shards(): early = lax.psum([part.astype(bf16) for part in early], both)]
    ppermute x14 -> x38, starting transfers between devices: 20.6 us -> 49.8 us  [swap(): lax.ppermute(array, axis, [(i, i ^ step) for i in range(lax.axis_size(axi...]
    all_to_all x6 -> x5, waiting for transfers between devices: 36.8 us -> 14.6 us  [sum_all(): return jnp.sum(lax.all_to_all(copies, both, 0, 0, tiled=False), axis=0)]
    concatenate x1 -> x4, other arithmetic: 1.89 us -> 23 us  [the longest x2 20.7 us: spread_first(): return jnp.concatenate(parts)]
    pallas_call x3 -> x6, Pallas kernels: 38.8 us -> 59 us  [the longest x3 40.9 us: mlp_forward(): pl.pallas_call(functools.partial(mlp_forward_kernel, 512), grid=(parts,),...]
    select_n x0 -> x8, other arithmetic: none -> 19.7 us  [in_order(): jnp.where(bit == 0, jnp.concatenate([own, other]), jnp.concatenate([other...]
  transfers between devices with their start and end apart: 56 -> 74, of which waited for: 18 -> 32; matrix products, arithmetic and copies ran while one was open for 23% -> 23% of each run, Pallas kernels for 21% -> 19%
where the time goes in v6:
time: 885 us; the launch traced here: 876 us
  Pallas kernels  258 us (29%)
  waiting for transfers between devices  236 us (27%)
  starting transfers between devices  128 us (14%)
  local copies, waits for them, and re-layouts  107 us (12%)
  other arithmetic  103 us (12%)
  matrix products  16 us (2%)
  between operations  15.8 us (2%)
  blocking collectives  11.2 us (1%)
    ppermute x38, waiting for transfers between devices, swap(): lax.ppermute(array, axis, [(i, i ^ step) for i in range(lax.axis_size(axi...  134 us
    ppermute x38, starting transfers between devices, swap(): lax.ppermute(array, axis, [(i, i ^ step) for i in range(lax.axis_size(axi...  49.8 us
    pallas_call x3, Pallas kernels, mlp_forward(): pl.pallas_call(functools.partial(mlp_forward_kernel, 512), grid=(parts,),...  40.9 us
    pallas_call x3, Pallas kernels, stencil_backward(): pl.pallas_call(functools.partial(stencil_backward_kernel, len(edges)), gr...  39.3 us
    pallas_call x3, Pallas kernels, stencil_forward(): pl.pallas_call(functools.partial(stencil_forward_kernel, len(edges)), gri...  38.5 us
    pallas_call x3, Pallas kernels, mlp_backward(): pl.pallas_call(functools.partial(mlp_backward_kernel, 512), grid=(pixels...  37.2 us
    pallas_call x3, Pallas kernels, kernel_grad(): pl.pallas_call(functools.partial(kernel_grad_kernel, len(edges)), grid=(t...  33.1 us
    pallas_call x2, Pallas kernels, unpack(): pl.pallas_call(unpack_kernel, grid_spec=pltpu.PrefetchScalarGridSpec(num_...  28.3 us
  transfers between devices with their start and end apart: 74, of which 32 were waited for; matrix products, arithmetic and copies ran while one was open for 23% of the time, Pallas kernels for 19%

profile of v6, /device:TPU:0, one launch (start us, length us, event | category | flops | bytes accessed | tf_op | source)
XLA Modules:
  0.0 875.7 jit_solution(3624898630482895973)
XLA Ops:
  19.1 15.1 %collective-permute-done.2 = bf16[13,32,400]{2,1,0:T(8,128)(2,1)S(1)} collective-permute-done((bf16[13,32,400]{2,1,0:T(8,128)(2,1)}, bf16[13,32,400]{2,1,0:T(8,128)(2,1)S(1)}, u32[]{:S(2)}, u32[]{:S(2)}) %collective-permute-start.2) | collective-permute-done | bytes 332832 | tf_op jit(solution)/shard_map/ppermute | solution.py:31
  34.2 9.0 %collective-permute-done.1 = bf16[13,32,400]{2,1,0:T(8,128)(2,1)} collective-permute-done((bf16[13,32,400]{2,1,0:T(8,128)(2,1)S(1)}, bf16[13,32,400]{2,1,0:T(8,128)(2,1)}, u32[]{:S(2)}, u32[]{:S(2)}) %collective-permute-start.1) | collective-permute-done | bytes 332832 | tf_op jit(solution)/shard_map/ppermute | solution.py:31
  53.9 15.0 %stencil_forward.3 = (f32[48,32,400]{2,1,0:T(8,128)}, f32[2,400]{1,0:T(2,128)}) custom-call(bf16[48,32,400]{2,1,0:T(8,128)(2,1)} %bitcast.306, bf16[48,3,400]{2,1,0:T(4,128)(2,1)} %copy-done.30, bf16[48,3,400]{2,1,0:T(4,128)(2,1)} %copy-done.31, f32[49,400]{1,0:T(8,128)} %reshape.400.refs_2_, f32[48,32,128]{2,1,0:T(8,128)} %broadcast_in_dim.125.refs_3_), custom_call_target="tpu_custom_call" | custom-call | tf_op jit(solution)/shard_map/stencil_forward/pallas_call | solution.py:197
  83.2 6.6 all-to-all-start
  89.7 38.7 %collective-permute-done.9 = bf16[100,800]{1,0:T(8,128)(2,1)S(1)} collective-permute-done((bf16[100,800]{1,0:T(8,128)(2,1)}, bf16[100,800]{1,0:T(8,128)(2,1)S(1)}, u32[]{:S(2)}, u32[]{:S(2)}) %collective-permute-start.9) | collective-permute-done | bytes 160032 | tf_op jit(solution)/shard_map/ppermute | solution.py:510
  141.4 5.5 concatenate.110
  159.5 14.8 %mlp_forward.3 = (bf16[1536,400]{1,0:T(8,128)(2,1)}, bf16[1536,1600]{1,0:T(8,128)(2,1)}, bf16[1536,1600]{1,0:T(8,128)(2,1)}, bf16[1536,400]{1,0:T(8,128)(2,1)}, ...) custom-call(f32[1536,400]{1,0:T(8,128)} %bitcast.312, bf16[1536,400]{1,0:T(8,128)(2,1)} %bitcast.307, ...), custom_call_target="tpu_custom_call" | custom-call | tf_op jit(solution)/shard_map/mlp_forward/pallas_call | solution.py:377
  184.7 8.5 stencil_forward.4
  207.8 6.7 all-to-all-done.1
  219.0 26.7 %all-gather.10.cloned.1.call-done.down = bf16[3200,800]{1,0:T(8,128)(2,1)} async-done(((bf16[800,800]{1,0:T(8,128)(2,1)}), bf16[3200,800]{1,0:T(8,128)(2,1)}) %all-gather.10.cloned.1.call-update) | async-done | bytes 5120016 | tf_op jit(solution)/shard_map/all_gather | solution.py:738
  246.6 13.5 %mlp_forward.4 = (bf16[384,800]{1,0:T(8,128)(2,1)}, bf16[384,3200]{1,0:T(8,128)(2,1)}, bf16[384,3200]{1,0:T(8,128)(2,1)}, bf16[384,800]{1,0:T(8,128)(2,1)}) custom-call(f32[384,800]{1,0:T(8,128)} %bitcast.332, bf16[384,800]{1,0:T(8,128)(2,1)} %get-tuple-element.83.source, f32[384,128]{1,0:T(8,128)} %broadcast_in_dim.135.sea, ...), custom_call_target="tpu_custom_call" | custom-call | tf_op jit(solution)/shard_map/mlp_forward/pallas_call | solution.py:377
  260.1 6.1 merge_forward.1.source
  276.1 14.9 %stencil_forward.5 = (f32[48,32,400]{2,1,0:T(8,128)}, f32[2,400]{1,0:T(2,128)}) custom-call(bf16[48,32,400]{2,1,0:T(8,128)(2,1)} %bitcast.310, bf16[48,3,400]{2,1,0:T(4,128)(2,1)} %copy-done.32, bf16[48,3,400]{2,1,0:T(4,128)(2,1)} %copy-done.33, f32[49,400]{1,0:T(8,128)} %reshape.415.refs_2_, f32[48,32,128]{2,1,0:T(8,128)} %broadcast_in_dim.125.refs_3_), custom_call_target="tpu_custom_call" | custom-call | tf_op jit(solution)/shard_map/stencil_forward/pallas_call | solution.py:197
  308.2 12.6 %mlp_forward.5 = (bf16[1536,400]{1,0:T(8,128)(2,1)}, bf16[1536,1600]{1,0:T(8,128)(2,1)}, bf16[1536,1600]{1,0:T(8,128)(2,1)}, bf16[1536,400]{1,0:T(8,128)(2,1)}) custom-call(f32[1536,400]{1,0:T(8,128)} %bitcast.315, bf16[1536,400]{1,0:T(8,128)(2,1)} %merge_forward.1.source, f32[1536,128]{1,0:T(8,128)} %broadcast_in_dim.126.sea, ...), custom_call_target="tpu_custom_call" | custom-call | tf_op jit(solution)/shard_map/mlp_forward/pallas_call | solution.py:377
  320.8 12.0 %mlp_backward.3 = (bf16[1536,400]{1,0:T(8,128)(2,1)}, bf16[1536,1600]{1,0:T(8,128)(2,1)}, f32[1536,400]{1,0:T(8,128)}, f32[2,400]{1,0:T(2,128)}, f32[1,400]{1,0:T(1,128)}, /*index=5*/f32[1,1600]{1,0:T(1,128)}) custom-call(bf16[1536,400]{1,0:T(8,128)(2,1)} %bitcast.330, f32[1536,400]{1,0:T(8,128)} %bitcast.316, bf16[1536,1600]{1,0:T(8,128)(2,1)} %get-tuple-element.92.slope, ...), custom_call_target="tpu_custom_call" | custom-call | tf_op jit(solution)/shard_map/mlp_backward/pallas_call | solution.py:437
  333.5 11.2 %all_to_all.40 = f32[32,2,400]{2,1,0:T(2,128)S(1)} all-to-all(f32[32,2,400]{2,1,0:T(2,128)S(1)} %broadcast_in_dim.148), channel_id=1, replica_groups=mesh['lat'=4,'lon'=8] {'lat','lon'}, dimensions={0} | all-to-all | bytes 204800 | tf_op jit(solution)/shard_map/all_to_all | solution.py:86
  358.4 15.1 %stencil_backward.3 = (bf16[48,32,400]{2,1,0:T(8,128)(2,1)}, f32[1,400]{1,0:T(1,128)}) custom-call(bf16[48,32,400]{2,1,0:T(8,128)(2,1)} %bitcast.318, bf16[48,3,400]{2,1,0:T(4,128)(2,1)} %copy-done.40, bf16[48,3,400]{2,1,0:T(4,128)(2,1)} %copy-done.41, f32[49,400]{1,0:T(8,128)} %reshape.415.refs_2_, f32[48,32,128]{2,1,0:T(8,128)} %broadcast_in_dim.125.refs_3_, ...), custom_call_target="tpu_custom_call" | custom-call | tf_op jit(solution)/shard_map/stencil_backward/pallas_call | solution.py:213
  373.5 5.0 merge_backward.1
  378.4 13.0 %mlp_backward.4 = (bf16[384,800]{1,0:T(8,128)(2,1)}, bf16[384,3200]{1,0:T(8,128)(2,1)}, f32[384,800]{1,0:T(8,128)}, f32[2,800]{1,0:T(2,128)}, f32[1,800]{1,0:T(1,128)}, /*index=5*/f32[1,3200]{1,0:T(1,128)}) custom-call(f32[384,800]{1,0:T(8,128)} %get-tuple-element.96.upstream, f32[384,800]{1,0:T(8,128)} %bitcast.333, ...), custom_call_target="tpu_custom_call" | custom-call | tf_op jit(solution)/shard_map/mlp_backward/pallas_call | solution.py:437
  391.4 11.2 %weight_grads.2 = bf16[2,25,800,128]{3,2,1,0:T(8,128)(2,1)} custom-call(bf16[384,800]{1,0:T(8,128)(2,1)} %get-tuple-element.100.grad_branch, bf16[384,800]{1,0:T(8,128)(2,1)} %get-tuple-element.101.normed, bf16[384,3200]{1,0:T(8,128)(2,1)} %get-tuple-element.102.active, bf16[384,3200]{1,0:T(8,128)(2,1)} %get-tuple-element.103.grad_hidden), custom_call_target="tpu_custom_call" | custom-call | tf_op jit(solution)/shard_map/weight_grads/pallas_call | solution.py:473
  402.6 6.3 fusion.4
  418.4 6.6 convolution_convert_fusion.1
  428.5 12.6 %kernel_grad.5 = f32[4,56,128]{2,1,0:T(8,128)} custom-call(bf16[48,32,400]{2,1,0:T(8,128)(2,1)} %bitcast.311, bf16[48,3,400]{2,1,0:T(4,128)(2,1)} %copy-done.32, bf16[48,3,400]{2,1,0:T(4,128)(2,1)} %copy-done.33, bf16[48,32,400]{2,1,0:T(8,128)(2,1)} %bitcast.319), custom_call_target="tpu_custom_call" | custom-call | tf_op jit(solution)/shard_map/kernel_grad/pallas_call | solution.py:229
  450.4 5.1 all-to-all-done.4
  461.2 7.7 kernel_grad.4
  469.0 5.1 fusion
  476.5 8.8 %stencil_backward.4 = (bf16[24,16,800]{2,1,0:T(8,128)(2,1)}, f32[1,800]{1,0:T(1,128)}) custom-call(bf16[24,16,800]{2,1,0:T(8,128)(2,1)} %bitcast.341, bf16[24,3,800]{2,1,0:T(4,128)(2,1)} %copy-done.46, bf16[24,3,800]{2,1,0:T(4,128)(2,1)} %copy-done.47, f32[49,800]{1,0:T(8,128)} %reshape.408.refs_2_, f32[24,16,128]{2,1,0:T(8,128)} %broadcast_in_dim.134.refs_3_, ...), custom_call_target="tpu_custom_call" | custom-call | tf_op jit(solution)/shard_map/stencil_backward/pallas_call | solution.py:213
  485.3 7.0 skip_backward.1.upstream
  492.4 12.3 %mlp_backward.5 = (bf16[1536,400]{1,0:T(8,128)(2,1)}, bf16[1536,1600]{1,0:T(8,128)(2,1)}, f32[1536,400]{1,0:T(8,128)}, f32[2,400]{1,0:T(2,128)}, f32[1,400]{1,0:T(1,128)}, /*index=5*/f32[1,1600]{1,0:T(1,128)}) custom-call(f32[1536,400]{1,0:T(8,128)} %skip_backward.1.upstream, f32[1536,400]{1,0:T(8,128)} %bitcast.313, ...), custom_call_target="tpu_custom_call" | custom-call | tf_op jit(solution)/shard_map/mlp_backward/pallas_call | solution.py:437
  527.7 12.7 %kernel_grad.3 = f32[4,56,128]{2,1,0:T(8,128)} custom-call(bf16[48,32,400]{2,1,0:T(8,128)(2,1)} %bitcast.308, bf16[48,3,400]{2,1,0:T(4,128)(2,1)} %copy-done.30, bf16[48,3,400]{2,1,0:T(4,128)(2,1)} %copy-done.31, bf16[48,32,400]{2,1,0:T(8,128)(2,1)} %bitcast.320), custom_call_target="tpu_custom_call" | custom-call | tf_op jit(solution)/shard_map/kernel_grad/pallas_call | solution.py:229
  546.2 7.7 collective-permute-done.31
  564.2 11.8 %weight_grads.3 = bf16[2,13,400,128]{3,2,1,0:T(8,128)(2,1)} custom-call(bf16[1536,400]{1,0:T(8,128)(2,1)} %get-tuple-element.118.grad_branch, bf16[1536,400]{1,0:T(8,128)(2,1)} %get-tuple-element.119.normed, bf16[1536,1600]{1,0:T(8,128)(2,1)} %get-tuple-element.120.active, bf16[1536,1600]{1,0:T(8,128)(2,1)} %get-tuple-element.122.grad_hidden), custom_call_target="tpu_custom_call" | custom-call | tf_op jit(solution)/shard_map/weight_grads/pallas_call | solution.py:473
  582.0 17.7 %collective-permute-done.50 = bf16[2528,128]{1,0:T(8,128)(2,1)S(1)} collective-permute-done((bf16[2528,128]{1,0:T(8,128)(2,1)S(1)}, bf16[2528,128]{1,0:T(8,128)(2,1)S(1)}, u32[]{:S(2)}, u32[]{:S(2)}) %collective-permute-start.50) | collective-permute-done | bytes 647200 | tf_op jit(solution)/shard_map/ppermute | solution.py:510
  611.5 12.1 %collective-permute-done.26.refs_0_ = bf16[48,3,400]{2,1,0:T(4,128)(2,1)S(1)} collective-permute-done((bf16[48,3,400]{2,1,0:T(4,128)(2,1)S(1)}, bf16[48,3,400]{2,1,0:T(4,128)(2,1)S(1)}, u32[]{:S(2)}, u32[]{:S(2)}) %collective-permute-start.26) | collective-permute-done | bytes 115232 | tf_op jit(solution)/shard_map/ppermute | solution.py:71
  624.3 15.3 %stencil_backward.5 = (bf16[48,32,400]{2,1,0:T(8,128)(2,1)}, f32[1,400]{1,0:T(1,128)}) custom-call(bf16[48,32,400]{2,1,0:T(8,128)(2,1)} %bitcast.322, bf16[48,3,400]{2,1,0:T(4,128)(2,1)} %copy-done.42, bf16[48,3,400]{2,1,0:T(4,128)(2,1)} %copy-done.43, f32[49,400]{1,0:T(8,128)} %reshape.400.refs_2_, f32[48,32,128]{2,1,0:T(8,128)} %broadcast_in_dim.125.refs_3_, ...), custom_call_target="tpu_custom_call" | custom-call | tf_op jit(solution)/shard_map/stencil_backward/pallas_call | solution.py:213
  646.7 16.8 %all-to-all-start.7 = ((f32[32,32,128]{2,1,0:T(8,128)}), f32[32,32,128]{2,1,0:T(8,128)}, u32[]{:S(2)}, u32[]{:S(2)}) async-start(f32[32,32,128]{2,1,0:T(8,128)} %broadcast_in_dim.151), calls=%async_computation.7 | async-start | bytes 1048576 | tf_op jit(solution)/shard_map/all_to_all | solution.py:627
  685.1 7.6 all-to-all-done.7
  696.7 9.7 %collective-permute-done.55 = bf16[2,632,128]{2,1,0:T(8,128)(2,1)} collective-permute-done((bf16[2,632,128]{2,1,0:T(8,128)(2,1)}, bf16[2,632,128]{2,1,0:T(8,128)(2,1)}, u32[]{:S(2)}, u32[]{:S(2)}) %collective-permute-start.55) | collective-permute-done | bytes 323616 | tf_op jit(solution)/shard_map/ppermute | solution.py:510
  714.7 8.8 %collective-permute-done.34 = bf16[1728,128]{1,0:T(8,128)(2,1)S(1)} collective-permute-done((bf16[1728,128]{1,0:T(8,128)(2,1)S(1)}, bf16[1728,128]{1,0:T(8,128)(2,1)S(1)}, u32[]{:S(2)}, u32[]{:S(2)}) %collective-permute-start.34) | collective-permute-done | bytes 442400 | tf_op jit(solution)/shard_map/ppermute | solution.py:510
  724.9 14.6 %collective-permute-done.36 = bf16[1728,128]{1,0:T(8,128)(2,1)S(1)} collective-permute-done((bf16[1728,128]{1,0:T(8,128)(2,1)S(1)}, bf16[1728,128]{1,0:T(8,128)(2,1)S(1)}, u32[]{:S(2)}, u32[]{:S(2)}) %collective-permute-start.36) | collective-permute-done | bytes 442400 | tf_op jit(solution)/shard_map/ppermute | solution.py:510
  752.5 5.9 collective-permute-done.39
  770.5 6.9 collective-permute-done.60
  777.4 9.0 %maximum_select_fusion.1 = bf16[10112,128]{1,0:T(8,128)(2,1)S(1)} fusion(bf16[5056,128]{1,0:T(8,128)(2,1)S(1)} %collective-permute-done.60, bf16[5056,128]{1,0:T(8,128)(2,1)S(1)} %maximum_select_fusion.3, pred[]{:T(512)S(6)} %eq.43), kind=kLoop, calls=%fused_computation.31 | loop fusion | flops 11649024 | bytes 5177345 | tf_op jit(solution)/shard_map/jit(_where)/select_n | solution.py:541
  786.4 9.2 %maximum_select_fusion = bf16[10112,128]{1,0:T(8,128)(2,1)S(1)} fusion(bf16[5056,128]{1,0:T(8,128)(2,1)S(1)} %collective-permute-done.58, bf16[5056,128]{1,0:T(8,128)(2,1)S(1)} %maximum_select_fusion.2, pred[]{:T(512)S(6)} %eq.42), kind=kLoop, calls=%fused_computation.30 | loop fusion | flops 11649024 | bytes 5177345 | tf_op jit(solution)/shard_map/jit(_where)/select_n | solution.py:541
  795.6 20.6 %pad_maximum_fusion.own = bf16[20224,128]{1,0:T(8,128)(2,1)} fusion(bf16[10112,128]{1,0:T(8,128)(2,1)S(1)} %maximum_select_fusion.1, bf16[10112,128]{1,0:T(8,128)(2,1)S(1)} %maximum_select_fusion), kind=kLoop, calls=%fused_computation.9 | loop fusion | flops 10354688 | bytes 10354688 | tf_op jit(solution)/shard_map/concatenate | solution.py:597
  820.6 8.4 collective-permute-done.47
  839.5 8.8 %unpack.2 = (f32[400,1600]{1,0:T(8,128)}, f32[400,1600]{1,0:T(8,128)}) custom-call(s32[1]{0:T(128)} %bitcast.101.core, bf16[6912,128]{1,0:T(8,128)(2,1)} %copy-done.7, bf16[6912,128]{1,0:T(8,128)(2,1)} %collective-permute-done.48.other), custom_call_target="tpu_custom_call" | custom-call | tf_op jit(solution)/shard_map/unpack/pallas_call | solution.py:495
  849.5 19.5 %unpack.3 = (f32[800,3200]{1,0:T(8,128)}, f32[800,3200]{1,0:T(8,128)}) custom-call(s32[1]{0:T(128)} %bitcast.101.core, bf16[20224,128]{1,0:T(8,128)(2,1)} %pad_maximum_fusion.own, bf16[20224,128]{1,0:T(8,128)(2,1)} %collective-permute-done.61.other), custom_call_target="tpu_custom_call" | custom-call | tf_op jit(solution)/shard_map/unpack/pallas_call | solution.py:495
  (531 shorter events, 304.2 us)
Async XLA Ops:
  7.2 208.0 %all-gather.12.cloned.1.call-start = ((), (), s32[]{:S(2)}) async-start(), calls=%async_computation.10 | async-start | bytes 3072000 | tf_op jit(solution)/shard_map/all_gather | solution.py:740
  10.4 208.6 %all-gather.8.cloned.1.call-start = ((), (), s32[]{:S(2)}) async-start(), calls=%async_computation.8 | async-start | bytes 6400000 | tf_op jit(solution)/shard_map/all_gather | solution.py:737
  11.2 234.6 %all-gather.10.cloned.1.call-start = ((), (), s32[]{:S(2)}) async-start(), calls=%async_computation.9 | async-start | bytes 7168000 | tf_op jit(solution)/shard_map/all_gather | solution.py:738
  11.9 286.8 %all-gather.14.cloned.1.call-start = ((), (), s32[]{:S(2)}) async-start(), calls=%async_computation.11 | async-start | bytes 1730560 | tf_op jit(solution)/shard_map/all_gather | solution.py:743
  13.5 20.7 %collective-permute-start.2 = (bf16[13,32,400]{2,1,0:T(8,128)(2,1)}, bf16[13,32,400]{2,1,0:T(8,128)(2,1)S(1)}, u32[]{:S(2)}, u32[]{:S(2)}) collective-permute-start(bf16[13,32,400]{2,1,0:T(8,128)(2,1)} %get-tuple-element.163), channel_id=1, source_target_pairs={{0,24},{8,16},{16,8},{24,0},{1,25},{9,17},{17,9},{25,1},{2,26},{10... | collective-permute-start | bytes 998408 | tf_op jit(solution)/shard_map/ppermute | solution.py:31
  17.4 25.8 %collective-permute-start.1 = (bf16[13,32,400]{2,1,0:T(8,128)(2,1)S(1)}, bf16[13,32,400]{2,1,0:T(8,128)(2,1)}, u32[]{:S(2)}, u32[]{:S(2)}) collective-permute-start(bf16[13,32,400]{2,1,0:T(8,128)(2,1)S(1)} %get-tuple-element.164), channel_id=1, source_target_pairs={{0,16},{8,24},{16,0},{24,8},{1,17},{9,25},{17,1},{25,9},{2,18},{10... | collective-permute-start | bytes 998408 | tf_op jit(solution)/shard_map/ppermute | solution.py:31
  17.9 25.6 %collective-permute-start = (bf16[13,32,400]{2,1,0:T(8,128)(2,1)S(1)}, bf16[13,32,400]{2,1,0:T(8,128)(2,1)}, u32[]{:S(2)}, u32[]{:S(2)}) collective-permute-start(bf16[13,32,400]{2,1,0:T(8,128)(2,1)S(1)} %get-tuple-element.165), channel_id=1, source_target_pairs={{0,8},{8,0},{16,24},{24,16},{1,9},{9,1},{17,25},{25,17},{2,10},{10... | collective-permute-start | bytes 998408 | tf_op jit(solution)/shard_map/ppermute | solution.py:31
  70.9 59.7 %collective-permute-start.7 = (bf16[800,400]{0,1:T(8,128)(2,1)S(1)}, bf16[800,400]{0,1:T(8,128)(2,1)}, u32[]{:S(2)}, u32[]{:S(2)}) collective-permute-start(bf16[800,400]{0,1:T(8,128)(2,1)S(1)} %copy.193), channel_id=1, source_target_pairs={{0,24},{8,16},{16,8},{24,0},{1,25},{9,17},{17,9},{25,1},{2,26},{10... | collective-permute-start | bytes 1920008 | tf_op jit(solution)/shard_map/ppermute | solution.py:510
  72.4 59.6 %collective-permute-start.6 = (bf16[800,400]{0,1:T(8,128)(2,1)S(1)}, bf16[800,400]{0,1:T(8,128)(2,1)}, u32[]{:S(2)}, u32[]{:S(2)}) collective-permute-start(bf16[800,400]{0,1:T(8,128)(2,1)S(1)} %copy.193), channel_id=1, source_target_pairs={{0,16},{8,24},{16,0},{24,8},{1,17},{9,25},{17,1},{25,9},{2,18},{10... | collective-permute-start | bytes 1920008 | tf_op jit(solution)/shard_map/ppermute | solution.py:510
  73.9 59.5 %collective-permute-start.5 = (bf16[800,400]{0,1:T(8,128)(2,1)S(1)}, bf16[800,400]{0,1:T(8,128)(2,1)}, u32[]{:S(2)}, u32[]{:S(2)}) collective-permute-start(bf16[800,400]{0,1:T(8,128)(2,1)S(1)} %copy.193), channel_id=1, source_target_pairs={{0,8},{8,0},{16,24},{24,16},{1,9},{9,1},{17,25},{25,17},{2,10},{10... | collective-permute-start | bytes 1920008 | tf_op jit(solution)/shard_map/ppermute | solution.py:510
  74.4 54.0 %collective-permute-start.9 = (bf16[100,800]{1,0:T(8,128)(2,1)}, bf16[100,800]{1,0:T(8,128)(2,1)S(1)}, u32[]{:S(2)}, u32[]{:S(2)}) collective-permute-start(bf16[100,800]{1,0:T(8,128)(2,1)} %param.40), channel_id=1, source_target_pairs={{0,16},{8,24},{16,0},{24,8},{1,17},{9,25},{17,1},{25,9},{2,18},{10... | collective-permute-start | bytes 480008 | tf_op jit(solution)/shard_map/ppermute | solution.py:510
  76.6 51.8 %collective-permute-start.8 = (bf16[100,800]{1,0:T(8,128)(2,1)}, bf16[100,800]{1,0:T(8,128)(2,1)S(1)}, u32[]{:S(2)}, u32[]{:S(2)}) collective-permute-start(bf16[100,800]{1,0:T(8,128)(2,1)} %param.40), channel_id=1, source_target_pairs={{0,8},{8,0},{16,24},{24,16},{1,9},{9,1},{17,25},{25,17},{2,10},{10... | collective-permute-start | bytes 480008 | tf_op jit(solution)/shard_map/ppermute | solution.py:510
  83.2 73.9 %all-to-all-start = ((f32[32,3,400]{2,1,0:T(4,128)}), f32[32,3,400]{2,1,0:T(4,128)S(1)}, u32[]{:S(2)}, u32[]{:S(2)}) async-start(f32[32,3,400]{2,1,0:T(4,128)} %broadcast_in_dim.127), calls=%async_computation | async-start | bytes 524288 | tf_op jit(solution)/shard_map/all_to_all | solution.py:86
  195.4 19.1 %all-to-all-start.1 = ((f32[32,3,800]{2,1,0:T(4,128)}), f32[32,3,800]{2,1,0:T(4,128)S(1)}, u32[]{:S(2)}, u32[]{:S(2)}) async-start(f32[32,3,800]{2,1,0:T(4,128)} %broadcast_in_dim.136), calls=%async_computation.1 | async-start | bytes 917504 | tf_op jit(solution)/shard_map/all_to_all | solution.py:86
  204.2 66.9 %collective-permute-start.20 = (bf16[12,32,400]{2,1,0:T(8,128)(2,1)}, bf16[12,32,400]{2,1,0:T(8,128)(2,1)}, u32[]{:S(2)}, u32[]{:S(2)}) collective-permute-start(bf16[12,32,400]{2,1,0:T(8,128)(2,1)} %get-tuple-element.183), channel_id=1, source_target_pairs={{0,24},{8,16},{16,8},{24,0},{1,25},{9,17},{17,9},{25,1},{2,26},{10... | collective-permute-start | bytes 921608 | tf_op jit(solution)/shard_map/ppermute | solution.py:31
  207.0 64.1 %collective-permute-start.19 = (bf16[12,32,400]{2,1,0:T(8,128)(2,1)}, bf16[12,32,400]{2,1,0:T(8,128)(2,1)}, u32[]{:S(2)}, u32[]{:S(2)}) collective-permute-start(bf16[12,32,400]{2,1,0:T(8,128)(2,1)} %get-tuple-element.184), channel_id=1, source_target_pairs={{0,16},{8,24},{16,0},{24,8},{1,17},{9,25},{17,1},{25,9},{2,18},{10... | collective-permute-start | bytes 921608 | tf_op jit(solution)/shard_map/ppermute | solution.py:31
  207.6 63.5 %collective-permute-start.18 = (bf16[12,32,400]{2,1,0:T(8,128)(2,1)}, bf16[12,32,400]{2,1,0:T(8,128)(2,1)}, u32[]{:S(2)}, u32[]{:S(2)}) collective-permute-start(bf16[12,32,400]{2,1,0:T(8,128)(2,1)} %get-tuple-element.185), channel_id=1, source_target_pairs={{0,8},{8,0},{16,24},{24,16},{1,9},{9,1},{17,25},{25,17},{2,10},{10... | collective-permute-start | bytes 921608 | tf_op jit(solution)/shard_map/ppermute | solution.py:31
  408.9 60.0 %collective-permute-start.23 = (bf16[20224,128]{1,0:T(8,128)(2,1)}, bf16[20224,128]{1,0:T(8,128)(2,1)}, u32[]{:S(2)}, u32[]{:S(2)}) collective-permute-start(bf16[20224,128]{1,0:T(8,128)(2,1)} %fusion.4), channel_id=1, source_target_pairs={{0,1},{1,0},{2,3},{3,2},{4,5},{5,4},{6,7},{7,6},{8,9},{9,8},{10,11... | collective-permute-start | bytes 15532040 | tf_op jit(solution)/shard_map/ppermute | solution.py:510
  414.8 26.3 %collective-permute-start.17 = (bf16[12,32,400]{2,1,0:T(8,128)(2,1)S(1)}, bf16[12,32,400]{2,1,0:T(8,128)(2,1)S(1)}, u32[]{:S(2)}, u32[]{:S(2)}) collective-permute-start(bf16[12,32,400]{2,1,0:T(8,128)(2,1)S(1)} %get-tuple-element.191), channel_id=1, source_target_pairs={{0,24},{8,16},{16,8},{24,0},{1,25},{9,17},{17,9},{25,1},{2,26},{10... | collective-permute-start | bytes 921608 | tf_op jit(solution)/shard_map/ppermute | solution.py:49
  416.1 25.0 %collective-permute-start.16 = (bf16[12,32,400]{2,1,0:T(8,128)(2,1)S(1)}, bf16[12,32,400]{2,1,0:T(8,128)(2,1)S(1)}, u32[]{:S(2)}, u32[]{:S(2)}) collective-permute-start(bf16[12,32,400]{2,1,0:T(8,128)(2,1)S(1)} %get-tuple-element.192), channel_id=1, source_target_pairs={{0,16},{8,24},{16,0},{24,8},{1,17},{9,25},{17,1},{25,9},{2,18},{10... | collective-permute-start | bytes 921608 | tf_op jit(solution)/shard_map/ppermute | solution.py:49
  417.3 23.9 %collective-permute-start.15 = (bf16[12,32,400]{2,1,0:T(8,128)(2,1)S(1)}, bf16[12,32,400]{2,1,0:T(8,128)(2,1)S(1)}, u32[]{:S(2)}, u32[]{:S(2)}) collective-permute-start(bf16[12,32,400]{2,1,0:T(8,128)(2,1)S(1)} %get-tuple-element.193), channel_id=1, source_target_pairs={{0,8},{8,0},{16,24},{24,16},{1,9},{9,1},{17,25},{25,17},{2,10},{10... | collective-permute-start | bytes 921608 | tf_op jit(solution)/shard_map/ppermute | solution.py:49
  446.0 220.7 %all-reduce.18.cloned.1.call-start = ((), (), s32[]{:S(2)}) async-start(), calls=%async_computation.12 | async-start | bytes 7577600 | tf_op jit(solution)/shard_map/psum | solution.py:784
  457.6 18.1 %collective-permute-start.24 = (bf16[24,3,800]{2,1,0:T(4,128)(2,1)S(1)}, bf16[24,3,800]{2,1,0:T(4,128)(2,1)S(1)}, u32[]{:S(2)}, u32[]{:S(2)}) collective-permute-start(bf16[24,3,800]{2,1,0:T(4,128)(2,1)S(1)} %get-tuple-element.212), channel_id=1, source_target_pairs={{0,1},{1,2},{2,3},{3,4},{4,5},{5,6},{6,7},{7,0},{8,9},{9,10},{10,1... | collective-permute-start | bytes 345608 | tf_op jit(solution)/shard_map/ppermute | solution.py:71
  458.3 17.5 %collective-permute-start.25 = (bf16[24,3,800]{2,1,0:T(4,128)(2,1)S(1)}, bf16[24,3,800]{2,1,0:T(4,128)(2,1)S(1)}, u32[]{:S(2)}, u32[]{:S(2)}) collective-permute-start(bf16[24,3,800]{2,1,0:T(4,128)(2,1)S(1)} %get-tuple-element.211), channel_id=1, source_target_pairs={{1,0},{2,1},{3,2},{4,3},{5,4},{6,5},{7,6},{0,7},{9,8},{10,9},{11,1... | collective-permute-start | bytes 345608 | tf_op jit(solution)/shard_map/ppermute | solution.py:72
  519.0 34.9 %collective-permute-start.31 = (bf16[5056,128]{1,0:T(8,128)(2,1)}, bf16[5056,128]{1,0:T(8,128)(2,1)}, u32[]{:S(2)}, u32[]{:S(2)}) collective-permute-start(bf16[5056,128]{1,0:T(8,128)(2,1)} %dynamic-slice_bitcast_fusion.2), channel_id=1, source_target_pairs={{0,8},{8,0},{16,24},{24,16},{1,9},{9,1},{17,25},{25,17},{2,10},{10... | collective-permute-start | bytes 3883016 | tf_op jit(solution)/shard_map/ppermute | solution.py:510
  521.8 38.8 %collective-permute-start.32 = (bf16[5056,128]{1,0:T(8,128)(2,1)}, bf16[5056,128]{1,0:T(8,128)(2,1)}, u32[]{:S(2)}, u32[]{:S(2)}) collective-permute-start(bf16[5056,128]{1,0:T(8,128)(2,1)} %dynamic-slice_bitcast_fusion.1), channel_id=1, source_target_pairs={{0,16},{8,24},{16,0},{24,8},{1,17},{9,25},{17,1},{25,9},{2,18},{10... | collective-permute-start | bytes 3883016 | tf_op jit(solution)/shard_map/ppermute | solution.py:510
  542.2 102.6 %all-to-all-start.6 = ((f32[32,32,128]{2,1,0:T(8,128)}), f32[32,32,128]{2,1,0:T(8,128)}, u32[]{:S(2)}, u32[]{:S(2)}) async-start(f32[32,32,128]{2,1,0:T(8,128)} %bitcast.98), calls=%async_computation.6 | async-start | bytes 1048576 | tf_op jit(solution)/shard_map/all_to_all | solution.py:625
  562.3 18.5 %collective-permute-start.49 = (bf16[2528,128]{1,0:T(8,128)(2,1)S(1)}, bf16[2528,128]{1,0:T(8,128)(2,1)}, u32[]{:S(2)}, u32[]{:S(2)}) collective-permute-start(bf16[2528,128]{1,0:T(8,128)(2,1)S(1)} %dynamic-slice_bitcast_fusion.4), channel_id=1, source_target_pairs={{0,16},{8,24},{16,0},{24,8},{1,17},{9,25},{17,1},{25,9},{2,18},{10... | collective-permute-start | bytes 1941512 | tf_op jit(solution)/shard_map/ppermute | solution.py:510
  579.3 128.9 %collective-permute-start.33 = (bf16[6912,128]{1,0:T(8,128)(2,1)}, bf16[6912,128]{1,0:T(8,128)(2,1)}, u32[]{:S(2)}, u32[]{:S(2)}) collective-permute-start(bf16[6912,128]{1,0:T(8,128)(2,1)} %dynamic-slice_bitcast_fusion), channel_id=1, source_target_pairs={{0,1},{1,0},{2,3},{3,2},{4,5},{5,4},{6,7},{7,6},{8,9},{9,8},{10,11... | collective-permute-start | bytes 5308424 | tf_op jit(solution)/shard_map/ppermute | solution.py:510
  579.3 20.4 %collective-permute-start.50 = (bf16[2528,128]{1,0:T(8,128)(2,1)S(1)}, bf16[2528,128]{1,0:T(8,128)(2,1)S(1)}, u32[]{:S(2)}, u32[]{:S(2)}) collective-permute-start(bf16[2528,128]{1,0:T(8,128)(2,1)S(1)} %dynamic-slice_bitcast_fusion.3), channel_id=1, source_target_pairs={{0,8},{8,0},{16,24},{24,16},{1,9},{9,1},{17,25},{25,17},{2,10},{10... | collective-permute-start | bytes 1941512 | tf_op jit(solution)/shard_map/ppermute | solution.py:510
  601.1 62.4 %collective-permute-start.53 = (bf16[2,632,128]{2,1,0:T(8,128)(2,1)}, bf16[2,632,128]{2,1,0:T(8,128)(2,1)}, u32[]{:S(2)}, u32[]{:S(2)}) collective-permute-start(bf16[2,632,128]{2,1,0:T(8,128)(2,1)} %get-tuple-element.206), channel_id=1, source_target_pairs={{0,6},{1,7},{2,4},{3,5},{4,2},{5,3},{6,0},{7,1},{8,14},{9,15},{10,... | collective-permute-start | bytes 970760 | tf_op jit(solution)/shard_map/ppermute | solution.py:510
  604.8 60.4 %collective-permute-start.52 = (bf16[2,632,128]{2,1,0:T(8,128)(2,1)}, bf16[2,632,128]{2,1,0:T(8,128)(2,1)}, u32[]{:S(2)}, u32[]{:S(2)}) collective-permute-start(bf16[2,632,128]{2,1,0:T(8,128)(2,1)} %get-tuple-element.205), channel_id=1, source_target_pairs={{0,4},{1,5},{2,6},{3,7},{4,0},{5,1},{6,2},{7,3},{8,12},{9,13},{10,... | collective-permute-start | bytes 970760 | tf_op jit(solution)/shard_map/ppermute | solution.py:510
  606.1 17.5 %collective-permute-start.26 = (bf16[48,3,400]{2,1,0:T(4,128)(2,1)S(1)}, bf16[48,3,400]{2,1,0:T(4,128)(2,1)S(1)}, u32[]{:S(2)}, u32[]{:S(2)}) collective-permute-start(bf16[48,3,400]{2,1,0:T(4,128)(2,1)S(1)} %get-tuple-element.175), channel_id=1, source_target_pairs={{0,1},{1,2},{2,3},{3,4},{4,5},{5,6},{6,7},{7,0},{8,9},{9,10},{10,1... | collective-permute-start | bytes 345608 | tf_op jit(solution)/shard_map/ppermute | solution.py:71
  639.7 33.5 %collective-permute-start.51 = (bf16[2,632,128]{2,1,0:T(8,128)(2,1)}, bf16[2,632,128]{2,1,0:T(8,128)(2,1)}, u32[]{:S(2)}, u32[]{:S(2)}) collective-permute-start(bf16[2,632,128]{2,1,0:T(8,128)(2,1)} %get-tuple-element.204), channel_id=1, source_target_pairs={{0,2},{1,3},{2,0},{3,1},{4,6},{5,7},{6,4},{7,5},{8,10},{9,11},{10,... | collective-permute-start | bytes 970760 | tf_op jit(solution)/shard_map/ppermute | solution.py:510
  643.7 35.0 %collective-permute-start.30 = (bf16[12,32,400]{2,1,0:T(8,128)(2,1)}, bf16[12,32,400]{2,1,0:T(8,128)(2,1)}, u32[]{:S(2)}, u32[]{:S(2)}) collective-permute-start(bf16[12,32,400]{2,1,0:T(8,128)(2,1)} %get-tuple-element.171), channel_id=1, source_target_pairs={{0,24},{8,16},{16,8},{24,0},{1,25},{9,17},{17,9},{25,1},{2,26},{10... | collective-permute-start | bytes 921608 | tf_op jit(solution)/shard_map/ppermute | solution.py:49
  646.7 45.9 %all-to-all-start.7 = ((f32[32,32,128]{2,1,0:T(8,128)}), f32[32,32,128]{2,1,0:T(8,128)}, u32[]{:S(2)}, u32[]{:S(2)}) async-start(f32[32,32,128]{2,1,0:T(8,128)} %broadcast_in_dim.151), calls=%async_computation.7 | async-start | bytes 1048576 | tf_op jit(solution)/shard_map/all_to_all | solution.py:627
  675.3 21.4 %collective-permute-start.56 = (bf16[2,632,128]{2,1,0:T(8,128)(2,1)}, bf16[2,632,128]{2,1,0:T(8,128)(2,1)}, u32[]{:S(2)}, u32[]{:S(2)}) collective-permute-start(bf16[2,632,128]{2,1,0:T(8,128)(2,1)} %fusion.28), channel_id=1, source_target_pairs={{0,6},{1,7},{2,4},{3,5},{4,2},{5,3},{6,0},{7,1},{8,14},{9,15},{10,... | collective-permute-start | bytes 970760 | tf_op jit(solution)/shard_map/ppermute | solution.py:510
  678.7 27.8 %collective-permute-start.55 = (bf16[2,632,128]{2,1,0:T(8,128)(2,1)}, bf16[2,632,128]{2,1,0:T(8,128)(2,1)}, u32[]{:S(2)}, u32[]{:S(2)}) collective-permute-start(bf16[2,632,128]{2,1,0:T(8,128)(2,1)} %fusion.28), channel_id=1, source_target_pairs={{0,4},{1,5},{2,6},{3,7},{4,0},{5,1},{6,2},{7,3},{8,12},{9,13},{10,... | collective-permute-start | bytes 970760 | tf_op jit(solution)/shard_map/ppermute | solution.py:510
  680.2 26.3 %collective-permute-start.54 = (bf16[2,632,128]{2,1,0:T(8,128)(2,1)}, bf16[2,632,128]{2,1,0:T(8,128)(2,1)}, u32[]{:S(2)}, u32[]{:S(2)}) collective-permute-start(bf16[2,632,128]{2,1,0:T(8,128)(2,1)} %fusion.28), channel_id=1, source_target_pairs={{0,2},{1,3},{2,0},{3,1},{4,6},{5,7},{6,4},{7,5},{8,10},{9,11},{10,... | collective-permute-start | bytes 970760 | tf_op jit(solution)/shard_map/ppermute | solution.py:510
  711.6 38.5 %collective-permute-start.59 = (bf16[2528,128]{1,0:T(8,128)(2,1)S(1)}, bf16[2528,128]{1,0:T(8,128)(2,1)S(1)}, u32[]{:S(2)}, u32[]{:S(2)}) collective-permute-start(bf16[2528,128]{1,0:T(8,128)(2,1)S(1)} %bitcast.376), channel_id=1, source_target_pairs={{0,8},{8,0},{16,24},{24,16},{1,9},{9,1},{17,25},{25,17},{2,10},{10... | collective-permute-start | bytes 1941512 | tf_op jit(solution)/shard_map/ppermute | solution.py:510
  712.6 50.4 %collective-permute-start.57 = (bf16[2528,128]{1,0:T(8,128)(2,1)S(1)}, bf16[2528,128]{1,0:T(8,128)(2,1)S(1)}, u32[]{:S(2)}, u32[]{:S(2)}) collective-permute-start(bf16[2528,128]{1,0:T(8,128)(2,1)S(1)} %bitcast.374), channel_id=1, source_target_pairs={{0,16},{8,24},{16,0},{24,8},{1,17},{9,25},{17,1},{25,9},{2,18},{10... | collective-permute-start | bytes 1941512 | tf_op jit(solution)/shard_map/ppermute | solution.py:510
  713.8 25.7 %collective-permute-start.36 = (bf16[1728,128]{1,0:T(8,128)(2,1)S(1)}, bf16[1728,128]{1,0:T(8,128)(2,1)S(1)}, u32[]{:S(2)}, u32[]{:S(2)}) collective-permute-start(bf16[1728,128]{1,0:T(8,128)(2,1)S(1)} %dynamic-slice_bitcast_fusion.5), channel_id=1, source_target_pairs={{0,16},{8,24},{16,0},{24,8},{1,17},{9,25},{17,1},{25,9},{2,18},{10... | collective-permute-start | bytes 1327112 | tf_op jit(solution)/shard_map/ppermute | solution.py:510
  723.6 18.2 %collective-permute-start.35 = (bf16[864,128]{1,0:T(8,128)(2,1)S(1)}, bf16[864,128]{1,0:T(8,128)(2,1)S(1)}, u32[]{:S(2)}, u32[]{:S(2)}) collective-permute-start(bf16[864,128]{1,0:T(8,128)(2,1)S(1)} %dynamic-slice_bitcast_fusion.32), channel_id=1, source_target_pairs={{0,16},{8,24},{16,0},{24,8},{1,17},{9,25},{17,1},{25,9},{2,18},{10... | collective-permute-start | bytes 663560 | tf_op jit(solution)/shard_map/ppermute | solution.py:510
  750.5 26.8 %collective-permute-start.60 = (bf16[5056,128]{1,0:T(8,128)(2,1)S(1)}, bf16[5056,128]{1,0:T(8,128)(2,1)S(1)}, u32[]{:S(2)}, u32[]{:S(2)}) collective-permute-start(bf16[5056,128]{1,0:T(8,128)(2,1)S(1)} %maximum_select_fusion.3), channel_id=1, source_target_pairs={{0,16},{8,24},{16,0},{24,8},{1,17},{9,25},{17,1},{25,9},{2,18},{10... | collective-permute-start | bytes 3883016 | tf_op jit(solution)/shard_map/ppermute | solution.py:510
  763.3 23.1 %collective-permute-start.58 = (bf16[5056,128]{1,0:T(8,128)(2,1)S(1)}, bf16[5056,128]{1,0:T(8,128)(2,1)S(1)}, u32[]{:S(2)}, u32[]{:S(2)}) collective-permute-start(bf16[5056,128]{1,0:T(8,128)(2,1)S(1)} %maximum_select_fusion.2), channel_id=1, source_target_pairs={{0,8},{8,0},{16,24},{24,16},{1,9},{9,1},{17,25},{25,17},{2,10},{10... | collective-permute-start | bytes 3883016 | tf_op jit(solution)/shard_map/ppermute | solution.py:510
  767.7 48.5 %collective-permute-start.46 = (bf16[864,128]{1,0:T(8,128)(2,1)S(1)}, bf16[864,128]{1,0:T(8,128)(2,1)S(1)}, u32[]{:S(2)}, u32[]{:S(2)}) collective-permute-start(bf16[864,128]{1,0:T(8,128)(2,1)S(1)} %bitcast.391), channel_id=1, source_target_pairs={{0,8},{8,0},{16,24},{24,16},{1,9},{9,1},{17,25},{25,17},{2,10},{10... | collective-permute-start | bytes 663560 | tf_op jit(solution)/shard_map/ppermute | solution.py:510
  769.0 49.9 %collective-permute-start.44 = (bf16[864,128]{1,0:T(8,128)(2,1)S(1)}, bf16[864,128]{1,0:T(8,128)(2,1)S(1)}, u32[]{:S(2)}, u32[]{:S(2)}) collective-permute-start(bf16[864,128]{1,0:T(8,128)(2,1)S(1)} %bitcast.389), channel_id=1, source_target_pairs={{0,16},{8,24},{16,0},{24,8},{1,17},{9,25},{17,1},{25,9},{2,18},{10... | collective-permute-start | bytes 663560 | tf_op jit(solution)/shard_map/ppermute | solution.py:510
  816.2 33.3 %collective-permute-start.61 = (bf16[20224,128]{1,0:T(8,128)(2,1)}, bf16[20224,128]{1,0:T(8,128)(2,1)}, u32[]{:S(2)}, u32[]{:S(2)}) collective-permute-start(bf16[20224,128]{1,0:T(8,128)(2,1)} %pad_maximum_fusion.own), channel_id=1, source_target_pairs={{0,1},{1,0},{2,3},{3,2},{4,5},{5,4},{6,7},{7,6},{8,9},{9,8},{10,11... | collective-permute-start | bytes 15532040 | tf_op jit(solution)/shard_map/ppermute | solution.py:510
  (117 other events, 1099.5 us)
Sparse Core Ops, SparseCore 0:
  10.5 52.6 all-gather.11
  65.1 91.5 all-gather.7
  158.6 87.1 all-gather.9
  247.5 29.4 all-gather.13
  453.3 149.5 all-reduce.17

commit v7 on v6

--- a/solution.py
+++ b/solution.py
@@ -22,7 +22,7 @@
     return [(i, (i // group) * group + ((i % group) ^ step)) for i in range(count)]
 
 
-def to_dates(tiles):
+def send_dates(tiles):
     dates, count = tiles.shape[0], lax.axis_size("lat")
     own = lax.axis_index("lat") % dates
     pieces = [lax.dynamic_index_in_dim(tiles, own, 0, keepdims=False)]
@@ -34,6 +34,12 @@
                 exchange_pairs(count, dates, step),
             )
         )
+    return pieces
+
+
+def to_dates(pieces):
+    dates = len(pieces)
+    own = lax.axis_index("lat") % dates
     stacked = jnp.stack(pieces)
     ordered = [lax.dynamic_index_in_dim(stacked, own ^ tile, 0, keepdims=False) for tile in range(dates)]
     return jnp.concatenate(ordered, axis=0)
@@ -60,8 +66,92 @@
     return lax.optimization_barrier((array, event))[0]
 
 
-def gathered(shard):
-    return exchange_all(shard, "lat", lax.axis_index("lat"), 1, lax.axis_size("lat"))
+def gathered(shard, event=None):
+    return exchange_all(shard, "lat", lax.axis_index("lat"), 1, lax.axis_size("lat"), event)
+
+
+def assemble(kernel, name, shape, arrays, copies):
+    tile, core = lax.axis_index("lat"), lax.axis_index("lon") % 2
+    return pl.pallas_call(
+        kernel,
+        in_specs=[pl.BlockSpec(memory_space=pltpu.SMEM)] + [pl.BlockSpec(memory_space=pl.ANY)] * len(arrays),
+        out_specs=pl.BlockSpec(memory_space=pltpu.VMEM),
+        out_shape=jax.ShapeDtypeStruct(shape, bf16),
+        scratch_shapes=[pltpu.SemaphoreType.DMA((copies,))],
+        compiler_params=room,
+        name=name,
+    )(jnp.stack([tile, core]).astype(jnp.int32), *arrays)
+
+
+def finish(copies):
+    for copy in copies:
+        copy.start()
+    for copy in copies:
+        copy.wait()
+
+
+def assemble_rows_kernel(place, shard, mine, theirs, out, sems):
+    tile, core = place[0], place[1]
+    rows = shard.shape[0]
+    half = rows // 2
+    copies = [(shard, tile * rows, rows)]
+    for step in range(1, mine.shape[0] + 1):
+        start = (tile ^ step) * rows
+        copies.append((mine.at[step - 1], start + core * half, half))
+        copies.append((theirs.at[step - 1], start + (1 - core) * half, half))
+    finish(
+        [
+            pltpu.make_async_copy(source, out.at[pl.ds(pl.multiple_of(start, 8), count)], sems.at[index])
+            for index, (source, start, count) in enumerate(copies)
+        ]
+    )
+
+
+def assemble_columns_kernel(place, mine, theirs, out, sems):
+    start = out.shape[1] - mine.shape[1]
+
+    def join(low, high):
+        finish(
+            [
+                pltpu.make_async_copy(low.at[:, :start], out.at[:, :start], sems.at[0]),
+                pltpu.make_async_copy(high, out.at[:, start:], sems.at[1]),
+            ]
+        )
+
+    @pl.when(place[1] == 0)
+    def _():
+        join(mine, theirs)
+
+    @pl.when(place[1] != 0)
+    def _():
+        join(theirs, mine)
+
+
+def gathered_by_rows(shard, event):
+    tiles = lax.axis_size("lat")
+    half = take(shard.reshape(2, -1, shard.shape[1]), lax.axis_index("lon") % 2)
+    mine = jnp.stack(after([swap(half, "lat", step) for step in range(1, tiles)], event))
+    shape = (tiles * shard.shape[0], shard.shape[1])
+    return assemble(assemble_rows_kernel, "assemble_rows", shape, (shard, mine, swap(mine, "lon", 1)), 2 * tiles - 1)
+
+
+def gathered_by_columns(shard):
+    columns = shard.shape[1]
+    start = columns // 2 // lanes * lanes
+    half = lax.dynamic_slice_in_dim(shard, lax.axis_index("lon") % 2 * start, columns - start, axis=1)
+    mine = lax.all_gather(half, "lat", axis=0, tiled=True)
+    return assemble(
+        assemble_columns_kernel, "assemble_columns", (mine.shape[0], columns), (mine, swap(mine, "lon", 1)), 2
+    )
+
+
+def gathered_pair(up, down, start, event):
+    channels = down.shape[1]
+    first = lax.axis_index("lon") % 2 == 0
+    shard = jnp.where(first, up.reshape(-1, channels), down)
+    mine = gathered(after(shard, start), event)
+    theirs = swap(mine, "lon", 1)
+    return jnp.where(first, mine, theirs).reshape(-1, up.shape[1]), jnp.where(first, theirs, mine)
 
 
 def borders(source, dates):
@@ -523,8 +613,9 @@
     return total.astype(bf16)
 
 
-def exchange_all(piece, axis, own, scale, count):
-    got = jnp.stack([piece] + [swap(piece, axis, scale * step) for step in range(1, count)])
+def exchange_all(piece, axis, own, scale, count, event=None):
+    got = [swap(piece, axis, scale * step) for step in range(1, count)]
+    got = jnp.stack([piece] + (got if event is None else after(got, event)))
     return jnp.concatenate([take(got, own ^ place) for place in range(count)], axis=0)
 
 
@@ -636,15 +727,14 @@
 
 
 def block_mix(source, params, sea, ocean, dates):
-    kernel, gain, shift = params[:3]
+    taps, gain, shift = params[:3]
     channels = source.shape[2]
-    taps = kernel.astype(f32).reshape(49, channels)
     edges = borders(source, dates)
     mixed, local = stencil_forward(source, edges, taps, sea)
     first, square, ocean = sum_all(jnp.concatenate([local, jnp.broadcast_to(ocean, (1, channels))]))
     mean = first / ocean
     factor = lax.rsqrt(square / ocean - mean * mean + epsilon)
-    scales = jnp.stack([mean, factor, gain.astype(f32), shift.astype(f32)])
+    scales = jnp.stack([mean, factor, gain, shift])
     return source, edges, taps, mixed.reshape(-1, channels), scales, ocean
 
 
@@ -658,9 +748,9 @@
         sea.reshape(-1, lanes),
         scales,
         up,
-        up_bias.astype(f32)[None],
+        up_bias,
         down,
-        down_bias.astype(f32)[None],
+        down_bias,
         pooling,
     )
     return output, coarse, mix + (normed, slope, active)
@@ -723,31 +813,29 @@
     wide = bottle_depth.shape[2]
     extra = jnp.swapaxes(ocean_mask, 1, 2).astype(bf16)[:, None]
     extra = jnp.pad(extra, ((0, 0), (0, 0), (0, 0), (0, channels - tile_rows)))
-    packed = to_dates(jnp.concatenate([fine_map, extra], axis=1)).reshape(dates, tile_rows + 1, breadth, channels)
+    pieces = send_dates(jnp.concatenate([fine_map, extra], axis=1))
+    kernels = (encode_depth, bottle_depth, decode_depth)
+    rows = (encode_up_bias, encode_down_bias, bottle_up_bias, bottle_down_bias, decode_up_bias, decode_down_bias)
+    small = (
+        [kernel.astype(f32).reshape(49, -1) for kernel in kernels],
+        [row.astype(f32)[None] for row in rows + (widen_bias, merge_bias)],
+        [row.astype(f32) for row in (encode_gain, encode_shift, bottle_gain, bottle_shift, decode_gain, decode_shift)],
+    )
+    pieces, (taps, rows, norms) = lax.optimization_barrier((pieces, small))
+    encode_up_bias, encode_down_bias, bottle_up_bias, bottle_down_bias, decode_up_bias, decode_down_bias = rows[:6]
+    widen_bias, merge_bias = rows[6:]
+    encode_norm, bottle_norm, decode_norm = [(taps[i], norms[2 * i], norms[2 * i + 1]) for i in range(3)]
+    packed = to_dates(pieces).reshape(dates, tile_rows + 1, breadth, channels)
     fine = packed[:, :tile_rows].reshape(-1, breadth, channels)
     ocean_band = jnp.swapaxes(packed[:, tile_rows, :, :tile_rows], 1, 2).reshape(-1, breadth).astype(f32)
     height = fine.shape[0]
     half_height, half_breadth = height // 2, breadth // 2
 
-    encode_rows = encode_up.size // channels
-    encode_pack = jnp.concatenate([encode_up.reshape(-1, channels), encode_down])
-    encode_pack = gathered(encode_pack).reshape(lax.axis_size("lat"), -1, channels)
-    encode_up = encode_pack[:, :encode_rows].reshape(channels, -1)
-    encode_down = encode_pack[:, encode_rows:].reshape(-1, channels)
-    bottle_up = lax.all_gather(bottle_up, "lat", axis=0, tiled=True)
-    bottle_down = lax.all_gather(bottle_down, "lat", axis=0, tiled=True)
-    decode_rows = decode_down.shape[0]
-    decode_pack = lax.all_gather(jnp.concatenate([decode_down, merge_weight]), "lat", axis=0, tiled=False)
-    decode_down = decode_pack[:, :decode_rows].reshape(-1, channels)
-    merge_weight = decode_pack[:, decode_rows:].reshape(-1, channels)
-    decode_up = lax.all_gather(decode_up, "lat", axis=0, tiled=True)
+    bottle_up = gathered_by_columns(bottle_up)
 
     coarse_band = jnp.max(ocean_band.reshape(half_height, 2, half_breadth, 2), axis=(1, 3))
     sea_fine = jnp.broadcast_to(ocean_band[..., None], (height, breadth, lanes))
     sea_coarse = jnp.broadcast_to(coarse_band[..., None], (half_height, half_breadth, lanes))
-    encode = (encode_depth, encode_gain, encode_shift, encode_up, encode_up_bias, encode_down, encode_down_bias)
-    bottle = (bottle_depth, bottle_gain, bottle_shift, bottle_up, bottle_up_bias, bottle_down, bottle_down_bias)
-    decode = (decode_depth, decode_gain, decode_shift, decode_up, decode_up_bias, decode_down, decode_down_bias)
     ocean_fine = jnp.sum(ocean_band)
     ocean_coarse = jnp.sum(coarse_band)
     parts = height * breadth // math.gcd(height * breadth, 384)
@@ -756,17 +844,29 @@
     members = jnp.asarray(block[:, None] == np.arange(pixel.size // 4), dtype=bf16)
     blocks = jnp.asarray(np.arange(pixel.size // 4)[:, None] == block, dtype=bf16)
 
-    mix = block_mix(fine, encode, sea_fine, ocean_fine, dates)
+    mix = block_mix(fine, encode_norm, sea_fine, ocean_fine, dates)
+    encode_up, encode_down = gathered_pair(encode_up, encode_down, fine, mix[3])
+    encode = encode_norm + (encode_up, encode_up_bias, encode_down, encode_down_bias)
     widen_weight = gathered(after(widen_weight, mix[3]))
     skip_rows, (pooled, coarse_in), encode_stored = block_forward(
-        mix, encode, sea_fine, (blocks, widen_weight, widen_bias.astype(f32)[None])
-    )
+        mix, encode, sea_fine, (blocks, widen_weight, widen_bias)
+    )
+    decode_up = lax.all_gather(after(decode_up, skip_rows), "lat", axis=0, tiled=True)
+    decode_down = lax.all_gather(after(decode_down, skip_rows), "lat", axis=0, tiled=True)
+    decode = decode_norm + (decode_up, decode_up_bias, decode_down, decode_down_bias)
+    bottle_down = gathered_by_rows(after(bottle_down, encode_stored[3]), skip_rows)
+    bottle = bottle_norm + (bottle_up, bottle_up_bias, bottle_down, bottle_down_bias)
     coarse_in = coarse_in.reshape(half_height, half_breadth, wide)
     mix = block_mix(coarse_in, bottle, sea_coarse, ocean_coarse, dates)
     coarse_low, _, coarse_stored = block_forward(mix, bottle, sea_coarse)
-    upstream = to_dates(after(out_grad, mix[3])).reshape(-1, channels)
-    merged = merge_forward(coarse_low, skip_rows, merge_weight, merge_bias.astype(f32)[None], members, parts)
+    merge_rows = merge_weight.shape[0]
+    merge_weight = jnp.pad(after(merge_weight, skip_rows), ((0, -merge_rows % 16), (0, 0)))
+    merge_weight = gathered(merge_weight, coarse_low).reshape(-1, merge_rows + -merge_rows % 16, channels)
+    merge_weight = merge_weight[:, :merge_rows].reshape(-1, channels)
+    upstream = send_dates(after(out_grad, mix[3]))
+    merged = merge_forward(coarse_low, skip_rows, merge_weight, merge_bias, members, parts)
     mix = block_mix(merged.reshape(fine.shape), decode, sea_fine, ocean_fine, dates)
+    upstream = to_dates(after(upstream, mix[3])).reshape(-1, channels)
     decode_rows, _, decode_stored = block_forward(mix, decode, sea_fine)
     result = from_dates(decode_rows.reshape(fine.shape), dates)
 
@@ -775,54 +875,42 @@
         cross_rows(decode_stored[6], grad_hidden),
         cross_rows(grad_branch, decode_stored[8]),
     ]
-    grad_mixed, grad_edges, *decode_norm = block_norm(grad_normed, local, sea_fine, decode_stored, dates)
-    decode_kernel = kernel_grad(*decode_stored[:2], grad_mixed)
+    grad_mixed, grad_edges, *decode_total = block_norm(grad_normed, local, sea_fine, decode_stored, dates)
+    decode_mixed = grad_mixed
     grad_merged, merge_sums = block_source(grad_mixed, grad_edges, upstream, sea_fine, decode_stored)
 
     block_sums, grad_coarse = merge_backward(grad_merged, merge_weight, blocks, wide, parts)
     early += [cross_rows(block_sums, coarse_low), cross_rows(grad_merged, skip_rows)]
+
+    grad_branch, grad_hidden, grad_normed, local, *bottle_small = block_hidden(
+        grad_coarse, bottle, sea_coarse, coarse_stored
+    )
+    decode_kernel = kernel_grad(*decode_stored[:2], after(decode_mixed, local))
+    early += [cross_rows(coarse_stored[6], grad_hidden), cross_rows(grad_branch, coarse_stored[8])]
     early = lax.psum([part.astype(bf16) for part in early], both)
     early = [total.astype(f32) for total in early]
-    decode_up_sum, decode_down_sum = early[0], early[1].T
-    merge_sum = jnp.concatenate(early[2:], axis=1).T
-
-    stages = group_stages()
-    grad_branch, grad_hidden, grad_normed, local, *bottle_small = block_hidden(
-        grad_coarse, bottle, sea_coarse, coarse_stored
-    )
-    pair = weight_grads(grad_branch, coarse_stored[6], coarse_stored[8], grad_hidden).reshape(2, -1, lanes)
-    grad_mixed, grad_edges, *bottle_norm = block_norm(grad_normed, local, sea_coarse, coarse_stored, dates)
+    decode_up_sum, decode_down_sum, bottle_up_sum, bottle_down_sum = early[0], early[1].T, early[4], early[5].T
+    merge_sum = jnp.concatenate(early[2:4], axis=1).T
+    grad_mixed, grad_edges, *bottle_total = block_norm(grad_normed, local, sea_coarse, coarse_stored, dates)
     bottle_kernel = kernel_grad(*coarse_stored[:2], grad_mixed)
-    state = stages[0](pair)
-    grad_mixed = after(grad_mixed, state)
     grad_wide, widen_sums = block_source(grad_mixed, grad_edges, grad_coarse, sea_coarse, coarse_stored)
     grad_skip = skip_backward(grad_merged, grad_wide, merge_weight, widen_weight, members, parts)
 
     grad_branch, grad_hidden, grad_normed, local, *encode_small = block_hidden(
         grad_skip, encode, sea_fine, encode_stored
     )
-    state = stages[1](state)
-    grad_hidden = after(grad_hidden, state)
     encode_pair = weight_grads(grad_branch, encode_stored[6], encode_stored[8], grad_hidden).reshape(2, -1, lanes)
-    grad_mixed, grad_edges, *encode_norm = block_norm(grad_normed, local, sea_fine, encode_stored, dates)
-    if len(stages) > 6:
-        state = stages[2](state)
-        grad_mixed = after(grad_mixed, state)
+    grad_mixed, grad_edges, *encode_total = block_norm(grad_normed, local, sea_fine, encode_stored, dates)
     encode_kernel = kernel_grad(*encode_stored[:2], grad_mixed)
     grad_fine, _ = block_source(grad_mixed, grad_edges, grad_skip, sea_fine, encode_stored)
-    for stage in stages[-5:]:
-        state = stage(state)
     core = (lax.axis_index("lon") % 2).astype(jnp.int32)[None]
-    bottle_up_sum, bottle_down_sum = unpack(core, *state, wide, bottle_up.shape[1])
-    bottle_down_sum = bottle_down_sum.T
-
     grad_widen = cross_rows(pooled, grad_wide).astype(bf16)
     widen_tiles = pl.cdiv(wide, 2 * lanes)
     grad_widen = jnp.pad(grad_widen, ((0, 0), (0, 2 * widen_tiles * lanes - wide)))
     grad_widen = grad_widen.reshape(channels, 2, widen_tiles, lanes).transpose(1, 2, 0, 3).reshape(2, -1, lanes)
     fine_grad = from_dates(grad_fine.reshape(fine.shape), dates)
     state = jnp.concatenate([encode_pair, grad_widen], axis=1)
-    for stage in stages:
+    for stage in group_stages():
         state = stage(state)
     own, other = state
     encode_up_sum, encode_down_sum = unpack(core, own, other, channels, encode_up.shape[1])
@@ -864,8 +952,8 @@
         result,
         fine_grad,
         kernel_sums[0],
-        encode_norm[0],
-        encode_norm[1],
+        encode_total[0],
+        encode_total[1],
         encode_up_sum,
         encode_upb,
         encode_down_sum,
@@ -873,8 +961,8 @@
         widen_sum,
         widen_b,
         kernel_sums[1],
-        bottle_norm[0],
-        bottle_norm[1],
+        bottle_total[0],
+        bottle_total[1],
         bottle_up_sum,
         bottle_upb,
         bottle_down_sum,
@@ -882,8 +970,8 @@
         merge_sum,
         bottle_merge_b,
         kernel_sums[2],
-        decode_norm[0],
-        decode_norm[1],
+        decode_total[0],
+        decode_total[1],
         decode_up_sum,
         decode_upb,
         decode_down_sum,

time: 885 us -> 696 us (0.79)
  waiting for transfers between devices: 236 us -> 156 us
  other arithmetic: 103 us -> 65.3 us
  local copies, waits for them, and re-layouts: 107 us -> 72.3 us
  Pallas kernels: 258 us -> 240 us
  starting transfers between devices: 128 us -> 112 us
  blocking collectives: 11.2 us -> 0 us
  matrix products: 16 us -> 25.9 us
    ppermute x38 -> x31, waiting for transfers between devices: 134 us -> 67.8 us  [swap(): lax.ppermute(array, axis, [(i, i ^ step) for i in range(lax.axis_size(axi...]
    psum x1, waiting for transfers between devices: 0.01 us -> 36.8 us  [shards(): early = lax.psum([part.astype(bf16) for part in early], both)]
    all_gather x4 -> x3, waiting for transfers between devices: 26.7 us -> 0.02 us  [the longest x1 0.02 us: gathered_by_columns(): mine = lax.all_gather(half, 'lat', axis=0, tiled=True)]
    concatenate x2 -> x1, other arithmetic: 20.7 us -> 0.12 us  [spread_first(): return jnp.concatenate(parts)]
    ppermute x6, waiting for transfers between devices: 25.2 us -> 5.64 us  [borders(): left = lax.ppermute(source[:, -3:], 'lon', forward)]
    pallas_call x2 -> x1, Pallas kernels: 28.3 us -> 8.84 us  [unpack(): pl.pallas_call(unpack_kernel, grid_spec=pltpu.PrefetchScalarGridSpec(num_...]
    select_n x8 -> x4, other arithmetic: 19.7 us -> 0.72 us  [in_order(): jnp.where(bit == 0, jnp.concatenate([own, other]), jnp.concatenate([other...]
    all_to_all x1, starting transfers between devices: 16.8 us -> 4.6 us  [sum_small(): lax.all_to_all(copies, both, 0, 0, tiled=False).reshape(padded, lanes)]
  transfers between devices with their start and end apart: 74 -> 67, of which waited for: 32 -> 23; matrix products, arithmetic and copies ran while one was open for 23% -> 19% of each run, Pallas kernels for 19% -> 26%
where the time goes in v7:
time: 696 us; the launch traced here: 688 us
  Pallas kernels  240 us (34%)
  waiting for transfers between devices  156 us (22%)
  starting transfers between devices  112 us (16%)
  local copies, waits for them, and re-layouts  72.3 us (10%)
  other arithmetic  65.3 us (9%)
  matrix products  25.9 us (4%)
  between operations  16.1 us (2%)
    ppermute x31, waiting for transfers between devices, swap(): lax.ppermute(array, axis, [(i, i ^ step) for i in range(lax.axis_size(axi...  67.8 us
    ppermute x31, starting transfers between devices, swap(): lax.ppermute(array, axis, [(i, i ^ step) for i in range(lax.axis_size(axi...  41.9 us
    pallas_call x3, Pallas kernels, mlp_forward(): pl.pallas_call(functools.partial(mlp_forward_kernel, 512), grid=(parts,),...  41.2 us
    pallas_call x3, Pallas kernels, stencil_backward(): pl.pallas_call(functools.partial(stencil_backward_kernel, len(edges)), gr...  39.5 us
    pallas_call x3, Pallas kernels, stencil_forward(): pl.pallas_call(functools.partial(stencil_forward_kernel, len(edges)), gri...  38.5 us
    pallas_call x3, Pallas kernels, mlp_backward(): pl.pallas_call(functools.partial(mlp_backward_kernel, 512), grid=(pixels...  37.6 us
    psum x1, waiting for transfers between devices, shards(): early = lax.psum([part.astype(bf16) for part in early], both)  36.8 us
    pallas_call x3, Pallas kernels, kernel_grad(): pl.pallas_call(functools.partial(kernel_grad_kernel, len(edges)), grid=(t...  32.9 us
  transfers between devices with their start and end apart: 67, of which 23 were waited for; matrix products, arithmetic and copies ran while one was open for 19% of the time, Pallas kernels for 26%

profile of v7, /device:TPU:0, one launch (start us, length us, event | category | flops | bytes accessed | tf_op | source)
XLA Modules:
  0.0 687.7 jit_solution(6808059746217451879)
XLA Ops:
  23.1 4.5 collective-permute-done
  27.6 4.8 collective-permute-done.1
  32.4 9.3 %collective-permute-done.2 = bf16[13,32,400]{2,1,0:T(8,128)(2,1)} collective-permute-done((bf16[13,32,400]{2,1,0:T(8,128)(2,1)S(1)}, bf16[13,32,400]{2,1,0:T(8,128)(2,1)}, u32[]{:S(2)}, u32[]{:S(2)}) %collective-permute-start.2) | collective-permute-done | bytes 332832 | tf_op jit(solution)/shard_map/ppermute | solution.py:31
  55.5 15.0 %stencil_forward.3 = (f32[48,32,400]{2,1,0:T(8,128)}, f32[2,400]{1,0:T(2,128)}) custom-call(bf16[48,32,400]{2,1,0:T(8,128)(2,1)} %bitcast.280, bf16[48,3,400]{2,1,0:T(4,128)(2,1)} %copy-done.33, bf16[48,3,400]{2,1,0:T(4,128)(2,1)} %copy-done.34, f32[49,400]{1,0:T(8,128)} %reshape.345.refs_2_, f32[48,32,128]{2,1,0:T(8,128)} %broadcast_in_dim.147.refs_3_), custom_call_target="tpu_custom_call" | custom-call | tf_op jit(solution)/shard_map/stencil_forward/pallas_call | solution.py:287
  70.6 6.0 collective-permute-done.7
  89.8 6.2 all-to-all-start
  101.9 4.5 all-to-all-done
  118.0 14.8 %mlp_forward.3 = (bf16[1536,400]{1,0:T(8,128)(2,1)}, bf16[1536,1600]{1,0:T(8,128)(2,1)}, bf16[1536,1600]{1,0:T(8,128)(2,1)}, bf16[1536,400]{1,0:T(8,128)(2,1)}, ...) custom-call(f32[1536,400]{1,0:T(8,128)} %bitcast.286, bf16[1536,400]{1,0:T(8,128)(2,1)} %bitcast.281, ...), custom_call_target="tpu_custom_call" | custom-call | tf_op jit(solution)/shard_map/mlp_forward/pallas_call | solution.py:467
  145.9 8.5 %stencil_forward.4 = (f32[24,16,800]{2,1,0:T(8,128)}, f32[2,800]{1,0:T(2,128)}) custom-call(bf16[24,16,800]{2,1,0:T(8,128)(2,1)} %bitcast.307, bf16[24,3,800]{2,1,0:T(4,128)(2,1)} %copy-done.38, bf16[24,3,800]{2,1,0:T(4,128)(2,1)} %copy-done.39, f32[49,800]{1,0:T(8,128)} %reshape.347.refs_2_, f32[24,16,128]{2,1,0:T(8,128)} %broadcast_in_dim.150.refs_3_), custom_call_target="tpu_custom_call" | custom-call | tf_op jit(solution)/shard_map/stencil_forward/pallas_call | solution.py:287
  156.5 4.1 all-to-all-start.1
  169.2 6.4 all-to-all-done.1
  177.0 5.9 assemble_rows.1.down
  184.0 5.5 assemble_columns.1.up
  190.3 13.8 %mlp_forward.4 = (bf16[384,800]{1,0:T(8,128)(2,1)}, bf16[384,3200]{1,0:T(8,128)(2,1)}, bf16[384,3200]{1,0:T(8,128)(2,1)}, bf16[384,800]{1,0:T(8,128)(2,1)}) custom-call(f32[384,800]{1,0:T(8,128)} %bitcast.301, bf16[384,800]{1,0:T(8,128)(2,1)} %get-tuple-element.133.source, f32[384,128]{1,0:T(8,128)} %broadcast_in_dim.151.sea, ...), custom_call_target="tpu_custom_call" | custom-call | tf_op jit(solution)/shard_map/mlp_forward/pallas_call | solution.py:467
  213.6 6.1 merge_forward.1.source
  229.9 15.0 %stencil_forward.5 = (f32[48,32,400]{2,1,0:T(8,128)}, f32[2,400]{1,0:T(2,128)}) custom-call(bf16[48,32,400]{2,1,0:T(8,128)(2,1)} %bitcast.284, bf16[48,3,400]{2,1,0:T(4,128)(2,1)} %copy-done.35, bf16[48,3,400]{2,1,0:T(4,128)(2,1)} %copy-done.36, f32[49,400]{1,0:T(8,128)} %reshape.349.refs_2_, f32[48,32,128]{2,1,0:T(8,128)} %broadcast_in_dim.147.refs_3_), custom_call_target="tpu_custom_call" | custom-call | tf_op jit(solution)/shard_map/stencil_forward/pallas_call | solution.py:287
  253.4 7.2 %all-to-all-done.2 = f32[32,3,400]{2,1,0:T(4,128)S(1)} async-done(((f32[32,3,400]{2,1,0:T(4,128)}), f32[32,3,400]{2,1,0:T(4,128)S(1)}, u32[]{:S(2)}, u32[]{:S(2)}) %all-to-all-start.2) | async-done | bytes 153632 | tf_op jit(solution)/shard_map/all_to_all | solution.py:176
  261.9 12.6 %mlp_forward.5 = (bf16[1536,400]{1,0:T(8,128)(2,1)}, bf16[1536,1600]{1,0:T(8,128)(2,1)}, bf16[1536,1600]{1,0:T(8,128)(2,1)}, bf16[1536,400]{1,0:T(8,128)(2,1)}) custom-call(f32[1536,400]{1,0:T(8,128)} %bitcast.289, bf16[1536,400]{1,0:T(8,128)(2,1)} %merge_forward.1.source, f32[1536,128]{1,0:T(8,128)} %broadcast_in_dim.148.sea, ...), custom_call_target="tpu_custom_call" | custom-call | tf_op jit(solution)/shard_map/mlp_forward/pallas_call | solution.py:467
  274.6 12.0 %mlp_backward.3 = (bf16[1536,400]{1,0:T(8,128)(2,1)}, bf16[1536,1600]{1,0:T(8,128)(2,1)}, f32[1536,400]{1,0:T(8,128)}, f32[2,400]{1,0:T(2,128)}, f32[1,400]{1,0:T(1,128)}, /*index=5*/f32[1,1600]{1,0:T(1,128)}) custom-call(bf16[1536,400]{1,0:T(8,128)(2,1)} %bitcast.297, f32[1536,400]{1,0:T(8,128)} %bitcast.290, bf16[1536,1600]{1,0:T(8,128)(2,1)} %get-tuple-element.167.slope, ...), custom_call_target="tpu_custom_call" | custom-call | tf_op jit(solution)/shard_map/mlp_backward/pallas_call | solution.py:527
  295.1 6.1 fusion.12
  317.4 15.2 %stencil_backward.3 = (bf16[48,32,400]{2,1,0:T(8,128)(2,1)}, f32[1,400]{1,0:T(1,128)}) custom-call(bf16[48,32,400]{2,1,0:T(8,128)(2,1)} %bitcast.292, bf16[48,3,400]{2,1,0:T(4,128)(2,1)} %copy-done.46, bf16[48,3,400]{2,1,0:T(4,128)(2,1)} %copy-done.47, f32[49,400]{1,0:T(8,128)} %reshape.349.refs_2_, f32[48,32,128]{2,1,0:T(8,128)} %broadcast_in_dim.147.refs_3_, ...), custom_call_target="tpu_custom_call" | custom-call | tf_op jit(solution)/shard_map/stencil_backward/pallas_call | solution.py:303
  332.6 5.1 merge_backward.1
  339.4 12.9 %mlp_backward.4 = (bf16[384,800]{1,0:T(8,128)(2,1)}, bf16[384,3200]{1,0:T(8,128)(2,1)}, f32[384,800]{1,0:T(8,128)}, f32[2,800]{1,0:T(2,128)}, f32[1,800]{1,0:T(1,128)}, /*index=5*/f32[1,3200]{1,0:T(1,128)}) custom-call(f32[384,800]{1,0:T(8,128)} %get-tuple-element.171.upstream, f32[384,800]{1,0:T(8,128)} %bitcast.302, ...), custom_call_target="tpu_custom_call" | custom-call | tf_op jit(solution)/shard_map/mlp_backward/pallas_call | solution.py:527
  353.8 5.3 all-to-all-start.4
  359.1 7.3 %fusion.2 = bf16[3200,800]{0,1:T(8,128)(2,1)} fusion(bf16[384,800]{1,0:T(8,128)(2,1)} %get-tuple-element.198, bf16[384,3200]{1,0:T(8,128)(2,1)} %get-tuple-element.199), kind=kOutput, calls=%fused_computation.5 | convolution fusion | flops 1968640000 | bytes 8192000 | tf_op jit(solution)/shard_map/dot_general | solution.py:722
  366.5 5.3 convolution_convert_fusion.1
  379.3 12.6 %kernel_grad.5 = f32[4,56,128]{2,1,0:T(8,128)} custom-call(bf16[48,32,400]{2,1,0:T(8,128)(2,1)} %bitcast.285, bf16[48,3,400]{2,1,0:T(4,128)(2,1)} %copy-done.35, bf16[48,3,400]{2,1,0:T(4,128)(2,1)} %copy-done.36, bf16[48,32,400]{2,1,0:T(8,128)(2,1)} %bitcast.293), custom_call_target="tpu_custom_call" | custom-call | tf_op jit(solution)/shard_map/kernel_grad/pallas_call | solution.py:319
  392.0 7.6 %kernel_grad.4 = f32[7,56,128]{2,1,0:T(8,128)} custom-call(bf16[24,16,800]{2,1,0:T(8,128)(2,1)} %bitcast.308, bf16[24,3,800]{2,1,0:T(4,128)(2,1)} %copy-done.38, bf16[24,3,800]{2,1,0:T(4,128)(2,1)} %copy-done.39, bf16[24,16,800]{2,1,0:T(8,128)(2,1)} %bitcast.305), custom_call_target="tpu_custom_call" | custom-call | tf_op jit(solution)/shard_map/kernel_grad/pallas_call | solution.py:319
  400.3 8.9 %stencil_backward.4 = (bf16[24,16,800]{2,1,0:T(8,128)(2,1)}, f32[1,800]{1,0:T(1,128)}) custom-call(bf16[24,16,800]{2,1,0:T(8,128)(2,1)} %bitcast.306, bf16[24,3,800]{2,1,0:T(4,128)(2,1)} %copy-done.51, bf16[24,3,800]{2,1,0:T(4,128)(2,1)} %copy-done.52, f32[49,800]{1,0:T(8,128)} %reshape.347.refs_2_, f32[24,16,128]{2,1,0:T(8,128)} %broadcast_in_dim.150.refs_3_, ...), custom_call_target="tpu_custom_call" | custom-call | tf_op jit(solution)/shard_map/stencil_backward/pallas_call | solution.py:303
  409.2 7.1 %skip_backward.1.upstream = f32[1536,400]{1,0:T(8,128)} custom-call(bf16[1536,400]{1,0:T(8,128)(2,1)} %bitcast.299, bf16[384,800]{1,0:T(8,128)(2,1)} %bitcast.323, bf16[1200,400]{1,0:T(8,128)(2,1)} %copy.141.merge, bf16[400,800]{1,0:T(8,128)(2,1)} %pad_maximum_fusion.18.refs_1_.widen, bf16[384,96]{1,0:T(8,128)(2,1)} %constant.286.clone.members), custom_call_target="tpu_custom_call" | custom-call | tf_op jit(solution)/shard_map/skip_backward/pallas_call | solution.py:510
  417.7 12.7 %mlp_backward.5 = (bf16[1536,400]{1,0:T(8,128)(2,1)}, bf16[1536,1600]{1,0:T(8,128)(2,1)}, f32[1536,400]{1,0:T(8,128)}, f32[2,400]{1,0:T(2,128)}, f32[1,400]{1,0:T(1,128)}, /*index=5*/f32[1,1600]{1,0:T(1,128)}) custom-call(f32[1536,400]{1,0:T(8,128)} %skip_backward.1.upstream, f32[1536,400]{1,0:T(8,128)} %bitcast.287, ...), custom_call_target="tpu_custom_call" | custom-call | tf_op jit(solution)/shard_map/mlp_backward/pallas_call | solution.py:527
  430.4 11.8 %weight_grads.1 = bf16[2,13,400,128]{3,2,1,0:T(8,128)(2,1)} custom-call(bf16[1536,400]{1,0:T(8,128)(2,1)} %get-tuple-element.189.grad_branch, bf16[1536,400]{1,0:T(8,128)(2,1)} %get-tuple-element.190.normed, bf16[1536,1600]{1,0:T(8,128)(2,1)} %get-tuple-element.191.active, bf16[1536,1600]{1,0:T(8,128)(2,1)} %get-tuple-element.192.grad_hidden), custom_call_target="tpu_custom_call" | custom-call | tf_op jit(solution)/shard_map/weight_grads/pallas_call | solution.py:563
  447.2 4.2 all-to-all-start.5
  451.7 7.9 %all-to-all-done.5 = f32[32,2,400]{2,1,0:T(2,128)S(1)} async-done(((f32[32,2,400]{2,1,0:T(2,128)}), f32[32,2,400]{2,1,0:T(2,128)S(1)}, u32[]{:S(2)}, u32[]{:S(2)}) %all-to-all-start.5) | async-done | bytes 102432 | tf_op jit(solution)/shard_map/all_to_all | solution.py:176
  472.7 12.6 %kernel_grad.3 = f32[4,56,128]{2,1,0:T(8,128)} custom-call(bf16[48,32,400]{2,1,0:T(8,128)(2,1)} %bitcast.282, bf16[48,3,400]{2,1,0:T(4,128)(2,1)} %copy-done.33, bf16[48,3,400]{2,1,0:T(4,128)(2,1)} %copy-done.34, bf16[48,32,400]{2,1,0:T(8,128)(2,1)} %bitcast.295), custom_call_target="tpu_custom_call" | custom-call | tf_op jit(solution)/shard_map/kernel_grad/pallas_call | solution.py:319
  490.7 15.5 %stencil_backward.5 = (bf16[48,32,400]{2,1,0:T(8,128)(2,1)}, f32[1,400]{1,0:T(1,128)}) custom-call(bf16[48,32,400]{2,1,0:T(8,128)(2,1)} %bitcast.296, bf16[48,3,400]{2,1,0:T(4,128)(2,1)} %copy-done.48, bf16[48,3,400]{2,1,0:T(4,128)(2,1)} %copy-done.49, f32[49,400]{1,0:T(8,128)} %reshape.345.refs_2_, f32[48,32,128]{2,1,0:T(8,128)} %broadcast_in_dim.147.refs_3_, ...), custom_call_target="tpu_custom_call" | custom-call | tf_op jit(solution)/shard_map/stencil_backward/pallas_call | solution.py:303
  509.6 11.3 %collective-permute-done.40 = bf16[1728,128]{1,0:T(8,128)(2,1)S(1)} collective-permute-done((bf16[1728,128]{1,0:T(8,128)(2,1)S(1)}, bf16[1728,128]{1,0:T(8,128)(2,1)S(1)}, u32[]{:S(2)}, u32[]{:S(2)}) %collective-permute-start.40) | collective-permute-done | bytes 442400 | tf_op jit(solution)/shard_map/ppermute | solution.py:600
  541.0 4.6 all-to-all-start.7
  545.6 6.3 collective-permute-done.45
  552.0 8.8 %collective-permute-start.47 = (bf16[2,216,128]{2,1,0:T(8,128)(2,1)S(1)}, bf16[2,216,128]{2,1,0:T(8,128)(2,1)S(1)}, u32[]{:S(2)}, u32[]{:S(2)}) collective-permute-start(bf16[2,216,128]{2,1,0:T(8,128)(2,1)S(1)} %fusion.24), channel_id=1, source_target_pairs={{0,2},{1,3},{2,0},{3,1},{4,6},{5,7},{6,4},{7,5},{8,10},{9,11},{10,... | collective-permute-start | bytes 331784 | tf_op jit(solution)/shard_map/ppermute | solution.py:600
  560.9 4.0 collective-permute-start.48
  566.5 14.3 %collective-permute-done.48 = bf16[2,216,128]{2,1,0:T(8,128)(2,1)S(1)} collective-permute-done((bf16[2,216,128]{2,1,0:T(8,128)(2,1)S(1)}, bf16[2,216,128]{2,1,0:T(8,128)(2,1)S(1)}, u32[]{:S(2)}, u32[]{:S(2)}) %collective-permute-start.48) | collective-permute-done | bytes 110624 | tf_op jit(solution)/shard_map/ppermute | solution.py:600
  589.3 5.8 collective-permute-done.52
  596.6 12.5 %collective-permute-done.51 = bf16[1728,128]{1,0:T(8,128)(2,1)S(1)} collective-permute-done((bf16[1728,128]{1,0:T(8,128)(2,1)S(1)}, bf16[1728,128]{1,0:T(8,128)(2,1)S(1)}, u32[]{:S(2)}, u32[]{:S(2)}) %collective-permute-start.51) | collective-permute-done | bytes 442400 | tf_op jit(solution)/shard_map/ppermute | solution.py:600
  616.8 8.8 %unpack.1 = (f32[400,1600]{1,0:T(8,128)}, f32[400,1600]{1,0:T(8,128)}) custom-call(s32[1]{0:T(128)} %bitcast.45.core, bf16[6912,128]{1,0:T(8,128)(2,1)} %copy-done.14, bf16[6912,128]{1,0:T(8,128)(2,1)} %collective-permute-done.54.other), custom_call_target="tpu_custom_call" | custom-call | tf_op jit(solution)/shard_map/unpack/pallas_call | solution.py:585
  626.9 36.8 %all-reduce.18.cloned.1.call-done = (bf16[800,3200]{1,0:T(8,128)(2,1)}, bf16[3200,800]{0,1:T(8,128)(2,1)}, bf16[400,400]{1,0:T(8,128)(2,1)}, bf16[400,800]{1,0:T...) async-done(((bf16[800,3200]{1,0:T(8,128)(2,1)}, bf16[3200,800]{0,1:T(8,128)(2,1)}, bf16[400,400]{1,0:T(8,128)(2,1)}, bf16[400,800]{1,0:T(8,128)(2,1)}, ...) | async-done | bytes 13760016 | tf_op jit(solution)/shard_map/psum | solution.py:890
  663.7 7.3 %convert_element_type.242 = f32[800,3200]{1,0:T(8,128)} convert(bf16[800,3200]{1,0:T(8,128)(2,1)} %get-tuple-element.207) | non-fusion elementwise | flops 2560000 | bytes 15360000 | tf_op jit(solution)/shard_map/convert_element_type | solution.py:891
  671.0 4.7 transpose.90
  (515 shorter events, 226.1 us)
Async XLA Ops:
  7.2 103.1 %all-gather.5.cloned.1.call-start = ((), (), s32[]{:S(2)}) async-start(), calls=%async_computation.8 | async-start | bytes 3328000 | tf_op jit(solution)/shard_map/all_gather | solution.py:142
  11.1 16.5 %collective-permute-start = (bf16[13,32,400]{2,1,0:T(8,128)(2,1)}, bf16[13,32,400]{2,1,0:T(8,128)(2,1)S(1)}, u32[]{:S(2)}, u32[]{:S(2)}) collective-permute-start(bf16[13,32,400]{2,1,0:T(8,128)(2,1)} %get-tuple-element.232), channel_id=1, source_target_pairs={{0,8},{8,0},{16,24},{24,16},{1,9},{9,1},{17,25},{25,17},{2,10},{10... | collective-permute-start | bytes 998408 | tf_op jit(solution)/shard_map/ppermute | solution.py:31
  14.0 18.4 %collective-permute-start.1 = (bf16[13,32,400]{2,1,0:T(8,128)(2,1)S(1)}, bf16[13,32,400]{2,1,0:T(8,128)(2,1)S(1)}, u32[]{:S(2)}, u32[]{:S(2)}) collective-permute-start(bf16[13,32,400]{2,1,0:T(8,128)(2,1)S(1)} %get-tuple-element.231), channel_id=1, source_target_pairs={{0,16},{8,24},{16,0},{24,8},{1,17},{9,25},{17,1},{25,9},{2,18},{10... | collective-permute-start | bytes 998408 | tf_op jit(solution)/shard_map/ppermute | solution.py:31
  15.6 26.1 %collective-permute-start.2 = (bf16[13,32,400]{2,1,0:T(8,128)(2,1)S(1)}, bf16[13,32,400]{2,1,0:T(8,128)(2,1)}, u32[]{:S(2)}, u32[]{:S(2)}) collective-permute-start(bf16[13,32,400]{2,1,0:T(8,128)(2,1)S(1)} %get-tuple-element.230), channel_id=1, source_target_pairs={{0,24},{8,16},{16,8},{24,0},{1,25},{9,17},{17,9},{25,1},{2,26},{10... | collective-permute-start | bytes 998408 | tf_op jit(solution)/shard_map/ppermute | solution.py:31
  43.5 27.1 %collective-permute-start.5 = (bf16[400,400]{1,0:T(8,128)(2,1)S(1)}, bf16[400,400]{1,0:T(8,128)(2,1)S(1)}, u32[]{:S(2)}, u32[]{:S(2)}) collective-permute-start(bf16[400,400]{1,0:T(8,128)(2,1)S(1)} %broadcast_select_fusion.2), channel_id=1, source_target_pairs={{0,8},{8,0},{16,24},{24,16},{1,9},{9,1},{17,25},{25,17},{2,10},{10... | collective-permute-start | bytes 960008 | tf_op jit(solution)/shard_map/ppermute | solution.py:600
  45.0 25.6 %collective-permute-start.6 = (bf16[400,400]{1,0:T(8,128)(2,1)S(1)}, bf16[400,400]{1,0:T(8,128)(2,1)}, u32[]{:S(2)}, u32[]{:S(2)}) collective-permute-start(bf16[400,400]{1,0:T(8,128)(2,1)S(1)} %broadcast_select_fusion.2), channel_id=1, source_target_pairs={{0,16},{8,24},{16,0},{24,8},{1,17},{9,25},{17,1},{25,9},{2,18},{10... | collective-permute-start | bytes 960008 | tf_op jit(solution)/shard_map/ppermute | solution.py:600
  45.6 31.0 %collective-permute-start.7 = (bf16[400,400]{1,0:T(8,128)(2,1)S(1)}, bf16[400,400]{1,0:T(8,128)(2,1)}, u32[]{:S(2)}, u32[]{:S(2)}) collective-permute-start(bf16[400,400]{1,0:T(8,128)(2,1)S(1)} %broadcast_select_fusion.2), channel_id=1, source_target_pairs={{0,24},{8,16},{16,8},{24,0},{1,25},{9,17},{17,9},{25,1},{2,26},{10... | collective-permute-start | bytes 960008 | tf_op jit(solution)/shard_map/ppermute | solution.py:600
  83.1 24.5 %collective-permute-start.8 = (bf16[1600,400]{0,1:T(8,128)(2,1)}, bf16[1600,400]{0,1:T(8,128)(2,1)}, u32[]{:S(2)}, u32[]{:S(2)}) collective-permute-start(bf16[1600,400]{0,1:T(8,128)(2,1)} %copy.136), channel_id=1, source_target_pairs={{0,1},{1,0},{2,3},{3,2},{4,5},{5,4},{6,7},{7,6},{8,9},{9,8},{10,11... | collective-permute-start | bytes 3840008 | tf_op jit(solution)/shard_map/ppermute | solution.py:600
  83.7 15.3 %collective-permute-start.9 = (bf16[100,800]{1,0:T(8,128)(2,1)S(1)}, bf16[100,800]{1,0:T(8,128)(2,1)S(1)}, u32[]{:S(2)}, u32[]{:S(2)}) collective-permute-start(bf16[100,800]{1,0:T(8,128)(2,1)S(1)} %copy-done.50), channel_id=1, source_target_pairs={{0,8},{8,0},{16,24},{24,16},{1,9},{9,1},{17,25},{25,17},{2,10},{10... | collective-permute-start | bytes 480008 | tf_op jit(solution)/shard_map/ppermute | solution.py:600
  85.5 14.8 %collective-permute-start.10 = (bf16[100,800]{1,0:T(8,128)(2,1)S(1)}, bf16[100,800]{1,0:T(8,128)(2,1)S(1)}, u32[]{:S(2)}, u32[]{:S(2)}) collective-permute-start(bf16[100,800]{1,0:T(8,128)(2,1)S(1)} %copy-done.50), channel_id=1, source_target_pairs={{0,16},{8,24},{16,0},{24,8},{1,17},{9,25},{17,1},{25,9},{2,18},{10... | collective-permute-start | bytes 480008 | tf_op jit(solution)/shard_map/ppermute | solution.py:600
  89.8 16.6 %all-to-all-start = ((f32[32,3,400]{2,1,0:T(4,128)}), f32[32,3,400]{2,1,0:T(4,128)S(1)}, u32[]{:S(2)}, u32[]{:S(2)}) async-start(f32[32,3,400]{2,1,0:T(4,128)} %broadcast_in_dim.149), calls=%async_computation | async-start | bytes 524288 | tf_op jit(solution)/shard_map/all_to_all | solution.py:176
  95.9 130.0 %all-gather.9.cloned.1.call-start = ((), (), s32[]{:S(2)}) async-start(), calls=%async_computation.10 | async-start | bytes 1730560 | tf_op jit(solution)/shard_map/all_gather | solution.py:854
  97.1 36.5 %collective-permute-start.15 = (bf16[400,800]{1,0:T(8,128)(2,1)}, bf16[400,800]{1,0:T(8,128)(2,1)}, u32[]{:S(2)}, u32[]{:S(2)}) collective-permute-start(bf16[400,800]{1,0:T(8,128)(2,1)} %dynamic-slice_bitcast_fusion.1), channel_id=1, source_target_pairs={{0,8},{8,0},{16,24},{24,16},{1,9},{9,1},{17,25},{25,17},{2,10},{10... | collective-permute-start | bytes 1920008 | tf_op jit(solution)/shard_map/ppermute | solution.py:600
  98.9 34.7 %collective-permute-start.16 = (bf16[400,800]{1,0:T(8,128)(2,1)}, bf16[400,800]{1,0:T(8,128)(2,1)}, u32[]{:S(2)}, u32[]{:S(2)}) collective-permute-start(bf16[400,800]{1,0:T(8,128)(2,1)} %dynamic-slice_bitcast_fusion.1), channel_id=1, source_target_pairs={{0,16},{8,24},{16,0},{24,8},{1,17},{9,25},{17,1},{25,9},{2,18},{10... | collective-permute-start | bytes 1920008 | tf_op jit(solution)/shard_map/ppermute | solution.py:600
  100.4 33.5 %collective-permute-start.17 = (bf16[400,800]{1,0:T(8,128)(2,1)}, bf16[400,800]{1,0:T(8,128)(2,1)}, u32[]{:S(2)}, u32[]{:S(2)}) collective-permute-start(bf16[400,800]{1,0:T(8,128)(2,1)} %dynamic-slice_bitcast_fusion.1), channel_id=1, source_target_pairs={{0,24},{8,16},{16,8},{24,0},{1,25},{9,17},{17,9},{25,1},{2,26},{10... | collective-permute-start | bytes 1920008 | tf_op jit(solution)/shard_map/ppermute | solution.py:600
  110.3 72.6 %collective-permute-start.14 = (bf16[800,1664]{1,0:T(8,128)(2,1)}, bf16[800,1664]{1,0:T(8,128)(2,1)}, u32[]{:S(2)}, u32[]{:S(2)}) collective-permute-start(bf16[800,1664]{1,0:T(8,128)(2,1)} %all-gather.5.cloned.1.call-done.mine), channel_id=1, source_target_pairs={{0,1},{1,0},{2,3},{3,2},{4,5},{5,4},{6,7},{7,6},{8,9},{9,8},{10,11... | collective-permute-start | bytes 7987208 | tf_op jit(solution)/shard_map/ppermute | solution.py:600
  135.8 41.2 %collective-permute-start.18 = (bf16[3,400,800]{2,1,0:T(8,128)(2,1)S(1)}, bf16[3,400,800]{2,1,0:T(8,128)(2,1)}, u32[]{:S(2)}, u32[]{:S(2)}) collective-permute-start(bf16[3,400,800]{2,1,0:T(8,128)(2,1)S(1)} %pad_maximum_fusion.3.mine), channel_id=1, source_target_pairs={{0,1},{1,0},{2,3},{3,2},{4,5},{5,4},{6,7},{7,6},{8,9},{9,8},{10,11... | collective-permute-start | bytes 5760008 | tf_op jit(solution)/shard_map/ppermute | solution.py:600
  156.5 19.1 %all-to-all-start.1 = ((f32[32,3,800]{2,1,0:T(4,128)}), f32[32,3,800]{2,1,0:T(4,128)S(1)}, u32[]{:S(2)}, u32[]{:S(2)}) async-start(f32[32,3,800]{2,1,0:T(4,128)} %broadcast_in_dim.152), calls=%async_computation.1 | async-start | bytes 917504 | tf_op jit(solution)/shard_map/all_to_all | solution.py:176
  160.6 101.3 %all-gather.7.cloned.1.call-start = ((), (), s32[]{:S(2)}) async-start(), calls=%async_computation.9 | async-start | bytes 2048000 | tf_op jit(solution)/shard_map/all_gather | solution.py:855
  163.3 40.8 %collective-permute-start.19 = (bf16[304,400]{0,1:T(8,128)(2,1)}, bf16[304,400]{0,1:T(8,128)(2,1)}, u32[]{:S(2)}, u32[]{:S(2)}) collective-permute-start(bf16[304,400]{0,1:T(8,128)(2,1)} %get-tuple-element.292), channel_id=1, source_target_pairs={{0,8},{8,0},{16,24},{24,16},{1,9},{9,1},{17,25},{25,17},{2,10},{10... | collective-permute-start | bytes 729608 | tf_op jit(solution)/shard_map/ppermute | solution.py:600
  165.1 41.2 %collective-permute-start.20 = (bf16[304,400]{0,1:T(8,128)(2,1)}, bf16[304,400]{0,1:T(8,128)(2,1)}, u32[]{:S(2)}, u32[]{:S(2)}) collective-permute-start(bf16[304,400]{0,1:T(8,128)(2,1)} %get-tuple-element.292), channel_id=1, source_target_pairs={{0,16},{8,24},{16,0},{24,8},{1,17},{9,25},{17,1},{25,9},{2,18},{10... | collective-permute-start | bytes 729608 | tf_op jit(solution)/shard_map/ppermute | solution.py:600
  166.6 39.7 %collective-permute-start.21 = (bf16[304,400]{0,1:T(8,128)(2,1)}, bf16[304,400]{0,1:T(8,128)(2,1)}, u32[]{:S(2)}, u32[]{:S(2)}) collective-permute-start(bf16[304,400]{0,1:T(8,128)(2,1)} %get-tuple-element.292), channel_id=1, source_target_pairs={{0,24},{8,16},{16,8},{24,0},{1,25},{9,17},{17,9},{25,1},{2,26},{10... | collective-permute-start | bytes 729608 | tf_op jit(solution)/shard_map/ppermute | solution.py:600
  177.0 67.9 %collective-permute-start.27 = (bf16[12,32,400]{2,1,0:T(8,128)(2,1)}, bf16[12,32,400]{2,1,0:T(8,128)(2,1)}, u32[]{:S(2)}, u32[]{:S(2)}) collective-permute-start(bf16[12,32,400]{2,1,0:T(8,128)(2,1)} %get-tuple-element.256), channel_id=1, source_target_pairs={{0,8},{8,0},{16,24},{24,16},{1,9},{9,1},{17,25},{25,17},{2,10},{10... | collective-permute-start | bytes 921608 | tf_op jit(solution)/shard_map/ppermute | solution.py:31
  182.9 62.0 %collective-permute-start.28 = (bf16[12,32,400]{2,1,0:T(8,128)(2,1)}, bf16[12,32,400]{2,1,0:T(8,128)(2,1)}, u32[]{:S(2)}, u32[]{:S(2)}) collective-permute-start(bf16[12,32,400]{2,1,0:T(8,128)(2,1)} %get-tuple-element.255), channel_id=1, source_target_pairs={{0,16},{8,24},{16,0},{24,8},{1,17},{9,25},{17,1},{25,9},{2,18},{10... | collective-permute-start | bytes 921608 | tf_op jit(solution)/shard_map/ppermute | solution.py:31
  204.1 40.8 %collective-permute-start.29 = (bf16[12,32,400]{2,1,0:T(8,128)(2,1)}, bf16[12,32,400]{2,1,0:T(8,128)(2,1)}, u32[]{:S(2)}, u32[]{:S(2)}) collective-permute-start(bf16[12,32,400]{2,1,0:T(8,128)(2,1)} %get-tuple-element.254), channel_id=1, source_target_pairs={{0,24},{8,16},{16,8},{24,0},{1,25},{9,17},{17,9},{25,1},{2,26},{10... | collective-permute-start | bytes 921608 | tf_op jit(solution)/shard_map/ppermute | solution.py:31
  287.9 16.8 %all-to-all-start.3 = ((f32[32,2,400]{2,1,0:T(2,128)}), f32[32,2,400]{2,1,0:T(2,128)S(1)}, u32[]{:S(2)}, u32[]{:S(2)}) async-start(f32[32,2,400]{2,1,0:T(2,128)} %broadcast_in_dim.154), calls=%async_computation.3 | async-start | bytes 262144 | tf_op jit(solution)/shard_map/all_to_all | solution.py:176
  291.6 21.2 %collective-permute-start.24 = (bf16[12,32,400]{2,1,0:T(8,128)(2,1)}, bf16[12,32,400]{2,1,0:T(8,128)(2,1)S(1)}, u32[]{:S(2)}, u32[]{:S(2)}) collective-permute-start(bf16[12,32,400]{2,1,0:T(8,128)(2,1)} %get-tuple-element.265), channel_id=1, source_target_pairs={{0,8},{8,0},{16,24},{24,16},{1,9},{9,1},{17,25},{25,17},{2,10},{10... | collective-permute-start | bytes 921608 | tf_op jit(solution)/shard_map/ppermute | solution.py:55
  293.3 19.5 %collective-permute-start.25 = (bf16[12,32,400]{2,1,0:T(8,128)(2,1)}, bf16[12,32,400]{2,1,0:T(8,128)(2,1)S(1)}, u32[]{:S(2)}, u32[]{:S(2)}) collective-permute-start(bf16[12,32,400]{2,1,0:T(8,128)(2,1)} %get-tuple-element.264), channel_id=1, source_target_pairs={{0,16},{8,24},{16,0},{24,8},{1,17},{9,25},{17,1},{25,9},{2,18},{10... | collective-permute-start | bytes 921608 | tf_op jit(solution)/shard_map/ppermute | solution.py:55
  294.7 18.8 %collective-permute-start.26 = (bf16[12,32,400]{2,1,0:T(8,128)(2,1)}, bf16[12,32,400]{2,1,0:T(8,128)(2,1)}, u32[]{:S(2)}, u32[]{:S(2)}) collective-permute-start(bf16[12,32,400]{2,1,0:T(8,128)(2,1)} %get-tuple-element.263), channel_id=1, source_target_pairs={{0,24},{8,16},{16,8},{24,0},{1,25},{9,17},{17,9},{25,1},{2,26},{10... | collective-permute-start | bytes 921608 | tf_op jit(solution)/shard_map/ppermute | solution.py:55
  353.8 18.0 %all-to-all-start.4 = ((f32[32,2,800]{2,1,0:T(2,128)}), f32[32,2,800]{2,1,0:T(2,128)S(1)}, u32[]{:S(2)}, u32[]{:S(2)}) async-start(f32[32,2,800]{2,1,0:T(2,128)} %broadcast_in_dim.155), calls=%async_computation.4 | async-start | bytes 458752 | tf_op jit(solution)/shard_map/all_to_all | solution.py:176
  359.1 304.6 %all-reduce.18.cloned.1.call-start = ((), (), s32[]{:S(2)}) async-start(), calls=%async_computation.11 | async-start | bytes 28057600 | tf_op jit(solution)/shard_map/psum | solution.py:890
  374.0 25.5 %collective-permute-start.32 = (bf16[24,3,800]{2,1,0:T(4,128)(2,1)S(1)}, bf16[24,3,800]{2,1,0:T(4,128)(2,1)S(1)}, u32[]{:S(2)}, u32[]{:S(2)}) collective-permute-start(bf16[24,3,800]{2,1,0:T(4,128)(2,1)S(1)} %get-tuple-element.279), channel_id=1, source_target_pairs={{0,1},{1,2},{2,3},{3,4},{4,5},{5,6},{6,7},{7,0},{8,9},{9,10},{10,1... | collective-permute-start | bytes 345608 | tf_op jit(solution)/shard_map/ppermute | solution.py:161
  374.3 25.2 %collective-permute-start.33 = (bf16[24,3,800]{2,1,0:T(4,128)(2,1)S(1)}, bf16[24,3,800]{2,1,0:T(4,128)(2,1)S(1)}, u32[]{:S(2)}, u32[]{:S(2)}) collective-permute-start(bf16[24,3,800]{2,1,0:T(4,128)(2,1)S(1)} %get-tuple-element.278), channel_id=1, source_target_pairs={{1,0},{2,1},{3,2},{4,3},{5,4},{6,5},{7,6},{0,7},{9,8},{10,9},{11,1... | collective-permute-start | bytes 345608 | tf_op jit(solution)/shard_map/ppermute | solution.py:162
  446.5 17.1 %collective-permute-start.39 = (bf16[6912,128]{1,0:T(8,128)(2,1)}, bf16[6912,128]{1,0:T(8,128)(2,1)}, u32[]{:S(2)}, u32[]{:S(2)}) collective-permute-start(bf16[6912,128]{1,0:T(8,128)(2,1)} %dynamic-slice_bitcast_fusion), channel_id=1, source_target_pairs={{0,1},{1,0},{2,3},{3,2},{4,5},{5,4},{6,7},{7,6},{8,9},{9,8},{10,11... | collective-permute-start | bytes 5308424 | tf_op jit(solution)/shard_map/ppermute | solution.py:600
  467.0 41.1 %collective-permute-start.42 = (bf16[1728,128]{1,0:T(8,128)(2,1)}, bf16[1728,128]{1,0:T(8,128)(2,1)}, u32[]{:S(2)}, u32[]{:S(2)}) collective-permute-start(bf16[1728,128]{1,0:T(8,128)(2,1)} %dynamic-slice_bitcast_fusion.2), channel_id=1, source_target_pairs={{0,16},{8,24},{16,0},{24,8},{1,17},{9,25},{17,1},{25,9},{2,18},{10... | collective-permute-start | bytes 1327112 | tf_op jit(solution)/shard_map/ppermute | solution.py:600
  469.2 20.8 %collective-permute-start.34 = (bf16[48,3,400]{2,1,0:T(4,128)(2,1)}, bf16[48,3,400]{2,1,0:T(4,128)(2,1)S(1)}, u32[]{:S(2)}, u32[]{:S(2)}) collective-permute-start(bf16[48,3,400]{2,1,0:T(4,128)(2,1)} %get-tuple-element.247), channel_id=1, source_target_pairs={{0,1},{1,2},{2,3},{3,4},{4,5},{5,6},{6,7},{7,0},{8,9},{9,10},{10,1... | collective-permute-start | bytes 345608 | tf_op jit(solution)/shard_map/ppermute | solution.py:161
  469.2 20.8 %collective-permute-start.35 = (bf16[48,3,400]{2,1,0:T(4,128)(2,1)S(1)}, bf16[48,3,400]{2,1,0:T(4,128)(2,1)S(1)}, u32[]{:S(2)}, u32[]{:S(2)}) collective-permute-start(bf16[48,3,400]{2,1,0:T(4,128)(2,1)S(1)} %get-tuple-element.246), channel_id=1, source_target_pairs={{1,0},{2,1},{3,2},{4,3},{5,4},{6,5},{7,6},{0,7},{9,8},{10,9},{11,1... | collective-permute-start | bytes 345608 | tf_op jit(solution)/shard_map/ppermute | solution.py:162
  487.1 53.0 %all-to-all-start.6 = ((f32[32,32,128]{2,1,0:T(8,128)}), f32[32,32,128]{2,1,0:T(8,128)S(1)}, u32[]{:S(2)}, u32[]{:S(2)}) async-start(f32[32,32,128]{2,1,0:T(8,128)} %bitcast.111), calls=%async_computation.6 | async-start | bytes 1048576 | tf_op jit(solution)/shard_map/all_to_all | solution.py:716
  509.3 16.9 %collective-permute-start.43 = (bf16[864,128]{1,0:T(8,128)(2,1)S(1)}, bf16[864,128]{1,0:T(8,128)(2,1)S(1)}, u32[]{:S(2)}, u32[]{:S(2)}) collective-permute-start(bf16[864,128]{1,0:T(8,128)(2,1)S(1)} %dynamic-slice_bitcast_fusion.34), channel_id=1, source_target_pairs={{0,8},{8,0},{16,24},{24,16},{1,9},{9,1},{17,25},{25,17},{2,10},{10... | collective-permute-start | bytes 663560 | tf_op jit(solution)/shard_map/ppermute | solution.py:600
  532.3 32.5 %collective-permute-start.36 = (bf16[12,32,400]{2,1,0:T(8,128)(2,1)}, bf16[12,32,400]{2,1,0:T(8,128)(2,1)S(1)}, u32[]{:S(2)}, u32[]{:S(2)}) collective-permute-start(bf16[12,32,400]{2,1,0:T(8,128)(2,1)} %get-tuple-element.245), channel_id=1, source_target_pairs={{0,8},{8,0},{16,24},{24,16},{1,9},{9,1},{17,25},{25,17},{2,10},{10... | collective-permute-start | bytes 921608 | tf_op jit(solution)/shard_map/ppermute | solution.py:55
  533.8 32.4 %collective-permute-start.37 = (bf16[12,32,400]{2,1,0:T(8,128)(2,1)}, bf16[12,32,400]{2,1,0:T(8,128)(2,1)S(1)}, u32[]{:S(2)}, u32[]{:S(2)}) collective-permute-start(bf16[12,32,400]{2,1,0:T(8,128)(2,1)} %get-tuple-element.244), channel_id=1, source_target_pairs={{0,16},{8,24},{16,0},{24,8},{1,17},{9,25},{17,1},{25,9},{2,18},{10... | collective-permute-start | bytes 921608 | tf_op jit(solution)/shard_map/ppermute | solution.py:55
  534.3 31.9 %collective-permute-start.38 = (bf16[12,32,400]{2,1,0:T(8,128)(2,1)}, bf16[12,32,400]{2,1,0:T(8,128)(2,1)S(1)}, u32[]{:S(2)}, u32[]{:S(2)}) collective-permute-start(bf16[12,32,400]{2,1,0:T(8,128)(2,1)} %get-tuple-element.243), channel_id=1, source_target_pairs={{0,24},{8,16},{16,8},{24,0},{1,25},{9,17},{17,9},{25,1},{2,26},{10... | collective-permute-start | bytes 921608 | tf_op jit(solution)/shard_map/ppermute | solution.py:55
  535.8 16.2 %collective-permute-start.45 = (bf16[2,216,128]{2,1,0:T(8,128)(2,1)}, bf16[2,216,128]{2,1,0:T(8,128)(2,1)S(1)}, u32[]{:S(2)}, u32[]{:S(2)}) collective-permute-start(bf16[2,216,128]{2,1,0:T(8,128)(2,1)} %get-tuple-element.289), channel_id=1, source_target_pairs={{0,4},{1,5},{2,6},{3,7},{4,0},{5,1},{6,2},{7,3},{8,12},{9,13},{10,... | collective-permute-start | bytes 331784 | tf_op jit(solution)/shard_map/ppermute | solution.py:600
  541.0 42.0 %all-to-all-start.7 = ((f32[32,32,128]{2,1,0:T(8,128)}), f32[32,32,128]{2,1,0:T(8,128)S(1)}, u32[]{:S(2)}, u32[]{:S(2)}) async-start(f32[32,32,128]{2,1,0:T(8,128)} %broadcast_in_dim.157), calls=%async_computation.7 | async-start | bytes 1048576 | tf_op jit(solution)/shard_map/all_to_all | solution.py:718
  560.9 19.9 %collective-permute-start.48 = (bf16[2,216,128]{2,1,0:T(8,128)(2,1)S(1)}, bf16[2,216,128]{2,1,0:T(8,128)(2,1)S(1)}, u32[]{:S(2)}, u32[]{:S(2)}) collective-permute-start(bf16[2,216,128]{2,1,0:T(8,128)(2,1)S(1)} %fusion.24), channel_id=1, source_target_pairs={{0,4},{1,5},{2,6},{3,7},{4,0},{5,1},{6,2},{7,3},{8,12},{9,13},{10,... | collective-permute-start | bytes 331784 | tf_op jit(solution)/shard_map/ppermute | solution.py:600
  564.8 16.0 %collective-permute-start.49 = (bf16[2,216,128]{2,1,0:T(8,128)(2,1)S(1)}, bf16[2,216,128]{2,1,0:T(8,128)(2,1)S(1)}, u32[]{:S(2)}, u32[]{:S(2)}) collective-permute-start(bf16[2,216,128]{2,1,0:T(8,128)(2,1)S(1)} %fusion.24), channel_id=1, source_target_pairs={{0,6},{1,7},{2,4},{3,5},{4,2},{5,3},{6,0},{7,1},{8,14},{9,15},{10,... | collective-permute-start | bytes 331784 | tf_op jit(solution)/shard_map/ppermute | solution.py:600
  587.4 21.6 %collective-permute-start.51 = (bf16[1728,128]{1,0:T(8,128)(2,1)S(1)}, bf16[1728,128]{1,0:T(8,128)(2,1)S(1)}, u32[]{:S(2)}, u32[]{:S(2)}) collective-permute-start(bf16[1728,128]{1,0:T(8,128)(2,1)S(1)} %maximum_select_fusion.2), channel_id=1, source_target_pairs={{0,8},{8,0},{16,24},{24,16},{1,9},{9,1},{17,25},{25,17},{2,10},{10... | collective-permute-start | bytes 1327112 | tf_op jit(solution)/shard_map/ppermute | solution.py:600
  595.2 15.6 %collective-permute-start.53 = (bf16[1728,128]{1,0:T(8,128)(2,1)S(1)}, bf16[1728,128]{1,0:T(8,128)(2,1)S(1)}, u32[]{:S(2)}, u32[]{:S(2)}) collective-permute-start(bf16[1728,128]{1,0:T(8,128)(2,1)S(1)} %maximum_select_fusion.3), channel_id=1, source_target_pairs={{0,16},{8,24},{16,0},{24,8},{1,17},{9,25},{17,1},{25,9},{2,18},{10... | collective-permute-start | bytes 1327112 | tf_op jit(solution)/shard_map/ppermute | solution.py:600
  (120 other events, 907.2 us)
Sparse Core Ops, SparseCore 0:
  10.5 67.8 all-gather.4
  132.9 27.1 all-gather.8
  167.0 38.7 all-gather.6
  379.4 284.2 all-reduce.17

commit v8 on v7

--- a/solution.py
+++ b/solution.py
@@ -145,11 +145,10 @@
     )
 
 
-def gathered_pair(up, down, start, event):
+def gathered_pair(up, down):
     channels = down.shape[1]
     first = lax.axis_index("lon") % 2 == 0
-    shard = jnp.where(first, up.reshape(-1, channels), down)
-    mine = gathered(after(shard, start), event)
+    mine = lax.all_gather(jnp.where(first, up.reshape(-1, channels), down), "lat", axis=0, tiled=True)
     theirs = swap(mine, "lon", 1)
     return jnp.where(first, mine, theirs).reshape(-1, up.shape[1]), jnp.where(first, theirs, mine)
 
@@ -170,10 +169,10 @@
     return left, right, lax.ppermute(last, "lat", down), lax.ppermute(first, "lat", up)
 
 
-def sum_all(local):
+def sum_all(local, event=()):
     count = lax.axis_size(both)
     copies = jnp.broadcast_to(local[None], (count,) + local.shape)
-    return jnp.sum(lax.all_to_all(copies, both, 0, 0, tiled=False), axis=0)
+    return jnp.sum(after(lax.all_to_all(copies, both, 0, 0, tiled=False), event), axis=0)
 
 
 def fill_extended(wide_ref, centre, edges):
@@ -726,12 +725,13 @@
     return lax.dot_general(former, latter, (((1,), (1,)), ((), ())), preferred_element_type=f32)
 
 
-def block_mix(source, params, sea, ocean, dates):
+def block_mix(source, params, sea, ocean, dates, event=()):
     taps, gain, shift = params[:3]
     channels = source.shape[2]
     edges = borders(source, dates)
     mixed, local = stencil_forward(source, edges, taps, sea)
-    first, square, ocean = sum_all(jnp.concatenate([local, jnp.broadcast_to(ocean, (1, channels))]))
+    totals = sum_all(jnp.concatenate([local, jnp.broadcast_to(ocean, (1, channels))]), event)
+    first, square, ocean = totals
     mean = first / ocean
     factor = lax.rsqrt(square / ocean - mean * mean + epsilon)
     scales = jnp.stack([mean, factor, gain, shift])
@@ -831,6 +831,7 @@
     height = fine.shape[0]
     half_height, half_breadth = height // 2, breadth // 2
 
+    encode_up, encode_down = gathered_pair(encode_up, encode_down)
     bottle_up = gathered_by_columns(bottle_up)
 
     coarse_band = jnp.max(ocean_band.reshape(half_height, 2, half_breadth, 2), axis=(1, 3))
@@ -845,7 +846,6 @@
     blocks = jnp.asarray(np.arange(pixel.size // 4)[:, None] == block, dtype=bf16)
 
     mix = block_mix(fine, encode_norm, sea_fine, ocean_fine, dates)
-    encode_up, encode_down = gathered_pair(encode_up, encode_down, fine, mix[3])
     encode = encode_norm + (encode_up, encode_up_bias, encode_down, encode_down_bias)
     widen_weight = gathered(after(widen_weight, mix[3]))
     skip_rows, (pooled, coarse_in), encode_stored = block_forward(
@@ -857,7 +857,7 @@
     bottle_down = gathered_by_rows(after(bottle_down, encode_stored[3]), skip_rows)
     bottle = bottle_norm + (bottle_up, bottle_up_bias, bottle_down, bottle_down_bias)
     coarse_in = coarse_in.reshape(half_height, half_breadth, wide)
-    mix = block_mix(coarse_in, bottle, sea_coarse, ocean_coarse, dates)
+    mix = block_mix(coarse_in, bottle, sea_coarse, ocean_coarse, dates, (bottle_up, bottle_down))
     coarse_low, _, coarse_stored = block_forward(mix, bottle, sea_coarse)
     merge_rows = merge_weight.shape[0]
     merge_weight = jnp.pad(after(merge_weight, skip_rows), ((0, -merge_rows % 16), (0, 0)))

time: 696 us -> 711 us (1.022)
  Pallas kernels: 240 us -> 252 us
  other arithmetic: 65.3 us -> 57.2 us
    all_gather x0 -> x1, waiting for transfers between devices: none -> 15.3 us  [gathered_pair(): lax.all_gather(jnp.where(first, up.reshape(-1, channels), down), 'lat', a...]
    all_to_all x6, waiting for transfers between devices: 26 us -> 15.3 us  [sum_all(): lax.all_to_all(copies, both, 0, 0, tiled=False)]
    psum x1, waiting for transfers between devices: 36.8 us -> 27.6 us  [shards(): early = lax.psum([part.astype(bf16) for part in early], both)]
    ppermute x31 -> x28, waiting for transfers between devices: 67.8 us -> 76.7 us  [swap(): lax.ppermute(array, axis, [(i, i ^ step) for i in range(lax.axis_size(axi...]
    unnamed x224 -> x208, local copies, waits for them, and re-layouts: 15.9 us -> 14.5 us
    ppermute x31 -> x28, starting transfers between devices: 41.9 us -> 42.5 us  [swap(): lax.ppermute(array, axis, [(i, i ^ step) for i in range(lax.axis_size(axi...]
  transfers between devices with their start and end apart: 67 -> 65, of which waited for: 23 -> 27; matrix products, arithmetic and copies ran while one was open for 19% -> 18% of each run, Pallas kernels for 26% -> 27%
where the time goes in v8:
time: 711 us; the launch traced here: 700 us
  Pallas kernels  252 us (35%)
  waiting for transfers between devices  162 us (23%)
  starting transfers between devices  111 us (16%)
  local copies, waits for them, and re-layouts  76.3 us (11%)
  other arithmetic  57.2 us (8%)
  matrix products  26 us (4%)
  between operations  16 us (2%)
    ppermute x28, waiting for transfers between devices, swap(): lax.ppermute(array, axis, [(i, i ^ step) for i in range(lax.axis_size(axi...  76.7 us
    pallas_call x3, Pallas kernels, stencil_backward(): pl.pallas_call(functools.partial(stencil_backward_kernel, len(edges)), gr...  45 us
    pallas_call x3, Pallas kernels, stencil_forward(): pl.pallas_call(functools.partial(stencil_forward_kernel, len(edges)), gri...  44.3 us
    ppermute x28, starting transfers between devices, swap(): lax.ppermute(array, axis, [(i, i ^ step) for i in range(lax.axis_size(axi...  42.5 us
    pallas_call x3, Pallas kernels, mlp_forward(): pl.pallas_call(functools.partial(mlp_forward_kernel, 512), grid=(parts,),...  40.9 us
    pallas_call x3, Pallas kernels, mlp_backward(): pl.pallas_call(functools.partial(mlp_backward_kernel, 512), grid=(pixels...  37.8 us
    pallas_call x3, Pallas kernels, kernel_grad(): pl.pallas_call(functools.partial(kernel_grad_kernel, len(edges)), grid=(t...  33.3 us
    psum x1, waiting for transfers between devices, shards(): early = lax.psum([part.astype(bf16) for part in early], both)  27.6 us
  transfers between devices with their start and end apart: 65, of which 27 were waited for; matrix products, arithmetic and copies ran while one was open for 18% of the time, Pallas kernels for 27%

profile of v8, /device:TPU:0, one launch (start us, length us, event | category | flops | bytes accessed | tf_op | source)
XLA Modules:
  0.0 699.7 jit_solution(5868487405648843608)
XLA Ops:
  24.2 4.1 collective-permute-done
  28.3 11.2 %collective-permute-done.1 = bf16[13,32,400]{2,1,0:T(8,128)(2,1)S(1)} collective-permute-done((bf16[13,32,400]{2,1,0:T(8,128)(2,1)S(1)}, bf16[13,32,400]{2,1,0:T(8,128)(2,1)S(1)}, u32[]{:S(2)}, u32[]{:S(2)}) %collective-permute-start.1) | collective-permute-done | bytes 332832 | tf_op jit(solution)/shard_map/ppermute | solution.py:31
  42.3 15.3 %all-gather.6.cloned.1.call-done = bf16[1600,400]{1,0:T(8,128)(2,1)} async-done(((bf16[400,400]{1,0:T(8,128)(2,1)}), bf16[1600,400]{1,0:T(8,128)(2,1)}) %all-gather.6.cloned.1.call-update) | async-done | bytes 1280016 | tf_op jit(solution)/shard_map/all_gather | solution.py:151
  70.2 17.6 %stencil_forward.3 = (f32[48,32,400]{2,1,0:T(8,128)}, f32[2,400]{1,0:T(2,128)}) custom-call(bf16[48,32,400]{2,1,0:T(8,128)(2,1)} %bitcast.268, bf16[48,3,400]{2,1,0:T(4,128)(2,1)} %copy-done.34, bf16[48,3,400]{2,1,0:T(4,128)(2,1)} %copy-done.35, f32[49,400]{1,0:T(8,128)} %reshape.345.refs_2_, f32[48,32,128]{2,1,0:T(8,128)} %broadcast_in_dim.147.refs_3_), custom_call_target="tpu_custom_call" | custom-call | tf_op jit(solution)/shard_map/stencil_forward/pallas_call | solution.py:286
  94.7 3.7 all-to-all-start
  102.9 7.1 %collective-permute-done.8 = bf16[100,800]{1,0:T(8,128)(2,1)S(1)} collective-permute-done((bf16[100,800]{1,0:T(8,128)(2,1)S(1)}, bf16[100,800]{1,0:T(8,128)(2,1)S(1)}, u32[]{:S(2)}, u32[]{:S(2)}) %collective-permute-start.8) | collective-permute-done | bytes 160032 | tf_op jit(solution)/shard_map/ppermute | solution.py:599
  119.8 4.4 reshape.303.up
  125.3 14.8 %mlp_forward.3 = (bf16[1536,400]{1,0:T(8,128)(2,1)}, bf16[1536,1600]{1,0:T(8,128)(2,1)}, bf16[1536,1600]{1,0:T(8,128)(2,1)}, bf16[1536,400]{1,0:T(8,128)(2,1)}, ...) custom-call(f32[1536,400]{1,0:T(8,128)} %bitcast.274, bf16[1536,400]{1,0:T(8,128)(2,1)} %bitcast.269, ...), custom_call_target="tpu_custom_call" | custom-call | tf_op jit(solution)/shard_map/mlp_forward/pallas_call | solution.py:466
  153.3 3.7 collective-permute-done.9.refs_0_
  157.8 9.3 %stencil_forward.4 = (f32[24,16,800]{2,1,0:T(8,128)}, f32[2,800]{1,0:T(2,128)}) custom-call(bf16[24,16,800]{2,1,0:T(8,128)(2,1)} %bitcast.295, bf16[24,3,800]{2,1,0:T(4,128)(2,1)} %copy-done.40, bf16[24,3,800]{2,1,0:T(4,128)(2,1)} %copy-done.39, f32[49,800]{1,0:T(8,128)} %reshape.347.refs_2_, f32[24,16,128]{2,1,0:T(8,128)} %broadcast_in_dim.150.refs_3_), custom_call_target="tpu_custom_call" | custom-call | tf_op jit(solution)/shard_map/stencil_forward/pallas_call | solution.py:286
  182.1 5.9 assemble_rows.1.down
  189.5 5.5 assemble_columns.1.up
  196.6 13.5 %mlp_forward.4 = (bf16[384,800]{1,0:T(8,128)(2,1)}, bf16[384,3200]{1,0:T(8,128)(2,1)}, bf16[384,3200]{1,0:T(8,128)(2,1)}, bf16[384,800]{1,0:T(8,128)(2,1)}) custom-call(f32[384,800]{1,0:T(8,128)} %bitcast.289, bf16[384,800]{1,0:T(8,128)(2,1)} %get-tuple-element.126.source, f32[384,128]{1,0:T(8,128)} %broadcast_in_dim.151.sea, ...), custom_call_target="tpu_custom_call" | custom-call | tf_op jit(solution)/shard_map/mlp_forward/pallas_call | solution.py:466
  218.0 6.1 merge_forward.1.source
  233.8 17.4 %stencil_forward.5 = (f32[48,32,400]{2,1,0:T(8,128)}, f32[2,400]{1,0:T(2,128)}) custom-call(bf16[48,32,400]{2,1,0:T(8,128)(2,1)} %bitcast.272, bf16[48,3,400]{2,1,0:T(4,128)(2,1)} %copy-done.36, bf16[48,3,400]{2,1,0:T(4,128)(2,1)} %copy-done.37, f32[49,400]{1,0:T(8,128)} %reshape.349.refs_2_, f32[48,32,128]{2,1,0:T(8,128)} %broadcast_in_dim.147.refs_3_), custom_call_target="tpu_custom_call" | custom-call | tf_op jit(solution)/shard_map/stencil_forward/pallas_call | solution.py:286
  253.4 4.8 all-to-all-start.2
  261.3 7.3 %all-to-all-done.2 = f32[32,3,400]{2,1,0:T(4,128)S(1)} async-done(((f32[32,3,400]{2,1,0:T(4,128)}), f32[32,3,400]{2,1,0:T(4,128)S(1)}, u32[]{:S(2)}, u32[]{:S(2)}) %all-to-all-start.2) | async-done | bytes 153632 | tf_op jit(solution)/shard_map/all_to_all | solution.py:175
  269.3 12.6 %mlp_forward.5 = (bf16[1536,400]{1,0:T(8,128)(2,1)}, bf16[1536,1600]{1,0:T(8,128)(2,1)}, bf16[1536,1600]{1,0:T(8,128)(2,1)}, bf16[1536,400]{1,0:T(8,128)(2,1)}) custom-call(f32[1536,400]{1,0:T(8,128)} %bitcast.277, bf16[1536,400]{1,0:T(8,128)(2,1)} %merge_forward.1.source, f32[1536,128]{1,0:T(8,128)} %broadcast_in_dim.148.sea, ...), custom_call_target="tpu_custom_call" | custom-call | tf_op jit(solution)/shard_map/mlp_forward/pallas_call | solution.py:466
  281.9 12.0 %mlp_backward.3 = (bf16[1536,400]{1,0:T(8,128)(2,1)}, bf16[1536,1600]{1,0:T(8,128)(2,1)}, f32[1536,400]{1,0:T(8,128)}, f32[2,400]{1,0:T(2,128)}, f32[1,400]{1,0:T(1,128)}, /*index=5*/f32[1,1600]{1,0:T(1,128)}) custom-call(bf16[1536,400]{1,0:T(8,128)(2,1)} %bitcast.285, f32[1536,400]{1,0:T(8,128)} %bitcast.278, bf16[1536,1600]{1,0:T(8,128)(2,1)} %get-tuple-element.161.slope, ...), custom_call_target="tpu_custom_call" | custom-call | tf_op jit(solution)/shard_map/mlp_backward/pallas_call | solution.py:526
  302.4 6.1 fusion.12
  315.9 3.7 collective-permute-start.28
  324.3 17.8 %stencil_backward.3 = (bf16[48,32,400]{2,1,0:T(8,128)(2,1)}, f32[1,400]{1,0:T(1,128)}) custom-call(bf16[48,32,400]{2,1,0:T(8,128)(2,1)} %bitcast.280, bf16[48,3,400]{2,1,0:T(4,128)(2,1)} %copy-done.48, bf16[48,3,400]{2,1,0:T(4,128)(2,1)} %copy-done.49, f32[49,400]{1,0:T(8,128)} %reshape.349.refs_2_, f32[48,32,128]{2,1,0:T(8,128)} %broadcast_in_dim.147.refs_3_, ...), custom_call_target="tpu_custom_call" | custom-call | tf_op jit(solution)/shard_map/stencil_backward/pallas_call | solution.py:302
  342.1 5.1 merge_backward.1
  348.8 12.9 %mlp_backward.4 = (bf16[384,800]{1,0:T(8,128)(2,1)}, bf16[384,3200]{1,0:T(8,128)(2,1)}, f32[384,800]{1,0:T(8,128)}, f32[2,800]{1,0:T(2,128)}, f32[1,800]{1,0:T(1,128)}, /*index=5*/f32[1,3200]{1,0:T(1,128)}) custom-call(f32[384,800]{1,0:T(8,128)} %get-tuple-element.165.upstream, f32[384,800]{1,0:T(8,128)} %bitcast.290, ...), custom_call_target="tpu_custom_call" | custom-call | tf_op jit(solution)/shard_map/mlp_backward/pallas_call | solution.py:526
  363.2 5.3 all-to-all-start.4
  368.6 7.3 %fusion.2 = bf16[3200,800]{0,1:T(8,128)(2,1)} fusion(bf16[384,800]{1,0:T(8,128)(2,1)} %get-tuple-element.192, bf16[384,3200]{1,0:T(8,128)(2,1)} %get-tuple-element.193), kind=kOutput, calls=%fused_computation.5 | convolution fusion | flops 1968640000 | bytes 8192000 | tf_op jit(solution)/shard_map/dot_general | solution.py:721
  375.9 5.3 convolution_convert_fusion.1
  389.1 12.8 %kernel_grad.5 = f32[4,56,128]{2,1,0:T(8,128)} custom-call(bf16[48,32,400]{2,1,0:T(8,128)(2,1)} %bitcast.273, bf16[48,3,400]{2,1,0:T(4,128)(2,1)} %copy-done.36, bf16[48,3,400]{2,1,0:T(4,128)(2,1)} %copy-done.37, bf16[48,32,400]{2,1,0:T(8,128)(2,1)} %bitcast.281), custom_call_target="tpu_custom_call" | custom-call | tf_op jit(solution)/shard_map/kernel_grad/pallas_call | solution.py:318
  402.0 7.6 %kernel_grad.4 = f32[7,56,128]{2,1,0:T(8,128)} custom-call(bf16[24,16,800]{2,1,0:T(8,128)(2,1)} %bitcast.296, bf16[24,3,800]{2,1,0:T(4,128)(2,1)} %copy-done.40, bf16[24,3,800]{2,1,0:T(4,128)(2,1)} %copy-done.39, bf16[24,16,800]{2,1,0:T(8,128)(2,1)} %bitcast.293), custom_call_target="tpu_custom_call" | custom-call | tf_op jit(solution)/shard_map/kernel_grad/pallas_call | solution.py:318
  410.3 9.5 %stencil_backward.4 = (bf16[24,16,800]{2,1,0:T(8,128)(2,1)}, f32[1,800]{1,0:T(1,128)}) custom-call(bf16[24,16,800]{2,1,0:T(8,128)(2,1)} %bitcast.294, bf16[24,3,800]{2,1,0:T(4,128)(2,1)} %copy-done.51, bf16[24,3,800]{2,1,0:T(4,128)(2,1)} %copy-done.52, f32[49,800]{1,0:T(8,128)} %reshape.347.refs_2_, f32[24,16,128]{2,1,0:T(8,128)} %broadcast_in_dim.150.refs_3_, ...), custom_call_target="tpu_custom_call" | custom-call | tf_op jit(solution)/shard_map/stencil_backward/pallas_call | solution.py:302
  419.9 7.1 %skip_backward.1.upstream = f32[1536,400]{1,0:T(8,128)} custom-call(bf16[1536,400]{1,0:T(8,128)(2,1)} %bitcast.287, bf16[384,800]{1,0:T(8,128)(2,1)} %bitcast.311, bf16[1200,400]{1,0:T(8,128)(2,1)} %copy.103.merge, bf16[400,800]{1,0:T(8,128)(2,1)} %pad_maximum_fusion.16.refs_1_.widen, bf16[384,96]{1,0:T(8,128)(2,1)} %constant.276.clone.members), custom_call_target="tpu_custom_call" | custom-call | tf_op jit(solution)/shard_map/skip_backward/pallas_call | solution.py:509
  428.4 12.8 %mlp_backward.5 = (bf16[1536,400]{1,0:T(8,128)(2,1)}, bf16[1536,1600]{1,0:T(8,128)(2,1)}, f32[1536,400]{1,0:T(8,128)}, f32[2,400]{1,0:T(2,128)}, f32[1,400]{1,0:T(1,128)}, /*index=5*/f32[1,1600]{1,0:T(1,128)}) custom-call(f32[1536,400]{1,0:T(8,128)} %skip_backward.1.upstream, f32[1536,400]{1,0:T(8,128)} %bitcast.275, ...), custom_call_target="tpu_custom_call" | custom-call | tf_op jit(solution)/shard_map/mlp_backward/pallas_call | solution.py:526
  441.3 11.8 %weight_grads.1 = bf16[2,13,400,128]{3,2,1,0:T(8,128)(2,1)} custom-call(bf16[1536,400]{1,0:T(8,128)(2,1)} %get-tuple-element.183.grad_branch, bf16[1536,400]{1,0:T(8,128)(2,1)} %get-tuple-element.184.normed, bf16[1536,1600]{1,0:T(8,128)(2,1)} %get-tuple-element.185.active, bf16[1536,1600]{1,0:T(8,128)(2,1)} %get-tuple-element.186.grad_hidden), custom_call_target="tpu_custom_call" | custom-call | tf_op jit(solution)/shard_map/weight_grads/pallas_call | solution.py:562
  458.1 4.0 all-to-all-start.5
  462.4 7.9 %all-to-all-done.5 = f32[32,2,400]{2,1,0:T(2,128)S(1)} async-done(((f32[32,2,400]{2,1,0:T(2,128)}), f32[32,2,400]{2,1,0:T(2,128)S(1)}, u32[]{:S(2)}, u32[]{:S(2)}) %all-to-all-start.5) | async-done | bytes 102432 | tf_op jit(solution)/shard_map/all_to_all | solution.py:175
  478.5 12.8 %kernel_grad.3 = f32[4,56,128]{2,1,0:T(8,128)} custom-call(bf16[48,32,400]{2,1,0:T(8,128)(2,1)} %bitcast.270, bf16[48,3,400]{2,1,0:T(4,128)(2,1)} %copy-done.34, bf16[48,3,400]{2,1,0:T(4,128)(2,1)} %copy-done.35, bf16[48,32,400]{2,1,0:T(8,128)(2,1)} %bitcast.283), custom_call_target="tpu_custom_call" | custom-call | tf_op jit(solution)/shard_map/kernel_grad/pallas_call | solution.py:318
  497.1 17.6 %stencil_backward.5 = (bf16[48,32,400]{2,1,0:T(8,128)(2,1)}, f32[1,400]{1,0:T(1,128)}) custom-call(bf16[48,32,400]{2,1,0:T(8,128)(2,1)} %bitcast.284, bf16[48,3,400]{2,1,0:T(4,128)(2,1)} %collective-permute-done.31.refs_0_, bf16[48,3,400]{2,1,0:T(4,128)(2,1)} %collective-permute-done.32.refs_1_, f32[49,400]{1,0:T(8,128)} %reshape.345.refs_2_, ...), custom_call_target="tpu_custom_call" | custom-call | tf_op jit(solution)/shard_map/stencil_backward/pallas_call | solution.py:302
  523.1 25.3 %collective-permute-done.37 = bf16[1728,128]{1,0:T(8,128)(2,1)S(1)} collective-permute-done((bf16[1728,128]{1,0:T(8,128)(2,1)S(1)}, bf16[1728,128]{1,0:T(8,128)(2,1)S(1)}, u32[]{:S(2)}, u32[]{:S(2)}) %collective-permute-start.37) | collective-permute-done | bytes 442400 | tf_op jit(solution)/shard_map/ppermute | solution.py:599
  561.7 5.3 all-to-all-start.7
  568.3 5.8 collective-permute-done.42
  575.4 12.1 %collective-permute-start.44 = (bf16[2,216,128]{2,1,0:T(8,128)(2,1)S(1)}, bf16[2,216,128]{2,1,0:T(8,128)(2,1)S(1)}, u32[]{:S(2)}, u32[]{:S(2)}) collective-permute-start(bf16[2,216,128]{2,1,0:T(8,128)(2,1)S(1)} %fusion.24), channel_id=1, source_target_pairs={{0,2},{1,3},{2,0},{3,1},{4,6},{5,7},{6,4},{7,5},{8,10},{9,11},{10,... | collective-permute-start | bytes 331784 | tf_op jit(solution)/shard_map/ppermute | solution.py:599
  590.6 10.6 %collective-permute-done.45 = bf16[2,216,128]{2,1,0:T(8,128)(2,1)S(1)} collective-permute-done((bf16[2,216,128]{2,1,0:T(8,128)(2,1)S(1)}, bf16[2,216,128]{2,1,0:T(8,128)(2,1)S(1)}, u32[]{:S(2)}, u32[]{:S(2)}) %collective-permute-start.45) | collective-permute-done | bytes 110624 | tf_op jit(solution)/shard_map/ppermute | solution.py:599
  606.5 7.2 %collective-permute-done.47 = bf16[864,128]{1,0:T(8,128)(2,1)S(1)} collective-permute-done((bf16[864,128]{1,0:T(8,128)(2,1)S(1)}, bf16[864,128]{1,0:T(8,128)(2,1)S(1)}, u32[]{:S(2)}, u32[]{:S(2)}) %collective-permute-start.47) | collective-permute-done | bytes 221216 | tf_op jit(solution)/shard_map/ppermute | solution.py:599
  619.4 10.8 %collective-permute-done.48 = bf16[1728,128]{1,0:T(8,128)(2,1)S(1)} collective-permute-done((bf16[1728,128]{1,0:T(8,128)(2,1)S(1)}, bf16[1728,128]{1,0:T(8,128)(2,1)S(1)}, u32[]{:S(2)}, u32[]{:S(2)}) %collective-permute-start.48) | collective-permute-done | bytes 442400 | tf_op jit(solution)/shard_map/ppermute | solution.py:599
  638.0 8.9 %unpack.1 = (f32[400,1600]{1,0:T(8,128)}, f32[400,1600]{1,0:T(8,128)}) custom-call(s32[1]{0:T(128)} %bitcast.37.core, bf16[6912,128]{1,0:T(8,128)(2,1)} %copy-done.14, bf16[6912,128]{1,0:T(8,128)(2,1)} %collective-permute-done.51.other), custom_call_target="tpu_custom_call" | custom-call | tf_op jit(solution)/shard_map/unpack/pallas_call | solution.py:584
  648.1 27.6 %all-reduce.18.cloned.1.call-done = (bf16[800,3200]{1,0:T(8,128)(2,1)}, bf16[3200,800]{0,1:T(8,128)(2,1)}, bf16[400,400]{1,0:T(8,128)(2,1)}, bf16[400,800]{1,0:T...) async-done(((bf16[800,3200]{1,0:T(8,128)(2,1)}, bf16[3200,800]{0,1:T(8,128)(2,1)}, bf16[400,400]{1,0:T(8,128)(2,1)}, bf16[400,800]{1,0:T(8,128)(2,1)}, ...) | async-done | bytes 13760016 | tf_op jit(solution)/shard_map/psum | solution.py:890
  675.7 7.3 %convert_element_type.242 = f32[800,3200]{1,0:T(8,128)} convert(bf16[800,3200]{1,0:T(8,128)(2,1)} %get-tuple-element.201) | non-fusion elementwise | flops 2560000 | bytes 15360000 | tf_op jit(solution)/shard_map/convert_element_type | solution.py:891
  683.0 4.7 transpose.90
  (492 shorter events, 214.0 us)
Async XLA Ops:
  7.2 50.3 %all-gather.6.cloned.1.call-start = ((), (), s32[]{:S(2)}) async-start(), calls=%async_computation.8 | async-start | bytes 2048000 | tf_op jit(solution)/shard_map/all_gather | solution.py:151
  9.7 105.8 %all-gather.8.cloned.1.call-start = ((), (), s32[]{:S(2)}) async-start(), calls=%async_computation.9 | async-start | bytes 3328000 | tf_op jit(solution)/shard_map/all_gather | solution.py:142
  11.6 16.7 %collective-permute-start = (bf16[13,32,400]{2,1,0:T(8,128)(2,1)S(1)}, bf16[13,32,400]{2,1,0:T(8,128)(2,1)S(1)}, u32[]{:S(2)}, u32[]{:S(2)}) collective-permute-start(bf16[13,32,400]{2,1,0:T(8,128)(2,1)S(1)} %get-tuple-element.226), channel_id=1, source_target_pairs={{0,8},{8,0},{16,24},{24,16},{1,9},{9,1},{17,25},{25,17},{2,10},{10... | collective-permute-start | bytes 998408 | tf_op jit(solution)/shard_map/ppermute | solution.py:31
  14.6 24.9 %collective-permute-start.1 = (bf16[13,32,400]{2,1,0:T(8,128)(2,1)S(1)}, bf16[13,32,400]{2,1,0:T(8,128)(2,1)S(1)}, u32[]{:S(2)}, u32[]{:S(2)}) collective-permute-start(bf16[13,32,400]{2,1,0:T(8,128)(2,1)S(1)} %get-tuple-element.225), channel_id=1, source_target_pairs={{0,16},{8,24},{16,0},{24,8},{1,17},{9,25},{17,1},{25,9},{2,18},{10... | collective-permute-start | bytes 998408 | tf_op jit(solution)/shard_map/ppermute | solution.py:31
  16.1 24.2 %collective-permute-start.2 = (bf16[13,32,400]{2,1,0:T(8,128)(2,1)S(1)}, bf16[13,32,400]{2,1,0:T(8,128)(2,1)S(1)}, u32[]{:S(2)}, u32[]{:S(2)}) collective-permute-start(bf16[13,32,400]{2,1,0:T(8,128)(2,1)S(1)} %get-tuple-element.224), channel_id=1, source_target_pairs={{0,24},{8,16},{16,8},{24,0},{1,25},{9,17},{17,9},{25,1},{2,26},{10... | collective-permute-start | bytes 998408 | tf_op jit(solution)/shard_map/ppermute | solution.py:31
  61.0 51.0 %collective-permute-start.5 = (bf16[1600,400]{0,1:T(8,128)(2,1)}, bf16[1600,400]{0,1:T(8,128)(2,1)}, u32[]{:S(2)}, u32[]{:S(2)}) collective-permute-start(bf16[1600,400]{0,1:T(8,128)(2,1)} %copy.99), channel_id=1, source_target_pairs={{0,1},{1,0},{2,3},{3,2},{4,5},{5,4},{6,7},{7,6},{8,9},{9,8},{10,11... | collective-permute-start | bytes 3840008 | tf_op jit(solution)/shard_map/ppermute | solution.py:599
  87.8 13.3 %collective-permute-start.6 = (bf16[100,800]{1,0:T(8,128)(2,1)S(1)}, bf16[100,800]{1,0:T(8,128)(2,1)S(1)}, u32[]{:S(2)}, u32[]{:S(2)}) collective-permute-start(bf16[100,800]{1,0:T(8,128)(2,1)S(1)} %copy-done.50), channel_id=1, source_target_pairs={{0,8},{8,0},{16,24},{24,16},{1,9},{9,1},{17,25},{25,17},{2,10},{10... | collective-permute-start | bytes 480008 | tf_op jit(solution)/shard_map/ppermute | solution.py:599
  89.9 20.1 %collective-permute-start.8 = (bf16[100,800]{1,0:T(8,128)(2,1)S(1)}, bf16[100,800]{1,0:T(8,128)(2,1)S(1)}, u32[]{:S(2)}, u32[]{:S(2)}) collective-permute-start(bf16[100,800]{1,0:T(8,128)(2,1)S(1)} %copy-done.50), channel_id=1, source_target_pairs={{0,24},{8,16},{16,8},{24,0},{1,25},{9,17},{17,9},{25,1},{2,26},{10... | collective-permute-start | bytes 480008 | tf_op jit(solution)/shard_map/ppermute | solution.py:599
  94.7 16.7 %all-to-all-start = ((f32[32,3,400]{2,1,0:T(4,128)}), f32[32,3,400]{2,1,0:T(4,128)S(1)}, u32[]{:S(2)}, u32[]{:S(2)}) async-start(f32[32,3,400]{2,1,0:T(4,128)} %broadcast_in_dim.149), calls=%async_computation | async-start | bytes 524288 | tf_op jit(solution)/shard_map/all_to_all | solution.py:175
  98.4 131.4 %all-gather.12.cloned.1.call-start = ((), (), s32[]{:S(2)}) async-start(), calls=%async_computation.11 | async-start | bytes 1730560 | tf_op jit(solution)/shard_map/all_gather | solution.py:854
  99.4 40.8 %collective-permute-start.12 = (bf16[400,800]{1,0:T(8,128)(2,1)}, bf16[400,800]{1,0:T(8,128)(2,1)}, u32[]{:S(2)}, u32[]{:S(2)}) collective-permute-start(bf16[400,800]{1,0:T(8,128)(2,1)} %dynamic-slice_bitcast_fusion.1), channel_id=1, source_target_pairs={{0,8},{8,0},{16,24},{24,16},{1,9},{9,1},{17,25},{25,17},{2,10},{10... | collective-permute-start | bytes 1920008 | tf_op jit(solution)/shard_map/ppermute | solution.py:599
  101.2 39.0 %collective-permute-start.13 = (bf16[400,800]{1,0:T(8,128)(2,1)}, bf16[400,800]{1,0:T(8,128)(2,1)}, u32[]{:S(2)}, u32[]{:S(2)}) collective-permute-start(bf16[400,800]{1,0:T(8,128)(2,1)} %dynamic-slice_bitcast_fusion.1), channel_id=1, source_target_pairs={{0,16},{8,24},{16,0},{24,8},{1,17},{9,25},{17,1},{25,9},{2,18},{10... | collective-permute-start | bytes 1920008 | tf_op jit(solution)/shard_map/ppermute | solution.py:599
  102.6 39.2 %collective-permute-start.14 = (bf16[400,800]{1,0:T(8,128)(2,1)}, bf16[400,800]{1,0:T(8,128)(2,1)}, u32[]{:S(2)}, u32[]{:S(2)}) collective-permute-start(bf16[400,800]{1,0:T(8,128)(2,1)} %dynamic-slice_bitcast_fusion.1), channel_id=1, source_target_pairs={{0,24},{8,16},{16,8},{24,0},{1,25},{9,17},{17,9},{25,1},{2,26},{10... | collective-permute-start | bytes 1920008 | tf_op jit(solution)/shard_map/ppermute | solution.py:599
  115.5 72.5 %collective-permute-start.11 = (bf16[800,1664]{1,0:T(8,128)(2,1)}, bf16[800,1664]{1,0:T(8,128)(2,1)}, u32[]{:S(2)}, u32[]{:S(2)}) collective-permute-start(bf16[800,1664]{1,0:T(8,128)(2,1)} %all-gather.8.cloned.1.call-done.mine), channel_id=1, source_target_pairs={{0,1},{1,0},{2,3},{3,2},{4,5},{5,4},{6,7},{7,6},{8,9},{9,8},{10,11... | collective-permute-start | bytes 7987208 | tf_op jit(solution)/shard_map/ppermute | solution.py:599
  143.8 36.7 %collective-permute-start.15 = (bf16[3,400,800]{2,1,0:T(8,128)(2,1)S(1)}, bf16[3,400,800]{2,1,0:T(8,128)(2,1)}, u32[]{:S(2)}, u32[]{:S(2)}) collective-permute-start(bf16[3,400,800]{2,1,0:T(8,128)(2,1)S(1)} %pad_maximum_fusion.3.mine), channel_id=1, source_target_pairs={{0,1},{1,0},{2,3},{3,2},{4,5},{5,4},{6,7},{7,6},{8,9},{9,8},{10,11... | collective-permute-start | bytes 5760008 | tf_op jit(solution)/shard_map/ppermute | solution.py:599
  169.3 25.7 %all-to-all-start.1 = ((f32[32,3,800]{2,1,0:T(4,128)}), f32[32,3,800]{2,1,0:T(4,128)S(1)}, u32[]{:S(2)}, u32[]{:S(2)}) async-start(f32[32,3,800]{2,1,0:T(4,128)} %broadcast_in_dim.152), calls=%async_computation.1 | async-start | bytes 917504 | tf_op jit(solution)/shard_map/all_to_all | solution.py:175
  171.9 97.4 %all-gather.10.cloned.1.call-start = ((), (), s32[]{:S(2)}) async-start(), calls=%async_computation.10 | async-start | bytes 2048000 | tf_op jit(solution)/shard_map/all_gather | solution.py:855
  174.4 35.7 %collective-permute-start.16 = (bf16[304,400]{0,1:T(8,128)(2,1)S(1)}, bf16[304,400]{0,1:T(8,128)(2,1)S(1)}, u32[]{:S(2)}, u32[]{:S(2)}) collective-permute-start(bf16[304,400]{0,1:T(8,128)(2,1)S(1)} %get-tuple-element.282), channel_id=1, source_target_pairs={{0,8},{8,0},{16,24},{24,16},{1,9},{9,1},{17,25},{25,17},{2,10},{10... | collective-permute-start | bytes 729608 | tf_op jit(solution)/shard_map/ppermute | solution.py:599
  176.0 34.5 %collective-permute-start.17 = (bf16[304,400]{0,1:T(8,128)(2,1)S(1)}, bf16[304,400]{0,1:T(8,128)(2,1)}, u32[]{:S(2)}, u32[]{:S(2)}) collective-permute-start(bf16[304,400]{0,1:T(8,128)(2,1)S(1)} %get-tuple-element.282), channel_id=1, source_target_pairs={{0,16},{8,24},{16,0},{24,8},{1,17},{9,25},{17,1},{25,9},{2,18},{10... | collective-permute-start | bytes 729608 | tf_op jit(solution)/shard_map/ppermute | solution.py:599
  177.5 33.0 %collective-permute-start.18 = (bf16[304,400]{0,1:T(8,128)(2,1)S(1)}, bf16[304,400]{0,1:T(8,128)(2,1)}, u32[]{:S(2)}, u32[]{:S(2)}) collective-permute-start(bf16[304,400]{0,1:T(8,128)(2,1)S(1)} %get-tuple-element.282), channel_id=1, source_target_pairs={{0,24},{8,16},{16,8},{24,0},{1,25},{9,17},{17,9},{25,1},{2,26},{10... | collective-permute-start | bytes 729608 | tf_op jit(solution)/shard_map/ppermute | solution.py:599
  180.4 70.9 %collective-permute-start.24 = (bf16[12,32,400]{2,1,0:T(8,128)(2,1)}, bf16[12,32,400]{2,1,0:T(8,128)(2,1)}, u32[]{:S(2)}, u32[]{:S(2)}) collective-permute-start(bf16[12,32,400]{2,1,0:T(8,128)(2,1)} %get-tuple-element.246), channel_id=1, source_target_pairs={{0,8},{8,0},{16,24},{24,16},{1,9},{9,1},{17,25},{25,17},{2,10},{10... | collective-permute-start | bytes 921608 | tf_op jit(solution)/shard_map/ppermute | solution.py:31
  188.0 63.3 %collective-permute-start.25 = (bf16[12,32,400]{2,1,0:T(8,128)(2,1)}, bf16[12,32,400]{2,1,0:T(8,128)(2,1)}, u32[]{:S(2)}, u32[]{:S(2)}) collective-permute-start(bf16[12,32,400]{2,1,0:T(8,128)(2,1)} %get-tuple-element.245), channel_id=1, source_target_pairs={{0,16},{8,24},{16,0},{24,8},{1,17},{9,25},{17,1},{25,9},{2,18},{10... | collective-permute-start | bytes 921608 | tf_op jit(solution)/shard_map/ppermute | solution.py:31
  210.1 41.2 %collective-permute-start.26 = (bf16[12,32,400]{2,1,0:T(8,128)(2,1)}, bf16[12,32,400]{2,1,0:T(8,128)(2,1)}, u32[]{:S(2)}, u32[]{:S(2)}) collective-permute-start(bf16[12,32,400]{2,1,0:T(8,128)(2,1)} %get-tuple-element.244), channel_id=1, source_target_pairs={{0,24},{8,16},{16,8},{24,0},{1,25},{9,17},{17,9},{25,1},{2,26},{10... | collective-permute-start | bytes 921608 | tf_op jit(solution)/shard_map/ppermute | solution.py:31
  253.4 15.2 %all-to-all-start.2 = ((f32[32,3,400]{2,1,0:T(4,128)}), f32[32,3,400]{2,1,0:T(4,128)S(1)}, u32[]{:S(2)}, u32[]{:S(2)}) async-start(f32[32,3,400]{2,1,0:T(4,128)} %broadcast_in_dim.153), calls=%async_computation.2 | async-start | bytes 524288 | tf_op jit(solution)/shard_map/all_to_all | solution.py:175
  295.3 16.9 %all-to-all-start.3 = ((f32[32,2,400]{2,1,0:T(2,128)}), f32[32,2,400]{2,1,0:T(2,128)S(1)}, u32[]{:S(2)}, u32[]{:S(2)}) async-start(f32[32,2,400]{2,1,0:T(2,128)} %broadcast_in_dim.154), calls=%async_computation.3 | async-start | bytes 262144 | tf_op jit(solution)/shard_map/all_to_all | solution.py:175
  298.9 20.7 %collective-permute-start.21 = (bf16[12,32,400]{2,1,0:T(8,128)(2,1)}, bf16[12,32,400]{2,1,0:T(8,128)(2,1)S(1)}, u32[]{:S(2)}, u32[]{:S(2)}) collective-permute-start(bf16[12,32,400]{2,1,0:T(8,128)(2,1)} %get-tuple-element.255), channel_id=1, source_target_pairs={{0,8},{8,0},{16,24},{24,16},{1,9},{9,1},{17,25},{25,17},{2,10},{10... | collective-permute-start | bytes 921608 | tf_op jit(solution)/shard_map/ppermute | solution.py:55
  300.7 19.1 %collective-permute-start.22 = (bf16[12,32,400]{2,1,0:T(8,128)(2,1)}, bf16[12,32,400]{2,1,0:T(8,128)(2,1)S(1)}, u32[]{:S(2)}, u32[]{:S(2)}) collective-permute-start(bf16[12,32,400]{2,1,0:T(8,128)(2,1)} %get-tuple-element.254), channel_id=1, source_target_pairs={{0,16},{8,24},{16,0},{24,8},{1,17},{9,25},{17,1},{25,9},{2,18},{10... | collective-permute-start | bytes 921608 | tf_op jit(solution)/shard_map/ppermute | solution.py:55
  302.1 18.7 %collective-permute-start.23 = (bf16[12,32,400]{2,1,0:T(8,128)(2,1)S(1)}, bf16[12,32,400]{2,1,0:T(8,128)(2,1)S(1)}, u32[]{:S(2)}, u32[]{:S(2)}) collective-permute-start(bf16[12,32,400]{2,1,0:T(8,128)(2,1)S(1)} %get-tuple-element.253), channel_id=1, source_target_pairs={{0,24},{8,16},{16,8},{24,0},{1,25},{9,17},{17,9},{25,1},{2,26},{10... | collective-permute-start | bytes 921608 | tf_op jit(solution)/shard_map/ppermute | solution.py:55
  363.2 18.0 %all-to-all-start.4 = ((f32[32,2,800]{2,1,0:T(2,128)}), f32[32,2,800]{2,1,0:T(2,128)S(1)}, u32[]{:S(2)}, u32[]{:S(2)}) async-start(f32[32,2,800]{2,1,0:T(2,128)} %broadcast_in_dim.155), calls=%async_computation.4 | async-start | bytes 458752 | tf_op jit(solution)/shard_map/all_to_all | solution.py:175
  368.5 307.2 %all-reduce.18.cloned.1.call-start = ((), (), s32[]{:S(2)}) async-start(), calls=%async_computation.12 | async-start | bytes 28057600 | tf_op jit(solution)/shard_map/psum | solution.py:890
  383.8 25.8 %collective-permute-start.29 = (bf16[24,3,800]{2,1,0:T(4,128)(2,1)S(1)}, bf16[24,3,800]{2,1,0:T(4,128)(2,1)S(1)}, u32[]{:S(2)}, u32[]{:S(2)}) collective-permute-start(bf16[24,3,800]{2,1,0:T(4,128)(2,1)S(1)} %get-tuple-element.269), channel_id=1, source_target_pairs={{0,1},{1,2},{2,3},{3,4},{4,5},{5,6},{6,7},{7,0},{8,9},{9,10},{10,1... | collective-permute-start | bytes 345608 | tf_op jit(solution)/shard_map/ppermute | solution.py:160
  384.1 25.5 %collective-permute-start.30 = (bf16[24,3,800]{2,1,0:T(4,128)(2,1)S(1)}, bf16[24,3,800]{2,1,0:T(4,128)(2,1)S(1)}, u32[]{:S(2)}, u32[]{:S(2)}) collective-permute-start(bf16[24,3,800]{2,1,0:T(4,128)(2,1)S(1)} %get-tuple-element.268), channel_id=1, source_target_pairs={{1,0},{2,1},{3,2},{4,3},{5,4},{6,5},{7,6},{0,7},{9,8},{10,9},{11,1... | collective-permute-start | bytes 345608 | tf_op jit(solution)/shard_map/ppermute | solution.py:161
  457.4 33.9 %collective-permute-start.36 = (bf16[6912,128]{1,0:T(8,128)(2,1)}, bf16[6912,128]{1,0:T(8,128)(2,1)S(1)}, u32[]{:S(2)}, u32[]{:S(2)}) collective-permute-start(bf16[6912,128]{1,0:T(8,128)(2,1)} %dynamic-slice_bitcast_fusion), channel_id=1, source_target_pairs={{0,1},{1,0},{2,3},{3,2},{4,5},{5,4},{6,7},{7,6},{8,9},{9,8},{10,11... | collective-permute-start | bytes 5308424 | tf_op jit(solution)/shard_map/ppermute | solution.py:599
  474.9 22.2 %collective-permute-start.31 = (bf16[48,3,400]{2,1,0:T(4,128)(2,1)}, bf16[48,3,400]{2,1,0:T(4,128)(2,1)}, u32[]{:S(2)}, u32[]{:S(2)}) collective-permute-start(bf16[48,3,400]{2,1,0:T(4,128)(2,1)} %get-tuple-element.237), channel_id=1, source_target_pairs={{0,1},{1,2},{2,3},{3,4},{4,5},{5,6},{6,7},{7,0},{8,9},{9,10},{10,1... | collective-permute-start | bytes 345608 | tf_op jit(solution)/shard_map/ppermute | solution.py:160
  475.2 21.9 %collective-permute-start.32 = (bf16[48,3,400]{2,1,0:T(4,128)(2,1)}, bf16[48,3,400]{2,1,0:T(4,128)(2,1)}, u32[]{:S(2)}, u32[]{:S(2)}) collective-permute-start(bf16[48,3,400]{2,1,0:T(4,128)(2,1)} %get-tuple-element.236), channel_id=1, source_target_pairs={{1,0},{2,1},{3,2},{4,3},{5,4},{6,5},{7,6},{0,7},{9,8},{10,9},{11,1... | collective-permute-start | bytes 345608 | tf_op jit(solution)/shard_map/ppermute | solution.py:161
  492.0 29.6 %collective-permute-start.39 = (bf16[1728,128]{1,0:T(8,128)(2,1)S(1)}, bf16[1728,128]{1,0:T(8,128)(2,1)}, u32[]{:S(2)}, u32[]{:S(2)}) collective-permute-start(bf16[1728,128]{1,0:T(8,128)(2,1)S(1)} %dynamic-slice_bitcast_fusion.2), channel_id=1, source_target_pairs={{0,16},{8,24},{16,0},{24,8},{1,17},{9,25},{17,1},{25,9},{2,18},{10... | collective-permute-start | bytes 1327112 | tf_op jit(solution)/shard_map/ppermute | solution.py:599
  494.2 66.6 %all-to-all-start.6 = ((f32[32,32,128]{2,1,0:T(8,128)}), f32[32,32,128]{2,1,0:T(8,128)S(1)}, u32[]{:S(2)}, u32[]{:S(2)}) async-start(f32[32,32,128]{2,1,0:T(8,128)} %bitcast.103), calls=%async_computation.6 | async-start | bytes 1048576 | tf_op jit(solution)/shard_map/all_to_all | solution.py:715
  516.2 43.5 %collective-permute-start.33 = (bf16[12,32,400]{2,1,0:T(8,128)(2,1)S(1)}, bf16[12,32,400]{2,1,0:T(8,128)(2,1)S(1)}, u32[]{:S(2)}, u32[]{:S(2)}) collective-permute-start(bf16[12,32,400]{2,1,0:T(8,128)(2,1)S(1)} %get-tuple-element.235), channel_id=1, source_target_pairs={{0,8},{8,0},{16,24},{24,16},{1,9},{9,1},{17,25},{25,17},{2,10},{10... | collective-permute-start | bytes 921608 | tf_op jit(solution)/shard_map/ppermute | solution.py:55
  518.0 42.5 %collective-permute-start.34 = (bf16[12,32,400]{2,1,0:T(8,128)(2,1)S(1)}, bf16[12,32,400]{2,1,0:T(8,128)(2,1)S(1)}, u32[]{:S(2)}, u32[]{:S(2)}) collective-permute-start(bf16[12,32,400]{2,1,0:T(8,128)(2,1)S(1)} %get-tuple-element.234), channel_id=1, source_target_pairs={{0,16},{8,24},{16,0},{24,8},{1,17},{9,25},{17,1},{25,9},{2,18},{10... | collective-permute-start | bytes 921608 | tf_op jit(solution)/shard_map/ppermute | solution.py:55
  519.5 41.0 %collective-permute-start.35 = (bf16[12,32,400]{2,1,0:T(8,128)(2,1)S(1)}, bf16[12,32,400]{2,1,0:T(8,128)(2,1)S(1)}, u32[]{:S(2)}, u32[]{:S(2)}) collective-permute-start(bf16[12,32,400]{2,1,0:T(8,128)(2,1)S(1)} %get-tuple-element.233), channel_id=1, source_target_pairs={{0,24},{8,16},{16,8},{24,0},{1,25},{9,17},{17,9},{25,1},{2,26},{10... | collective-permute-start | bytes 921608 | tf_op jit(solution)/shard_map/ppermute | solution.py:55
  519.8 28.6 %collective-permute-start.37 = (bf16[1728,128]{1,0:T(8,128)(2,1)S(1)}, bf16[1728,128]{1,0:T(8,128)(2,1)S(1)}, u32[]{:S(2)}, u32[]{:S(2)}) collective-permute-start(bf16[1728,128]{1,0:T(8,128)(2,1)S(1)} %dynamic-slice_bitcast_fusion.3), channel_id=1, source_target_pairs={{0,8},{8,0},{16,24},{24,16},{1,9},{9,1},{17,25},{25,17},{2,10},{10... | collective-permute-start | bytes 1327112 | tf_op jit(solution)/shard_map/ppermute | solution.py:599
  522.8 30.0 %collective-permute-start.40 = (bf16[864,128]{1,0:T(8,128)(2,1)S(1)}, bf16[864,128]{1,0:T(8,128)(2,1)S(1)}, u32[]{:S(2)}, u32[]{:S(2)}) collective-permute-start(bf16[864,128]{1,0:T(8,128)(2,1)S(1)} %dynamic-slice_bitcast_fusion.30), channel_id=1, source_target_pairs={{0,8},{8,0},{16,24},{24,16},{1,9},{9,1},{17,25},{25,17},{2,10},{10... | collective-permute-start | bytes 663560 | tf_op jit(solution)/shard_map/ppermute | solution.py:599
  557.2 16.9 %collective-permute-start.42 = (bf16[2,216,128]{2,1,0:T(8,128)(2,1)}, bf16[2,216,128]{2,1,0:T(8,128)(2,1)}, u32[]{:S(2)}, u32[]{:S(2)}) collective-permute-start(bf16[2,216,128]{2,1,0:T(8,128)(2,1)} %get-tuple-element.279), channel_id=1, source_target_pairs={{0,4},{1,5},{2,6},{3,7},{4,0},{5,1},{6,2},{7,3},{8,12},{9,13},{10,... | collective-permute-start | bytes 331784 | tf_op jit(solution)/shard_map/ppermute | solution.py:599
  559.7 14.7 %collective-permute-start.43 = (bf16[2,216,128]{2,1,0:T(8,128)(2,1)}, bf16[2,216,128]{2,1,0:T(8,128)(2,1)}, u32[]{:S(2)}, u32[]{:S(2)}) collective-permute-start(bf16[2,216,128]{2,1,0:T(8,128)(2,1)} %get-tuple-element.280), channel_id=1, source_target_pairs={{0,6},{1,7},{2,4},{3,5},{4,2},{5,3},{6,0},{7,1},{8,14},{9,15},{10,... | collective-permute-start | bytes 331784 | tf_op jit(solution)/shard_map/ppermute | solution.py:599
  561.7 43.2 %all-to-all-start.7 = ((f32[32,32,128]{2,1,0:T(8,128)}), f32[32,32,128]{2,1,0:T(8,128)S(1)}, u32[]{:S(2)}, u32[]{:S(2)}) async-start(f32[32,32,128]{2,1,0:T(8,128)} %broadcast_in_dim.157), calls=%async_computation.7 | async-start | bytes 1048576 | tf_op jit(solution)/shard_map/all_to_all | solution.py:717
  575.4 15.2 %collective-permute-start.44 = (bf16[2,216,128]{2,1,0:T(8,128)(2,1)S(1)}, bf16[2,216,128]{2,1,0:T(8,128)(2,1)S(1)}, u32[]{:S(2)}, u32[]{:S(2)}) collective-permute-start(bf16[2,216,128]{2,1,0:T(8,128)(2,1)S(1)} %fusion.24), channel_id=1, source_target_pairs={{0,2},{1,3},{2,0},{3,1},{4,6},{5,7},{6,4},{7,5},{8,10},{9,11},{10,... | collective-permute-start | bytes 331784 | tf_op jit(solution)/shard_map/ppermute | solution.py:599
  587.5 13.7 %collective-permute-start.45 = (bf16[2,216,128]{2,1,0:T(8,128)(2,1)S(1)}, bf16[2,216,128]{2,1,0:T(8,128)(2,1)S(1)}, u32[]{:S(2)}, u32[]{:S(2)}) collective-permute-start(bf16[2,216,128]{2,1,0:T(8,128)(2,1)S(1)} %fusion.24), channel_id=1, source_target_pairs={{0,4},{1,5},{2,6},{3,7},{4,0},{5,1},{6,2},{7,3},{8,12},{9,13},{10,... | collective-permute-start | bytes 331784 | tf_op jit(solution)/shard_map/ppermute | solution.py:599
  613.8 16.4 %collective-permute-start.48 = (bf16[1728,128]{1,0:T(8,128)(2,1)S(1)}, bf16[1728,128]{1,0:T(8,128)(2,1)S(1)}, u32[]{:S(2)}, u32[]{:S(2)}) collective-permute-start(bf16[1728,128]{1,0:T(8,128)(2,1)S(1)} %maximum_select_fusion.2), channel_id=1, source_target_pairs={{0,8},{8,0},{16,24},{24,16},{1,9},{9,1},{17,25},{25,17},{2,10},{10... | collective-permute-start | bytes 1327112 | tf_op jit(solution)/shard_map/ppermute | solution.py:599
  (110 other events, 802.8 us)
Sparse Core Ops, SparseCore 0:
  10.5 47.0 all-gather.5
  59.9 52.7 all-gather.7
  141.9 28.4 all-gather.11
  178.0 46.7 all-gather.9
  389.2 286.4 all-reduce.17

commit v9 on v8

--- a/solution.py
+++ b/solution.py
@@ -135,20 +135,21 @@
     return assemble(assemble_rows_kernel, "assemble_rows", shape, (shard, mine, swap(mine, "lon", 1)), 2 * tiles - 1)
 
 
-def gathered_by_columns(shard):
+def gathered_by_columns(shard, event):
     columns = shard.shape[1]
     start = columns // 2 // lanes * lanes
     half = lax.dynamic_slice_in_dim(shard, lax.axis_index("lon") % 2 * start, columns - start, axis=1)
-    mine = lax.all_gather(half, "lat", axis=0, tiled=True)
+    mine = after(lax.all_gather(half, "lat", axis=0, tiled=True), event)
     return assemble(
         assemble_columns_kernel, "assemble_columns", (mine.shape[0], columns), (mine, swap(mine, "lon", 1)), 2
     )
 
 
-def gathered_pair(up, down):
+def gathered_pair(up, down, event):
     channels = down.shape[1]
     first = lax.axis_index("lon") % 2 == 0
     mine = lax.all_gather(jnp.where(first, up.reshape(-1, channels), down), "lat", axis=0, tiled=True)
+    mine = after(mine, event)
     theirs = swap(mine, "lon", 1)
     return jnp.where(first, mine, theirs).reshape(-1, up.shape[1]), jnp.where(first, theirs, mine)
 
@@ -831,8 +832,6 @@
     height = fine.shape[0]
     half_height, half_breadth = height // 2, breadth // 2
 
-    encode_up, encode_down = gathered_pair(encode_up, encode_down)
-    bottle_up = gathered_by_columns(bottle_up)
 
     coarse_band = jnp.max(ocean_band.reshape(half_height, 2, half_breadth, 2), axis=(1, 3))
     sea_fine = jnp.broadcast_to(ocean_band[..., None], (height, breadth, lanes))
@@ -846,6 +845,7 @@
     blocks = jnp.asarray(np.arange(pixel.size // 4)[:, None] == block, dtype=bf16)
 
     mix = block_mix(fine, encode_norm, sea_fine, ocean_fine, dates)
+    encode_up, encode_down = gathered_pair(encode_up, encode_down, mix[3])
     encode = encode_norm + (encode_up, encode_up_bias, encode_down, encode_down_bias)
     widen_weight = gathered(after(widen_weight, mix[3]))
     skip_rows, (pooled, coarse_in), encode_stored = block_forward(
@@ -854,6 +854,7 @@
     decode_up = lax.all_gather(after(decode_up, skip_rows), "lat", axis=0, tiled=True)
     decode_down = lax.all_gather(after(decode_down, skip_rows), "lat", axis=0, tiled=True)
     decode = decode_norm + (decode_up, decode_up_bias, decode_down, decode_down_bias)
+    bottle_up = gathered_by_columns(bottle_up, skip_rows)
     bottle_down = gathered_by_rows(after(bottle_down, encode_stored[3]), skip_rows)
     bottle = bottle_norm + (bottle_up, bottle_up_bias, bottle_down, bottle_down_bias)
     coarse_in = coarse_in.reshape(half_height, half_breadth, wide)

time: 711 us -> 693 us (0.975)
  Pallas kernels: 252 us -> 240 us
  starting transfers between devices: 111 us -> 119 us
  waiting for transfers between devices: 162 us -> 154 us
    all_gather x1, waiting for transfers between devices: 15.3 us -> 0.02 us  [gathered_pair(): lax.all_gather(jnp.where(first, up.reshape(-1, channels), down), 'lat', a...]
    all_gather x1, waiting for transfers between devices: 0.01 us -> 8.1 us  [gathered_by_columns(): mine = after(lax.all_gather(half, 'lat', axis=0, tiled=True), event)]
    ppermute x28, starting transfers between devices: 42.5 us -> 50.5 us  [swap(): lax.ppermute(array, axis, [(i, i ^ step) for i in range(lax.axis_size(axi...]
    unnamed x208 -> x218, local copies, waits for them, and re-layouts: 14.5 us -> 14.1 us
  transfers between devices with their start and end apart: 65 -> 65, of which waited for: 27 -> 23; matrix products, arithmetic and copies ran while one was open for 18% -> 18% of each run, Pallas kernels for 27% -> 27%
where the time goes in v9:
time: 693 us; the launch traced here: 686 us
  Pallas kernels  240 us (35%)
  waiting for transfers between devices  154 us (22%)
  starting transfers between devices  119 us (17%)
  local copies, waits for them, and re-layouts  71.7 us (10%)
  other arithmetic  59.1 us (9%)
  matrix products  25.9 us (4%)
  between operations  16.1 us (2%)
    ppermute x28, waiting for transfers between devices, swap(): lax.ppermute(array, axis, [(i, i ^ step) for i in range(lax.axis_size(axi...  75.5 us
    ppermute x28, starting transfers between devices, swap(): lax.ppermute(array, axis, [(i, i ^ step) for i in range(lax.axis_size(axi...  50.5 us
    pallas_call x3, Pallas kernels, mlp_forward(): pl.pallas_call(functools.partial(mlp_forward_kernel, 512), grid=(parts,),...  40.9 us
    pallas_call x3, Pallas kernels, stencil_backward(): pl.pallas_call(functools.partial(stencil_backward_kernel, len(edges)), gr...  39.4 us
    pallas_call x3, Pallas kernels, stencil_forward(): pl.pallas_call(functools.partial(stencil_forward_kernel, len(edges)), gri...  38.5 us
    pallas_call x3, Pallas kernels, mlp_backward(): pl.pallas_call(functools.partial(mlp_backward_kernel, 512), grid=(pixels...  37.8 us
    pallas_call x3, Pallas kernels, kernel_grad(): pl.pallas_call(functools.partial(kernel_grad_kernel, len(edges)), grid=(t...  32.9 us
    psum x1, waiting for transfers between devices, shards(): early = lax.psum([part.astype(bf16) for part in early], both)  28.5 us
  transfers between devices with their start and end apart: 65, of which 23 were waited for; matrix products, arithmetic and copies ran while one was open for 18% of the time, Pallas kernels for 27%

profile of v9, /device:TPU:0, one launch (start us, length us, event | category | flops | bytes accessed | tf_op | source)
XLA Modules:
  0.0 686.1 jit_solution(3269016047204933469)
XLA Ops:
  23.1 5.3 collective-permute-done
  28.3 11.2 %collective-permute-done.1 = bf16[13,32,400]{2,1,0:T(8,128)(2,1)S(1)} collective-permute-done((bf16[13,32,400]{2,1,0:T(8,128)(2,1)S(1)}, bf16[13,32,400]{2,1,0:T(8,128)(2,1)S(1)}, u32[]{:S(2)}, u32[]{:S(2)}) %collective-permute-start.1) | collective-permute-done | bytes 332832 | tf_op jit(solution)/shard_map/ppermute | solution.py:31
  49.6 15.0 %stencil_forward.3 = (f32[48,32,400]{2,1,0:T(8,128)}, f32[2,400]{1,0:T(2,128)}) custom-call(bf16[48,32,400]{2,1,0:T(8,128)(2,1)} %bitcast.268, bf16[48,3,400]{2,1,0:T(4,128)(2,1)} %copy-done.31, bf16[48,3,400]{2,1,0:T(4,128)(2,1)} %copy-done.32, f32[49,400]{1,0:T(8,128)} %reshape.345.refs_2_, f32[48,32,128]{2,1,0:T(8,128)} %broadcast_in_dim.147.refs_3_), custom_call_target="tpu_custom_call" | custom-call | tf_op jit(solution)/shard_map/stencil_forward/pallas_call | solution.py:287
  83.0 7.0 %collective-permute-start.14 = (bf16[400,800]{1,0:T(8,128)(2,1)}, bf16[400,800]{1,0:T(8,128)(2,1)}, u32[]{:S(2)}, u32[]{:S(2)}) collective-permute-start(bf16[400,800]{1,0:T(8,128)(2,1)} %dynamic-slice_bitcast_fusion.1), channel_id=1, source_target_pairs={{0,24},{8,16},{16,8},{24,0},{1,25},{9,17},{17,9},{25,1},{2,26},{10... | collective-permute-start | bytes 1920008 | tf_op jit(solution)/shard_map/ppermute | solution.py:600
  98.2 4.4 reshape.303.up
  103.8 14.8 %mlp_forward.3 = (bf16[1536,400]{1,0:T(8,128)(2,1)}, bf16[1536,1600]{1,0:T(8,128)(2,1)}, bf16[1536,1600]{1,0:T(8,128)(2,1)}, bf16[1536,400]{1,0:T(8,128)(2,1)}, ...) custom-call(f32[1536,400]{1,0:T(8,128)} %bitcast.274, bf16[1536,400]{1,0:T(8,128)(2,1)} %bitcast.269, ...), custom_call_target="tpu_custom_call" | custom-call | tf_op jit(solution)/shard_map/mlp_forward/pallas_call | solution.py:467
  118.6 8.1 %all-gather.8.cloned.1.call-done.mine = bf16[800,1664]{1,0:T(8,128)(2,1)} async-done(((bf16[200,1664]{1,0:T(8,128)(2,1)}), bf16[800,1664]{1,0:T(8,128)(2,1)}) %all-gather.8.cloned.1.call-update) | async-done | bytes 2662416 | tf_op jit(solution)/shard_map/all_gather | solution.py:142
  127.8 6.5 collective-permute-done.14
  149.9 8.5 %stencil_forward.4 = (f32[24,16,800]{2,1,0:T(8,128)}, f32[2,800]{1,0:T(2,128)}) custom-call(bf16[24,16,800]{2,1,0:T(8,128)(2,1)} %bitcast.295, bf16[24,3,800]{2,1,0:T(4,128)(2,1)} %copy-done.37, bf16[24,3,800]{2,1,0:T(4,128)(2,1)} %copy-done.36, f32[49,800]{1,0:T(8,128)} %reshape.347.refs_2_, f32[24,16,128]{2,1,0:T(8,128)} %broadcast_in_dim.150.refs_3_), custom_call_target="tpu_custom_call" | custom-call | tf_op jit(solution)/shard_map/stencil_forward/pallas_call | solution.py:287
  174.0 5.9 assemble_rows.1.down
  181.2 5.5 assemble_columns.1.up
  188.8 13.5 %mlp_forward.4 = (bf16[384,800]{1,0:T(8,128)(2,1)}, bf16[384,3200]{1,0:T(8,128)(2,1)}, bf16[384,3200]{1,0:T(8,128)(2,1)}, bf16[384,800]{1,0:T(8,128)(2,1)}) custom-call(f32[384,800]{1,0:T(8,128)} %bitcast.289, bf16[384,800]{1,0:T(8,128)(2,1)} %get-tuple-element.129.source, f32[384,128]{1,0:T(8,128)} %broadcast_in_dim.151.sea, ...), custom_call_target="tpu_custom_call" | custom-call | tf_op jit(solution)/shard_map/mlp_forward/pallas_call | solution.py:467
  209.8 6.1 merge_forward.1.source
  226.1 15.0 %stencil_forward.5 = (f32[48,32,400]{2,1,0:T(8,128)}, f32[2,400]{1,0:T(2,128)}) custom-call(bf16[48,32,400]{2,1,0:T(8,128)(2,1)} %bitcast.272, bf16[48,3,400]{2,1,0:T(4,128)(2,1)} %copy-done.33, bf16[48,3,400]{2,1,0:T(4,128)(2,1)} %copy-done.34, f32[49,400]{1,0:T(8,128)} %reshape.349.refs_2_, f32[48,32,128]{2,1,0:T(8,128)} %broadcast_in_dim.147.refs_3_), custom_call_target="tpu_custom_call" | custom-call | tf_op jit(solution)/shard_map/stencil_forward/pallas_call | solution.py:287
  243.2 5.2 all-to-all-start.2
  251.6 7.2 %all-to-all-done.2 = f32[32,3,400]{2,1,0:T(4,128)S(1)} async-done(((f32[32,3,400]{2,1,0:T(4,128)}), f32[32,3,400]{2,1,0:T(4,128)S(1)}, u32[]{:S(2)}, u32[]{:S(2)}) %all-to-all-start.2) | async-done | bytes 153632 | tf_op jit(solution)/shard_map/all_to_all | solution.py:176
  260.1 12.6 %mlp_forward.5 = (bf16[1536,400]{1,0:T(8,128)(2,1)}, bf16[1536,1600]{1,0:T(8,128)(2,1)}, bf16[1536,1600]{1,0:T(8,128)(2,1)}, bf16[1536,400]{1,0:T(8,128)(2,1)}) custom-call(f32[1536,400]{1,0:T(8,128)} %bitcast.277, bf16[1536,400]{1,0:T(8,128)(2,1)} %merge_forward.1.source, f32[1536,128]{1,0:T(8,128)} %broadcast_in_dim.148.sea, ...), custom_call_target="tpu_custom_call" | custom-call | tf_op jit(solution)/shard_map/mlp_forward/pallas_call | solution.py:467
  272.7 12.0 %mlp_backward.3 = (bf16[1536,400]{1,0:T(8,128)(2,1)}, bf16[1536,1600]{1,0:T(8,128)(2,1)}, f32[1536,400]{1,0:T(8,128)}, f32[2,400]{1,0:T(2,128)}, f32[1,400]{1,0:T(1,128)}, /*index=5*/f32[1,1600]{1,0:T(1,128)}) custom-call(bf16[1536,400]{1,0:T(8,128)(2,1)} %bitcast.285, f32[1536,400]{1,0:T(8,128)} %bitcast.278, bf16[1536,1600]{1,0:T(8,128)(2,1)} %get-tuple-element.165.slope, ...), custom_call_target="tpu_custom_call" | custom-call | tf_op jit(solution)/shard_map/mlp_backward/pallas_call | solution.py:527
  293.3 6.1 fusion.12
  307.3 3.7 collective-permute-start.28
  315.6 15.2 %stencil_backward.3 = (bf16[48,32,400]{2,1,0:T(8,128)(2,1)}, f32[1,400]{1,0:T(1,128)}) custom-call(bf16[48,32,400]{2,1,0:T(8,128)(2,1)} %bitcast.280, bf16[48,3,400]{2,1,0:T(4,128)(2,1)} %copy-done.45, bf16[48,3,400]{2,1,0:T(4,128)(2,1)} %copy-done.46, f32[49,400]{1,0:T(8,128)} %reshape.349.refs_2_, f32[48,32,128]{2,1,0:T(8,128)} %broadcast_in_dim.147.refs_3_, ...), custom_call_target="tpu_custom_call" | custom-call | tf_op jit(solution)/shard_map/stencil_backward/pallas_call | solution.py:303
  330.8 5.1 merge_backward.1
  337.5 13.0 %mlp_backward.4 = (bf16[384,800]{1,0:T(8,128)(2,1)}, bf16[384,3200]{1,0:T(8,128)(2,1)}, f32[384,800]{1,0:T(8,128)}, f32[2,800]{1,0:T(2,128)}, f32[1,800]{1,0:T(1,128)}, /*index=5*/f32[1,3200]{1,0:T(1,128)}) custom-call(f32[384,800]{1,0:T(8,128)} %get-tuple-element.169.upstream, f32[384,800]{1,0:T(8,128)} %bitcast.290, ...), custom_call_target="tpu_custom_call" | custom-call | tf_op jit(solution)/shard_map/mlp_backward/pallas_call | solution.py:527
  351.9 5.3 all-to-all-start.4
  357.3 7.3 %fusion.2 = bf16[3200,800]{0,1:T(8,128)(2,1)} fusion(bf16[384,800]{1,0:T(8,128)(2,1)} %get-tuple-element.196, bf16[384,3200]{1,0:T(8,128)(2,1)} %get-tuple-element.197), kind=kOutput, calls=%fused_computation.5 | convolution fusion | flops 1968640000 | bytes 8192000 | tf_op jit(solution)/shard_map/dot_general | solution.py:722
  364.7 5.3 convolution_convert_fusion.1
  377.5 12.6 %kernel_grad.5 = f32[4,56,128]{2,1,0:T(8,128)} custom-call(bf16[48,32,400]{2,1,0:T(8,128)(2,1)} %bitcast.273, bf16[48,3,400]{2,1,0:T(4,128)(2,1)} %copy-done.33, bf16[48,3,400]{2,1,0:T(4,128)(2,1)} %copy-done.34, bf16[48,32,400]{2,1,0:T(8,128)(2,1)} %bitcast.281), custom_call_target="tpu_custom_call" | custom-call | tf_op jit(solution)/shard_map/kernel_grad/pallas_call | solution.py:319
  390.2 7.6 %kernel_grad.4 = f32[7,56,128]{2,1,0:T(8,128)} custom-call(bf16[24,16,800]{2,1,0:T(8,128)(2,1)} %bitcast.296, bf16[24,3,800]{2,1,0:T(4,128)(2,1)} %copy-done.37, bf16[24,3,800]{2,1,0:T(4,128)(2,1)} %copy-done.36, bf16[24,16,800]{2,1,0:T(8,128)(2,1)} %bitcast.293), custom_call_target="tpu_custom_call" | custom-call | tf_op jit(solution)/shard_map/kernel_grad/pallas_call | solution.py:319
  398.5 8.9 %stencil_backward.4 = (bf16[24,16,800]{2,1,0:T(8,128)(2,1)}, f32[1,800]{1,0:T(1,128)}) custom-call(bf16[24,16,800]{2,1,0:T(8,128)(2,1)} %bitcast.294, bf16[24,3,800]{2,1,0:T(4,128)(2,1)} %copy-done.48, bf16[24,3,800]{2,1,0:T(4,128)(2,1)} %copy-done.49, f32[49,800]{1,0:T(8,128)} %reshape.347.refs_2_, f32[24,16,128]{2,1,0:T(8,128)} %broadcast_in_dim.150.refs_3_, ...), custom_call_target="tpu_custom_call" | custom-call | tf_op jit(solution)/shard_map/stencil_backward/pallas_call | solution.py:303
  407.4 7.1 %skip_backward.1.upstream = f32[1536,400]{1,0:T(8,128)} custom-call(bf16[1536,400]{1,0:T(8,128)(2,1)} %bitcast.287, bf16[384,800]{1,0:T(8,128)(2,1)} %bitcast.311, bf16[1200,400]{1,0:T(8,128)(2,1)} %copy.103.merge, bf16[400,800]{1,0:T(8,128)(2,1)} %pad_maximum_fusion.16.refs_1_.widen, bf16[384,96]{1,0:T(8,128)(2,1)} %constant.276.clone.members), custom_call_target="tpu_custom_call" | custom-call | tf_op jit(solution)/shard_map/skip_backward/pallas_call | solution.py:510
  415.9 12.8 %mlp_backward.5 = (bf16[1536,400]{1,0:T(8,128)(2,1)}, bf16[1536,1600]{1,0:T(8,128)(2,1)}, f32[1536,400]{1,0:T(8,128)}, f32[2,400]{1,0:T(2,128)}, f32[1,400]{1,0:T(1,128)}, /*index=5*/f32[1,1600]{1,0:T(1,128)}) custom-call(f32[1536,400]{1,0:T(8,128)} %skip_backward.1.upstream, f32[1536,400]{1,0:T(8,128)} %bitcast.275, ...), custom_call_target="tpu_custom_call" | custom-call | tf_op jit(solution)/shard_map/mlp_backward/pallas_call | solution.py:527
  428.7 11.8 %weight_grads.1 = bf16[2,13,400,128]{3,2,1,0:T(8,128)(2,1)} custom-call(bf16[1536,400]{1,0:T(8,128)(2,1)} %get-tuple-element.187.grad_branch, bf16[1536,400]{1,0:T(8,128)(2,1)} %get-tuple-element.188.normed, bf16[1536,1600]{1,0:T(8,128)(2,1)} %get-tuple-element.189.active, bf16[1536,1600]{1,0:T(8,128)(2,1)} %get-tuple-element.190.grad_hidden), custom_call_target="tpu_custom_call" | custom-call | tf_op jit(solution)/shard_map/weight_grads/pallas_call | solution.py:563
  445.5 4.2 all-to-all-start.5
  449.9 7.9 %all-to-all-done.5 = f32[32,2,400]{2,1,0:T(2,128)S(1)} async-done(((f32[32,2,400]{2,1,0:T(2,128)}), f32[32,2,400]{2,1,0:T(2,128)S(1)}, u32[]{:S(2)}, u32[]{:S(2)}) %all-to-all-start.5) | async-done | bytes 102432 | tf_op jit(solution)/shard_map/all_to_all | solution.py:176
  457.9 3.8 multiply_convert_fusion
  466.4 12.6 %kernel_grad.3 = f32[4,56,128]{2,1,0:T(8,128)} custom-call(bf16[48,32,400]{2,1,0:T(8,128)(2,1)} %bitcast.270, bf16[48,3,400]{2,1,0:T(4,128)(2,1)} %copy-done.31, bf16[48,3,400]{2,1,0:T(4,128)(2,1)} %copy-done.32, bf16[48,32,400]{2,1,0:T(8,128)(2,1)} %bitcast.283), custom_call_target="tpu_custom_call" | custom-call | tf_op jit(solution)/shard_map/kernel_grad/pallas_call | solution.py:319
  486.8 15.3 %stencil_backward.5 = (bf16[48,32,400]{2,1,0:T(8,128)(2,1)}, f32[1,400]{1,0:T(1,128)}) custom-call(bf16[48,32,400]{2,1,0:T(8,128)(2,1)} %bitcast.284, bf16[48,3,400]{2,1,0:T(4,128)(2,1)} %copy-done.44, bf16[48,3,400]{2,1,0:T(4,128)(2,1)} %collective-permute-done.32.refs_1_, f32[49,400]{1,0:T(8,128)} %reshape.345.refs_2_, ...), custom_call_target="tpu_custom_call" | custom-call | tf_op jit(solution)/shard_map/stencil_backward/pallas_call | solution.py:303
  509.6 26.7 %collective-permute-done.37 = bf16[1728,128]{1,0:T(8,128)(2,1)S(1)} collective-permute-done((bf16[1728,128]{1,0:T(8,128)(2,1)S(1)}, bf16[1728,128]{1,0:T(8,128)(2,1)S(1)}, u32[]{:S(2)}, u32[]{:S(2)}) %collective-permute-start.37) | collective-permute-done | bytes 442400 | tf_op jit(solution)/shard_map/ppermute | solution.py:600
  549.0 5.5 all-to-all-start.7
  554.5 6.8 collective-permute-done.42
  561.7 12.1 %collective-permute-start.44 = (bf16[2,216,128]{2,1,0:T(8,128)(2,1)S(1)}, bf16[2,216,128]{2,1,0:T(8,128)(2,1)S(1)}, u32[]{:S(2)}, u32[]{:S(2)}) collective-permute-start(bf16[2,216,128]{2,1,0:T(8,128)(2,1)S(1)} %fusion.24), channel_id=1, source_target_pairs={{0,2},{1,3},{2,0},{3,1},{4,6},{5,7},{6,4},{7,5},{8,10},{9,11},{10,... | collective-permute-start | bytes 331784 | tf_op jit(solution)/shard_map/ppermute | solution.py:600
  577.3 11.3 %collective-permute-done.45 = bf16[2,216,128]{2,1,0:T(8,128)(2,1)S(1)} collective-permute-done((bf16[2,216,128]{2,1,0:T(8,128)(2,1)S(1)}, bf16[2,216,128]{2,1,0:T(8,128)(2,1)S(1)}, u32[]{:S(2)}, u32[]{:S(2)}) %collective-permute-start.45) | collective-permute-done | bytes 110624 | tf_op jit(solution)/shard_map/ppermute | solution.py:600
  594.0 7.0 %collective-permute-done.47 = bf16[864,128]{1,0:T(8,128)(2,1)S(1)} collective-permute-done((bf16[864,128]{1,0:T(8,128)(2,1)S(1)}, bf16[864,128]{1,0:T(8,128)(2,1)S(1)}, u32[]{:S(2)}, u32[]{:S(2)}) %collective-permute-start.47) | collective-permute-done | bytes 221216 | tf_op jit(solution)/shard_map/ppermute | solution.py:600
  606.8 10.3 %collective-permute-done.48 = bf16[1728,128]{1,0:T(8,128)(2,1)S(1)} collective-permute-done((bf16[1728,128]{1,0:T(8,128)(2,1)S(1)}, bf16[1728,128]{1,0:T(8,128)(2,1)S(1)}, u32[]{:S(2)}, u32[]{:S(2)}) %collective-permute-start.48) | collective-permute-done | bytes 442400 | tf_op jit(solution)/shard_map/ppermute | solution.py:600
  623.4 9.0 %unpack.1 = (f32[400,1600]{1,0:T(8,128)}, f32[400,1600]{1,0:T(8,128)}) custom-call(s32[1]{0:T(128)} %bitcast.37.core, bf16[6912,128]{1,0:T(8,128)(2,1)} %copy-done.14, bf16[6912,128]{1,0:T(8,128)(2,1)} %collective-permute-done.51.other), custom_call_target="tpu_custom_call" | custom-call | tf_op jit(solution)/shard_map/unpack/pallas_call | solution.py:585
  633.6 28.5 %all-reduce.18.cloned.1.call-done = (bf16[800,3200]{1,0:T(8,128)(2,1)}, bf16[3200,800]{0,1:T(8,128)(2,1)}, bf16[400,400]{1,0:T(8,128)(2,1)}, bf16[400,800]{1,0:T...) async-done(((bf16[800,3200]{1,0:T(8,128)(2,1)}, bf16[3200,800]{0,1:T(8,128)(2,1)}, bf16[400,400]{1,0:T(8,128)(2,1)}, bf16[400,800]{1,0:T(8,128)(2,1)}, ...) | async-done | bytes 13760016 | tf_op jit(solution)/shard_map/psum | solution.py:891
  662.1 7.3 %convert_element_type.242 = f32[800,3200]{1,0:T(8,128)} convert(bf16[800,3200]{1,0:T(8,128)(2,1)} %get-tuple-element.205) | non-fusion elementwise | flops 2560000 | bytes 15360000 | tf_op jit(solution)/shard_map/convert_element_type | solution.py:892
  669.4 4.7 transpose.90
  (502 shorter events, 211.6 us)
Async XLA Ops:
  7.2 57.5 %all-gather.6.cloned.1.call-start = ((), (), s32[]{:S(2)}) async-start(), calls=%async_computation.8 | async-start | bytes 2048000 | tf_op jit(solution)/shard_map/all_gather | solution.py:151
  9.7 117.0 %all-gather.8.cloned.1.call-start = ((), (), s32[]{:S(2)}) async-start(), calls=%async_computation.9 | async-start | bytes 3328000 | tf_op jit(solution)/shard_map/all_gather | solution.py:142
  11.6 16.7 %collective-permute-start = (bf16[13,32,400]{2,1,0:T(8,128)(2,1)S(1)}, bf16[13,32,400]{2,1,0:T(8,128)(2,1)S(1)}, u32[]{:S(2)}, u32[]{:S(2)}) collective-permute-start(bf16[13,32,400]{2,1,0:T(8,128)(2,1)S(1)} %get-tuple-element.230), channel_id=1, source_target_pairs={{0,8},{8,0},{16,24},{24,16},{1,9},{9,1},{17,25},{25,17},{2,10},{10... | collective-permute-start | bytes 998408 | tf_op jit(solution)/shard_map/ppermute | solution.py:31
  14.6 24.9 %collective-permute-start.1 = (bf16[13,32,400]{2,1,0:T(8,128)(2,1)S(1)}, bf16[13,32,400]{2,1,0:T(8,128)(2,1)S(1)}, u32[]{:S(2)}, u32[]{:S(2)}) collective-permute-start(bf16[13,32,400]{2,1,0:T(8,128)(2,1)S(1)} %get-tuple-element.229), channel_id=1, source_target_pairs={{0,16},{8,24},{16,0},{24,8},{1,17},{9,25},{17,1},{25,9},{2,18},{10... | collective-permute-start | bytes 998408 | tf_op jit(solution)/shard_map/ppermute | solution.py:31
  16.1 24.2 %collective-permute-start.2 = (bf16[13,32,400]{2,1,0:T(8,128)(2,1)S(1)}, bf16[13,32,400]{2,1,0:T(8,128)(2,1)S(1)}, u32[]{:S(2)}, u32[]{:S(2)}) collective-permute-start(bf16[13,32,400]{2,1,0:T(8,128)(2,1)S(1)} %get-tuple-element.228), channel_id=1, source_target_pairs={{0,24},{8,16},{16,8},{24,0},{1,25},{9,17},{17,9},{25,1},{2,26},{10... | collective-permute-start | bytes 998408 | tf_op jit(solution)/shard_map/ppermute | solution.py:31
  67.5 26.0 %collective-permute-start.5 = (bf16[1600,400]{0,1:T(8,128)(2,1)S(1)}, bf16[1600,400]{0,1:T(8,128)(2,1)}, u32[]{:S(2)}, u32[]{:S(2)}) collective-permute-start(bf16[1600,400]{0,1:T(8,128)(2,1)S(1)} %copy.99), channel_id=1, source_target_pairs={{0,1},{1,0},{2,3},{3,2},{4,5},{5,4},{6,7},{7,6},{8,9},{9,8},{10,11... | collective-permute-start | bytes 3840008 | tf_op jit(solution)/shard_map/ppermute | solution.py:600
  71.8 18.2 %collective-permute-start.8 = (bf16[100,800]{1,0:T(8,128)(2,1)S(1)}, bf16[100,800]{1,0:T(8,128)(2,1)}, u32[]{:S(2)}, u32[]{:S(2)}) collective-permute-start(bf16[100,800]{1,0:T(8,128)(2,1)S(1)} %copy-done.47), channel_id=1, source_target_pairs={{0,24},{8,16},{16,8},{24,0},{1,25},{9,17},{17,9},{25,1},{2,26},{10... | collective-permute-start | bytes 480008 | tf_op jit(solution)/shard_map/ppermute | solution.py:600
  75.5 16.8 %all-to-all-start = ((f32[32,3,400]{2,1,0:T(4,128)}), f32[32,3,400]{2,1,0:T(4,128)S(1)}, u32[]{:S(2)}, u32[]{:S(2)}) async-start(f32[32,3,400]{2,1,0:T(4,128)} %broadcast_in_dim.149), calls=%async_computation | async-start | bytes 524288 | tf_op jit(solution)/shard_map/all_to_all | solution.py:176
  78.5 143.1 %all-gather.12.cloned.1.call-start = ((), (), s32[]{:S(2)}) async-start(), calls=%async_computation.11 | async-start | bytes 1730560 | tf_op jit(solution)/shard_map/all_gather | solution.py:854
  79.7 48.1 %collective-permute-start.12 = (bf16[400,800]{1,0:T(8,128)(2,1)}, bf16[400,800]{1,0:T(8,128)(2,1)}, u32[]{:S(2)}, u32[]{:S(2)}) collective-permute-start(bf16[400,800]{1,0:T(8,128)(2,1)} %dynamic-slice_bitcast_fusion.1), channel_id=1, source_target_pairs={{0,8},{8,0},{16,24},{24,16},{1,9},{9,1},{17,25},{25,17},{2,10},{10... | collective-permute-start | bytes 1920008 | tf_op jit(solution)/shard_map/ppermute | solution.py:600
  81.4 46.4 %collective-permute-start.13 = (bf16[400,800]{1,0:T(8,128)(2,1)}, bf16[400,800]{1,0:T(8,128)(2,1)}, u32[]{:S(2)}, u32[]{:S(2)}) collective-permute-start(bf16[400,800]{1,0:T(8,128)(2,1)} %dynamic-slice_bitcast_fusion.1), channel_id=1, source_target_pairs={{0,16},{8,24},{16,0},{24,8},{1,17},{9,25},{17,1},{25,9},{2,18},{10... | collective-permute-start | bytes 1920008 | tf_op jit(solution)/shard_map/ppermute | solution.py:600
  83.0 51.3 %collective-permute-start.14 = (bf16[400,800]{1,0:T(8,128)(2,1)}, bf16[400,800]{1,0:T(8,128)(2,1)}, u32[]{:S(2)}, u32[]{:S(2)}) collective-permute-start(bf16[400,800]{1,0:T(8,128)(2,1)} %dynamic-slice_bitcast_fusion.1), channel_id=1, source_target_pairs={{0,24},{8,16},{16,8},{24,0},{1,25},{9,17},{17,9},{25,1},{2,26},{10... | collective-permute-start | bytes 1920008 | tf_op jit(solution)/shard_map/ppermute | solution.py:600
  126.7 53.2 %collective-permute-start.11 = (bf16[800,1664]{1,0:T(8,128)(2,1)}, bf16[800,1664]{1,0:T(8,128)(2,1)}, u32[]{:S(2)}, u32[]{:S(2)}) collective-permute-start(bf16[800,1664]{1,0:T(8,128)(2,1)} %all-gather.8.cloned.1.call-done.mine), channel_id=1, source_target_pairs={{0,1},{1,0},{2,3},{3,2},{4,5},{5,4},{6,7},{7,6},{8,9},{9,8},{10,11... | collective-permute-start | bytes 7987208 | tf_op jit(solution)/shard_map/ppermute | solution.py:600
  136.3 35.7 %collective-permute-start.15 = (bf16[3,400,800]{2,1,0:T(8,128)(2,1)S(1)}, bf16[3,400,800]{2,1,0:T(8,128)(2,1)}, u32[]{:S(2)}, u32[]{:S(2)}) collective-permute-start(bf16[3,400,800]{2,1,0:T(8,128)(2,1)S(1)} %pad_maximum_fusion.3.mine), channel_id=1, source_target_pairs={{0,1},{1,0},{2,3},{3,2},{4,5},{5,4},{6,7},{7,6},{8,9},{9,8},{10,11... | collective-permute-start | bytes 5760008 | tf_op jit(solution)/shard_map/ppermute | solution.py:600
  160.5 26.2 %all-to-all-start.1 = ((f32[32,3,800]{2,1,0:T(4,128)}), f32[32,3,800]{2,1,0:T(4,128)S(1)}, u32[]{:S(2)}, u32[]{:S(2)}) async-start(f32[32,3,800]{2,1,0:T(4,128)} %broadcast_in_dim.152), calls=%async_computation.1 | async-start | bytes 917504 | tf_op jit(solution)/shard_map/all_to_all | solution.py:176
  163.3 96.7 %all-gather.10.cloned.1.call-start = ((), (), s32[]{:S(2)}) async-start(), calls=%async_computation.10 | async-start | bytes 2048000 | tf_op jit(solution)/shard_map/all_gather | solution.py:855
  166.1 36.2 %collective-permute-start.16 = (bf16[304,400]{0,1:T(8,128)(2,1)}, bf16[304,400]{0,1:T(8,128)(2,1)}, u32[]{:S(2)}, u32[]{:S(2)}) collective-permute-start(bf16[304,400]{0,1:T(8,128)(2,1)} %get-tuple-element.286), channel_id=1, source_target_pairs={{0,8},{8,0},{16,24},{24,16},{1,9},{9,1},{17,25},{25,17},{2,10},{10... | collective-permute-start | bytes 729608 | tf_op jit(solution)/shard_map/ppermute | solution.py:600
  168.0 34.6 %collective-permute-start.17 = (bf16[304,400]{0,1:T(8,128)(2,1)}, bf16[304,400]{0,1:T(8,128)(2,1)}, u32[]{:S(2)}, u32[]{:S(2)}) collective-permute-start(bf16[304,400]{0,1:T(8,128)(2,1)} %get-tuple-element.286), channel_id=1, source_target_pairs={{0,16},{8,24},{16,0},{24,8},{1,17},{9,25},{17,1},{25,9},{2,18},{10... | collective-permute-start | bytes 729608 | tf_op jit(solution)/shard_map/ppermute | solution.py:600
  169.3 33.3 %collective-permute-start.18 = (bf16[304,400]{0,1:T(8,128)(2,1)}, bf16[304,400]{0,1:T(8,128)(2,1)}, u32[]{:S(2)}, u32[]{:S(2)}) collective-permute-start(bf16[304,400]{0,1:T(8,128)(2,1)} %get-tuple-element.286), channel_id=1, source_target_pairs={{0,24},{8,16},{16,8},{24,0},{1,25},{9,17},{17,9},{25,1},{2,26},{10... | collective-permute-start | bytes 729608 | tf_op jit(solution)/shard_map/ppermute | solution.py:600
  172.0 69.1 %collective-permute-start.24 = (bf16[12,32,400]{2,1,0:T(8,128)(2,1)}, bf16[12,32,400]{2,1,0:T(8,128)(2,1)}, u32[]{:S(2)}, u32[]{:S(2)}) collective-permute-start(bf16[12,32,400]{2,1,0:T(8,128)(2,1)} %get-tuple-element.250), channel_id=1, source_target_pairs={{0,8},{8,0},{16,24},{24,16},{1,9},{9,1},{17,25},{25,17},{2,10},{10... | collective-permute-start | bytes 921608 | tf_op jit(solution)/shard_map/ppermute | solution.py:31
  179.8 61.2 %collective-permute-start.25 = (bf16[12,32,400]{2,1,0:T(8,128)(2,1)}, bf16[12,32,400]{2,1,0:T(8,128)(2,1)}, u32[]{:S(2)}, u32[]{:S(2)}) collective-permute-start(bf16[12,32,400]{2,1,0:T(8,128)(2,1)} %get-tuple-element.249), channel_id=1, source_target_pairs={{0,16},{8,24},{16,0},{24,8},{1,17},{9,25},{17,1},{25,9},{2,18},{10... | collective-permute-start | bytes 921608 | tf_op jit(solution)/shard_map/ppermute | solution.py:31
  202.3 38.8 %collective-permute-start.26 = (bf16[12,32,400]{2,1,0:T(8,128)(2,1)}, bf16[12,32,400]{2,1,0:T(8,128)(2,1)}, u32[]{:S(2)}, u32[]{:S(2)}) collective-permute-start(bf16[12,32,400]{2,1,0:T(8,128)(2,1)} %get-tuple-element.248), channel_id=1, source_target_pairs={{0,24},{8,16},{16,8},{24,0},{1,25},{9,17},{17,9},{25,1},{2,26},{10... | collective-permute-start | bytes 921608 | tf_op jit(solution)/shard_map/ppermute | solution.py:31
  243.2 15.6 %all-to-all-start.2 = ((f32[32,3,400]{2,1,0:T(4,128)}), f32[32,3,400]{2,1,0:T(4,128)S(1)}, u32[]{:S(2)}, u32[]{:S(2)}) async-start(f32[32,3,400]{2,1,0:T(4,128)} %broadcast_in_dim.153), calls=%async_computation.2 | async-start | bytes 524288 | tf_op jit(solution)/shard_map/all_to_all | solution.py:176
  286.1 16.8 %all-to-all-start.3 = ((f32[32,2,400]{2,1,0:T(2,128)}), f32[32,2,400]{2,1,0:T(2,128)S(1)}, u32[]{:S(2)}, u32[]{:S(2)}) async-start(f32[32,2,400]{2,1,0:T(2,128)} %broadcast_in_dim.154), calls=%async_computation.3 | async-start | bytes 262144 | tf_op jit(solution)/shard_map/all_to_all | solution.py:176
  289.8 21.2 %collective-permute-start.21 = (bf16[12,32,400]{2,1,0:T(8,128)(2,1)}, bf16[12,32,400]{2,1,0:T(8,128)(2,1)S(1)}, u32[]{:S(2)}, u32[]{:S(2)}) collective-permute-start(bf16[12,32,400]{2,1,0:T(8,128)(2,1)} %get-tuple-element.259), channel_id=1, source_target_pairs={{0,8},{8,0},{16,24},{24,16},{1,9},{9,1},{17,25},{25,17},{2,10},{10... | collective-permute-start | bytes 921608 | tf_op jit(solution)/shard_map/ppermute | solution.py:55
  291.5 19.5 %collective-permute-start.22 = (bf16[12,32,400]{2,1,0:T(8,128)(2,1)}, bf16[12,32,400]{2,1,0:T(8,128)(2,1)S(1)}, u32[]{:S(2)}, u32[]{:S(2)}) collective-permute-start(bf16[12,32,400]{2,1,0:T(8,128)(2,1)} %get-tuple-element.258), channel_id=1, source_target_pairs={{0,16},{8,24},{16,0},{24,8},{1,17},{9,25},{17,1},{25,9},{2,18},{10... | collective-permute-start | bytes 921608 | tf_op jit(solution)/shard_map/ppermute | solution.py:55
  292.9 18.8 %collective-permute-start.23 = (bf16[12,32,400]{2,1,0:T(8,128)(2,1)}, bf16[12,32,400]{2,1,0:T(8,128)(2,1)}, u32[]{:S(2)}, u32[]{:S(2)}) collective-permute-start(bf16[12,32,400]{2,1,0:T(8,128)(2,1)} %get-tuple-element.257), channel_id=1, source_target_pairs={{0,24},{8,16},{16,8},{24,0},{1,25},{9,17},{17,9},{25,1},{2,26},{10... | collective-permute-start | bytes 921608 | tf_op jit(solution)/shard_map/ppermute | solution.py:55
  351.9 18.0 %all-to-all-start.4 = ((f32[32,2,800]{2,1,0:T(2,128)}), f32[32,2,800]{2,1,0:T(2,128)S(1)}, u32[]{:S(2)}, u32[]{:S(2)}) async-start(f32[32,2,800]{2,1,0:T(2,128)} %broadcast_in_dim.155), calls=%async_computation.4 | async-start | bytes 458752 | tf_op jit(solution)/shard_map/all_to_all | solution.py:176
  357.3 304.8 %all-reduce.18.cloned.1.call-start = ((), (), s32[]{:S(2)}) async-start(), calls=%async_computation.12 | async-start | bytes 28057600 | tf_op jit(solution)/shard_map/psum | solution.py:891
  372.2 25.5 %collective-permute-start.29 = (bf16[24,3,800]{2,1,0:T(4,128)(2,1)S(1)}, bf16[24,3,800]{2,1,0:T(4,128)(2,1)S(1)}, u32[]{:S(2)}, u32[]{:S(2)}) collective-permute-start(bf16[24,3,800]{2,1,0:T(4,128)(2,1)S(1)} %get-tuple-element.273), channel_id=1, source_target_pairs={{0,1},{1,2},{2,3},{3,4},{4,5},{5,6},{6,7},{7,0},{8,9},{9,10},{10,1... | collective-permute-start | bytes 345608 | tf_op jit(solution)/shard_map/ppermute | solution.py:161
  372.5 25.2 %collective-permute-start.30 = (bf16[24,3,800]{2,1,0:T(4,128)(2,1)S(1)}, bf16[24,3,800]{2,1,0:T(4,128)(2,1)S(1)}, u32[]{:S(2)}, u32[]{:S(2)}) collective-permute-start(bf16[24,3,800]{2,1,0:T(4,128)(2,1)S(1)} %get-tuple-element.272), channel_id=1, source_target_pairs={{1,0},{2,1},{3,2},{4,3},{5,4},{6,5},{7,6},{0,7},{9,8},{10,9},{11,1... | collective-permute-start | bytes 345608 | tf_op jit(solution)/shard_map/ppermute | solution.py:162
  444.8 34.3 %collective-permute-start.36 = (bf16[6912,128]{1,0:T(8,128)(2,1)}, bf16[6912,128]{1,0:T(8,128)(2,1)}, u32[]{:S(2)}, u32[]{:S(2)}) collective-permute-start(bf16[6912,128]{1,0:T(8,128)(2,1)} %dynamic-slice_bitcast_fusion), channel_id=1, source_target_pairs={{0,1},{1,0},{2,3},{3,2},{4,5},{5,4},{6,7},{7,6},{8,9},{9,8},{10,11... | collective-permute-start | bytes 5308424 | tf_op jit(solution)/shard_map/ppermute | solution.py:600
  462.8 23.3 %collective-permute-start.31 = (bf16[48,3,400]{2,1,0:T(4,128)(2,1)}, bf16[48,3,400]{2,1,0:T(4,128)(2,1)S(1)}, u32[]{:S(2)}, u32[]{:S(2)}) collective-permute-start(bf16[48,3,400]{2,1,0:T(4,128)(2,1)} %get-tuple-element.241), channel_id=1, source_target_pairs={{0,1},{1,2},{2,3},{3,4},{4,5},{5,6},{6,7},{7,0},{8,9},{9,10},{10,1... | collective-permute-start | bytes 345608 | tf_op jit(solution)/shard_map/ppermute | solution.py:161
  463.2 23.0 %collective-permute-start.32 = (bf16[48,3,400]{2,1,0:T(4,128)(2,1)}, bf16[48,3,400]{2,1,0:T(4,128)(2,1)}, u32[]{:S(2)}, u32[]{:S(2)}) collective-permute-start(bf16[48,3,400]{2,1,0:T(4,128)(2,1)} %get-tuple-element.240), channel_id=1, source_target_pairs={{1,0},{2,1},{3,2},{4,3},{5,4},{6,5},{7,6},{0,7},{9,8},{10,9},{11,1... | collective-permute-start | bytes 345608 | tf_op jit(solution)/shard_map/ppermute | solution.py:162
  481.2 27.9 %collective-permute-start.39 = (bf16[1728,128]{1,0:T(8,128)(2,1)S(1)}, bf16[1728,128]{1,0:T(8,128)(2,1)S(1)}, u32[]{:S(2)}, u32[]{:S(2)}) collective-permute-start(bf16[1728,128]{1,0:T(8,128)(2,1)S(1)} %dynamic-slice_bitcast_fusion.2), channel_id=1, source_target_pairs={{0,16},{8,24},{16,0},{24,8},{1,17},{9,25},{17,1},{25,9},{2,18},{10... | collective-permute-start | bytes 1327112 | tf_op jit(solution)/shard_map/ppermute | solution.py:600
  483.3 64.8 %all-to-all-start.6 = ((f32[32,32,128]{2,1,0:T(8,128)}), f32[32,32,128]{2,1,0:T(8,128)S(1)}, u32[]{:S(2)}, u32[]{:S(2)}) async-start(f32[32,32,128]{2,1,0:T(8,128)} %bitcast.103), calls=%async_computation.6 | async-start | bytes 1048576 | tf_op jit(solution)/shard_map/all_to_all | solution.py:716
  503.7 43.5 %collective-permute-start.33 = (bf16[12,32,400]{2,1,0:T(8,128)(2,1)S(1)}, bf16[12,32,400]{2,1,0:T(8,128)(2,1)S(1)}, u32[]{:S(2)}, u32[]{:S(2)}) collective-permute-start(bf16[12,32,400]{2,1,0:T(8,128)(2,1)S(1)} %get-tuple-element.239), channel_id=1, source_target_pairs={{0,8},{8,0},{16,24},{24,16},{1,9},{9,1},{17,25},{25,17},{2,10},{10... | collective-permute-start | bytes 921608 | tf_op jit(solution)/shard_map/ppermute | solution.py:55
  505.5 42.4 %collective-permute-start.34 = (bf16[12,32,400]{2,1,0:T(8,128)(2,1)S(1)}, bf16[12,32,400]{2,1,0:T(8,128)(2,1)S(1)}, u32[]{:S(2)}, u32[]{:S(2)}) collective-permute-start(bf16[12,32,400]{2,1,0:T(8,128)(2,1)S(1)} %get-tuple-element.238), channel_id=1, source_target_pairs={{0,16},{8,24},{16,0},{24,8},{1,17},{9,25},{17,1},{25,9},{2,18},{10... | collective-permute-start | bytes 921608 | tf_op jit(solution)/shard_map/ppermute | solution.py:55
  507.0 40.9 %collective-permute-start.35 = (bf16[12,32,400]{2,1,0:T(8,128)(2,1)S(1)}, bf16[12,32,400]{2,1,0:T(8,128)(2,1)S(1)}, u32[]{:S(2)}, u32[]{:S(2)}) collective-permute-start(bf16[12,32,400]{2,1,0:T(8,128)(2,1)S(1)} %get-tuple-element.237), channel_id=1, source_target_pairs={{0,24},{8,16},{16,8},{24,0},{1,25},{9,17},{17,9},{25,1},{2,26},{10... | collective-permute-start | bytes 921608 | tf_op jit(solution)/shard_map/ppermute | solution.py:55
  507.3 29.0 %collective-permute-start.37 = (bf16[1728,128]{1,0:T(8,128)(2,1)S(1)}, bf16[1728,128]{1,0:T(8,128)(2,1)S(1)}, u32[]{:S(2)}, u32[]{:S(2)}) collective-permute-start(bf16[1728,128]{1,0:T(8,128)(2,1)S(1)} %dynamic-slice_bitcast_fusion.3), channel_id=1, source_target_pairs={{0,8},{8,0},{16,24},{24,16},{1,9},{9,1},{17,25},{25,17},{2,10},{10... | collective-permute-start | bytes 1327112 | tf_op jit(solution)/shard_map/ppermute | solution.py:600
  509.2 31.0 %collective-permute-start.40 = (bf16[864,128]{1,0:T(8,128)(2,1)S(1)}, bf16[864,128]{1,0:T(8,128)(2,1)S(1)}, u32[]{:S(2)}, u32[]{:S(2)}) collective-permute-start(bf16[864,128]{1,0:T(8,128)(2,1)S(1)} %dynamic-slice_bitcast_fusion.30), channel_id=1, source_target_pairs={{0,8},{8,0},{16,24},{24,16},{1,9},{9,1},{17,25},{25,17},{2,10},{10... | collective-permute-start | bytes 663560 | tf_op jit(solution)/shard_map/ppermute | solution.py:600
  544.6 16.7 %collective-permute-start.42 = (bf16[2,216,128]{2,1,0:T(8,128)(2,1)}, bf16[2,216,128]{2,1,0:T(8,128)(2,1)S(1)}, u32[]{:S(2)}, u32[]{:S(2)}) collective-permute-start(bf16[2,216,128]{2,1,0:T(8,128)(2,1)} %get-tuple-element.283), channel_id=1, source_target_pairs={{0,4},{1,5},{2,6},{3,7},{4,0},{5,1},{6,2},{7,3},{8,12},{9,13},{10,... | collective-permute-start | bytes 331784 | tf_op jit(solution)/shard_map/ppermute | solution.py:600
  547.1 14.5 %collective-permute-start.43 = (bf16[2,216,128]{2,1,0:T(8,128)(2,1)}, bf16[2,216,128]{2,1,0:T(8,128)(2,1)S(1)}, u32[]{:S(2)}, u32[]{:S(2)}) collective-permute-start(bf16[2,216,128]{2,1,0:T(8,128)(2,1)} %get-tuple-element.284), channel_id=1, source_target_pairs={{0,6},{1,7},{2,4},{3,5},{4,2},{5,3},{6,0},{7,1},{8,14},{9,15},{10,... | collective-permute-start | bytes 331784 | tf_op jit(solution)/shard_map/ppermute | solution.py:600
  549.0 43.4 %all-to-all-start.7 = ((f32[32,32,128]{2,1,0:T(8,128)}), f32[32,32,128]{2,1,0:T(8,128)S(1)}, u32[]{:S(2)}, u32[]{:S(2)}) async-start(f32[32,32,128]{2,1,0:T(8,128)} %broadcast_in_dim.157), calls=%async_computation.7 | async-start | bytes 1048576 | tf_op jit(solution)/shard_map/all_to_all | solution.py:718
  561.7 15.6 %collective-permute-start.44 = (bf16[2,216,128]{2,1,0:T(8,128)(2,1)S(1)}, bf16[2,216,128]{2,1,0:T(8,128)(2,1)S(1)}, u32[]{:S(2)}, u32[]{:S(2)}) collective-permute-start(bf16[2,216,128]{2,1,0:T(8,128)(2,1)S(1)} %fusion.24), channel_id=1, source_target_pairs={{0,2},{1,3},{2,0},{3,1},{4,6},{5,7},{6,4},{7,5},{8,10},{9,11},{10,... | collective-permute-start | bytes 331784 | tf_op jit(solution)/shard_map/ppermute | solution.py:600
  573.8 14.8 %collective-permute-start.45 = (bf16[2,216,128]{2,1,0:T(8,128)(2,1)S(1)}, bf16[2,216,128]{2,1,0:T(8,128)(2,1)S(1)}, u32[]{:S(2)}, u32[]{:S(2)}) collective-permute-start(bf16[2,216,128]{2,1,0:T(8,128)(2,1)S(1)} %fusion.24), channel_id=1, source_target_pairs={{0,4},{1,5},{2,6},{3,7},{4,0},{5,1},{6,2},{7,3},{8,12},{9,13},{10,... | collective-permute-start | bytes 331784 | tf_op jit(solution)/shard_map/ppermute | solution.py:600
  575.4 13.2 %collective-permute-start.46 = (bf16[2,216,128]{2,1,0:T(8,128)(2,1)S(1)}, bf16[2,216,128]{2,1,0:T(8,128)(2,1)S(1)}, u32[]{:S(2)}, u32[]{:S(2)}) collective-permute-start(bf16[2,216,128]{2,1,0:T(8,128)(2,1)S(1)} %fusion.24), channel_id=1, source_target_pairs={{0,6},{1,7},{2,4},{3,5},{4,2},{5,3},{6,0},{7,1},{8,14},{9,15},{10,... | collective-permute-start | bytes 331784 | tf_op jit(solution)/shard_map/ppermute | solution.py:600
  601.2 16.0 %collective-permute-start.48 = (bf16[1728,128]{1,0:T(8,128)(2,1)S(1)}, bf16[1728,128]{1,0:T(8,128)(2,1)S(1)}, u32[]{:S(2)}, u32[]{:S(2)}) collective-permute-start(bf16[1728,128]{1,0:T(8,128)(2,1)S(1)} %maximum_select_fusion.2), channel_id=1, source_target_pairs={{0,8},{8,0},{16,24},{24,16},{1,9},{9,1},{17,25},{25,17},{2,10},{10... | collective-permute-start | bytes 1327112 | tf_op jit(solution)/shard_map/ppermute | solution.py:600
  (115 other events, 773.1 us)
Sparse Core Ops, SparseCore 0:
  10.5 47.0 all-gather.5
  60.0 66.6 all-gather.7
  134.5 30.6 all-gather.11
  169.7 46.4 all-gather.9
  377.6 284.4 all-reduce.17

commit v10 on v9

--- a/solution.py
+++ b/solution.py
@@ -130,9 +130,11 @@
 def gathered_by_rows(shard, event):
     tiles = lax.axis_size("lat")
     half = take(shard.reshape(2, -1, shard.shape[1]), lax.axis_index("lon") % 2)
-    mine = jnp.stack(after([swap(half, "lat", step) for step in range(1, tiles)], event))
+    mine, event = lax.optimization_barrier(([swap(half, "lat", step) for step in range(1, tiles)], event))
+    mine = jnp.stack(mine)
+    arrays = (shard, mine, swap(mine, "lon", 1))
     shape = (tiles * shard.shape[0], shard.shape[1])
-    return assemble(assemble_rows_kernel, "assemble_rows", shape, (shard, mine, swap(mine, "lon", 1)), 2 * tiles - 1)
+    return assemble(assemble_rows_kernel, "assemble_rows", shape, arrays, 2 * tiles - 1), event
 
 
 def gathered_by_columns(shard, event):
@@ -726,17 +728,19 @@
     return lax.dot_general(former, latter, (((1,), (1,)), ((), ())), preferred_element_type=f32)
 
 
-def block_mix(source, params, sea, ocean, dates, event=()):
+def block_mix(source, params, sea, ocean, dates, between=lambda mixed: ()):
     taps, gain, shift = params[:3]
     channels = source.shape[2]
     edges = borders(source, dates)
     mixed, local = stencil_forward(source, edges, taps, sea)
+    event = between(mixed)
     totals = sum_all(jnp.concatenate([local, jnp.broadcast_to(ocean, (1, channels))]), event)
     first, square, ocean = totals
     mean = first / ocean
     factor = lax.rsqrt(square / ocean - mean * mean + epsilon)
     scales = jnp.stack([mean, factor, gain, shift])
-    return source, edges, taps, mixed.reshape(-1, channels), scales, ocean
+    mix = source, edges, taps, mixed.reshape(-1, channels), scales, ocean
+    return (mix, event) if event else mix
 
 
 def block_forward(mix, params, sea, pooling=()):
@@ -854,11 +858,17 @@
     decode_up = lax.all_gather(after(decode_up, skip_rows), "lat", axis=0, tiled=True)
     decode_down = lax.all_gather(after(decode_down, skip_rows), "lat", axis=0, tiled=True)
     decode = decode_norm + (decode_up, decode_up_bias, decode_down, decode_down_bias)
-    bottle_up = gathered_by_columns(bottle_up, skip_rows)
-    bottle_down = gathered_by_rows(after(bottle_down, encode_stored[3]), skip_rows)
+    coarse_in = coarse_in.reshape(half_height, half_breadth, wide)
+    bottle_down, coarse_in = gathered_by_rows(after(bottle_down, encode_stored[3]), coarse_in)
+    mix, (bottle_up, bottle_down) = block_mix(
+        coarse_in,
+        bottle_norm,
+        sea_coarse,
+        ocean_coarse,
+        dates,
+        lambda mixed: (gathered_by_columns(bottle_up, mixed), bottle_down),
+    )
     bottle = bottle_norm + (bottle_up, bottle_up_bias, bottle_down, bottle_down_bias)
-    coarse_in = coarse_in.reshape(half_height, half_breadth, wide)
-    mix = block_mix(coarse_in, bottle, sea_coarse, ocean_coarse, dates, (bottle_up, bottle_down))
     coarse_low, _, coarse_stored = block_forward(mix, bottle, sea_coarse)
     merge_rows = merge_weight.shape[0]
     merge_weight = jnp.pad(after(merge_weight, skip_rows), ((0, -merge_rows % 16), (0, 0)))

time: 693 us -> 694 us (level)
    ppermute x28, waiting for transfers between devices: 75.5 us -> 84 us  [swap(): lax.ppermute(array, axis, [(i, i ^ step) for i in range(lax.axis_size(axi...]
    all_gather x1, waiting for transfers between devices: 8.1 us -> 0.01 us  [gathered_by_columns(): mine = after(lax.all_gather(half, 'lat', axis=0, tiled=True), event)]
  transfers between devices with their start and end apart: 65 -> 65, of which waited for: 23 -> 20; matrix products, arithmetic and copies ran while one was open for 18% -> 18% of each run, Pallas kernels for 27% -> 27%
where the time goes in v10:
time: 694 us; the launch traced here: 684 us
  Pallas kernels  240 us (35%)
  waiting for transfers between devices  152 us (22%)
  starting transfers between devices  118 us (17%)
  local copies, waits for them, and re-layouts  72.2 us (10%)
  other arithmetic  59.1 us (9%)
  matrix products  25.9 us (4%)
  between operations  16.2 us (2%)
    ppermute x28, waiting for transfers between devices, swap(): lax.ppermute(array, axis, [(i, i ^ step) for i in range(lax.axis_size(axi...  84 us
    ppermute x28, starting transfers between devices, swap(): lax.ppermute(array, axis, [(i, i ^ step) for i in range(lax.axis_size(axi...  50.2 us
    pallas_call x3, Pallas kernels, mlp_forward(): pl.pallas_call(functools.partial(mlp_forward_kernel, 512), grid=(parts,),...  40.9 us
    pallas_call x3, Pallas kernels, stencil_backward(): pl.pallas_call(functools.partial(stencil_backward_kernel, len(edges)), gr...  39.4 us
    pallas_call x3, Pallas kernels, stencil_forward(): pl.pallas_call(functools.partial(stencil_forward_kernel, len(edges)), gri...  38.5 us
    pallas_call x3, Pallas kernels, mlp_backward(): pl.pallas_call(functools.partial(mlp_backward_kernel, 512), grid=(pixels...  37.8 us
    pallas_call x3, Pallas kernels, kernel_grad(): pl.pallas_call(functools.partial(kernel_grad_kernel, len(edges)), grid=(t...  32.9 us
    psum x1, waiting for transfers between devices, shards(): early = lax.psum([part.astype(bf16) for part in early], both)  28.6 us
  transfers between devices with their start and end apart: 65, of which 20 were waited for; matrix products, arithmetic and copies ran while one was open for 18% of the time, Pallas kernels for 27%

profile of v10, /device:TPU:0, one launch (start us, length us, event | category | flops | bytes accessed | tf_op | source)
XLA Modules:
  0.0 683.6 jit_solution(7607976308364860773)
XLA Ops:
  23.1 5.3 collective-permute-done
  28.3 11.2 %collective-permute-done.1 = bf16[13,32,400]{2,1,0:T(8,128)(2,1)S(1)} collective-permute-done((bf16[13,32,400]{2,1,0:T(8,128)(2,1)S(1)}, bf16[13,32,400]{2,1,0:T(8,128)(2,1)S(1)}, u32[]{:S(2)}, u32[]{:S(2)}) %collective-permute-start.1) | collective-permute-done | bytes 332832 | tf_op jit(solution)/shard_map/ppermute | solution.py:31
  49.6 15.0 %stencil_forward.3 = (f32[48,32,400]{2,1,0:T(8,128)}, f32[2,400]{1,0:T(2,128)}) custom-call(bf16[48,32,400]{2,1,0:T(8,128)(2,1)} %bitcast.269, bf16[48,3,400]{2,1,0:T(4,128)(2,1)} %copy-done.30, bf16[48,3,400]{2,1,0:T(4,128)(2,1)} %copy-done.31, f32[49,400]{1,0:T(8,128)} %reshape.349.refs_2_, f32[48,32,128]{2,1,0:T(8,128)} %broadcast_in_dim.147.refs_3_), custom_call_target="tpu_custom_call" | custom-call | tf_op jit(solution)/shard_map/stencil_forward/pallas_call | solution.py:289
  83.0 7.0 %collective-permute-start.7 = (bf16[400,800]{1,0:T(8,128)(2,1)}, bf16[400,800]{1,0:T(8,128)(2,1)}, u32[]{:S(2)}, u32[]{:S(2)}) collective-permute-start(bf16[400,800]{1,0:T(8,128)(2,1)} %dynamic-slice_bitcast_fusion.1), channel_id=1, source_target_pairs={{0,24},{8,16},{16,8},{24,0},{1,25},{9,17},{17,9},{25,1},{2,26},{10... | collective-permute-start | bytes 1920008 | tf_op jit(solution)/shard_map/ppermute | solution.py:602
  98.2 4.4 reshape.307.up
  103.8 14.8 %mlp_forward.3 = (bf16[1536,400]{1,0:T(8,128)(2,1)}, bf16[1536,1600]{1,0:T(8,128)(2,1)}, bf16[1536,1600]{1,0:T(8,128)(2,1)}, bf16[1536,400]{1,0:T(8,128)(2,1)}, ...) custom-call(f32[1536,400]{1,0:T(8,128)} %bitcast.275, bf16[1536,400]{1,0:T(8,128)(2,1)} %bitcast.270, ...), custom_call_target="tpu_custom_call" | custom-call | tf_op jit(solution)/shard_map/mlp_forward/pallas_call | solution.py:469
  118.6 15.7 %collective-permute-done.7 = bf16[400,800]{1,0:T(8,128)(2,1)} collective-permute-done((bf16[400,800]{1,0:T(8,128)(2,1)}, bf16[400,800]{1,0:T(8,128)(2,1)}, u32[]{:S(2)}, u32[]{:S(2)}) %collective-permute-start.7) | collective-permute-done | bytes 640032 | tf_op jit(solution)/shard_map/ppermute | solution.py:602
  143.2 8.4 %stencil_forward.4 = (f32[24,16,800]{2,1,0:T(8,128)}, f32[2,800]{1,0:T(2,128)}) custom-call(bf16[24,16,800]{2,1,0:T(8,128)(2,1)} %bitcast.297, bf16[24,3,800]{2,1,0:T(4,128)(2,1)} %copy-done.35, bf16[24,3,800]{2,1,0:T(4,128)(2,1)} %copy-done.36, f32[49,800]{1,0:T(8,128)} %reshape.351.refs_2_, f32[24,16,128]{2,1,0:T(8,128)} %broadcast_in_dim.150.refs_3_), custom_call_target="tpu_custom_call" | custom-call | tf_op jit(solution)/shard_map/stencil_forward/pallas_call | solution.py:289
  174.8 5.9 assemble_rows.1.down
  182.3 5.5 assemble_columns.1.up
  189.9 13.5 %mlp_forward.4 = (bf16[384,800]{1,0:T(8,128)(2,1)}, bf16[384,3200]{1,0:T(8,128)(2,1)}, bf16[384,3200]{1,0:T(8,128)(2,1)}, bf16[384,800]{1,0:T(8,128)(2,1)}) custom-call(f32[384,800]{1,0:T(8,128)} %bitcast.290, bf16[384,800]{1,0:T(8,128)(2,1)} %get-tuple-element.131, f32[384,128]{1,0:T(8,128)} %broadcast_in_dim.151.sea, f32[4,800]{1,0:T(4,128)} %pad_maximum_fusion.19.scales, ...), custom_call_target="tpu_custom_call" | custom-call | tf_op jit(solution)/shard_map/mlp_forward/pallas_call | solution.py:469
  211.0 6.1 merge_forward.1.source
  218.4 4.0 collective-permute-start.20
  227.6 15.0 %stencil_forward.5 = (f32[48,32,400]{2,1,0:T(8,128)}, f32[2,400]{1,0:T(2,128)}) custom-call(bf16[48,32,400]{2,1,0:T(8,128)(2,1)} %bitcast.273, bf16[48,3,400]{2,1,0:T(4,128)(2,1)} %copy-done.32, bf16[48,3,400]{2,1,0:T(4,128)(2,1)} %copy-done.33, f32[49,400]{1,0:T(8,128)} %reshape.353.refs_2_, f32[48,32,128]{2,1,0:T(8,128)} %broadcast_in_dim.147.refs_3_), custom_call_target="tpu_custom_call" | custom-call | tf_op jit(solution)/shard_map/stencil_forward/pallas_call | solution.py:289
  244.8 4.8 all-to-all-start.2
  252.7 7.2 %all-to-all-done.2 = f32[32,3,400]{2,1,0:T(4,128)S(1)} async-done(((f32[32,3,400]{2,1,0:T(4,128)}), f32[32,3,400]{2,1,0:T(4,128)S(1)}, u32[]{:S(2)}, u32[]{:S(2)}) %all-to-all-start.2) | async-done | bytes 153632 | tf_op jit(solution)/shard_map/all_to_all | solution.py:178
  261.2 12.6 %mlp_forward.5 = (bf16[1536,400]{1,0:T(8,128)(2,1)}, bf16[1536,1600]{1,0:T(8,128)(2,1)}, bf16[1536,1600]{1,0:T(8,128)(2,1)}, bf16[1536,400]{1,0:T(8,128)(2,1)}) custom-call(f32[1536,400]{1,0:T(8,128)} %bitcast.278, bf16[1536,400]{1,0:T(8,128)(2,1)} %merge_forward.1.source, f32[1536,128]{1,0:T(8,128)} %broadcast_in_dim.148.sea, ...), custom_call_target="tpu_custom_call" | custom-call | tf_op jit(solution)/shard_map/mlp_forward/pallas_call | solution.py:469
  273.9 12.0 %mlp_backward.3 = (bf16[1536,400]{1,0:T(8,128)(2,1)}, bf16[1536,1600]{1,0:T(8,128)(2,1)}, f32[1536,400]{1,0:T(8,128)}, f32[2,400]{1,0:T(2,128)}, f32[1,400]{1,0:T(1,128)}, /*index=5*/f32[1,1600]{1,0:T(1,128)}) custom-call(bf16[1536,400]{1,0:T(8,128)(2,1)} %bitcast.286, f32[1536,400]{1,0:T(8,128)} %bitcast.279, bf16[1536,1600]{1,0:T(8,128)(2,1)} %get-tuple-element.167.slope, ...), custom_call_target="tpu_custom_call" | custom-call | tf_op jit(solution)/shard_map/mlp_backward/pallas_call | solution.py:529
  294.4 6.1 fusion.12
  316.8 15.2 %stencil_backward.3 = (bf16[48,32,400]{2,1,0:T(8,128)(2,1)}, f32[1,400]{1,0:T(1,128)}) custom-call(bf16[48,32,400]{2,1,0:T(8,128)(2,1)} %bitcast.281, bf16[48,3,400]{2,1,0:T(4,128)(2,1)} %copy-done.44, bf16[48,3,400]{2,1,0:T(4,128)(2,1)} %copy-done.45, f32[49,400]{1,0:T(8,128)} %reshape.353.refs_2_, f32[48,32,128]{2,1,0:T(8,128)} %broadcast_in_dim.147.refs_3_, ...), custom_call_target="tpu_custom_call" | custom-call | tf_op jit(solution)/shard_map/stencil_backward/pallas_call | solution.py:305
  332.0 5.1 merge_backward.1
  338.7 13.0 %mlp_backward.4 = (bf16[384,800]{1,0:T(8,128)(2,1)}, bf16[384,3200]{1,0:T(8,128)(2,1)}, f32[384,800]{1,0:T(8,128)}, f32[2,800]{1,0:T(2,128)}, f32[1,800]{1,0:T(1,128)}, /*index=5*/f32[1,3200]{1,0:T(1,128)}) custom-call(f32[384,800]{1,0:T(8,128)} %get-tuple-element.171.upstream, f32[384,800]{1,0:T(8,128)} %bitcast.291, ...), custom_call_target="tpu_custom_call" | custom-call | tf_op jit(solution)/shard_map/mlp_backward/pallas_call | solution.py:529
  353.1 5.3 all-to-all-start.4
  358.5 7.3 %fusion.2 = bf16[3200,800]{0,1:T(8,128)(2,1)} fusion(bf16[384,800]{1,0:T(8,128)(2,1)} %get-tuple-element.198, bf16[384,3200]{1,0:T(8,128)(2,1)} %get-tuple-element.199), kind=kOutput, calls=%fused_computation.5 | convolution fusion | flops 1968640000 | bytes 8192000 | tf_op jit(solution)/shard_map/dot_general | solution.py:724
  365.9 5.3 convolution_convert_fusion.1
  378.7 12.6 %kernel_grad.5 = f32[4,56,128]{2,1,0:T(8,128)} custom-call(bf16[48,32,400]{2,1,0:T(8,128)(2,1)} %bitcast.274, bf16[48,3,400]{2,1,0:T(4,128)(2,1)} %copy-done.32, bf16[48,3,400]{2,1,0:T(4,128)(2,1)} %copy-done.33, bf16[48,32,400]{2,1,0:T(8,128)(2,1)} %bitcast.282), custom_call_target="tpu_custom_call" | custom-call | tf_op jit(solution)/shard_map/kernel_grad/pallas_call | solution.py:321
  391.3 7.6 %kernel_grad.4 = f32[7,56,128]{2,1,0:T(8,128)} custom-call(bf16[24,16,800]{2,1,0:T(8,128)(2,1)} %bitcast.298, bf16[24,3,800]{2,1,0:T(4,128)(2,1)} %copy-done.35, bf16[24,3,800]{2,1,0:T(4,128)(2,1)} %copy-done.36, bf16[24,16,800]{2,1,0:T(8,128)(2,1)} %bitcast.294), custom_call_target="tpu_custom_call" | custom-call | tf_op jit(solution)/shard_map/kernel_grad/pallas_call | solution.py:321
  399.7 8.9 %stencil_backward.4 = (bf16[24,16,800]{2,1,0:T(8,128)(2,1)}, f32[1,800]{1,0:T(1,128)}) custom-call(bf16[24,16,800]{2,1,0:T(8,128)(2,1)} %bitcast.295, bf16[24,3,800]{2,1,0:T(4,128)(2,1)} %copy-done.47, bf16[24,3,800]{2,1,0:T(4,128)(2,1)} %copy-done.48, f32[49,800]{1,0:T(8,128)} %reshape.351.refs_2_, f32[24,16,128]{2,1,0:T(8,128)} %broadcast_in_dim.150.refs_3_, ...), custom_call_target="tpu_custom_call" | custom-call | tf_op jit(solution)/shard_map/stencil_backward/pallas_call | solution.py:305
  408.5 7.1 %skip_backward.1.upstream = f32[1536,400]{1,0:T(8,128)} custom-call(bf16[1536,400]{1,0:T(8,128)(2,1)} %bitcast.288, bf16[384,800]{1,0:T(8,128)(2,1)} %bitcast.312, bf16[1200,400]{1,0:T(8,128)(2,1)} %copy.103.merge, bf16[400,800]{1,0:T(8,128)(2,1)} %pad_maximum_fusion.16.refs_1_.widen, bf16[384,96]{1,0:T(8,128)(2,1)} %constant.276.clone.members), custom_call_target="tpu_custom_call" | custom-call | tf_op jit(solution)/shard_map/skip_backward/pallas_call | solution.py:512
  417.1 12.8 %mlp_backward.5 = (bf16[1536,400]{1,0:T(8,128)(2,1)}, bf16[1536,1600]{1,0:T(8,128)(2,1)}, f32[1536,400]{1,0:T(8,128)}, f32[2,400]{1,0:T(2,128)}, f32[1,400]{1,0:T(1,128)}, /*index=5*/f32[1,1600]{1,0:T(1,128)}) custom-call(f32[1536,400]{1,0:T(8,128)} %skip_backward.1.upstream, f32[1536,400]{1,0:T(8,128)} %bitcast.276, ...), custom_call_target="tpu_custom_call" | custom-call | tf_op jit(solution)/shard_map/mlp_backward/pallas_call | solution.py:529
  429.9 11.8 %weight_grads.1 = bf16[2,13,400,128]{3,2,1,0:T(8,128)(2,1)} custom-call(bf16[1536,400]{1,0:T(8,128)(2,1)} %get-tuple-element.189.grad_branch, bf16[1536,400]{1,0:T(8,128)(2,1)} %get-tuple-element.190.normed, bf16[1536,1600]{1,0:T(8,128)(2,1)} %get-tuple-element.191.active, bf16[1536,1600]{1,0:T(8,128)(2,1)} %get-tuple-element.192.grad_hidden), custom_call_target="tpu_custom_call" | custom-call | tf_op jit(solution)/shard_map/weight_grads/pallas_call | solution.py:565
  446.6 4.2 all-to-all-start.5
  451.1 7.9 %all-to-all-done.5 = f32[32,2,400]{2,1,0:T(2,128)S(1)} async-done(((f32[32,2,400]{2,1,0:T(2,128)}), f32[32,2,400]{2,1,0:T(2,128)S(1)}, u32[]{:S(2)}, u32[]{:S(2)}) %all-to-all-start.5) | async-done | bytes 102432 | tf_op jit(solution)/shard_map/all_to_all | solution.py:178
  459.1 3.8 multiply_convert_fusion
  467.6 12.6 %kernel_grad.3 = f32[4,56,128]{2,1,0:T(8,128)} custom-call(bf16[48,32,400]{2,1,0:T(8,128)(2,1)} %bitcast.271, bf16[48,3,400]{2,1,0:T(4,128)(2,1)} %copy-done.30, bf16[48,3,400]{2,1,0:T(4,128)(2,1)} %copy-done.31, bf16[48,32,400]{2,1,0:T(8,128)(2,1)} %bitcast.284), custom_call_target="tpu_custom_call" | custom-call | tf_op jit(solution)/shard_map/kernel_grad/pallas_call | solution.py:321
  488.0 15.3 %stencil_backward.5 = (bf16[48,32,400]{2,1,0:T(8,128)(2,1)}, f32[1,400]{1,0:T(1,128)}) custom-call(bf16[48,32,400]{2,1,0:T(8,128)(2,1)} %bitcast.285, bf16[48,3,400]{2,1,0:T(4,128)(2,1)} %copy-done.43, bf16[48,3,400]{2,1,0:T(4,128)(2,1)} %collective-permute-done.32.refs_1_, f32[49,400]{1,0:T(8,128)} %reshape.349.refs_2_, ...), custom_call_target="tpu_custom_call" | custom-call | tf_op jit(solution)/shard_map/stencil_backward/pallas_call | solution.py:305
  510.7 27.6 %collective-permute-done.37 = bf16[1728,128]{1,0:T(8,128)(2,1)S(1)} collective-permute-done((bf16[1728,128]{1,0:T(8,128)(2,1)S(1)}, bf16[1728,128]{1,0:T(8,128)(2,1)S(1)}, u32[]{:S(2)}, u32[]{:S(2)}) %collective-permute-start.37) | collective-permute-done | bytes 442400 | tf_op jit(solution)/shard_map/ppermute | solution.py:602
  539.2 4.3 collective-permute-done.40
  543.5 6.0 collective-permute-done.38
  555.9 4.5 all-to-all-start.7
  563.6 8.9 %collective-permute-start.44 = (bf16[2,216,128]{2,1,0:T(8,128)(2,1)S(1)}, bf16[2,216,128]{2,1,0:T(8,128)(2,1)S(1)}, u32[]{:S(2)}, u32[]{:S(2)}) collective-permute-start(bf16[2,216,128]{2,1,0:T(8,128)(2,1)S(1)} %fusion.24), channel_id=1, source_target_pairs={{0,2},{1,3},{2,0},{3,1},{4,6},{5,7},{6,4},{7,5},{8,10},{9,11},{10,... | collective-permute-start | bytes 331784 | tf_op jit(solution)/shard_map/ppermute | solution.py:602
  576.8 12.9 %collective-permute-done.45 = bf16[2,216,128]{2,1,0:T(8,128)(2,1)S(1)} collective-permute-done((bf16[2,216,128]{2,1,0:T(8,128)(2,1)S(1)}, bf16[2,216,128]{2,1,0:T(8,128)(2,1)S(1)}, u32[]{:S(2)}, u32[]{:S(2)}) %collective-permute-start.45) | collective-permute-done | bytes 110624 | tf_op jit(solution)/shard_map/ppermute | solution.py:602
  599.9 5.6 collective-permute-done.49
  607.6 7.0 %collective-permute-done.48 = bf16[1728,128]{1,0:T(8,128)(2,1)S(1)} collective-permute-done((bf16[1728,128]{1,0:T(8,128)(2,1)S(1)}, bf16[1728,128]{1,0:T(8,128)(2,1)S(1)}, u32[]{:S(2)}, u32[]{:S(2)}) %collective-permute-start.48) | collective-permute-done | bytes 442400 | tf_op jit(solution)/shard_map/ppermute | solution.py:602
  620.8 9.0 %unpack.1 = (f32[400,1600]{1,0:T(8,128)}, f32[400,1600]{1,0:T(8,128)}) custom-call(s32[1]{0:T(128)} %bitcast.40.core, bf16[6912,128]{1,0:T(8,128)(2,1)} %copy-done.13, bf16[6912,128]{1,0:T(8,128)(2,1)} %collective-permute-done.51.other), custom_call_target="tpu_custom_call" | custom-call | tf_op jit(solution)/shard_map/unpack/pallas_call | solution.py:587
  631.0 28.6 %all-reduce.18.cloned.1.call-done = (bf16[800,3200]{1,0:T(8,128)(2,1)}, bf16[3200,800]{0,1:T(8,128)(2,1)}, bf16[400,400]{1,0:T(8,128)(2,1)}, bf16[400,800]{1,0:T...) async-done(((bf16[800,3200]{1,0:T(8,128)(2,1)}, bf16[3200,800]{0,1:T(8,128)(2,1)}, bf16[400,400]{1,0:T(8,128)(2,1)}, bf16[400,800]{1,0:T(8,128)(2,1)}, ...) | async-done | bytes 13760016 | tf_op jit(solution)/shard_map/psum | solution.py:901
  659.6 7.3 %convert_element_type.242 = f32[800,3200]{1,0:T(8,128)} convert(bf16[800,3200]{1,0:T(8,128)(2,1)} %get-tuple-element.207) | non-fusion elementwise | flops 2560000 | bytes 15360000 | tf_op jit(solution)/shard_map/convert_element_type | solution.py:902
  666.8 4.7 transpose.90
  (502 shorter events, 210.8 us)
Async XLA Ops:
  7.2 57.5 %all-gather.6.cloned.1.call-start = ((), (), s32[]{:S(2)}) async-start(), calls=%async_computation.8 | async-start | bytes 2048000 | tf_op jit(solution)/shard_map/all_gather | solution.py:153
  9.7 141.9 %all-gather.8.cloned.1.call-start = ((), (), s32[]{:S(2)}) async-start(), calls=%async_computation.9 | async-start | bytes 3328000 | tf_op jit(solution)/shard_map/all_gather | solution.py:144
  11.6 16.7 %collective-permute-start = (bf16[13,32,400]{2,1,0:T(8,128)(2,1)S(1)}, bf16[13,32,400]{2,1,0:T(8,128)(2,1)S(1)}, u32[]{:S(2)}, u32[]{:S(2)}) collective-permute-start(bf16[13,32,400]{2,1,0:T(8,128)(2,1)S(1)} %get-tuple-element.232), channel_id=1, source_target_pairs={{0,8},{8,0},{16,24},{24,16},{1,9},{9,1},{17,25},{25,17},{2,10},{10... | collective-permute-start | bytes 998408 | tf_op jit(solution)/shard_map/ppermute | solution.py:31
  14.6 24.9 %collective-permute-start.1 = (bf16[13,32,400]{2,1,0:T(8,128)(2,1)S(1)}, bf16[13,32,400]{2,1,0:T(8,128)(2,1)S(1)}, u32[]{:S(2)}, u32[]{:S(2)}) collective-permute-start(bf16[13,32,400]{2,1,0:T(8,128)(2,1)S(1)} %get-tuple-element.231), channel_id=1, source_target_pairs={{0,16},{8,24},{16,0},{24,8},{1,17},{9,25},{17,1},{25,9},{2,18},{10... | collective-permute-start | bytes 998408 | tf_op jit(solution)/shard_map/ppermute | solution.py:31
  16.1 24.2 %collective-permute-start.2 = (bf16[13,32,400]{2,1,0:T(8,128)(2,1)S(1)}, bf16[13,32,400]{2,1,0:T(8,128)(2,1)S(1)}, u32[]{:S(2)}, u32[]{:S(2)}) collective-permute-start(bf16[13,32,400]{2,1,0:T(8,128)(2,1)S(1)} %get-tuple-element.230), channel_id=1, source_target_pairs={{0,24},{8,16},{16,8},{24,0},{1,25},{9,17},{17,9},{25,1},{2,26},{10... | collective-permute-start | bytes 998408 | tf_op jit(solution)/shard_map/ppermute | solution.py:31
  67.5 26.0 %collective-permute-start.8 = (bf16[1600,400]{0,1:T(8,128)(2,1)S(1)}, bf16[1600,400]{0,1:T(8,128)(2,1)}, u32[]{:S(2)}, u32[]{:S(2)}) collective-permute-start(bf16[1600,400]{0,1:T(8,128)(2,1)S(1)} %copy.99), channel_id=1, source_target_pairs={{0,1},{1,0},{2,3},{3,2},{4,5},{5,4},{6,7},{7,6},{8,9},{9,8},{10,11... | collective-permute-start | bytes 3840008 | tf_op jit(solution)/shard_map/ppermute | solution.py:602
  71.2 11.8 %collective-permute-start.10 = (bf16[100,800]{1,0:T(8,128)(2,1)S(1)}, bf16[100,800]{1,0:T(8,128)(2,1)}, u32[]{:S(2)}, u32[]{:S(2)}) collective-permute-start(bf16[100,800]{1,0:T(8,128)(2,1)S(1)} %copy-done.46), channel_id=1, source_target_pairs={{0,16},{8,24},{16,0},{24,8},{1,17},{9,25},{17,1},{25,9},{2,18},{10... | collective-permute-start | bytes 480008 | tf_op jit(solution)/shard_map/ppermute | solution.py:602
  71.8 18.2 %collective-permute-start.11 = (bf16[100,800]{1,0:T(8,128)(2,1)S(1)}, bf16[100,800]{1,0:T(8,128)(2,1)}, u32[]{:S(2)}, u32[]{:S(2)}) collective-permute-start(bf16[100,800]{1,0:T(8,128)(2,1)S(1)} %copy-done.46), channel_id=1, source_target_pairs={{0,24},{8,16},{16,8},{24,0},{1,25},{9,17},{17,9},{25,1},{2,26},{10... | collective-permute-start | bytes 480008 | tf_op jit(solution)/shard_map/ppermute | solution.py:602
  75.5 16.8 %all-to-all-start = ((f32[32,3,400]{2,1,0:T(4,128)}), f32[32,3,400]{2,1,0:T(4,128)S(1)}, u32[]{:S(2)}, u32[]{:S(2)}) async-start(f32[32,3,400]{2,1,0:T(4,128)} %broadcast_in_dim.149), calls=%async_computation | async-start | bytes 524288 | tf_op jit(solution)/shard_map/all_to_all | solution.py:178
  78.5 144.7 %all-gather.12.cloned.1.call-start = ((), (), s32[]{:S(2)}) async-start(), calls=%async_computation.11 | async-start | bytes 1730560 | tf_op jit(solution)/shard_map/all_gather | solution.py:858
  79.5 39.1 %collective-permute-start.5 = (bf16[400,800]{1,0:T(8,128)(2,1)}, bf16[400,800]{1,0:T(8,128)(2,1)}, u32[]{:S(2)}, u32[]{:S(2)}) collective-permute-start(bf16[400,800]{1,0:T(8,128)(2,1)} %dynamic-slice_bitcast_fusion.1), channel_id=1, source_target_pairs={{0,8},{8,0},{16,24},{24,16},{1,9},{9,1},{17,25},{25,17},{2,10},{10... | collective-permute-start | bytes 1920008 | tf_op jit(solution)/shard_map/ppermute | solution.py:602
  81.4 37.2 %collective-permute-start.6 = (bf16[400,800]{1,0:T(8,128)(2,1)}, bf16[400,800]{1,0:T(8,128)(2,1)}, u32[]{:S(2)}, u32[]{:S(2)}) collective-permute-start(bf16[400,800]{1,0:T(8,128)(2,1)} %dynamic-slice_bitcast_fusion.1), channel_id=1, source_target_pairs={{0,16},{8,24},{16,0},{24,8},{1,17},{9,25},{17,1},{25,9},{2,18},{10... | collective-permute-start | bytes 1920008 | tf_op jit(solution)/shard_map/ppermute | solution.py:602
  83.0 51.3 %collective-permute-start.7 = (bf16[400,800]{1,0:T(8,128)(2,1)}, bf16[400,800]{1,0:T(8,128)(2,1)}, u32[]{:S(2)}, u32[]{:S(2)}) collective-permute-start(bf16[400,800]{1,0:T(8,128)(2,1)} %dynamic-slice_bitcast_fusion.1), channel_id=1, source_target_pairs={{0,24},{8,16},{16,8},{24,0},{1,25},{9,17},{17,9},{25,1},{2,26},{10... | collective-permute-start | bytes 1920008 | tf_op jit(solution)/shard_map/ppermute | solution.py:602
  151.6 29.1 %collective-permute-start.14 = (bf16[800,1664]{1,0:T(8,128)(2,1)}, bf16[800,1664]{1,0:T(8,128)(2,1)}, u32[]{:S(2)}, u32[]{:S(2)}) collective-permute-start(bf16[800,1664]{1,0:T(8,128)(2,1)} %all-gather.8.cloned.1.call-done.mine), channel_id=1, source_target_pairs={{0,1},{1,0},{2,3},{3,2},{4,5},{5,4},{6,7},{7,6},{8,9},{9,8},{10,11... | collective-permute-start | bytes 7987208 | tf_op jit(solution)/shard_map/ppermute | solution.py:602
  155.1 17.9 %collective-permute-start.15 = (bf16[3,400,800]{2,1,0:T(8,128)(2,1)S(1)}, bf16[3,400,800]{2,1,0:T(8,128)(2,1)}, u32[]{:S(2)}, u32[]{:S(2)}) collective-permute-start(bf16[3,400,800]{2,1,0:T(8,128)(2,1)S(1)} %pad_maximum_fusion.3.mine), channel_id=1, source_target_pairs={{0,1},{1,0},{2,3},{3,2},{4,5},{5,4},{6,7},{7,6},{8,9},{9,8},{10,11... | collective-permute-start | bytes 5760008 | tf_op jit(solution)/shard_map/ppermute | solution.py:602
  161.4 26.4 %all-to-all-start.1 = ((f32[32,3,800]{2,1,0:T(4,128)}), f32[32,3,800]{2,1,0:T(4,128)S(1)}, u32[]{:S(2)}, u32[]{:S(2)}) async-start(f32[32,3,800]{2,1,0:T(4,128)} %broadcast_in_dim.152), calls=%async_computation.1 | async-start | bytes 917504 | tf_op jit(solution)/shard_map/all_to_all | solution.py:178
  164.5 96.8 %all-gather.10.cloned.1.call-start = ((), (), s32[]{:S(2)}) async-start(), calls=%async_computation.10 | async-start | bytes 2048000 | tf_op jit(solution)/shard_map/all_gather | solution.py:859
  166.9 36.5 %collective-permute-start.16 = (bf16[304,400]{0,1:T(8,128)(2,1)}, bf16[304,400]{0,1:T(8,128)(2,1)}, u32[]{:S(2)}, u32[]{:S(2)}) collective-permute-start(bf16[304,400]{0,1:T(8,128)(2,1)} %get-tuple-element.288), channel_id=1, source_target_pairs={{0,8},{8,0},{16,24},{24,16},{1,9},{9,1},{17,25},{25,17},{2,10},{10... | collective-permute-start | bytes 729608 | tf_op jit(solution)/shard_map/ppermute | solution.py:602
  168.7 35.0 %collective-permute-start.17 = (bf16[304,400]{0,1:T(8,128)(2,1)}, bf16[304,400]{0,1:T(8,128)(2,1)}, u32[]{:S(2)}, u32[]{:S(2)}) collective-permute-start(bf16[304,400]{0,1:T(8,128)(2,1)} %get-tuple-element.288), channel_id=1, source_target_pairs={{0,16},{8,24},{16,0},{24,8},{1,17},{9,25},{17,1},{25,9},{2,18},{10... | collective-permute-start | bytes 729608 | tf_op jit(solution)/shard_map/ppermute | solution.py:602
  170.2 33.5 %collective-permute-start.18 = (bf16[304,400]{0,1:T(8,128)(2,1)}, bf16[304,400]{0,1:T(8,128)(2,1)}, u32[]{:S(2)}, u32[]{:S(2)}) collective-permute-start(bf16[304,400]{0,1:T(8,128)(2,1)} %get-tuple-element.288), channel_id=1, source_target_pairs={{0,24},{8,16},{16,8},{24,0},{1,25},{9,17},{17,9},{25,1},{2,26},{10... | collective-permute-start | bytes 729608 | tf_op jit(solution)/shard_map/ppermute | solution.py:602
  173.1 69.6 %collective-permute-start.24 = (bf16[12,32,400]{2,1,0:T(8,128)(2,1)}, bf16[12,32,400]{2,1,0:T(8,128)(2,1)}, u32[]{:S(2)}, u32[]{:S(2)}) collective-permute-start(bf16[12,32,400]{2,1,0:T(8,128)(2,1)} %get-tuple-element.252), channel_id=1, source_target_pairs={{0,8},{8,0},{16,24},{24,16},{1,9},{9,1},{17,25},{25,17},{2,10},{10... | collective-permute-start | bytes 921608 | tf_op jit(solution)/shard_map/ppermute | solution.py:31
  180.7 61.9 %collective-permute-start.25 = (bf16[12,32,400]{2,1,0:T(8,128)(2,1)}, bf16[12,32,400]{2,1,0:T(8,128)(2,1)}, u32[]{:S(2)}, u32[]{:S(2)}) collective-permute-start(bf16[12,32,400]{2,1,0:T(8,128)(2,1)} %get-tuple-element.251), channel_id=1, source_target_pairs={{0,16},{8,24},{16,0},{24,8},{1,17},{9,25},{17,1},{25,9},{2,18},{10... | collective-permute-start | bytes 921608 | tf_op jit(solution)/shard_map/ppermute | solution.py:31
  203.4 39.3 %collective-permute-start.26 = (bf16[12,32,400]{2,1,0:T(8,128)(2,1)}, bf16[12,32,400]{2,1,0:T(8,128)(2,1)}, u32[]{:S(2)}, u32[]{:S(2)}) collective-permute-start(bf16[12,32,400]{2,1,0:T(8,128)(2,1)} %get-tuple-element.250), channel_id=1, source_target_pairs={{0,24},{8,16},{16,8},{24,0},{1,25},{9,17},{17,9},{25,1},{2,26},{10... | collective-permute-start | bytes 921608 | tf_op jit(solution)/shard_map/ppermute | solution.py:31
  244.8 15.2 %all-to-all-start.2 = ((f32[32,3,400]{2,1,0:T(4,128)}), f32[32,3,400]{2,1,0:T(4,128)S(1)}, u32[]{:S(2)}, u32[]{:S(2)}) async-start(f32[32,3,400]{2,1,0:T(4,128)} %broadcast_in_dim.153), calls=%async_computation.2 | async-start | bytes 524288 | tf_op jit(solution)/shard_map/all_to_all | solution.py:178
  287.3 16.8 %all-to-all-start.3 = ((f32[32,2,400]{2,1,0:T(2,128)}), f32[32,2,400]{2,1,0:T(2,128)S(1)}, u32[]{:S(2)}, u32[]{:S(2)}) async-start(f32[32,2,400]{2,1,0:T(2,128)} %broadcast_in_dim.154), calls=%async_computation.3 | async-start | bytes 262144 | tf_op jit(solution)/shard_map/all_to_all | solution.py:178
  290.9 21.2 %collective-permute-start.21 = (bf16[12,32,400]{2,1,0:T(8,128)(2,1)}, bf16[12,32,400]{2,1,0:T(8,128)(2,1)S(1)}, u32[]{:S(2)}, u32[]{:S(2)}) collective-permute-start(bf16[12,32,400]{2,1,0:T(8,128)(2,1)} %get-tuple-element.261), channel_id=1, source_target_pairs={{0,8},{8,0},{16,24},{24,16},{1,9},{9,1},{17,25},{25,17},{2,10},{10... | collective-permute-start | bytes 921608 | tf_op jit(solution)/shard_map/ppermute | solution.py:55
  292.7 19.5 %collective-permute-start.22 = (bf16[12,32,400]{2,1,0:T(8,128)(2,1)}, bf16[12,32,400]{2,1,0:T(8,128)(2,1)S(1)}, u32[]{:S(2)}, u32[]{:S(2)}) collective-permute-start(bf16[12,32,400]{2,1,0:T(8,128)(2,1)} %get-tuple-element.260), channel_id=1, source_target_pairs={{0,16},{8,24},{16,0},{24,8},{1,17},{9,25},{17,1},{25,9},{2,18},{10... | collective-permute-start | bytes 921608 | tf_op jit(solution)/shard_map/ppermute | solution.py:55
  294.1 18.8 %collective-permute-start.23 = (bf16[12,32,400]{2,1,0:T(8,128)(2,1)}, bf16[12,32,400]{2,1,0:T(8,128)(2,1)}, u32[]{:S(2)}, u32[]{:S(2)}) collective-permute-start(bf16[12,32,400]{2,1,0:T(8,128)(2,1)} %get-tuple-element.259), channel_id=1, source_target_pairs={{0,24},{8,16},{16,8},{24,0},{1,25},{9,17},{17,9},{25,1},{2,26},{10... | collective-permute-start | bytes 921608 | tf_op jit(solution)/shard_map/ppermute | solution.py:55
  353.1 18.0 %all-to-all-start.4 = ((f32[32,2,800]{2,1,0:T(2,128)}), f32[32,2,800]{2,1,0:T(2,128)S(1)}, u32[]{:S(2)}, u32[]{:S(2)}) async-start(f32[32,2,800]{2,1,0:T(2,128)} %broadcast_in_dim.155), calls=%async_computation.4 | async-start | bytes 458752 | tf_op jit(solution)/shard_map/all_to_all | solution.py:178
  358.4 301.1 %all-reduce.18.cloned.1.call-start = ((), (), s32[]{:S(2)}) async-start(), calls=%async_computation.12 | async-start | bytes 28057600 | tf_op jit(solution)/shard_map/psum | solution.py:901
  373.4 25.5 %collective-permute-start.29 = (bf16[24,3,800]{2,1,0:T(4,128)(2,1)S(1)}, bf16[24,3,800]{2,1,0:T(4,128)(2,1)S(1)}, u32[]{:S(2)}, u32[]{:S(2)}) collective-permute-start(bf16[24,3,800]{2,1,0:T(4,128)(2,1)S(1)} %get-tuple-element.275), channel_id=1, source_target_pairs={{0,1},{1,2},{2,3},{3,4},{4,5},{5,6},{6,7},{7,0},{8,9},{9,10},{10,1... | collective-permute-start | bytes 345608 | tf_op jit(solution)/shard_map/ppermute | solution.py:163
  373.7 25.2 %collective-permute-start.30 = (bf16[24,3,800]{2,1,0:T(4,128)(2,1)S(1)}, bf16[24,3,800]{2,1,0:T(4,128)(2,1)S(1)}, u32[]{:S(2)}, u32[]{:S(2)}) collective-permute-start(bf16[24,3,800]{2,1,0:T(4,128)(2,1)S(1)} %get-tuple-element.274), channel_id=1, source_target_pairs={{1,0},{2,1},{3,2},{4,3},{5,4},{6,5},{7,6},{0,7},{9,8},{10,9},{11,1... | collective-permute-start | bytes 345608 | tf_op jit(solution)/shard_map/ppermute | solution.py:164
  445.9 34.3 %collective-permute-start.36 = (bf16[6912,128]{1,0:T(8,128)(2,1)}, bf16[6912,128]{1,0:T(8,128)(2,1)}, u32[]{:S(2)}, u32[]{:S(2)}) collective-permute-start(bf16[6912,128]{1,0:T(8,128)(2,1)} %dynamic-slice_bitcast_fusion), channel_id=1, source_target_pairs={{0,1},{1,0},{2,3},{3,2},{4,5},{5,4},{6,7},{7,6},{8,9},{9,8},{10,11... | collective-permute-start | bytes 5308424 | tf_op jit(solution)/shard_map/ppermute | solution.py:602
  446.6 12.3 %all-to-all-start.5 = ((f32[32,2,400]{2,1,0:T(2,128)}), f32[32,2,400]{2,1,0:T(2,128)S(1)}, u32[]{:S(2)}, u32[]{:S(2)}) async-start(f32[32,2,400]{2,1,0:T(2,128)} %broadcast_in_dim.156), calls=%async_computation.5 | async-start | bytes 262144 | tf_op jit(solution)/shard_map/all_to_all | solution.py:178
  464.0 23.3 %collective-permute-start.31 = (bf16[48,3,400]{2,1,0:T(4,128)(2,1)}, bf16[48,3,400]{2,1,0:T(4,128)(2,1)S(1)}, u32[]{:S(2)}, u32[]{:S(2)}) collective-permute-start(bf16[48,3,400]{2,1,0:T(4,128)(2,1)} %get-tuple-element.243), channel_id=1, source_target_pairs={{0,1},{1,2},{2,3},{3,4},{4,5},{5,6},{6,7},{7,0},{8,9},{9,10},{10,1... | collective-permute-start | bytes 345608 | tf_op jit(solution)/shard_map/ppermute | solution.py:163
  464.3 23.0 %collective-permute-start.32 = (bf16[48,3,400]{2,1,0:T(4,128)(2,1)}, bf16[48,3,400]{2,1,0:T(4,128)(2,1)}, u32[]{:S(2)}, u32[]{:S(2)}) collective-permute-start(bf16[48,3,400]{2,1,0:T(4,128)(2,1)} %get-tuple-element.242), channel_id=1, source_target_pairs={{1,0},{2,1},{3,2},{4,3},{5,4},{6,5},{7,6},{0,7},{9,8},{10,9},{11,1... | collective-permute-start | bytes 345608 | tf_op jit(solution)/shard_map/ppermute | solution.py:164
  482.4 27.9 %collective-permute-start.39 = (bf16[1728,128]{1,0:T(8,128)(2,1)S(1)}, bf16[1728,128]{1,0:T(8,128)(2,1)S(1)}, u32[]{:S(2)}, u32[]{:S(2)}) collective-permute-start(bf16[1728,128]{1,0:T(8,128)(2,1)S(1)} %dynamic-slice_bitcast_fusion.2), channel_id=1, source_target_pairs={{0,16},{8,24},{16,0},{24,8},{1,17},{9,25},{17,1},{25,9},{2,18},{10... | collective-permute-start | bytes 1327112 | tf_op jit(solution)/shard_map/ppermute | solution.py:602
  484.5 70.5 %all-to-all-start.6 = ((f32[32,32,128]{2,1,0:T(8,128)}), f32[32,32,128]{2,1,0:T(8,128)S(1)}, u32[]{:S(2)}, u32[]{:S(2)}) async-start(f32[32,32,128]{2,1,0:T(8,128)} %bitcast.104), calls=%async_computation.6 | async-start | bytes 1048576 | tf_op jit(solution)/shard_map/all_to_all | solution.py:718
  504.8 49.1 %collective-permute-start.35 = (bf16[12,32,400]{2,1,0:T(8,128)(2,1)S(1)}, bf16[12,32,400]{2,1,0:T(8,128)(2,1)S(1)}, u32[]{:S(2)}, u32[]{:S(2)}) collective-permute-start(bf16[12,32,400]{2,1,0:T(8,128)(2,1)S(1)} %get-tuple-element.239), channel_id=1, source_target_pairs={{0,24},{8,16},{16,8},{24,0},{1,25},{9,17},{17,9},{25,1},{2,26},{10... | collective-permute-start | bytes 921608 | tf_op jit(solution)/shard_map/ppermute | solution.py:55
  507.6 47.1 %collective-permute-start.33 = (bf16[12,32,400]{2,1,0:T(8,128)(2,1)S(1)}, bf16[12,32,400]{2,1,0:T(8,128)(2,1)S(1)}, u32[]{:S(2)}, u32[]{:S(2)}) collective-permute-start(bf16[12,32,400]{2,1,0:T(8,128)(2,1)S(1)} %get-tuple-element.241), channel_id=1, source_target_pairs={{0,8},{8,0},{16,24},{24,16},{1,9},{9,1},{17,25},{25,17},{2,10},{10... | collective-permute-start | bytes 921608 | tf_op jit(solution)/shard_map/ppermute | solution.py:55
  508.1 46.5 %collective-permute-start.34 = (bf16[12,32,400]{2,1,0:T(8,128)(2,1)S(1)}, bf16[12,32,400]{2,1,0:T(8,128)(2,1)S(1)}, u32[]{:S(2)}, u32[]{:S(2)}) collective-permute-start(bf16[12,32,400]{2,1,0:T(8,128)(2,1)S(1)} %get-tuple-element.240), channel_id=1, source_target_pairs={{0,16},{8,24},{16,0},{24,8},{1,17},{9,25},{17,1},{25,9},{2,18},{10... | collective-permute-start | bytes 921608 | tf_op jit(solution)/shard_map/ppermute | solution.py:55
  508.4 29.9 %collective-permute-start.37 = (bf16[1728,128]{1,0:T(8,128)(2,1)S(1)}, bf16[1728,128]{1,0:T(8,128)(2,1)S(1)}, u32[]{:S(2)}, u32[]{:S(2)}) collective-permute-start(bf16[1728,128]{1,0:T(8,128)(2,1)S(1)} %dynamic-slice_bitcast_fusion.3), channel_id=1, source_target_pairs={{0,8},{8,0},{16,24},{24,16},{1,9},{9,1},{17,25},{25,17},{2,10},{10... | collective-permute-start | bytes 1327112 | tf_op jit(solution)/shard_map/ppermute | solution.py:602
  510.4 33.1 %collective-permute-start.40 = (bf16[864,128]{1,0:T(8,128)(2,1)S(1)}, bf16[864,128]{1,0:T(8,128)(2,1)S(1)}, u32[]{:S(2)}, u32[]{:S(2)}) collective-permute-start(bf16[864,128]{1,0:T(8,128)(2,1)S(1)} %dynamic-slice_bitcast_fusion.30), channel_id=1, source_target_pairs={{0,8},{8,0},{16,24},{24,16},{1,9},{9,1},{17,25},{25,17},{2,10},{10... | collective-permute-start | bytes 663560 | tf_op jit(solution)/shard_map/ppermute | solution.py:602
  555.9 38.2 %all-to-all-start.7 = ((f32[32,32,128]{2,1,0:T(8,128)}), f32[32,32,128]{2,1,0:T(8,128)S(1)}, u32[]{:S(2)}, u32[]{:S(2)}) async-start(f32[32,32,128]{2,1,0:T(8,128)} %broadcast_in_dim.157), calls=%async_computation.7 | async-start | bytes 1048576 | tf_op jit(solution)/shard_map/all_to_all | solution.py:720
  563.6 13.2 %collective-permute-start.44 = (bf16[2,216,128]{2,1,0:T(8,128)(2,1)S(1)}, bf16[2,216,128]{2,1,0:T(8,128)(2,1)S(1)}, u32[]{:S(2)}, u32[]{:S(2)}) collective-permute-start(bf16[2,216,128]{2,1,0:T(8,128)(2,1)S(1)} %fusion.24), channel_id=1, source_target_pairs={{0,2},{1,3},{2,0},{3,1},{4,6},{5,7},{6,4},{7,5},{8,10},{9,11},{10,... | collective-permute-start | bytes 331784 | tf_op jit(solution)/shard_map/ppermute | solution.py:602
  572.5 17.1 %collective-permute-start.45 = (bf16[2,216,128]{2,1,0:T(8,128)(2,1)S(1)}, bf16[2,216,128]{2,1,0:T(8,128)(2,1)S(1)}, u32[]{:S(2)}, u32[]{:S(2)}) collective-permute-start(bf16[2,216,128]{2,1,0:T(8,128)(2,1)S(1)} %fusion.24), channel_id=1, source_target_pairs={{0,4},{1,5},{2,6},{3,7},{4,0},{5,1},{6,2},{7,3},{8,12},{9,13},{10,... | collective-permute-start | bytes 331784 | tf_op jit(solution)/shard_map/ppermute | solution.py:602
  575.3 14.4 %collective-permute-start.46 = (bf16[2,216,128]{2,1,0:T(8,128)(2,1)S(1)}, bf16[2,216,128]{2,1,0:T(8,128)(2,1)S(1)}, u32[]{:S(2)}, u32[]{:S(2)}) collective-permute-start(bf16[2,216,128]{2,1,0:T(8,128)(2,1)S(1)} %fusion.24), channel_id=1, source_target_pairs={{0,6},{1,7},{2,4},{3,5},{4,2},{5,3},{6,0},{7,1},{8,14},{9,15},{10,... | collective-permute-start | bytes 331784 | tf_op jit(solution)/shard_map/ppermute | solution.py:602
  597.5 17.1 %collective-permute-start.48 = (bf16[1728,128]{1,0:T(8,128)(2,1)S(1)}, bf16[1728,128]{1,0:T(8,128)(2,1)S(1)}, u32[]{:S(2)}, u32[]{:S(2)}) collective-permute-start(bf16[1728,128]{1,0:T(8,128)(2,1)S(1)} %maximum_select_fusion.2), channel_id=1, source_target_pairs={{0,8},{8,0},{16,24},{24,16},{1,9},{9,1},{17,25},{25,17},{2,10},{10... | collective-permute-start | bytes 1327112 | tf_op jit(solution)/shard_map/ppermute | solution.py:602
  (115 other events, 741.8 us)
Sparse Core Ops, SparseCore 0:
  10.5 47.0 all-gather.5
  60.0 66.6 all-gather.7
  153.3 43.3 all-gather.11
  198.4 35.9 all-gather.9
  378.8 280.6 all-reduce.17
